TPU v7x, 512 devices: a whole 4x8x8 slice. The times are simulated.
512 devices in a mesh: ens: 16 (over x_lo, y), lat: 32 (over z, x_hi, core).
Axes of the slice: x: 4 (x_hi: 2, x_lo: 2; x = x_hi * 2 + x_lo), y: 8, z: 8, core: 2. Of those that a mesh axis runs over, the one named last changes fastest.
Arguments:
- latent_fields: bfloat16 [16, 96, 256, 128], P('ens', 'lat'), may hold values from -6 to 6
- target_fields: bfloat16 [96, 72, 128], P('lat'), may hold values from -9 to 9
- filters: bfloat16 [3, 256, 256], replicated, may hold values from -0.375 to 0.375
- decoder: bfloat16 [256, 72], replicated, may hold values from -0.375 to 0.375
- cycle_basis: float32 [96, 3, 10], replicated, may hold values from -1.8 to 1.8
- cycle_offsets: int32 [96, 10], replicated, may hold values from -8 to 8
Outputs:
- latent_grad: bfloat16 [16, 96, 256, 128], P('ens', 'lat')
- filter_grad: float32 [256, 3, 256], P('lat', None, 'ens')
Inputs may be any that keep to these rules, and one draw needn't show every extreme that they name: `cycle_offsets`: a tap's longitude offset is the same for every longitude of its cycle.
All inputs are finite; a program needn't handle non-finite values.
Results may differ from a plain program's by a relative error of at most 0.022.
Values may be sent and summed in bfloat16 or wider, within the bound.
No kernel may reach another device: no remote copies, remote signals or barrier semaphores. Data moves between devices by JAX's collectives and lax.ppermute only.
A program may use at most 64 MiB of HBM per device.

v0:
```python
import math

import jax
import jax.numpy as jnp
from jax import lax
from jax.sharding import PartitionSpec as P

HALO = 2
SIDE = 2


DELTA = 0.25


def with_halo(block, sides, width):
    for axis, dim in sides:
        count = lax.axis_size(axis)
        forward = [(i, i + 1) for i in range(count - 1)]
        backward = [(target, source) for source, target in forward]
        low = lax.ppermute(
            lax.slice_in_dim(block, block.shape[dim] - width, None, axis=dim), axis, forward
        )
        high = lax.ppermute(lax.slice_in_dim(block, 0, width, axis=dim), axis, backward)
        block = jnp.concatenate([low, block, high], axis=dim)
    return block


def from_behind(shard, axis, by):
    count = lax.axis_size(axis)
    return lax.ppermute(shard, axis, [(i, (i + by) % count) for i in range(count)])


def smooth_slope(differ):
    return differ / jnp.sqrt(differ * differ + DELTA * DELTA)


def roll_rows(source, starts):
    lon_count = source.shape[-1]
    doubled = jnp.concatenate([source, source], axis=-1)
    last_axis = source.ndim - 2

    def one_row(row, begin):
        return lax.dynamic_slice_in_dim(row, begin, lon_count, last_axis)

    return jax.vmap(one_row)(doubled, jnp.mod(starts, lon_count))


def body(latent_fields, target_fields, filters, decoder, cycle_basis, cycle_offsets):
    member_field = latent_fields[0]
    band_rows, channels, lon_count = member_field.shape
    kernels = filters.shape[0]
    tap_count = cycle_basis.shape[2]
    members = lax.axis_size("ens")
    lat_count = band_rows * lax.axis_size("lat")
    first_cycle = lax.axis_index("lat") * band_rows
    basis_padded = jnp.pad(cycle_basis, ((HALO, HALO), (0, 0), (0, 0)))
    offsets_padded = jnp.pad(cycle_offsets, ((HALO, HALO), (0, 0)))
    band_basis = lax.dynamic_slice_in_dim(basis_padded, first_cycle, band_rows + 2 * HALO, 0)
    band_offsets = lax.dynamic_slice_in_dim(offsets_padded, first_cycle, band_rows + 2 * HALO, 0)
    wide_field = with_halo(member_field, (("lat", 0),), HALO)
    projected = jnp.einsum(
        "icj,kcd->ikdj", wide_field, filters, preferred_element_type=jnp.float32
    ).astype(jnp.bfloat16)
    conv_out = jnp.zeros((band_rows, channels, lon_count), jnp.float32)
    for tap_index in range(tap_count):
        row_step = tap_index // SIDE - HALO
        source = projected[HALO + row_step : HALO + row_step + band_rows]
        shifts = band_offsets[HALO : HALO + band_rows, tap_index]
        moved = roll_rows(source, shifts)
        weights = band_basis[HALO : HALO + band_rows, :, tap_index]
        conv_out = conv_out + jnp.sum(weights[:, :, None, None] * moved, axis=1)
    hidden = (member_field.astype(jnp.float32) + conv_out).astype(jnp.bfloat16)
    predicted = jnp.einsum("icj,cv->ivj", hidden, decoder, preferred_element_type=jnp.float32)
    rounded = predicted.astype(jnp.bfloat16)
    own_wide = rounded.astype(jnp.float32)
    empty_sum = jnp.zeros(predicted.shape, jnp.float32)

    def pass_step(turn, carry):
        visitor, running = carry
        visitor = from_behind(visitor, "ens", 1)
        return (visitor, running + smooth_slope(own_wide - visitor.astype(jnp.float32)))

    _, pair_sum = lax.fori_loop(0, members - 1, pass_step, (rounded, empty_sum))
    cycle_index = (first_cycle + jnp.arange(band_rows, dtype=jnp.int32)).astype(jnp.float32)
    area = jnp.cos(jnp.pi * (cycle_index + 0.5) / lat_count - jnp.pi / 2)
    pred_grad = area[:, None, None] * (
        smooth_slope(predicted - target_fields.astype(jnp.float32)) - pair_sum / (members - 1)
    )
    pred_grad = pred_grad.astype(jnp.bfloat16)
    grad_hidden = jnp.einsum(
        "ivj,cv->icj", pred_grad, decoder, preferred_element_type=jnp.float32
    ).astype(jnp.bfloat16)
    grad_wide = with_halo(grad_hidden, (("lat", 0),), HALO)
    adjoint = jnp.zeros((band_rows, kernels, channels, lon_count), jnp.float32)
    for tap_index in range(tap_count):
        row_step = tap_index // SIDE - HALO
        start = HALO - row_step
        source = grad_wide[start : start + band_rows]
        weights = band_basis[start : start + band_rows, :, tap_index]
        shifts = band_offsets[start : start + band_rows, tap_index]
        moved = roll_rows(source, 0 - shifts)
        adjoint = adjoint + weights[:, :, None, None] * moved[:, None]
    adjoint = adjoint.astype(jnp.bfloat16)
    latent_grad = grad_hidden.astype(jnp.float32) + jnp.einsum(
        "ikdj,kcd->icj", adjoint, filters, preferred_element_type=jnp.float32
    )
    latent_grad = latent_grad.astype(jnp.bfloat16)
    owned_rows = lax.psum_scatter(
        jnp.einsum(
            "icj,ikdj->ckd", member_field, adjoint, preferred_element_type=jnp.float32
        ).astype(jnp.bfloat16),
        "lat",
        scatter_dimension=0,
        tiled=True,
    ).astype(jnp.float32)
    owned = lax.psum_scatter(owned_rows, "ens", scatter_dimension=2, tiled=True)
    factor = 1.0 / math.sqrt(members * lat_count * lon_count)
    return (latent_grad[None], owned * factor)


def solution(mesh):
    placed = (P("ens", "lat", None, None), P("lat", None, None), P(), P(), P(), P())
    return jax.shard_map(
        body,
        mesh=mesh,
        in_specs=placed,
        out_specs=(P("ens", "lat", None, None), P("lat", None, "ens")),
        check_vma=False,
    )
```

profile of v0, /device:TPU:6, one launch (start us, length us, event | category | flops | bytes accessed | tf_op | source)
XLA Modules:
  0.0 619.5 jit_solution(1493035695213395755)
XLA Ops:
  10.3 5.1 collective-permute-start.2
  31.0 2.4 gather_fusion.8
  37.1 2.4 gather_fusion.5
  42.9 2.4 gather_fusion.7
  53.1 2.4 gather_fusion.2
  56.5 2.4 gather_fusion.1
  58.9 2.4 gather_fusion
  67.0 13.4 %multiply_reduce_fusion.7 = f32[3,256,128]{1,2,0:T(8,128)S(1)} fusion(bf16[3,3,256,128]{2,1,3,0:T(4,128)(2,1)S(1)} %copy-done.5, f32[3,3]{1,0:T(4,128)S(1)} %bitcast.141), kind=kLoop, calls=%fused_computation.30 | loop fusion | flops 786432 | bytes 983076 | tf_op jit(solution)/shard_map/reduce_sum | solution.py:71
  85.3 123.9 %while.13 = (s32[]{:T(128)}, bf16[3,72,128]{2,1,0:T(8,128)(2,1)S(1)}, f32[3,72,128]{2,1,0:T(8,128)S(1)}, f32[3,72,128]{2,1,0:T(8,128)S(1)}, s32[]{:T(128)}, /*index=5*/s32[]{:T(128)}) while((s32[]{:T(128)}, bf16[3,72,128]{2,1,0:T(8,128)(2,1)S(1)}, f32[3,72,128]{2,1,0:T(8,128)S(1)}, f32[3,72,128]{2,1,0:T(8,128)S(1)}, s32[]{:T(128)}, ...), condition=%wide.region_11.12_spmd.clone, body=%wide.region_10.11_spmd.clone.sunk | while | flops 193539 | bytes 718967 | solution.py:83
  85.3 3.5 collective-permute-start
  88.8 4.7 collective-permute-done
  95.5 6.2 %collective-permute-done = bf16[3,72,128]{2,1,0:T(8,128)(2,1)S(1)} collective-permute-done((bf16[3,72,128]{2,1,0:T(8,128)(2,1)S(1)}, bf16[3,72,128]{2,1,0:T(8,128)(2,1)S(1)}, u32[]{:S(2)}, u32[]{:S(2)}) %collective-permute-start) | collective-permute-done | bytes 55328 | tf_op jit(solution)/shard_map/while/body/eval_jaxpr/ppermute | solution.py:30
  103.7 6.2 %collective-permute-done = bf16[3,72,128]{2,1,0:T(8,128)(2,1)S(1)} collective-permute-done((bf16[3,72,128]{2,1,0:T(8,128)(2,1)S(1)}, bf16[3,72,128]{2,1,0:T(8,128)(2,1)S(1)}, u32[]{:S(2)}, u32[]{:S(2)}) %collective-permute-start) | collective-permute-done | bytes 55328 | tf_op jit(solution)/shard_map/while/body/eval_jaxpr/ppermute | solution.py:30
  112.0 6.2 %collective-permute-done = bf16[3,72,128]{2,1,0:T(8,128)(2,1)S(1)} collective-permute-done((bf16[3,72,128]{2,1,0:T(8,128)(2,1)S(1)}, bf16[3,72,128]{2,1,0:T(8,128)(2,1)S(1)}, u32[]{:S(2)}, u32[]{:S(2)}) %collective-permute-start) | collective-permute-done | bytes 55328 | tf_op jit(solution)/shard_map/while/body/eval_jaxpr/ppermute | solution.py:30
  120.2 6.2 %collective-permute-done = bf16[3,72,128]{2,1,0:T(8,128)(2,1)S(1)} collective-permute-done((bf16[3,72,128]{2,1,0:T(8,128)(2,1)S(1)}, bf16[3,72,128]{2,1,0:T(8,128)(2,1)S(1)}, u32[]{:S(2)}, u32[]{:S(2)}) %collective-permute-start) | collective-permute-done | bytes 55328 | tf_op jit(solution)/shard_map/while/body/eval_jaxpr/ppermute | solution.py:30
  128.4 6.4 %collective-permute-done = bf16[3,72,128]{2,1,0:T(8,128)(2,1)S(1)} collective-permute-done((bf16[3,72,128]{2,1,0:T(8,128)(2,1)S(1)}, bf16[3,72,128]{2,1,0:T(8,128)(2,1)S(1)}, u32[]{:S(2)}, u32[]{:S(2)}) %collective-permute-start) | collective-permute-done | bytes 55328 | tf_op jit(solution)/shard_map/while/body/eval_jaxpr/ppermute | solution.py:30
  136.9 6.2 %collective-permute-done = bf16[3,72,128]{2,1,0:T(8,128)(2,1)S(1)} collective-permute-done((bf16[3,72,128]{2,1,0:T(8,128)(2,1)S(1)}, bf16[3,72,128]{2,1,0:T(8,128)(2,1)S(1)}, u32[]{:S(2)}, u32[]{:S(2)}) %collective-permute-start) | collective-permute-done | bytes 55328 | tf_op jit(solution)/shard_map/while/body/eval_jaxpr/ppermute | solution.py:30
  145.1 6.2 %collective-permute-done = bf16[3,72,128]{2,1,0:T(8,128)(2,1)S(1)} collective-permute-done((bf16[3,72,128]{2,1,0:T(8,128)(2,1)S(1)}, bf16[3,72,128]{2,1,0:T(8,128)(2,1)S(1)}, u32[]{:S(2)}, u32[]{:S(2)}) %collective-permute-start) | collective-permute-done | bytes 55328 | tf_op jit(solution)/shard_map/while/body/eval_jaxpr/ppermute | solution.py:30
  153.4 6.2 %collective-permute-done = bf16[3,72,128]{2,1,0:T(8,128)(2,1)S(1)} collective-permute-done((bf16[3,72,128]{2,1,0:T(8,128)(2,1)S(1)}, bf16[3,72,128]{2,1,0:T(8,128)(2,1)S(1)}, u32[]{:S(2)}, u32[]{:S(2)}) %collective-permute-start) | collective-permute-done | bytes 55328 | tf_op jit(solution)/shard_map/while/body/eval_jaxpr/ppermute | solution.py:30
  161.6 6.2 %collective-permute-done = bf16[3,72,128]{2,1,0:T(8,128)(2,1)S(1)} collective-permute-done((bf16[3,72,128]{2,1,0:T(8,128)(2,1)S(1)}, bf16[3,72,128]{2,1,0:T(8,128)(2,1)S(1)}, u32[]{:S(2)}, u32[]{:S(2)}) %collective-permute-start) | collective-permute-done | bytes 55328 | tf_op jit(solution)/shard_map/while/body/eval_jaxpr/ppermute | solution.py:30
  169.9 6.2 %collective-permute-done = bf16[3,72,128]{2,1,0:T(8,128)(2,1)S(1)} collective-permute-done((bf16[3,72,128]{2,1,0:T(8,128)(2,1)S(1)}, bf16[3,72,128]{2,1,0:T(8,128)(2,1)S(1)}, u32[]{:S(2)}, u32[]{:S(2)}) %collective-permute-start) | collective-permute-done | bytes 55328 | tf_op jit(solution)/shard_map/while/body/eval_jaxpr/ppermute | solution.py:30
  178.1 6.2 %collective-permute-done = bf16[3,72,128]{2,1,0:T(8,128)(2,1)S(1)} collective-permute-done((bf16[3,72,128]{2,1,0:T(8,128)(2,1)S(1)}, bf16[3,72,128]{2,1,0:T(8,128)(2,1)S(1)}, u32[]{:S(2)}, u32[]{:S(2)}) %collective-permute-start) | collective-permute-done | bytes 55328 | tf_op jit(solution)/shard_map/while/body/eval_jaxpr/ppermute | solution.py:30
  186.4 6.3 %collective-permute-done = bf16[3,72,128]{2,1,0:T(8,128)(2,1)S(1)} collective-permute-done((bf16[3,72,128]{2,1,0:T(8,128)(2,1)S(1)}, bf16[3,72,128]{2,1,0:T(8,128)(2,1)S(1)}, u32[]{:S(2)}, u32[]{:S(2)}) %collective-permute-start) | collective-permute-done | bytes 55328 | tf_op jit(solution)/shard_map/while/body/eval_jaxpr/ppermute | solution.py:30
  194.7 6.2 %collective-permute-done = bf16[3,72,128]{2,1,0:T(8,128)(2,1)S(1)} collective-permute-done((bf16[3,72,128]{2,1,0:T(8,128)(2,1)S(1)}, bf16[3,72,128]{2,1,0:T(8,128)(2,1)S(1)}, u32[]{:S(2)}, u32[]{:S(2)}) %collective-permute-start) | collective-permute-done | bytes 55328 | tf_op jit(solution)/shard_map/while/body/eval_jaxpr/ppermute | solution.py:30
  202.9 6.2 %collective-permute-done = bf16[3,72,128]{2,1,0:T(8,128)(2,1)S(1)} collective-permute-done((bf16[3,72,128]{2,1,0:T(8,128)(2,1)S(1)}, bf16[3,72,128]{2,1,0:T(8,128)(2,1)S(1)}, u32[]{:S(2)}, u32[]{:S(2)}) %collective-permute-start) | collective-permute-done | bytes 55328 | tf_op jit(solution)/shard_map/while/body/eval_jaxpr/ppermute | solution.py:30
  211.5 2.4 collective-permute-start.4
  236.6 2.7 gather_fusion.18
  242.9 2.5 gather_fusion.17
  251.9 2.5 gather_fusion.19
  255.7 3.9 add_convert_fusion
  264.0 269.3 %all-reduce.25.cloned.1.call-done = bf16[256,3,256]{2,1,0:T(4,128)(2,1)} async-done(((bf16[256,3,256]{2,1,0:T(4,128)(2,1)}), bf16[256,3,256]{2,1,0:T(4,128)(2,1)}) %all-reduce.25.cloned.1.call-update) | async-done | bytes 393232
  536.6 74.1 %reduce-scatter.4.cloned.1.call-done = f32[16,24]{1,0:T(8,128)} async-done(((f32[256,24]{1,0:T(8,128)}), f32[16,24]{1,0:T(8,128)}) %reduce-scatter.4.cloned.1.call-update) | async-done | bytes 1552
  (228 shorter events, 117.3 us)
Async XLA Ops:
  7.2 20.8 %copy-start = (bf16[3,256,256]{2,1,0:T(8,128)(2,1)S(1)}, bf16[3,256,256]{2,1,0:T(8,128)(2,1)}, u32[]{:S(2)}) copy-start(bf16[3,256,256]{2,1,0:T(8,128)(2,1)} %param.10) | copy-start | bytes 1179652
  7.2 526.1 %all-reduce.25.cloned.1.call-start = ((), (), s32[]{:S(2)}) async-start(), calls=%async_computation.2 | async-start | bytes 1048576
  8.4 19.5 %collective-permute-start.1 = (bf16[2,256,128]{1,2,0:T(8,128)(2,1)S(1)}, bf16[2,256,128]{1,2,0:T(8,128)(2,1)S(1)}, u32[]{:S(2)}, u32[]{:S(2)}) collective-permute-start(bf16[2,256,128]{1,2,0:T(8,128)(2,1)S(1)} %get-tuple-element.75), channel_id=1, source_target_pairs={{0,1},{1,2},{2,3},{3,4},{4,5},{5,6},{6,7},{7,8},{8,9},{9,10},{10,1... | collective-permute-start | bytes 393224 | tf_op jit(solution)/shard_map/ppermute | solution.py:20
  10.3 17.6 %collective-permute-start.2 = (bf16[2,256,128]{1,2,0:T(8,128)(2,1)S(1)}, bf16[2,256,128]{1,2,0:T(8,128)(2,1)S(1)}, u32[]{:S(2)}, u32[]{:S(2)}) collective-permute-start(bf16[2,256,128]{1,2,0:T(8,128)(2,1)S(1)} %get-tuple-element.76), channel_id=1, source_target_pairs={{1,0},{2,1},{3,2},{4,3},{5,4},{6,5},{7,6},{8,7},{9,8},{10,9},{11,1... | collective-permute-start | bytes 393224 | tf_op jit(solution)/shard_map/ppermute | solution.py:23
  85.2 124.0 %copy-start.21 = (bf16[3,72,128]{2,1,0:T(8,128)(2,1)S(1)}, bf16[3,72,128]{2,1,0:T(8,128)(2,1)}, u32[]{:S(2)}) copy-start(bf16[3,72,128]{2,1,0:T(8,128)(2,1)} %param.9) | copy-start | bytes 165892
  85.2 124.0 %copy-start.33 = (f32[3]{0:T(128)S(1)}, f32[3]{0:T(128)}, u32[]{:S(2)}) copy-start(f32[3]{0:T(128)} %add_cosine_fusion) | copy-start | bytes 40
  85.2 128.7 %copy-start.18 = (f32[96,3,10]{0,1,2:T(4,128)S(1)}, f32[96,3,10]{0,1,2:T(4,128)}, u32[]{:S(2)}) copy-start(f32[96,3,10]{0,1,2:T(4,128)} %param.12) | copy-start | bytes 34564
  85.2 128.8 %copy-start.32 = (f32[3,3,1]{0,1,2:T(4,128)S(1)}, f32[3,3,1]{0,1,2:T(4,128)}, u32[]{:S(2)}) copy-start(f32[3,3,1]{0,1,2:T(4,128)} %get-tuple-element.88) | copy-start | bytes 112
  85.2 128.9 %copy-start.31 = (f32[3,3,1]{0,1,2:T(4,128)S(1)}, f32[3,3,1]{0,1,2:T(4,128)}, u32[]{:S(2)}) copy-start(f32[3,3,1]{0,1,2:T(4,128)} %get-tuple-element.90) | copy-start | bytes 112
  85.2 129.0 %copy-start.30 = (f32[3,3,1]{0,1,2:T(4,128)S(1)}, f32[3,3,1]{0,1,2:T(4,128)}, u32[]{:S(2)}) copy-start(f32[3,3,1]{0,1,2:T(4,128)} %get-tuple-element.91) | copy-start | bytes 112
  85.2 129.1 %copy-start.29 = (f32[3,3,1]{0,1,2:T(4,128)S(1)}, f32[3,3,1]{0,1,2:T(4,128)}, u32[]{:S(2)}) copy-start(f32[3,3,1]{0,1,2:T(4,128)} %get-tuple-element.92) | copy-start | bytes 112
  85.3 129.2 %copy-start.28 = (f32[3,3,1]{0,1,2:T(4,128)S(1)}, f32[3,3,1]{0,1,2:T(4,128)}, u32[]{:S(2)}) copy-start(f32[3,3,1]{0,1,2:T(4,128)} %get-tuple-element.83) | copy-start | bytes 112
  85.3 129.2 %copy-start.27 = (f32[3,3,1]{0,1,2:T(4,128)S(1)}, f32[3,3,1]{0,1,2:T(4,128)}, u32[]{:S(2)}) copy-start(f32[3,3,1]{0,1,2:T(4,128)} %get-tuple-element.77) | copy-start | bytes 112
  85.3 8.2 %collective-permute-start = (bf16[3,72,128]{2,1,0:T(8,128)(2,1)S(1)}, bf16[3,72,128]{2,1,0:T(8,128)(2,1)S(1)}, u32[]{:S(2)}, u32[]{:S(2)}) collective-permute-start(bf16[3,72,128]{2,1,0:T(8,128)(2,1)S(1)} %get-tuple-element.154), channel_id=1, source_target_pairs={{0,32},{32,64},{64,96},{96,128},{128,160},{160,192},{192,224},{224... | collective-permute-start | bytes 165896 | tf_op jit(solution)/shard_map/while/body/eval_jaxpr/ppermute | solution.py:30
  93.5 8.2 %collective-permute-start = (bf16[3,72,128]{2,1,0:T(8,128)(2,1)S(1)}, bf16[3,72,128]{2,1,0:T(8,128)(2,1)S(1)}, u32[]{:S(2)}, u32[]{:S(2)}) collective-permute-start(bf16[3,72,128]{2,1,0:T(8,128)(2,1)S(1)} %get-tuple-element.154), channel_id=1, source_target_pairs={{0,32},{32,64},{64,96},{96,128},{128,160},{160,192},{192,224},{224... | collective-permute-start | bytes 165896 | tf_op jit(solution)/shard_map/while/body/eval_jaxpr/ppermute | solution.py:30
  101.8 8.2 %collective-permute-start = (bf16[3,72,128]{2,1,0:T(8,128)(2,1)S(1)}, bf16[3,72,128]{2,1,0:T(8,128)(2,1)S(1)}, u32[]{:S(2)}, u32[]{:S(2)}) collective-permute-start(bf16[3,72,128]{2,1,0:T(8,128)(2,1)S(1)} %get-tuple-element.154), channel_id=1, source_target_pairs={{0,32},{32,64},{64,96},{96,128},{128,160},{160,192},{192,224},{224... | collective-permute-start | bytes 165896 | tf_op jit(solution)/shard_map/while/body/eval_jaxpr/ppermute | solution.py:30
  110.0 8.2 %collective-permute-start = (bf16[3,72,128]{2,1,0:T(8,128)(2,1)S(1)}, bf16[3,72,128]{2,1,0:T(8,128)(2,1)S(1)}, u32[]{:S(2)}, u32[]{:S(2)}) collective-permute-start(bf16[3,72,128]{2,1,0:T(8,128)(2,1)S(1)} %get-tuple-element.154), channel_id=1, source_target_pairs={{0,32},{32,64},{64,96},{96,128},{128,160},{160,192},{192,224},{224... | collective-permute-start | bytes 165896 | tf_op jit(solution)/shard_map/while/body/eval_jaxpr/ppermute | solution.py:30
  118.3 8.2 %collective-permute-start = (bf16[3,72,128]{2,1,0:T(8,128)(2,1)S(1)}, bf16[3,72,128]{2,1,0:T(8,128)(2,1)S(1)}, u32[]{:S(2)}, u32[]{:S(2)}) collective-permute-start(bf16[3,72,128]{2,1,0:T(8,128)(2,1)S(1)} %get-tuple-element.154), channel_id=1, source_target_pairs={{0,32},{32,64},{64,96},{96,128},{128,160},{160,192},{192,224},{224... | collective-permute-start | bytes 165896 | tf_op jit(solution)/shard_map/while/body/eval_jaxpr/ppermute | solution.py:30
  126.5 8.4 %collective-permute-start = (bf16[3,72,128]{2,1,0:T(8,128)(2,1)S(1)}, bf16[3,72,128]{2,1,0:T(8,128)(2,1)S(1)}, u32[]{:S(2)}, u32[]{:S(2)}) collective-permute-start(bf16[3,72,128]{2,1,0:T(8,128)(2,1)S(1)} %get-tuple-element.154), channel_id=1, source_target_pairs={{0,32},{32,64},{64,96},{96,128},{128,160},{160,192},{192,224},{224... | collective-permute-start | bytes 165896 | tf_op jit(solution)/shard_map/while/body/eval_jaxpr/ppermute | solution.py:30
  135.0 8.2 %collective-permute-start = (bf16[3,72,128]{2,1,0:T(8,128)(2,1)S(1)}, bf16[3,72,128]{2,1,0:T(8,128)(2,1)S(1)}, u32[]{:S(2)}, u32[]{:S(2)}) collective-permute-start(bf16[3,72,128]{2,1,0:T(8,128)(2,1)S(1)} %get-tuple-element.154), channel_id=1, source_target_pairs={{0,32},{32,64},{64,96},{96,128},{128,160},{160,192},{192,224},{224... | collective-permute-start | bytes 165896 | tf_op jit(solution)/shard_map/while/body/eval_jaxpr/ppermute | solution.py:30
  143.2 8.2 %collective-permute-start = (bf16[3,72,128]{2,1,0:T(8,128)(2,1)S(1)}, bf16[3,72,128]{2,1,0:T(8,128)(2,1)S(1)}, u32[]{:S(2)}, u32[]{:S(2)}) collective-permute-start(bf16[3,72,128]{2,1,0:T(8,128)(2,1)S(1)} %get-tuple-element.154), channel_id=1, source_target_pairs={{0,32},{32,64},{64,96},{96,128},{128,160},{160,192},{192,224},{224... | collective-permute-start | bytes 165896 | tf_op jit(solution)/shard_map/while/body/eval_jaxpr/ppermute | solution.py:30
  151.4 8.2 %collective-permute-start = (bf16[3,72,128]{2,1,0:T(8,128)(2,1)S(1)}, bf16[3,72,128]{2,1,0:T(8,128)(2,1)S(1)}, u32[]{:S(2)}, u32[]{:S(2)}) collective-permute-start(bf16[3,72,128]{2,1,0:T(8,128)(2,1)S(1)} %get-tuple-element.154), channel_id=1, source_target_pairs={{0,32},{32,64},{64,96},{96,128},{128,160},{160,192},{192,224},{224... | collective-permute-start | bytes 165896 | tf_op jit(solution)/shard_map/while/body/eval_jaxpr/ppermute | solution.py:30
  159.7 8.2 %collective-permute-start = (bf16[3,72,128]{2,1,0:T(8,128)(2,1)S(1)}, bf16[3,72,128]{2,1,0:T(8,128)(2,1)S(1)}, u32[]{:S(2)}, u32[]{:S(2)}) collective-permute-start(bf16[3,72,128]{2,1,0:T(8,128)(2,1)S(1)} %get-tuple-element.154), channel_id=1, source_target_pairs={{0,32},{32,64},{64,96},{96,128},{128,160},{160,192},{192,224},{224... | collective-permute-start | bytes 165896 | tf_op jit(solution)/shard_map/while/body/eval_jaxpr/ppermute | solution.py:30
  167.9 8.2 %collective-permute-start = (bf16[3,72,128]{2,1,0:T(8,128)(2,1)S(1)}, bf16[3,72,128]{2,1,0:T(8,128)(2,1)S(1)}, u32[]{:S(2)}, u32[]{:S(2)}) collective-permute-start(bf16[3,72,128]{2,1,0:T(8,128)(2,1)S(1)} %get-tuple-element.154), channel_id=1, source_target_pairs={{0,32},{32,64},{64,96},{96,128},{128,160},{160,192},{192,224},{224... | collective-permute-start | bytes 165896 | tf_op jit(solution)/shard_map/while/body/eval_jaxpr/ppermute | solution.py:30
  176.2 8.2 %collective-permute-start = (bf16[3,72,128]{2,1,0:T(8,128)(2,1)S(1)}, bf16[3,72,128]{2,1,0:T(8,128)(2,1)S(1)}, u32[]{:S(2)}, u32[]{:S(2)}) collective-permute-start(bf16[3,72,128]{2,1,0:T(8,128)(2,1)S(1)} %get-tuple-element.154), channel_id=1, source_target_pairs={{0,32},{32,64},{64,96},{96,128},{128,160},{160,192},{192,224},{224... | collective-permute-start | bytes 165896 | tf_op jit(solution)/shard_map/while/body/eval_jaxpr/ppermute | solution.py:30
  184.4 8.2 %collective-permute-start = (bf16[3,72,128]{2,1,0:T(8,128)(2,1)S(1)}, bf16[3,72,128]{2,1,0:T(8,128)(2,1)S(1)}, u32[]{:S(2)}, u32[]{:S(2)}) collective-permute-start(bf16[3,72,128]{2,1,0:T(8,128)(2,1)S(1)} %get-tuple-element.154), channel_id=1, source_target_pairs={{0,32},{32,64},{64,96},{96,128},{128,160},{160,192},{192,224},{224... | collective-permute-start | bytes 165896 | tf_op jit(solution)/shard_map/while/body/eval_jaxpr/ppermute | solution.py:30
  192.7 8.2 %collective-permute-start = (bf16[3,72,128]{2,1,0:T(8,128)(2,1)S(1)}, bf16[3,72,128]{2,1,0:T(8,128)(2,1)S(1)}, u32[]{:S(2)}, u32[]{:S(2)}) collective-permute-start(bf16[3,72,128]{2,1,0:T(8,128)(2,1)S(1)} %get-tuple-element.154), channel_id=1, source_target_pairs={{0,32},{32,64},{64,96},{96,128},{128,160},{160,192},{192,224},{224... | collective-permute-start | bytes 165896 | tf_op jit(solution)/shard_map/while/body/eval_jaxpr/ppermute | solution.py:30
  201.0 8.2 %collective-permute-start = (bf16[3,72,128]{2,1,0:T(8,128)(2,1)S(1)}, bf16[3,72,128]{2,1,0:T(8,128)(2,1)S(1)}, u32[]{:S(2)}, u32[]{:S(2)}) collective-permute-start(bf16[3,72,128]{2,1,0:T(8,128)(2,1)S(1)} %get-tuple-element.154), channel_id=1, source_target_pairs={{0,32},{32,64},{64,96},{96,128},{128,160},{160,192},{192,224},{224... | collective-permute-start | bytes 165896 | tf_op jit(solution)/shard_map/while/body/eval_jaxpr/ppermute | solution.py:30
  209.6 9.9 %collective-permute-start.3 = (bf16[2,256,128]{1,2,0:T(8,128)(2,1)S(1)}, bf16[2,256,128]{1,2,0:T(8,128)(2,1)S(1)}, u32[]{:S(2)}, u32[]{:S(2)}) collective-permute-start(bf16[2,256,128]{1,2,0:T(8,128)(2,1)S(1)} %get-tuple-element.73), channel_id=1, source_target_pairs={{1,0},{2,1},{3,2},{4,3},{5,4},{6,5},{7,6},{8,7},{9,8},{10,9},{11,1... | collective-permute-start | bytes 393224 | tf_op jit(solution)/shard_map/ppermute | solution.py:23
  211.5 8.8 %collective-permute-start.4 = (bf16[2,256,128]{1,2,0:T(8,128)(2,1)S(1)}, bf16[2,256,128]{1,2,0:T(8,128)(2,1)S(1)}, u32[]{:S(2)}, u32[]{:S(2)}) collective-permute-start(bf16[2,256,128]{1,2,0:T(8,128)(2,1)S(1)} %get-tuple-element.74), channel_id=1, source_target_pairs={{0,1},{1,2},{2,3},{3,4},{4,5},{5,6},{6,7},{7,8},{8,9},{9,10},{10,1... | collective-permute-start | bytes 393224 | tf_op jit(solution)/shard_map/ppermute | solution.py:20
  262.0 273.5 %copy-start.17 = (bf16[3,3,256,128]{2,1,3,0:T(4,128)(2,1)S(1)}, bf16[3,3,256,128]{2,1,3,0:T(4,128)(2,1)}, u32[]{:S(2)}) copy-start(bf16[3,3,256,128]{2,1,3,0:T(4,128)(2,1)} %copy-done.16) | copy-start | bytes 1769476
  262.0 348.7 %reduce-scatter.4.cloned.1.call-start = ((), (), s32[]{:S(2)}) async-start(), calls=%async_computation.1 | async-start | bytes 139264
  (23 other events, 159.8 us)
Sparse Core Ops, SparseCore 0:
  262.1 271.1 all-reduce.24
  536.3 74.3 reduce-scatter.3
where the time goes:
time: 630 us; the launch traced here: 619 us
  waiting for transfers between devices  436 us (69%)
  local copies, waits for them, and re-layouts  86.8 us (14%)
  starting transfers between devices  41.8 us (7%)
  other arithmetic  36.1 us (6%)
  between operations  15.9 us (3%)
    unnamed x4, waiting for transfers between devices  343 us
    ppermute x15, waiting for transfers between devices, from_behind(): lax.ppermute(shard, axis, [(i, (i + by) % count) for i in range(count)])  92.1 us
    gather x30, local copies, waits for them, and re-layouts, one_row(): return lax.dynamic_slice_in_dim(row, begin, lon_count, last_axis)  51.4 us
    ppermute x15, starting transfers between devices, from_behind(): lax.ppermute(shard, axis, [(i, (i + by) % count) for i in range(count)])  30.4 us
    reduce_sum x9, other arithmetic, body(): conv_out = conv_out + jnp.sum(weights[:, :, None, None] * moved, axis=1)  23.2 us
  transfers between devices with their start and end apart: 21, of which 18 were waited for; matrix products, arithmetic and copies ran while one was open for 3% of the time, Pallas kernels for 0%

commit v1 on v0

v1 whole, which is shorter than its diff:
```python
import functools
import math

import jax
import jax.numpy as jnp
import numpy as np
from jax import lax
from jax.experimental import pallas as pl
from jax.experimental.pallas import tpu as pltpu
from jax.sharding import PartitionSpec as P

HALO = 2
SIDE = 2
REACH = 2 * HALO + 1
DELTA = 0.25
BF = jnp.bfloat16
F32 = jnp.float32
VMEM = pl.BlockSpec(memory_space=pltpu.VMEM)
SMEM = pl.BlockSpec(memory_space=pltpu.SMEM)


def smooth_slope(differ):
    return differ * lax.rsqrt(differ * differ + DELTA * DELTA)


def dot_nn(a, b):
    return lax.dot_general(a, b, (((1,), (0,)), ((), ())), preferred_element_type=F32)


def dot_nt(a, b):
    return lax.dot_general(a, b, (((1,), (1,)), ((), ())), preferred_element_type=F32)


def call(kernel, out, specs, flops, moved):
    many = isinstance(out, (tuple, list))
    return pl.pallas_call(
        kernel,
        out_shape=out,
        in_specs=specs,
        out_specs=tuple([VMEM] * len(out)) if many else VMEM,
        compiler_params=pltpu.CompilerParams(vmem_limit_bytes=32 * 2**20),
        cost_estimate=pl.CostEstimate(flops=flops, bytes_accessed=moved, transcendentals=0),
    )


def prepare(rows, kernels, taps, lat_count, first, basis, offsets, filters, dec_t, dec_p, ahead, back, w_fwd, w_bwd):
    lon = ahead.shape[1] // REACH
    chan = filters.shape[1]
    base = first[0]
    lag = (lax.broadcasted_iota(jnp.int32, (lon, lon), 0) - lax.broadcasted_iota(jnp.int32, (lon, lon), 1)) & (lon - 1)

    def block(out, row, source, slot, step, sign):
        cycle = base + source
        inside = jnp.logical_and(cycle >= 0, cycle < lat_count)
        cycle = jnp.clip(cycle, 0, lat_count - 1)
        one, two = SIDE * step, SIDE * step + 1
        off_one, off_two = offsets[cycle, one], offsets[cycle, two]
        mask_one = lag == ((sign * off_one) & (lon - 1))
        mask_two = lag == ((sign * off_two) & (lon - 1))
        for k in range(kernels):
            weight_one = jnp.where(inside, basis[cycle, k * taps + one], 0.0)
            weight_two = jnp.where(inside, basis[cycle, k * taps + two], 0.0)
            weight_two = weight_two + jnp.where(off_one == off_two, weight_one, 0.0)
            value = jnp.where(mask_two, weight_two, jnp.where(mask_one, weight_one, 0.0))
            out[row, slot * lon : (slot + 1) * lon, k * lon : (k + 1) * lon] = value.astype(BF)

    for row in range(rows):
        for slot in range(REACH):
            block(ahead, row, row, slot, slot, 1)
            block(back, row, row + slot - HALO, slot, REACH - 1 - slot, -1)
    w_fwd[:, :chan] = dec_t[...]
    w_bwd[0] = dec_p[...]
    for k in range(kernels):
        w_fwd[:, (k + 1) * chan : (k + 2) * chan] = dot_nt(dec_t[...], filters[k]).astype(BF)
        w_bwd[k + 1] = dot_nn(filters[k], dec_p[...]).astype(BF)


def forward(rows, kernels, field, low, high, ahead, w_fwd, packed, predicted, mixed):
    lon = field.shape[2]
    chan = field.shape[1]
    wide = [low[0], low[1]] + [field[i] for i in range(rows)] + [high[0], high[1]]
    per = packed.shape[1]
    padded = predicted.shape[1]
    pieces = padded // per
    for i in range(rows):
        source = jnp.concatenate(wide[i : i + REACH], axis=1)
        taps = dot_nn(source, ahead[i]).astype(BF)
        for k in range(kernels):
            mixed[i, k * chan : (k + 1) * chan, :] = taps[:, k * lon : (k + 1) * lon]
        stack = jnp.concatenate([wide[i + HALO]] + [taps[:, k * lon : (k + 1) * lon] for k in range(kernels)], axis=0)
        pred = dot_nn(w_fwd[...], stack)
        predicted[i] = pred
        rounded = pred.astype(BF)
        for q in range(pieces):
            packed[i * pieces + q] = rounded[q * per : (q + 1) * per]
    for q in range(rows * pieces, packed.shape[0]):
        packed[q] = jnp.zeros(packed.shape[1:], BF)


def pairs(visitors, sums):
    members, height, _ = visitors.shape
    for start in range(0, height, 8):
        values = [visitors[m].astype(F32)[start : start + 8] for m in range(members)]
        totals = [None] * members
        for m in range(members):
            for n in range(m + 1, members):
                slope = smooth_slope(values[m] - values[n])
                totals[m] = slope if totals[m] is None else totals[m] + slope
                totals[n] = -slope if totals[n] is None else totals[n] - slope
        for m in range(members):
            sums[m, start : start + 8, :] = totals[m]


def gradient(rows, kernels, members, first, area, sums, predicted, target, mixed, pred_grad, partial):
    variables = target.shape[1]
    padded = predicted.shape[1]
    per = sums.shape[1]
    pieces = padded // per
    lon = predicted.shape[2]
    chan = mixed.shape[1] // kernels
    grads = []
    for i in range(rows):
        pair_sum = jnp.concatenate([sums[i * pieces + q] for q in range(pieces)], axis=0)
        aim = jnp.concatenate([target[i].astype(F32), jnp.zeros((padded - variables, lon), F32)], axis=0)
        grad = area[first[0] + i] * (smooth_slope(predicted[i] - aim) - pair_sum * (1.0 / (members - 1)))
        grad = grad.astype(BF)
        pred_grad[i] = grad
        grads.append(jnp.concatenate([grad, jnp.zeros((lon - padded, lon), BF)], axis=0))
    total = dot_nt(
        jnp.concatenate([mixed[i] for i in range(rows)], axis=1), jnp.concatenate(grads, axis=1)
    )
    owners = partial.shape[0]
    own = chan // owners
    for owner in range(owners):
        partial[owner] = jnp.concatenate(
            [total[k * chan + owner * own : k * chan + (owner + 1) * own] for k in range(kernels)], axis=0
        ).astype(BF)


def band_sum(factor, parts, dec_wide, spread):
    owners, height, lanes = parts.shape
    total = parts[0].astype(F32)
    for owner in range(1, owners):
        total = total + parts[owner].astype(F32)
    total = jnp.concatenate([total * factor, jnp.zeros((lanes - height, lanes), F32)], axis=0)
    upper = total.astype(BF)
    lower = (total - upper.astype(F32)).astype(BF)
    result = dot_nt(dec_wide[...], upper) + dot_nt(dec_wide[...], lower)
    per = spread.shape[1]
    for member in range(spread.shape[0]):
        spread[member] = result[member * per : (member + 1) * per]


def member_sum(parts, owned):
    own, kernels, width = owned.shape
    total = parts[0]
    for member in range(1, parts.shape[0]):
        total = total + parts[member]
    turned = total.T
    for k in range(kernels):
        owned[:, k, :] = turned[k * own : (k + 1) * own]


def adjoint(rows, kernels, pred_grad, low, high, back, w_bwd, result):
    lon = pred_grad.shape[2]
    wide = [low[0], low[1]] + [pred_grad[i] for i in range(rows)] + [high[0], high[1]]
    for i in range(rows):
        taps = dot_nn(jnp.concatenate(wide[i : i + REACH], axis=1), back[i]).astype(BF)
        total = dot_nn(w_bwd[0], wide[i + HALO])
        for k in range(kernels):
            total = total + dot_nn(w_bwd[k + 1], taps[:, k * lon : (k + 1) * lon])
        result[i] = total.astype(BF)


def halos(block, axis):
    count = lax.axis_size(axis)
    up = [(i, i + 1) for i in range(count - 1)]
    down = [(target, source) for source, target in up]
    return lax.ppermute(block[-HALO:], axis, up), lax.ppermute(block[:HALO], axis, down)


def body(latent_fields, target_fields, filters, decoder, cycle_basis, cycle_offsets):
    field = latent_fields[0]
    rows, chan, lon = field.shape
    lat_count, kernels, taps = cycle_basis.shape
    variables = decoder.shape[1]
    members, bands = lax.axis_size("ens"), lax.axis_size("lat")
    per = 16
    padded = -(-variables // per) * per
    first = (lax.axis_index("lat") * rows).astype(jnp.int32).reshape(1)
    area = jnp.asarray(np.cos(np.pi * (np.arange(lat_count) + 0.5) / lat_count - np.pi / 2), F32)
    dec_p = jnp.pad(decoder, ((0, 0), (0, padded - variables)))
    dec_wide = jnp.pad(decoder, ((0, 0), (0, lon - variables)))

    low, high = halos(field, "lat")
    ahead, back, w_fwd, w_bwd = call(
        functools.partial(prepare, rows, kernels, taps, lat_count),
        (
            jax.ShapeDtypeStruct((rows, REACH * lon, kernels * lon), BF),
            jax.ShapeDtypeStruct((rows, REACH * lon, kernels * lon), BF),
            jax.ShapeDtypeStruct((padded, (kernels + 1) * chan), BF),
            jax.ShapeDtypeStruct((kernels + 1, chan, padded), BF),
        ),
        [SMEM, SMEM, SMEM, VMEM, VMEM, VMEM],
        60_000_000,
        4_000_000,
    )(first, cycle_basis.reshape(lat_count, kernels * taps), cycle_offsets, filters, dec_p.T, dec_p)
    packed, predicted, mixed = call(
        functools.partial(forward, rows, kernels),
        (
            jax.ShapeDtypeStruct((members, per, lon), BF),
            jax.ShapeDtypeStruct((rows, padded, lon), F32),
            jax.ShapeDtypeStruct((rows, kernels * chan, lon), BF),
        ),
        [VMEM] * 5,
        450_000_000,
        3_000_000,
    )(field, low, high, ahead, w_fwd)
    visitors = lax.all_to_all(packed, "ens", 0, 0, tiled=True)
    sums = call(pairs, jax.ShapeDtypeStruct((members, per, lon), F32), [VMEM], 2_000_000, 200_000)(visitors)
    sums = lax.all_to_all(sums, "ens", 0, 0, tiled=True)
    own = chan // bands
    pred_grad, partial = call(
        functools.partial(gradient, rows, kernels, members),
        (
            jax.ShapeDtypeStruct((rows, padded, lon), BF),
            jax.ShapeDtypeStruct((bands, kernels * own, lon), BF),
        ),
        [SMEM, SMEM] + [VMEM] * 4,
        80_000_000,
        1_200_000,
    )(first, area, sums, predicted, target_fields, mixed)
    grad_low, grad_high = halos(pred_grad, "lat")
    parts = lax.all_to_all(partial, "lat", 0, 0, tiled=True)
    factor = 1.0 / math.sqrt(members * lat_count * lon)
    width = chan // members
    spread = call(
        functools.partial(band_sum, factor),
        jax.ShapeDtypeStruct((members, width, lon), F32),
        [VMEM] * 2,
        20_000_000,
        400_000,
    )(parts, dec_wide)
    spread = lax.all_to_all(spread, "ens", 0, 0, tiled=True)
    latent_grad = call(
        functools.partial(adjoint, rows, kernels),
        jax.ShapeDtypeStruct((rows, chan, lon), BF),
        [VMEM] * 5,
        200_000_000,
        2_000_000,
    )(pred_grad, grad_low, grad_high, back, w_bwd)
    owned = call(
        member_sum, jax.ShapeDtypeStruct((own, kernels, width), F32), [VMEM], 100_000, 150_000
    )(spread)
    return latent_grad[None], owned


def solution(mesh):
    placed = (P("ens", "lat", None, None), P("lat", None, None), P(), P(), P(), P())
    return jax.shard_map(
        body,
        mesh=mesh,
        in_specs=placed,
        out_specs=(P("ens", "lat", None, None), P("lat", None, "ens")),
        check_vma=False,
    )
```

time: 630 us -> 86.8 us (0.14)
  the two profiles are of different devices: /device:TPU:6 before, /device:TPU:1 now
where the time goes in v1:
time: 86.8 us; the launch traced here: 85.4 us
  starting transfers between devices  34.9 us (40%)
  blocking collectives  22.5 us (26%)
  waiting for transfers between devices  12.9 us (15%)
  Pallas kernels  8.99 us (10%)
  local copies, waits for them, and re-layouts  5.33 us (6%)
    all_to_all x1, starting transfers between devices, body(): parts = lax.all_to_all(partial, 'lat', 0, 0, tiled=True)  13.4 us
    all_to_all x1, blocking collectives, body(): visitors = lax.all_to_all(packed, 'ens', 0, 0, tiled=True)  12.2 us
    all_to_all x1, waiting for transfers between devices, body(): parts = lax.all_to_all(partial, 'lat', 0, 0, tiled=True)  11.8 us
    ppermute x2, starting transfers between devices, halos(): lax.ppermute(block[:HALO], axis, down)  11.4 us
    all_to_all x1, blocking collectives, body(): sums = lax.all_to_all(sums, 'ens', 0, 0, tiled=True)  10.3 us
    ppermute x2, starting transfers between devices, halos(): lax.ppermute(block[-HALO:], axis, up)  6.4 us
    unnamed x12, local copies, waits for them, and re-layouts  4.01 us
    all_to_all x1, starting transfers between devices, body(): spread = lax.all_to_all(spread, 'ens', 0, 0, tiled=True)  3.66 us
  transfers between devices with their start and end apart: 6, of which 2 were waited for; matrix products, arithmetic and copies ran while one was open for 3% of the time, Pallas kernels for 6%

profile of v1, /device:TPU:1, one launch (start us, length us, event | category | flops | bytes accessed | tf_op | source)
XLA Modules:
  0.0 85.4 jit_solution(1469440856904939836)
XLA Ops:
  0.6 1.1 %slice_bitcast_fusion = (bf16[2,256,128]{2,1,0:T(8,128)(2,1)S(1)}, bf16[2,256,128]{2,1,0:T(8,128)(2,1)S(1)}) fusion(bf16[1,3,256,128]{3,2,1,0:T(8,128)(2,1)} %param.7), kind=kLoop, calls=%fused_computation | loop fusion | bytes 524288 | tf_op jit(solution)/shard_map/slice | solution.py:179
  1.7 8.8 %collective-permute-start.1 = (bf16[2,256,128]{2,1,0:T(8,128)(2,1)S(1)}, bf16[2,256,128]{2,1,0:T(8,128)(2,1)S(1)}, u32[]{:S(2)}, u32[]{:S(2)}) collective-permute-start(bf16[2,256,128]{2,1,0:T(8,128)(2,1)S(1)} %get-tuple-element.24), channel_id=1, source_target_pairs={{1,0},{2,1},{3,2},{4,3},{5,4},{6,5},{7,6},{8,7},{9,8},{10,9},{11,1... | collective-permute-start | bytes 393224 | tf_op jit(solution)/shard_map/ppermute | solution.py:179
  10.5 1.9 %collective-permute-start = (bf16[2,256,128]{2,1,0:T(8,128)(2,1)S(1)}, bf16[2,256,128]{2,1,0:T(8,128)(2,1)S(1)}, u32[]{:S(2)}, u32[]{:S(2)}) collective-permute-start(bf16[2,256,128]{2,1,0:T(8,128)(2,1)S(1)} %get-tuple-element.25), channel_id=1, source_target_pairs={{0,1},{1,2},{2,3},{3,4},{4,5},{5,6},{6,7},{7,8},{8,9},{9,10},{10,1... | collective-permute-start | bytes 393224 | tf_op jit(solution)/shard_map/ppermute | solution.py:179
  12.4 0.7 copy.15
  13.2 0.1 copy.17.basis
  13.3 0.8 copy.18.offsets
  14.1 0.9 %copy.16 = bf16[256,72]{1,0:T(8,128)(2,1)S(1)} copy(bf16[256,72]{0,1:T(8,128)(2,1)} %param.10) | data formatting | bytes 73728 | tf_op args[3]
  15.0 0.1 copy.19.dec_t
  15.1 0.0 copy-start.1
  15.1 1.0 %copy-done.1 = bf16[3,256,256]{2,1,0:T(8,128)(2,1)S(1)} copy-done((bf16[3,256,256]{2,1,0:T(8,128)(2,1)S(1)}, bf16[3,256,256]{2,1,0:T(8,128)(2,1)}, u32[]{:S(2)}) %copy-start.1) | copy-done | bytes 393240
  16.1 3.3 %shard_map.86 = (bf16[3,640,384]{2,1,0:T(8,128)(2,1)S(1)}, bf16[3,640,384]{2,1,0:T(8,128)(2,1)S(1)}, bf16[80,1024]{1,0:T(8,128)(2,1)S(1)}, bf16[4,256,80]{2,1,0:T(8,128)(2,1)S(1)}) custom-call(s32[1]{0:T(128)} %bitcast.first, f32[96,30]{1,0:T(8,128)S(1)} %copy.17.basis, s32[96,10]{1,0:T(8,128)S(1)} %copy.18.offsets, bf16[3,256,256]{2,1,0:T(8,128)(2,1)S(1)} %copy-done.1, ...), custom_call_target="tpu_custom_call" | custom-call | flops 60000000 | bytes 4000000 | tf_op jit(solution)/shard_map/pallas_call | solution.py:196
  19.4 0.0 copy-start.2
  19.4 0.0 copy-start.3
  19.4 0.0 collective-permute-done.1.high
  19.4 0.0 collective-permute-done.low
  19.4 1.3 %shard_map.87 = (bf16[16,16,128]{2,1,0:T(8,128)(2,1)S(1)}, f32[3,80,128]{2,1,0:T(8,128)S(1)}, bf16[3,768,128]{2,1,0:T(8,128)(2,1)S(1)}) custom-call(bf16[3,256,128]{2,1,0:T(8,128)(2,1)S(1)} %bitcast.11, bf16[2,256,128]{2,1,0:T(8,128)(2,1)S(1)} %collective-permute-done.low, bf16[2,256,128]{2,1,0:T(8,128)(2,1)S(1)} %collective-permute-done.1.high, ...), custom_call_target="tpu_custom_call" | custom-call | flops 450000000 | bytes 3000000 | tf_op jit(solution)/shard_map/pallas_call | solution.py:208
  20.7 12.2 %all_to_all.20.visitors = bf16[16,16,128]{2,1,0:T(8,128)(2,1)S(1)} all-to-all(bf16[16,16,128]{2,1,0:T(8,128)(2,1)S(1)} %get-tuple-element.13), channel_id=1, replica_groups=mesh['ens'=16,'lat'=32] {'ens'}, dimensions={0} | all-to-all | bytes 131072 | tf_op jit(solution)/shard_map/all_to_all | solution.py:219
  32.9 0.2 shard_map.88
  33.2 10.3 %all_to_all.21.sums = f32[16,16,128]{2,1,0:T(8,128)S(1)} all-to-all(f32[16,16,128]{2,1,0:T(8,128)S(1)} %shard_map.88), channel_id=1, replica_groups=mesh['ens'=16,'lat'=32] {'ens'}, dimensions={0} | all-to-all | bytes 262144 | tf_op jit(solution)/shard_map/all_to_all | solution.py:221
  43.5 1.5 %shard_map.89 = (bf16[3,80,128]{2,1,0:T(8,128)(2,1)S(1)}, bf16[32,24,128]{2,1,0:T(8,128)(2,1)}) custom-call(s32[1]{0:T(128)} %bitcast.first, f32[96]{0:T(128)S(1)} %copy-done.3, f32[16,16,128]{2,1,0:T(8,128)S(1)} %all_to_all.21.sums, f32[3,80,128]{2,1,0:T(8,128)S(1)} %get-tuple-element.14.predicted, bf16[3,72,128]{2,1,0:T(8,128)(2,1)S(1)} %copy-done.2, ...), custom_call_target="tpu_custom_call" | custom-call | flops 80000000 | bytes 1200000 | tf_op jit(solution)/shard_map/pallas_call | solution.py:223
  45.0 13.4 %all-to-all-start.2 = ((bf16[32,24,128]{2,1,0:T(8,128)(2,1)}), bf16[32,24,128]{2,1,0:T(8,128)(2,1)S(1)}, u32[]{:S(2)}, u32[]{:S(2)}) async-start(bf16[32,24,128]{2,1,0:T(8,128)(2,1)} %get-tuple-element.19), calls=%async_computation.2 | async-start | bytes 393216 | tf_op jit(solution)/shard_map/all_to_all | solution.py:234
  58.5 11.8 %all-to-all-done.2.parts = bf16[32,24,128]{2,1,0:T(8,128)(2,1)S(1)} async-done(((bf16[32,24,128]{2,1,0:T(8,128)(2,1)}), bf16[32,24,128]{2,1,0:T(8,128)(2,1)S(1)}, u32[]{:S(2)}, u32[]{:S(2)}) %all-to-all-start.2) | async-done | bytes 196640 | tf_op jit(solution)/shard_map/all_to_all | solution.py:234
  70.3 0.9 %shard_map.91 = f32[16,16,128]{2,1,0:T(8,128)} custom-call(bf16[32,24,128]{2,1,0:T(8,128)(2,1)S(1)} %all-to-all-done.2.parts, bf16[256,128]{1,0:T(8,128)(2,1)S(1)} %pad.9.dec_wide), custom_call_target="tpu_custom_call" | custom-call | flops 20000000 | bytes 400000 | tf_op jit(solution)/shard_map/pallas_call | solution.py:237
  71.2 3.7 %all-to-all-start.3 = ((f32[16,16,128]{2,1,0:T(8,128)}), f32[16,16,128]{2,1,0:T(8,128)S(1)}, u32[]{:S(2)}, u32[]{:S(2)}) async-start(f32[16,16,128]{2,1,0:T(8,128)} %shard_map.91), calls=%async_computation.3 | async-start | bytes 262144 | tf_op jit(solution)/shard_map/all_to_all | solution.py:244
  74.9 2.6 %collective-permute-start.3 = (bf16[2,80,128]{2,1,0:T(8,128)(2,1)S(1)}, bf16[2,80,128]{2,1,0:T(8,128)(2,1)S(1)}, u32[]{:S(2)}, u32[]{:S(2)}) collective-permute-start(bf16[2,80,128]{2,1,0:T(8,128)(2,1)S(1)} %get-tuple-element.28), channel_id=1, source_target_pairs={{1,0},{2,1},{3,2},{4,3},{5,4},{6,5},{7,6},{8,7},{9,8},{10,9},{11,1... | collective-permute-start | bytes 122888 | tf_op jit(solution)/shard_map/ppermute | solution.py:179
  77.5 4.5 %collective-permute-start.2 = (bf16[2,80,128]{2,1,0:T(8,128)(2,1)S(1)}, bf16[2,80,128]{2,1,0:T(8,128)(2,1)S(1)}, u32[]{:S(2)}, u32[]{:S(2)}) collective-permute-start(bf16[2,80,128]{2,1,0:T(8,128)(2,1)S(1)} %get-tuple-element.29), channel_id=1, source_target_pairs={{0,1},{1,2},{2,3},{3,4},{4,5},{5,6},{6,7},{7,8},{8,9},{9,10},{10,1... | collective-permute-start | bytes 122888 | tf_op jit(solution)/shard_map/ppermute | solution.py:179
  82.0 0.0 collective-permute-done.3.high
  82.0 1.1 %collective-permute-done.2.low = bf16[2,80,128]{2,1,0:T(8,128)(2,1)S(1)} collective-permute-done((bf16[2,80,128]{2,1,0:T(8,128)(2,1)S(1)}, bf16[2,80,128]{2,1,0:T(8,128)(2,1)S(1)}, u32[]{:S(2)}, u32[]{:S(2)}) %collective-permute-start.2) | collective-permute-done | bytes 40992 | tf_op jit(solution)/shard_map/ppermute | solution.py:179
  83.1 1.7 %shard_map.90 = bf16[3,256,128]{2,1,0:T(8,128)(2,1)} custom-call(bf16[3,80,128]{2,1,0:T(8,128)(2,1)S(1)} %get-tuple-element.16.pred_grad, bf16[2,80,128]{2,1,0:T(8,128)(2,1)S(1)} %collective-permute-done.2.low, bf16[2,80,128]{2,1,0:T(8,128)(2,1)S(1)} %collective-permute-done.3.high, bf16[3,640,384]{2,1,0:T(8,128)(2,1)S(1)} %get-tuple-element.17.back, ...), custom_call_target="tpu_custom_call" | custom-call | flops 200000000 | bytes 2000000 | tf_op jit(solution)/shard_map/pallas_call | solution.py:245
  84.7 0.0 all-to-all-done.3.parts
  84.7 0.1 shard_map.92
  84.8 0.6 copy.21
  (8 shorter events, 0.1 us)
Async XLA Ops:
  0.6 18.8 %copy-start = (bf16[1,3,256,128]{3,2,1,0:T(8,128)(2,1)S(1)}, bf16[1,3,256,128]{3,2,1,0:T(8,128)(2,1)}, u32[]{:S(2)}) copy-start(bf16[1,3,256,128]{3,2,1,0:T(8,128)(2,1)} %param.7) | copy-start | bytes 589828
  1.7 17.7 %collective-permute-start.1 = (bf16[2,256,128]{2,1,0:T(8,128)(2,1)S(1)}, bf16[2,256,128]{2,1,0:T(8,128)(2,1)S(1)}, u32[]{:S(2)}, u32[]{:S(2)}) collective-permute-start(bf16[2,256,128]{2,1,0:T(8,128)(2,1)S(1)} %get-tuple-element.24), channel_id=1, source_target_pairs={{1,0},{2,1},{3,2},{4,3},{5,4},{6,5},{7,6},{8,7},{9,8},{10,9},{11,1... | collective-permute-start | bytes 393224 | tf_op jit(solution)/shard_map/ppermute | solution.py:179
  10.5 8.9 %collective-permute-start = (bf16[2,256,128]{2,1,0:T(8,128)(2,1)S(1)}, bf16[2,256,128]{2,1,0:T(8,128)(2,1)S(1)}, u32[]{:S(2)}, u32[]{:S(2)}) collective-permute-start(bf16[2,256,128]{2,1,0:T(8,128)(2,1)S(1)} %get-tuple-element.25), channel_id=1, source_target_pairs={{0,1},{1,2},{2,3},{3,4},{4,5},{5,6},{6,7},{7,8},{8,9},{9,10},{10,1... | collective-permute-start | bytes 393224 | tf_op jit(solution)/shard_map/ppermute | solution.py:179
  15.1 1.0 %copy-start.1 = (bf16[3,256,256]{2,1,0:T(8,128)(2,1)S(1)}, bf16[3,256,256]{2,1,0:T(8,128)(2,1)}, u32[]{:S(2)}) copy-start(bf16[3,256,256]{2,1,0:T(8,128)(2,1)} %filters.1) | copy-start | bytes 1179652
  19.4 24.1 %copy-start.2 = (bf16[3,72,128]{2,1,0:T(8,128)(2,1)S(1)}, bf16[3,72,128]{2,1,0:T(8,128)(2,1)}, u32[]{:S(2)}) copy-start(bf16[3,72,128]{2,1,0:T(8,128)(2,1)} %target.1) | copy-start | bytes 165892
  19.4 24.1 %copy-start.3 = (f32[96]{0:T(128)S(1)}, f32[96]{0:T(128)}, u32[]{:S(2)}) copy-start(f32[96]{0:T(128)} %constant.11.clone.area) | copy-start | bytes 1156
  45.0 25.3 %all-to-all-start.2 = ((bf16[32,24,128]{2,1,0:T(8,128)(2,1)}), bf16[32,24,128]{2,1,0:T(8,128)(2,1)S(1)}, u32[]{:S(2)}, u32[]{:S(2)}) async-start(bf16[32,24,128]{2,1,0:T(8,128)(2,1)} %get-tuple-element.19), calls=%async_computation.2 | async-start | bytes 393216 | tf_op jit(solution)/shard_map/all_to_all | solution.py:234
  71.2 13.5 %all-to-all-start.3 = ((f32[16,16,128]{2,1,0:T(8,128)}), f32[16,16,128]{2,1,0:T(8,128)S(1)}, u32[]{:S(2)}, u32[]{:S(2)}) async-start(f32[16,16,128]{2,1,0:T(8,128)} %shard_map.91), calls=%async_computation.3 | async-start | bytes 262144 | tf_op jit(solution)/shard_map/all_to_all | solution.py:244
  74.9 7.1 %collective-permute-start.3 = (bf16[2,80,128]{2,1,0:T(8,128)(2,1)S(1)}, bf16[2,80,128]{2,1,0:T(8,128)(2,1)S(1)}, u32[]{:S(2)}, u32[]{:S(2)}) collective-permute-start(bf16[2,80,128]{2,1,0:T(8,128)(2,1)S(1)} %get-tuple-element.28), channel_id=1, source_target_pairs={{1,0},{2,1},{3,2},{4,3},{5,4},{6,5},{7,6},{8,7},{9,8},{10,9},{11,1... | collective-permute-start | bytes 122888 | tf_op jit(solution)/shard_map/ppermute | solution.py:179
  77.5 5.6 %collective-permute-start.2 = (bf16[2,80,128]{2,1,0:T(8,128)(2,1)S(1)}, bf16[2,80,128]{2,1,0:T(8,128)(2,1)S(1)}, u32[]{:S(2)}, u32[]{:S(2)}) collective-permute-start(bf16[2,80,128]{2,1,0:T(8,128)(2,1)S(1)} %get-tuple-element.29), channel_id=1, source_target_pairs={{0,1},{1,2},{2,3},{3,4},{4,5},{5,6},{6,7},{7,8},{8,9},{9,10},{10,1... | collective-permute-start | bytes 122888 | tf_op jit(solution)/shard_map/ppermute | solution.py:179

commit v2 on v1

--- a/solution.py
+++ b/solution.py
@@ -31,48 +31,73 @@
     return lax.dot_general(a, b, (((1,), (1,)), ((), ())), preferred_element_type=F32)
 
 
-def call(kernel, out, specs, flops, moved):
+def call(kernel, out, specs, flops, moved, scratch=()):
     many = isinstance(out, (tuple, list))
     return pl.pallas_call(
         kernel,
         out_shape=out,
         in_specs=specs,
         out_specs=tuple([VMEM] * len(out)) if many else VMEM,
+        scratch_shapes=list(scratch),
         compiler_params=pltpu.CompilerParams(vmem_limit_bytes=32 * 2**20),
         cost_estimate=pl.CostEstimate(flops=flops, bytes_accessed=moved, transcendentals=0),
     )
 
 
-def prepare(rows, kernels, taps, lat_count, first, basis, offsets, filters, dec_t, dec_p, ahead, back, w_fwd, w_bwd):
-    lon = ahead.shape[1] // REACH
-    chan = filters.shape[1]
-    base = first[0]
-    lag = (lax.broadcasted_iota(jnp.int32, (lon, lon), 0) - lax.broadcasted_iota(jnp.int32, (lon, lon), 1)) & (lon - 1)
-
-    def block(out, row, source, slot, step, sign):
-        cycle = base + source
-        inside = jnp.logical_and(cycle >= 0, cycle < lat_count)
-        cycle = jnp.clip(cycle, 0, lat_count - 1)
-        one, two = SIDE * step, SIDE * step + 1
-        off_one, off_two = offsets[cycle, one], offsets[cycle, two]
-        mask_one = lag == ((sign * off_one) & (lon - 1))
-        mask_two = lag == ((sign * off_two) & (lon - 1))
-        for k in range(kernels):
-            weight_one = jnp.where(inside, basis[cycle, k * taps + one], 0.0)
-            weight_two = jnp.where(inside, basis[cycle, k * taps + two], 0.0)
-            weight_two = weight_two + jnp.where(off_one == off_two, weight_one, 0.0)
-            value = jnp.where(mask_two, weight_two, jnp.where(mask_one, weight_one, 0.0))
-            out[row, slot * lon : (slot + 1) * lon, k * lon : (k + 1) * lon] = value.astype(BF)
-
+def tap_block(taps, lat_count, lag, base, basis, offsets, out, row, source, slot, step, sign):
+    kernels, lon = basis.shape[1], lag.shape[0]
+    cycle = base + source
+    inside = jnp.logical_and(cycle >= 0, cycle < lat_count)
+    cycle = jnp.clip(cycle, 0, lat_count - 1)
+    one, two = SIDE * step, SIDE * step + 1
+    off_one, off_two = offsets[one, cycle], offsets[two, cycle]
+    mask_one = lag == ((sign * off_one) & (lon - 1))
+    mask_two = lag == ((sign * off_two) & (lon - 1))
+    for k in range(kernels):
+        weight_one = jnp.where(inside, basis[one, k, cycle], 0.0)
+        weight_two = jnp.where(inside, basis[two, k, cycle], 0.0)
+        weight_two = weight_two + jnp.where(off_one == off_two, weight_one, 0.0)
+        value = jnp.where(mask_two, weight_two, jnp.where(mask_one, weight_one, 0.0))
+        out[row, slot * lon : (slot + 1) * lon, k * lon : (k + 1) * lon] = value.astype(BF)
+
+
+def lags(lon):
+    return (lax.broadcasted_iota(jnp.int32, (lon, lon), 0) - lax.broadcasted_iota(jnp.int32, (lon, lon), 1)) & (lon - 1)
+
+
+def padded_rows(dec_t, padded):
+    rows, chan = dec_t.shape
+    return jnp.concatenate([dec_t[...].astype(F32), jnp.zeros((padded - rows, chan), F32)], axis=0).astype(BF)
+
+
+def prepare_ahead(rows, taps, lat_count, first, basis, offsets, filters, dec_t, ahead, w_fwd, held, sem):
+    fetch = pltpu.make_async_copy(filters, held, sem)
+    fetch.start()
+    lag = lags(ahead.shape[1] // REACH)
     for row in range(rows):
         for slot in range(REACH):
-            block(ahead, row, row, slot, slot, 1)
-            block(back, row, row + slot - HALO, slot, REACH - 1 - slot, -1)
-    w_fwd[:, :chan] = dec_t[...]
-    w_bwd[0] = dec_p[...]
+            tap_block(taps, lat_count, lag, first[0], basis, offsets, ahead, row, row, slot, slot, 1)
+    kernels, chan = held.shape[:2]
+    dec = padded_rows(dec_t, w_fwd.shape[0])
+    w_fwd[:, :chan] = dec
+    fetch.wait()
     for k in range(kernels):
-        w_fwd[:, (k + 1) * chan : (k + 2) * chan] = dot_nt(dec_t[...], filters[k]).astype(BF)
-        w_bwd[k + 1] = dot_nn(filters[k], dec_p[...]).astype(BF)
+        w_fwd[:, (k + 1) * chan : (k + 2) * chan] = dot_nt(dec, held[k]).astype(BF)
+
+
+def prepare_back(rows, taps, lat_count, first, basis, offsets, filters, dec_t, back, w_bwd):
+    lag = lags(back.shape[1] // REACH)
+    for row in range(rows):
+        for slot in range(REACH):
+            step = REACH - 1 - slot
+            tap_block(taps, lat_count, lag, first[0], basis, offsets, back, row, row + slot - HALO, slot, step, -1)
+    kernels, chan = filters.shape[:2]
+    dec = padded_rows(dec_t, w_bwd.shape[2])
+    rank = (chan, chan)
+    unit = lax.broadcasted_iota(jnp.int32, rank, 0) == lax.broadcasted_iota(jnp.int32, rank, 1)
+    w_bwd[0] = dot_nt(jnp.where(unit, 1.0, 0.0).astype(BF), dec).astype(BF)
+    for k in range(kernels):
+        w_bwd[k + 1] = dot_nt(filters[k], dec).astype(BF)
 
 
 def forward(rows, kernels, field, low, high, ahead, w_fwd, packed, predicted, mixed):
@@ -137,7 +162,7 @@
         ).astype(BF)
 
 
-def band_sum(factor, parts, dec_wide, spread):
+def band_sum(factor, parts, w_bwd, spread):
     owners, height, lanes = parts.shape
     total = parts[0].astype(F32)
     for owner in range(1, owners):
@@ -145,20 +170,22 @@
     total = jnp.concatenate([total * factor, jnp.zeros((lanes - height, lanes), F32)], axis=0)
     upper = total.astype(BF)
     lower = (total - upper.astype(F32)).astype(BF)
-    result = dot_nt(dec_wide[...], upper) + dot_nt(dec_wide[...], lower)
+    dec = w_bwd[0]
+    padded = dec.shape[1]
+    result = dot_nt(dec, upper[:, :padded]) + dot_nt(dec, lower[:, :padded])
     per = spread.shape[1]
     for member in range(spread.shape[0]):
         spread[member] = result[member * per : (member + 1) * per]
 
 
 def member_sum(parts, owned):
-    own, kernels, width = owned.shape
+    kernels, own, width = owned.shape
     total = parts[0]
     for member in range(1, parts.shape[0]):
         total = total + parts[member]
     turned = total.T
     for k in range(kernels):
-        owned[:, k, :] = turned[k * own : (k + 1) * own]
+        owned[k] = turned[k * own : (k + 1) * own, :width]
 
 
 def adjoint(rows, kernels, pred_grad, low, high, back, w_bwd, result):
@@ -189,22 +216,32 @@
     padded = -(-variables // per) * per
     first = (lax.axis_index("lat") * rows).astype(jnp.int32).reshape(1)
     area = jnp.asarray(np.cos(np.pi * (np.arange(lat_count) + 0.5) / lat_count - np.pi / 2), F32)
-    dec_p = jnp.pad(decoder, ((0, 0), (0, padded - variables)))
-    dec_wide = jnp.pad(decoder, ((0, 0), (0, lon - variables)))
+    dec_t = decoder.T
+    basis = cycle_basis.transpose(2, 1, 0)
+    offsets = cycle_offsets.T
 
     low, high = halos(field, "lat")
-    ahead, back, w_fwd, w_bwd = call(
-        functools.partial(prepare, rows, kernels, taps, lat_count),
+    ahead, w_fwd = call(
+        functools.partial(prepare_ahead, rows, taps, lat_count),
         (
             jax.ShapeDtypeStruct((rows, REACH * lon, kernels * lon), BF),
+            jax.ShapeDtypeStruct((padded, (kernels + 1) * chan), BF),
+        ),
+        [SMEM, SMEM, SMEM, pl.BlockSpec(memory_space=pltpu.HBM), VMEM],
+        30_000_000,
+        2_000_000,
+        [pltpu.VMEM(filters.shape, BF), pltpu.SemaphoreType.DMA],
+    )(first, basis, offsets, filters, dec_t)
+    back, w_bwd = call(
+        functools.partial(prepare_back, rows, taps, lat_count),
+        (
             jax.ShapeDtypeStruct((rows, REACH * lon, kernels * lon), BF),
-            jax.ShapeDtypeStruct((padded, (kernels + 1) * chan), BF),
             jax.ShapeDtypeStruct((kernels + 1, chan, padded), BF),
         ),
-        [SMEM, SMEM, SMEM, VMEM, VMEM, VMEM],
-        60_000_000,
-        4_000_000,
-    )(first, cycle_basis.reshape(lat_count, kernels * taps), cycle_offsets, filters, dec_p.T, dec_p)
+        [SMEM, SMEM, SMEM, VMEM, VMEM],
+        50_000_000,
+        2_000_000,
+    )(first, basis, offsets, filters, dec_t)
     packed, predicted, mixed = call(
         functools.partial(forward, rows, kernels),
         (
@@ -230,8 +267,16 @@
         80_000_000,
         1_200_000,
     )(first, area, sums, predicted, target_fields, mixed)
+    parts = lax.all_to_all(partial, "lat", 0, 0, tiled=True)
     grad_low, grad_high = halos(pred_grad, "lat")
-    parts = lax.all_to_all(partial, "lat", 0, 0, tiled=True)
+    latent_grad = call(
+        functools.partial(adjoint, rows, kernels),
+        jax.ShapeDtypeStruct((rows, chan, lon), BF),
+        [VMEM] * 5,
+        200_000_000,
+        2_000_000,
+    )(pred_grad, grad_low, grad_high, back, w_bwd)
+    parts, latent_grad = lax.optimization_barrier((parts, latent_grad))
     factor = 1.0 / math.sqrt(members * lat_count * lon)
     width = chan // members
     spread = call(
@@ -240,19 +285,12 @@
         [VMEM] * 2,
         20_000_000,
         400_000,
-    )(parts, dec_wide)
+    )(parts, w_bwd)
     spread = lax.all_to_all(spread, "ens", 0, 0, tiled=True)
-    latent_grad = call(
-        functools.partial(adjoint, rows, kernels),
-        jax.ShapeDtypeStruct((rows, chan, lon), BF),
-        [VMEM] * 5,
-        200_000_000,
-        2_000_000,
-    )(pred_grad, grad_low, grad_high, back, w_bwd)
     owned = call(
-        member_sum, jax.ShapeDtypeStruct((own, kernels, width), F32), [VMEM], 100_000, 150_000
+        member_sum, jax.ShapeDtypeStruct((kernels, own, width), F32), [VMEM], 100_000, 150_000
     )(spread)
-    return latent_grad[None], owned
+    return latent_grad[None], owned.transpose(1, 0, 2)
 
 
 def solution(mesh):

time: 86.8 us -> 84.8 us (0.977)
  the two profiles are of different devices: /device:TPU:1 before, /device:TPU:64 now
where the time goes in v2:
time: 84.8 us; the launch traced here: 84.1 us
  blocking collectives  39.6 us (47%)
  starting transfers between devices  23.7 us (28%)
  Pallas kernels  9.23 us (11%)
  waiting for transfers between devices  5.68 us (7%)
  local copies, waits for them, and re-layouts  5.15 us (6%)
    all_to_all x1, blocking collectives, body(): visitors = lax.all_to_all(packed, 'ens', 0, 0, tiled=True)  15.8 us
    all_to_all x1, blocking collectives, body(): spread = lax.all_to_all(spread, 'ens', 0, 0, tiled=True)  12.6 us
    all_to_all x1, starting transfers between devices, body(): parts = lax.all_to_all(partial, 'lat', 0, 0, tiled=True)  11.7 us
    all_to_all x1, blocking collectives, body(): sums = lax.all_to_all(sums, 'ens', 0, 0, tiled=True)  11.2 us
    ppermute x2, starting transfers between devices, halos(): lax.ppermute(block[:HALO], axis, down)  8.09 us
    ppermute x2, waiting for transfers between devices, halos(): lax.ppermute(block[-HALO:], axis, up)  5.67 us
    unnamed x22, local copies, waits for them, and re-layouts  4.14 us
    ppermute x2, starting transfers between devices, halos(): lax.ppermute(block[-HALO:], axis, up)  3.84 us
  transfers between devices with their start and end apart: 5, of which 2 were waited for; matrix products, arithmetic and copies ran while one was open for 0% of the time, Pallas kernels for 6%

profile of v2, /device:TPU:64, one launch (start us, length us, event | category | flops | bytes accessed | tf_op | source)
XLA Modules:
  0.0 84.1 jit_solution(15988630721910988924)
XLA Ops:
  0.6 1.0 %slice_bitcast_fusion = (bf16[2,256,128]{2,1,0:T(8,128)(2,1)S(1)}, bf16[2,256,128]{2,1,0:T(8,128)(2,1)S(1)}) fusion(bf16[1,3,256,128]{3,2,1,0:T(8,128)(2,1)} %param.7), kind=kLoop, calls=%fused_computation | loop fusion | bytes 524288 | tf_op jit(solution)/shard_map/slice | solution.py:206
  1.6 3.5 %collective-permute-start.1 = (bf16[2,256,128]{2,1,0:T(8,128)(2,1)S(1)}, bf16[2,256,128]{2,1,0:T(8,128)(2,1)S(1)}, u32[]{:S(2)}, u32[]{:S(2)}) collective-permute-start(bf16[2,256,128]{2,1,0:T(8,128)(2,1)S(1)} %get-tuple-element.24), channel_id=1, source_target_pairs={{1,0},{2,1},{3,2},{4,3},{5,4},{6,5},{7,6},{8,7},{9,8},{10,9},{11,1... | collective-permute-start | bytes 393224 | tf_op jit(solution)/shard_map/ppermute | solution.py:206
  5.1 1.9 %collective-permute-start = (bf16[2,256,128]{2,1,0:T(8,128)(2,1)S(1)}, bf16[2,256,128]{2,1,0:T(8,128)(2,1)S(1)}, u32[]{:S(2)}, u32[]{:S(2)}) collective-permute-start(bf16[2,256,128]{2,1,0:T(8,128)(2,1)S(1)} %get-tuple-element.25), channel_id=1, source_target_pairs={{0,1},{1,2},{2,3},{3,4},{4,5},{5,6},{6,7},{7,8},{8,9},{9,10},{10,1... | collective-permute-start | bytes 393224 | tf_op jit(solution)/shard_map/ppermute | solution.py:206
  7.0 0.0 copy-start
  7.0 1.0 %copy-done = bf16[3,256,256]{2,1,0:T(8,128)(2,1)S(1)} copy-done((bf16[3,256,256]{2,1,0:T(8,128)(2,1)S(1)}, bf16[3,256,256]{2,1,0:T(8,128)(2,1)}, u32[]{:S(2)}) %copy-start) | copy-done | bytes 393240
  8.0 0.8 copy-done.3
  8.8 0.7 copy-done.5
  9.5 0.7 copy-done.8
  10.2 1.9 %shard_map.86 = (bf16[3,640,384]{2,1,0:T(8,128)(2,1)S(1)}, bf16[80,1024]{1,0:T(8,128)(2,1)S(1)}) custom-call(s32[1]{0:T(128)} %bitcast.first, f32[10,3,96]{2,1,0:T(4,128)S(1)} %bitcast.14, s32[10,96]{1,0:T(8,128)S(1)} %bitcast.16, bf16[3,256,256]{2,1,0:T(8,128)(2,1)S(1)} %copy-done, bf16[72,256]{1,0:T(8,128)(2,1)S(1)} %bitcast.12), custom_call_target="tpu_custom_call" | custom-call | flops 30000000 | bytes 2000000 | tf_op jit(solution)/shard_map/pallas_call | solution.py:224
  12.2 0.0 collective-permute-done.1.high
  12.2 1.6 %collective-permute-done.low = bf16[2,256,128]{2,1,0:T(8,128)(2,1)S(1)} collective-permute-done((bf16[2,256,128]{2,1,0:T(8,128)(2,1)S(1)}, bf16[2,256,128]{2,1,0:T(8,128)(2,1)S(1)}, u32[]{:S(2)}, u32[]{:S(2)}) %collective-permute-start) | collective-permute-done | bytes 131104 | tf_op jit(solution)/shard_map/ppermute | solution.py:206
  13.8 0.9 %copy-done.2 = bf16[1,3,256,128]{3,2,1,0:T(8,128)(2,1)S(1)} copy-done((bf16[1,3,256,128]{3,2,1,0:T(8,128)(2,1)S(1)}, bf16[1,3,256,128]{3,2,1,0:T(8,128)(2,1)}, u32[]{:S(2)}) %copy-start.2) | copy-done | bytes 196632
  14.7 1.3 %shard_map.87 = (bf16[16,16,128]{2,1,0:T(8,128)(2,1)S(1)}, f32[3,80,128]{2,1,0:T(8,128)S(1)}, bf16[3,768,128]{2,1,0:T(8,128)(2,1)S(1)}) custom-call(bf16[3,256,128]{2,1,0:T(8,128)(2,1)S(1)} %bitcast.11, bf16[2,256,128]{2,1,0:T(8,128)(2,1)S(1)} %collective-permute-done.low, bf16[2,256,128]{2,1,0:T(8,128)(2,1)S(1)} %collective-permute-done.1.high, ...), custom_call_target="tpu_custom_call" | custom-call | flops 450000000 | bytes 3000000 | tf_op jit(solution)/shard_map/pallas_call | solution.py:245
  16.0 0.0 copy-start.1
  16.0 0.0 copy-start.4
  16.0 0.0 copy-start.6
  16.0 0.0 copy-start.9
  16.1 15.8 %all_to_all.20.visitors = bf16[16,16,128]{2,1,0:T(8,128)(2,1)S(1)} all-to-all(bf16[16,16,128]{2,1,0:T(8,128)(2,1)S(1)} %get-tuple-element.15), channel_id=1, replica_groups=mesh['ens'=16,'lat'=32] {'ens'}, dimensions={0} | all-to-all | bytes 131072 | tf_op jit(solution)/shard_map/all_to_all | solution.py:256
  31.8 0.2 shard_map.88
  32.1 11.2 %all_to_all.21.sums = f32[16,16,128]{2,1,0:T(8,128)S(1)} all-to-all(f32[16,16,128]{2,1,0:T(8,128)S(1)} %shard_map.88), channel_id=1, replica_groups=mesh['ens'=16,'lat'=32] {'ens'}, dimensions={0} | all-to-all | bytes 262144 | tf_op jit(solution)/shard_map/all_to_all | solution.py:258
  43.3 1.5 %shard_map.89 = (bf16[3,80,128]{2,1,0:T(8,128)(2,1)S(1)}, bf16[32,24,128]{2,1,0:T(8,128)(2,1)}) custom-call(s32[1]{0:T(128)} %bitcast.first, f32[96]{0:T(128)S(1)} %copy-done.10, f32[16,16,128]{2,1,0:T(8,128)S(1)} %all_to_all.21.sums, f32[3,80,128]{2,1,0:T(8,128)S(1)} %get-tuple-element.16.predicted, bf16[3,72,128]{2,1,0:T(8,128)(2,1)S(1)} %copy-done.7, ...), custom_call_target="tpu_custom_call" | custom-call | flops 80000000 | bytes 1200000 | tf_op jit(solution)/shard_map/pallas_call | solution.py:260
  44.8 11.7 %all-to-all-start.2 = ((bf16[32,24,128]{2,1,0:T(8,128)(2,1)}), bf16[32,24,128]{2,1,0:T(8,128)(2,1)S(1)}, u32[]{:S(2)}, u32[]{:S(2)}) async-start(bf16[32,24,128]{2,1,0:T(8,128)(2,1)} %get-tuple-element.18), calls=%async_computation.2 | async-start | bytes 393216 | tf_op jit(solution)/shard_map/all_to_all | solution.py:270
  56.6 4.6 %collective-permute-start.3 = (bf16[2,80,128]{2,1,0:T(8,128)(2,1)S(1)}, bf16[2,80,128]{2,1,0:T(8,128)(2,1)S(1)}, u32[]{:S(2)}, u32[]{:S(2)}) collective-permute-start(bf16[2,80,128]{2,1,0:T(8,128)(2,1)S(1)} %get-tuple-element.26), channel_id=1, source_target_pairs={{1,0},{2,1},{3,2},{4,3},{5,4},{6,5},{7,6},{8,7},{9,8},{10,9},{11,1... | collective-permute-start | bytes 122888 | tf_op jit(solution)/shard_map/ppermute | solution.py:206
  61.3 1.9 %collective-permute-start.2 = (bf16[2,80,128]{2,1,0:T(8,128)(2,1)S(1)}, bf16[2,80,128]{2,1,0:T(8,128)(2,1)S(1)}, u32[]{:S(2)}, u32[]{:S(2)}) collective-permute-start(bf16[2,80,128]{2,1,0:T(8,128)(2,1)S(1)} %get-tuple-element.27), channel_id=1, source_target_pairs={{0,1},{1,2},{2,3},{3,4},{4,5},{5,6},{6,7},{7,8},{8,9},{9,10},{10,1... | collective-permute-start | bytes 122888 | tf_op jit(solution)/shard_map/ppermute | solution.py:206
  63.2 1.7 %shard_map.90 = (bf16[3,640,384]{2,1,0:T(8,128)(2,1)S(1)}, bf16[4,256,80]{2,1,0:T(8,128)(2,1)S(1)}) custom-call(s32[1]{0:T(128)} %bitcast.first, f32[10,3,96]{2,1,0:T(4,128)S(1)} %bitcast.15, s32[10,96]{1,0:T(8,128)S(1)} %bitcast.17, bf16[3,256,256]{2,1,0:T(8,128)(2,1)S(1)} %copy-done.1, bf16[72,256]{1,0:T(8,128)(2,1)S(1)} %bitcast.13), custom_call_target="tpu_custom_call" | custom-call | flops 50000000 | bytes 2000000 | tf_op jit(solution)/shard_map/pallas_call | solution.py:235
  64.9 0.0 collective-permute-done.3.high
  64.9 4.0 %collective-permute-done.2.low = bf16[2,80,128]{2,1,0:T(8,128)(2,1)S(1)} collective-permute-done((bf16[2,80,128]{2,1,0:T(8,128)(2,1)S(1)}, bf16[2,80,128]{2,1,0:T(8,128)(2,1)S(1)}, u32[]{:S(2)}, u32[]{:S(2)}) %collective-permute-start.2) | collective-permute-done | bytes 40992 | tf_op jit(solution)/shard_map/ppermute | solution.py:206
  69.0 1.7 %shard_map.91 = bf16[3,256,128]{2,1,0:T(8,128)(2,1)} custom-call(bf16[3,80,128]{2,1,0:T(8,128)(2,1)S(1)} %get-tuple-element.19.pred_grad, bf16[2,80,128]{2,1,0:T(8,128)(2,1)S(1)} %collective-permute-done.2.low, bf16[2,80,128]{2,1,0:T(8,128)(2,1)S(1)} %collective-permute-done.3.high, bf16[3,640,384]{2,1,0:T(8,128)(2,1)S(1)} %get-tuple-element.20.back, ...), custom_call_target="tpu_custom_call" | custom-call | flops 200000000 | bytes 2000000 | tf_op jit(solution)/shard_map/pallas_call | solution.py:272
  70.6 0.0 all-to-all-done.2.parts
  70.6 0.2 shard_map.92
  70.9 12.6 %all_to_all.22.parts = f32[16,16,128]{2,1,0:T(8,128)S(1)} all-to-all(f32[16,16,128]{2,1,0:T(8,128)S(1)} %shard_map.92), channel_id=1, replica_groups=mesh['ens'=16,'lat'=32] {'ens'}, dimensions={0} | all-to-all | bytes 262144 | tf_op jit(solution)/shard_map/all_to_all | solution.py:289
  83.5 0.7 shard_map.93
  (13 shorter events, 0.0 us)
Async XLA Ops:
  1.6 10.5 %collective-permute-start.1 = (bf16[2,256,128]{2,1,0:T(8,128)(2,1)S(1)}, bf16[2,256,128]{2,1,0:T(8,128)(2,1)S(1)}, u32[]{:S(2)}, u32[]{:S(2)}) collective-permute-start(bf16[2,256,128]{2,1,0:T(8,128)(2,1)S(1)} %get-tuple-element.24), channel_id=1, source_target_pairs={{1,0},{2,1},{3,2},{4,3},{5,4},{6,5},{7,6},{8,7},{9,8},{10,9},{11,1... | collective-permute-start | bytes 393224 | tf_op jit(solution)/shard_map/ppermute | solution.py:206
  5.1 8.7 %collective-permute-start = (bf16[2,256,128]{2,1,0:T(8,128)(2,1)S(1)}, bf16[2,256,128]{2,1,0:T(8,128)(2,1)S(1)}, u32[]{:S(2)}, u32[]{:S(2)}) collective-permute-start(bf16[2,256,128]{2,1,0:T(8,128)(2,1)S(1)} %get-tuple-element.25), channel_id=1, source_target_pairs={{0,1},{1,2},{2,3},{3,4},{4,5},{5,6},{6,7},{7,8},{8,9},{9,10},{10,1... | collective-permute-start | bytes 393224 | tf_op jit(solution)/shard_map/ppermute | solution.py:206
  7.0 1.0 %copy-start = (bf16[3,256,256]{2,1,0:T(8,128)(2,1)S(1)}, bf16[3,256,256]{2,1,0:T(8,128)(2,1)}, u32[]{:S(2)}) copy-start(bf16[3,256,256]{2,1,0:T(8,128)(2,1)} %filters.3) | copy-start | bytes 1179652
  8.0 0.8 copy-start.3
  8.8 0.7 copy-start.5
  9.5 0.7 copy-start.8
  10.2 33.1 %copy-start.7 = (bf16[3,72,128]{2,1,0:T(8,128)(2,1)S(1)}, bf16[3,72,128]{2,1,0:T(8,128)(2,1)}, u32[]{:S(2)}) copy-start(bf16[3,72,128]{2,1,0:T(8,128)(2,1)} %target.1) | copy-start | bytes 165892
  10.2 33.1 %copy-start.10 = (f32[96]{0:T(128)S(1)}, f32[96]{0:T(128)}, u32[]{:S(2)}) copy-start(f32[96]{0:T(128)} %constant.8.clone.area) | copy-start | bytes 1156
  13.8 0.9 %copy-start.2 = (bf16[1,3,256,128]{3,2,1,0:T(8,128)(2,1)S(1)}, bf16[1,3,256,128]{3,2,1,0:T(8,128)(2,1)}, u32[]{:S(2)}) copy-start(bf16[1,3,256,128]{3,2,1,0:T(8,128)(2,1)} %param.7) | copy-start | bytes 589828
  16.0 47.2 %copy-start.1 = (bf16[3,256,256]{2,1,0:T(8,128)(2,1)S(1)}, bf16[3,256,256]{2,1,0:T(8,128)(2,1)}, u32[]{:S(2)}) copy-start(bf16[3,256,256]{2,1,0:T(8,128)(2,1)} %filters.3) | copy-start | bytes 1179652
  16.0 47.2 %copy-start.4 = (bf16[256,72]{0,1:T(8,128)(2,1)S(1)}, bf16[256,72]{0,1:T(8,128)(2,1)}, u32[]{:S(2)}) copy-start(bf16[256,72]{0,1:T(8,128)(2,1)} %param.10) | copy-start | bytes 110596
  16.0 47.2 %copy-start.6 = (f32[96,3,10]{0,1,2:T(4,128)S(1)}, f32[96,3,10]{0,1,2:T(4,128)}, u32[]{:S(2)}) copy-start(f32[96,3,10]{0,1,2:T(4,128)} %param.11) | copy-start | bytes 34564
  16.0 47.2 %copy-start.9 = (s32[96,10]{0,1:T(8,128)S(1)}, s32[96,10]{0,1:T(8,128)}, u32[]{:S(2)}) copy-start(s32[96,10]{0,1:T(8,128)} %param.12) | copy-start | bytes 11524
  44.8 25.8 %all-to-all-start.2 = ((bf16[32,24,128]{2,1,0:T(8,128)(2,1)}), bf16[32,24,128]{2,1,0:T(8,128)(2,1)S(1)}, u32[]{:S(2)}, u32[]{:S(2)}) async-start(bf16[32,24,128]{2,1,0:T(8,128)(2,1)} %get-tuple-element.18), calls=%async_computation.2 | async-start | bytes 393216 | tf_op jit(solution)/shard_map/all_to_all | solution.py:270
  56.6 8.3 %collective-permute-start.3 = (bf16[2,80,128]{2,1,0:T(8,128)(2,1)S(1)}, bf16[2,80,128]{2,1,0:T(8,128)(2,1)S(1)}, u32[]{:S(2)}, u32[]{:S(2)}) collective-permute-start(bf16[2,80,128]{2,1,0:T(8,128)(2,1)S(1)} %get-tuple-element.26), channel_id=1, source_target_pairs={{1,0},{2,1},{3,2},{4,3},{5,4},{6,5},{7,6},{8,7},{9,8},{10,9},{11,1... | collective-permute-start | bytes 122888 | tf_op jit(solution)/shard_map/ppermute | solution.py:206
  61.3 7.7 %collective-permute-start.2 = (bf16[2,80,128]{2,1,0:T(8,128)(2,1)S(1)}, bf16[2,80,128]{2,1,0:T(8,128)(2,1)S(1)}, u32[]{:S(2)}, u32[]{:S(2)}) collective-permute-start(bf16[2,80,128]{2,1,0:T(8,128)(2,1)S(1)} %get-tuple-element.27), channel_id=1, source_target_pairs={{0,1},{1,2},{2,3},{3,4},{4,5},{5,6},{6,7},{7,8},{8,9},{9,10},{10,1... | collective-permute-start | bytes 122888 | tf_op jit(solution)/shard_map/ppermute | solution.py:206

commit v3 on v2

--- a/solution.py
+++ b/solution.py
@@ -70,17 +70,22 @@
     return jnp.concatenate([dec_t[...].astype(F32), jnp.zeros((padded - rows, chan), F32)], axis=0).astype(BF)
 
 
-def prepare_ahead(rows, taps, lat_count, first, basis, offsets, filters, dec_t, ahead, w_fwd, held, sem):
-    fetch = pltpu.make_async_copy(filters, held, sem)
-    fetch.start()
+def prepare_ahead(
+    rows, taps, lat_count, first, basis, offsets, filters, dec_in, field, ahead, w_fwd, held, near, dec_t, sems
+):
+    moves = ((filters, held), (dec_in, dec_t), (field, near))
+    moves = [pltpu.make_async_copy(source, target, sems.at[n]) for n, (source, target) in enumerate(moves)]
+    for move in moves:
+        move.start()
     lag = lags(ahead.shape[1] // REACH)
     for row in range(rows):
         for slot in range(REACH):
             tap_block(taps, lat_count, lag, first[0], basis, offsets, ahead, row, row, slot, slot, 1)
     kernels, chan = held.shape[:2]
+    for move in moves:
+        move.wait()
     dec = padded_rows(dec_t, w_fwd.shape[0])
     w_fwd[:, :chan] = dec
-    fetch.wait()
     for k in range(kernels):
         w_fwd[:, (k + 1) * chan : (k + 2) * chan] = dot_nt(dec, held[k]).astype(BF)
 
@@ -221,17 +226,22 @@
     offsets = cycle_offsets.T
 
     low, high = halos(field, "lat")
-    ahead, w_fwd = call(
+    stay = functools.partial(pltpu.with_memory_space_constraint, memory_space=pltpu.HBM)
+    hbm = pl.BlockSpec(memory_space=pltpu.HBM)
+    ahead, w_fwd, held, near, dec_near = call(
         functools.partial(prepare_ahead, rows, taps, lat_count),
         (
             jax.ShapeDtypeStruct((rows, REACH * lon, kernels * lon), BF),
             jax.ShapeDtypeStruct((padded, (kernels + 1) * chan), BF),
+            jax.ShapeDtypeStruct(filters.shape, BF),
+            jax.ShapeDtypeStruct(field.shape, BF),
+            jax.ShapeDtypeStruct(dec_t.shape, BF),
         ),
-        [SMEM, SMEM, SMEM, pl.BlockSpec(memory_space=pltpu.HBM), VMEM],
+        [SMEM, SMEM, SMEM, hbm, hbm, hbm],
         30_000_000,
         2_000_000,
-        [pltpu.VMEM(filters.shape, BF), pltpu.SemaphoreType.DMA],
-    )(first, basis, offsets, filters, dec_t)
+        [pltpu.SemaphoreType.DMA((3,))],
+    )(first, stay(basis), stay(offsets), stay(filters), stay(dec_t), stay(field))
     back, w_bwd = call(
         functools.partial(prepare_back, rows, taps, lat_count),
         (
@@ -241,7 +251,7 @@
         [SMEM, SMEM, SMEM, VMEM, VMEM],
         50_000_000,
         2_000_000,
-    )(first, basis, offsets, filters, dec_t)
+    )(first, stay(basis), stay(offsets), held, dec_near)
     packed, predicted, mixed = call(
         functools.partial(forward, rows, kernels),
         (
@@ -252,8 +262,9 @@
         [VMEM] * 5,
         450_000_000,
         3_000_000,
-    )(field, low, high, ahead, w_fwd)
+    )(near, low, high, ahead, w_fwd)
     visitors = lax.all_to_all(packed, "ens", 0, 0, tiled=True)
+    visitors, back, w_bwd = lax.optimization_barrier((visitors, back, w_bwd))
     sums = call(pairs, jax.ShapeDtypeStruct((members, per, lon), F32), [VMEM], 2_000_000, 200_000)(visitors)
     sums = lax.all_to_all(sums, "ens", 0, 0, tiled=True)
     own = chan // bands

time: 84.8 us -> 83.1 us (0.980)
  blocking collectives: 39.6 us -> 22.6 us
  waiting for transfers between devices: 5.68 us -> 16.7 us
  starting transfers between devices: 23.7 us -> 30.8 us
  local copies, waits for them, and re-layouts: 5.15 us -> 1.02 us
  Pallas kernels: 9.23 us -> 10.6 us
    all_to_all x1 -> x0, blocking collectives: 15.8 us -> none  [body(): visitors = lax.all_to_all(packed, 'ens', 0, 0, tiled=True)]
    all_to_all x0 -> x1, starting transfers between devices: none -> 7.23 us  [body(): visitors = lax.all_to_all(packed, 'ens', 0, 0, tiled=True)]
    all_to_all x0 -> x1, waiting for transfers between devices: none -> 6.7 us  [body(): visitors = lax.all_to_all(packed, 'ens', 0, 0, tiled=True)]
    ppermute x2, waiting for transfers between devices: 5.67 us -> 10 us  [halos(): lax.ppermute(block[-HALO:], axis, up)]
    unnamed x22 -> x4, local copies, waits for them, and re-layouts: 4.14 us -> 0.01 us
    all_to_all x1, blocking collectives: 12.6 us -> 11.5 us  [body(): spread = lax.all_to_all(spread, 'ens', 0, 0, tiled=True)]
  transfers between devices with their start and end apart: 5 -> 6, of which waited for: 2 -> 3; matrix products, arithmetic and copies ran while one was open for 0% -> 0% of each run, Pallas kernels for 6% -> 7%
where the time goes in v3:
time: 83.1 us; the launch traced here: 82.5 us
  starting transfers between devices  30.8 us (37%)
  blocking collectives  22.6 us (27%)
  waiting for transfers between devices  16.7 us (20%)
  Pallas kernels  10.6 us (13%)
  local copies, waits for them, and re-layouts  1.02 us (1%)
    all_to_all x1, starting transfers between devices, body(): parts = lax.all_to_all(partial, 'lat', 0, 0, tiled=True)  11.6 us
    all_to_all x1, blocking collectives, body(): spread = lax.all_to_all(spread, 'ens', 0, 0, tiled=True)  11.5 us
    all_to_all x1, blocking collectives, body(): sums = lax.all_to_all(sums, 'ens', 0, 0, tiled=True)  11.2 us
    ppermute x2, waiting for transfers between devices, halos(): lax.ppermute(block[-HALO:], axis, up)  10 us
    ppermute x2, starting transfers between devices, halos(): lax.ppermute(block[:HALO], axis, down)  8.09 us
    all_to_all x1, starting transfers between devices, body(): visitors = lax.all_to_all(packed, 'ens', 0, 0, tiled=True)  7.23 us
    all_to_all x1, waiting for transfers between devices, body(): visitors = lax.all_to_all(packed, 'ens', 0, 0, tiled=True)  6.7 us
    ppermute x2, starting transfers between devices, halos(): lax.ppermute(block[-HALO:], axis, up)  3.84 us
  transfers between devices with their start and end apart: 6, of which 3 were waited for; matrix products, arithmetic and copies ran while one was open for 0% of the time, Pallas kernels for 7%

profile of v3, /device:TPU:64, one launch (start us, length us, event | category | flops | bytes accessed | tf_op | source)
XLA Modules:
  0.0 82.5 jit_solution(2260496202524473004)
XLA Ops:
  0.6 1.0 %slice_bitcast_fusion = (bf16[2,256,128]{2,1,0:T(8,128)(2,1)S(1)}, bf16[2,256,128]{2,1,0:T(8,128)(2,1)S(1)}) fusion(bf16[1,3,256,128]{3,2,1,0:T(8,128)(2,1)} %param.7), kind=kLoop, calls=%fused_computation | loop fusion | bytes 524288 | tf_op jit(solution)/shard_map/slice | solution.py:211
  1.6 3.5 %collective-permute-start.1 = (bf16[2,256,128]{2,1,0:T(8,128)(2,1)S(1)}, bf16[2,256,128]{2,1,0:T(8,128)(2,1)S(1)}, u32[]{:S(2)}, u32[]{:S(2)}) collective-permute-start(bf16[2,256,128]{2,1,0:T(8,128)(2,1)S(1)} %get-tuple-element.36), channel_id=1, source_target_pairs={{1,0},{2,1},{3,2},{4,3},{5,4},{6,5},{7,6},{8,7},{9,8},{10,9},{11,1... | collective-permute-start | bytes 393224 | tf_op jit(solution)/shard_map/ppermute | solution.py:211
  5.1 1.9 %collective-permute-start = (bf16[2,256,128]{2,1,0:T(8,128)(2,1)S(1)}, bf16[2,256,128]{2,1,0:T(8,128)(2,1)S(1)}, u32[]{:S(2)}, u32[]{:S(2)}) collective-permute-start(bf16[2,256,128]{2,1,0:T(8,128)(2,1)S(1)} %get-tuple-element.37), channel_id=1, source_target_pairs={{0,1},{1,2},{2,3},{3,4},{4,5},{5,6},{6,7},{7,8},{8,9},{9,10},{10,1... | collective-permute-start | bytes 393224 | tf_op jit(solution)/shard_map/ppermute | solution.py:211
  7.0 2.5 %shard_map.86 = (bf16[3,640,384]{2,1,0:T(8,128)(2,1)S(1)}, bf16[80,1024]{1,0:T(8,128)(2,1)S(1)}, bf16[3,256,256]{2,1,0:T(8,128)(2,1)S(1)}, bf16[3,256,128]{2,1,0:T(8,128)(2,1)S(1)}, bf16[72,256]{1,0:T(8,128)(2,1)S(1)}) custom-call(s32[1]{0:T(128)} %bitcast.first, f32[10,3,96]{2,1,0:T(4,128)} %bitcast.13, s32[10,96]{1,0:T(8,128)} %bitcast.16, ...), custom_call_target="tpu_custom_call" | custom-call | flops 30000000 | bytes 2000000 | tf_op jit(solution)/shard_map/pallas_call | solution.py:231
  9.5 0.0 collective-permute-done.1.high
  9.5 4.2 %collective-permute-done.low = bf16[2,256,128]{2,1,0:T(8,128)(2,1)S(1)} collective-permute-done((bf16[2,256,128]{2,1,0:T(8,128)(2,1)S(1)}, bf16[2,256,128]{2,1,0:T(8,128)(2,1)S(1)}, u32[]{:S(2)}, u32[]{:S(2)}) %collective-permute-start) | collective-permute-done | bytes 131104 | tf_op jit(solution)/shard_map/ppermute | solution.py:211
  13.8 0.0 copy-start
  13.8 0.0 copy-start.1
  13.8 1.9 %shard_map.87 = (bf16[16,16,128]{2,1,0:T(8,128)(2,1)}, f32[3,80,128]{2,1,0:T(8,128)S(1)}, bf16[3,768,128]{2,1,0:T(8,128)(2,1)S(1)}) custom-call(bf16[3,256,128]{2,1,0:T(8,128)(2,1)S(1)} %get-tuple-element.19.field, bf16[2,256,128]{2,1,0:T(8,128)(2,1)S(1)} %collective-permute-done.low, bf16[2,256,128]{2,1,0:T(8,128)(2,1)S(1)} %collective-permute-done.1.high, ...), custom_call_target="tpu_custom_call" | custom-call | flops 450000000 | bytes 3000000 | tf_op jit(solution)/shard_map/pallas_call | solution.py:255
  15.7 7.2 %all-to-all-start = ((bf16[16,16,128]{2,1,0:T(8,128)(2,1)}), bf16[16,16,128]{2,1,0:T(8,128)(2,1)S(1)}, u32[]{:S(2)}, u32[]{:S(2)}) async-start(bf16[16,16,128]{2,1,0:T(8,128)(2,1)} %get-tuple-element.22), calls=%async_computation | async-start | bytes 131072 | tf_op jit(solution)/shard_map/all_to_all | solution.py:266
  22.9 1.8 %shard_map.88 = (bf16[3,640,384]{2,1,0:T(8,128)(2,1)S(1)}, bf16[4,256,80]{2,1,0:T(8,128)(2,1)S(1)}) custom-call(s32[1]{0:T(128)} %bitcast.first, f32[10,3,96]{2,1,0:T(4,128)} %bitcast.14, s32[10,96]{1,0:T(8,128)} %bitcast.17, bf16[3,256,256]{2,1,0:T(8,128)(2,1)S(1)} %get-tuple-element.23.filters, bf16[72,256]{1,0:T(8,128)(2,1)S(1)} %get-tuple-element.24.dec_t), custom_call_target="tpu_custom_call" | custom-call | flops 50000000 | bytes 2000000 | tf_op jit(solution)/shard_map/pallas_call | solution.py:245
  24.8 6.7 %all-to-all-done.visitors = bf16[16,16,128]{2,1,0:T(8,128)(2,1)S(1)} async-done(((bf16[16,16,128]{2,1,0:T(8,128)(2,1)}), bf16[16,16,128]{2,1,0:T(8,128)(2,1)S(1)}, u32[]{:S(2)}, u32[]{:S(2)}) %all-to-all-start) | async-done | bytes 65568 | tf_op jit(solution)/shard_map/all_to_all | solution.py:266
  31.5 0.2 shard_map.89
  31.7 11.2 %all_to_all.20.sums = f32[16,16,128]{2,1,0:T(8,128)S(1)} all-to-all(f32[16,16,128]{2,1,0:T(8,128)S(1)} %shard_map.89), channel_id=1, replica_groups=mesh['ens'=16,'lat'=32] {'ens'}, dimensions={0} | all-to-all | bytes 262144 | tf_op jit(solution)/shard_map/all_to_all | solution.py:269
  42.9 0.0 copy-done
  42.9 0.0 copy-done.1
  42.9 1.5 %shard_map.90 = (bf16[3,80,128]{2,1,0:T(8,128)(2,1)S(1)}, bf16[32,24,128]{2,1,0:T(8,128)(2,1)}) custom-call(s32[1]{0:T(128)} %bitcast.first, f32[96]{0:T(128)S(1)} %copy-done.1, f32[16,16,128]{2,1,0:T(8,128)S(1)} %all_to_all.20.sums, f32[3,80,128]{2,1,0:T(8,128)S(1)} %get-tuple-element.28.predicted, bf16[3,72,128]{2,1,0:T(8,128)(2,1)S(1)} %copy-done, ...), custom_call_target="tpu_custom_call" | custom-call | flops 80000000 | bytes 1200000 | tf_op jit(solution)/shard_map/pallas_call | solution.py:271
  44.4 11.6 %all-to-all-start.2 = ((bf16[32,24,128]{2,1,0:T(8,128)(2,1)}), bf16[32,24,128]{2,1,0:T(8,128)(2,1)S(1)}, u32[]{:S(2)}, u32[]{:S(2)}) async-start(bf16[32,24,128]{2,1,0:T(8,128)(2,1)} %get-tuple-element.30), calls=%async_computation.2 | async-start | bytes 393216 | tf_op jit(solution)/shard_map/all_to_all | solution.py:281
  56.1 4.6 %collective-permute-start.3 = (bf16[2,80,128]{2,1,0:T(8,128)(2,1)S(1)}, bf16[2,80,128]{2,1,0:T(8,128)(2,1)S(1)}, u32[]{:S(2)}, u32[]{:S(2)}) collective-permute-start(bf16[2,80,128]{2,1,0:T(8,128)(2,1)S(1)} %get-tuple-element.38), channel_id=1, source_target_pairs={{1,0},{2,1},{3,2},{4,3},{5,4},{6,5},{7,6},{8,7},{9,8},{10,9},{11,1... | collective-permute-start | bytes 122888 | tf_op jit(solution)/shard_map/ppermute | solution.py:211
  60.7 1.9 %collective-permute-start.2 = (bf16[2,80,128]{2,1,0:T(8,128)(2,1)S(1)}, bf16[2,80,128]{2,1,0:T(8,128)(2,1)S(1)}, u32[]{:S(2)}, u32[]{:S(2)}) collective-permute-start(bf16[2,80,128]{2,1,0:T(8,128)(2,1)S(1)} %get-tuple-element.39), channel_id=1, source_target_pairs={{0,1},{1,2},{2,3},{3,4},{4,5},{5,6},{6,7},{7,8},{8,9},{9,10},{10,1... | collective-permute-start | bytes 122888 | tf_op jit(solution)/shard_map/ppermute | solution.py:211
  62.6 0.0 collective-permute-done.3.high
  62.7 5.8 %collective-permute-done.2.low = bf16[2,80,128]{2,1,0:T(8,128)(2,1)S(1)} collective-permute-done((bf16[2,80,128]{2,1,0:T(8,128)(2,1)S(1)}, bf16[2,80,128]{2,1,0:T(8,128)(2,1)S(1)}, u32[]{:S(2)}, u32[]{:S(2)}) %collective-permute-start.2) | collective-permute-done | bytes 40992 | tf_op jit(solution)/shard_map/ppermute | solution.py:211
  68.4 1.7 %shard_map.91 = bf16[3,256,128]{2,1,0:T(8,128)(2,1)} custom-call(bf16[3,80,128]{2,1,0:T(8,128)(2,1)S(1)} %get-tuple-element.31.pred_grad, bf16[2,80,128]{2,1,0:T(8,128)(2,1)S(1)} %collective-permute-done.2.low, bf16[2,80,128]{2,1,0:T(8,128)(2,1)S(1)} %collective-permute-done.3.high, bf16[3,640,384]{2,1,0:T(8,128)(2,1)S(1)} %get-tuple-element.32.back, ...), custom_call_target="tpu_custom_call" | custom-call | flops 200000000 | bytes 2000000 | tf_op jit(solution)/shard_map/pallas_call | solution.py:283
  70.1 0.0 all-to-all-done.2.parts
  70.1 0.2 shard_map.92
  70.3 11.5 %all_to_all.21.parts = f32[16,16,128]{2,1,0:T(8,128)S(1)} all-to-all(f32[16,16,128]{2,1,0:T(8,128)S(1)} %shard_map.92), channel_id=1, replica_groups=mesh['ens'=16,'lat'=32] {'ens'}, dimensions={0} | all-to-all | bytes 262144 | tf_op jit(solution)/shard_map/all_to_all | solution.py:300
  81.8 0.7 shard_map.93
  (1 shorter events, 0.0 us)
Async XLA Ops:
  1.6 7.9 %collective-permute-start.1 = (bf16[2,256,128]{2,1,0:T(8,128)(2,1)S(1)}, bf16[2,256,128]{2,1,0:T(8,128)(2,1)S(1)}, u32[]{:S(2)}, u32[]{:S(2)}) collective-permute-start(bf16[2,256,128]{2,1,0:T(8,128)(2,1)S(1)} %get-tuple-element.36), channel_id=1, source_target_pairs={{1,0},{2,1},{3,2},{4,3},{5,4},{6,5},{7,6},{8,7},{9,8},{10,9},{11,1... | collective-permute-start | bytes 393224 | tf_op jit(solution)/shard_map/ppermute | solution.py:211
  5.1 8.7 %collective-permute-start = (bf16[2,256,128]{2,1,0:T(8,128)(2,1)S(1)}, bf16[2,256,128]{2,1,0:T(8,128)(2,1)S(1)}, u32[]{:S(2)}, u32[]{:S(2)}) collective-permute-start(bf16[2,256,128]{2,1,0:T(8,128)(2,1)S(1)} %get-tuple-element.37), channel_id=1, source_target_pairs={{0,1},{1,2},{2,3},{3,4},{4,5},{5,6},{6,7},{7,8},{8,9},{9,10},{10,1... | collective-permute-start | bytes 393224 | tf_op jit(solution)/shard_map/ppermute | solution.py:211
  13.8 29.1 %copy-start = (bf16[3,72,128]{2,1,0:T(8,128)(2,1)S(1)}, bf16[3,72,128]{2,1,0:T(8,128)(2,1)}, u32[]{:S(2)}) copy-start(bf16[3,72,128]{2,1,0:T(8,128)(2,1)} %target.1) | copy-start | bytes 165892
  13.8 29.1 %copy-start.1 = (f32[96]{0:T(128)S(1)}, f32[96]{0:T(128)}, u32[]{:S(2)}) copy-start(f32[96]{0:T(128)} %constant.8.clone.area) | copy-start | bytes 1156
  15.7 15.8 %all-to-all-start = ((bf16[16,16,128]{2,1,0:T(8,128)(2,1)}), bf16[16,16,128]{2,1,0:T(8,128)(2,1)S(1)}, u32[]{:S(2)}, u32[]{:S(2)}) async-start(bf16[16,16,128]{2,1,0:T(8,128)(2,1)} %get-tuple-element.22), calls=%async_computation | async-start | bytes 131072 | tf_op jit(solution)/shard_map/all_to_all | solution.py:266
  44.4 25.7 %all-to-all-start.2 = ((bf16[32,24,128]{2,1,0:T(8,128)(2,1)}), bf16[32,24,128]{2,1,0:T(8,128)(2,1)S(1)}, u32[]{:S(2)}, u32[]{:S(2)}) async-start(bf16[32,24,128]{2,1,0:T(8,128)(2,1)} %get-tuple-element.30), calls=%async_computation.2 | async-start | bytes 393216 | tf_op jit(solution)/shard_map/all_to_all | solution.py:281
  56.1 6.6 %collective-permute-start.3 = (bf16[2,80,128]{2,1,0:T(8,128)(2,1)S(1)}, bf16[2,80,128]{2,1,0:T(8,128)(2,1)S(1)}, u32[]{:S(2)}, u32[]{:S(2)}) collective-permute-start(bf16[2,80,128]{2,1,0:T(8,128)(2,1)S(1)} %get-tuple-element.38), channel_id=1, source_target_pairs={{1,0},{2,1},{3,2},{4,3},{5,4},{6,5},{7,6},{8,7},{9,8},{10,9},{11,1... | collective-permute-start | bytes 122888 | tf_op jit(solution)/shard_map/ppermute | solution.py:211
  60.7 7.7 %collective-permute-start.2 = (bf16[2,80,128]{2,1,0:T(8,128)(2,1)S(1)}, bf16[2,80,128]{2,1,0:T(8,128)(2,1)S(1)}, u32[]{:S(2)}, u32[]{:S(2)}) collective-permute-start(bf16[2,80,128]{2,1,0:T(8,128)(2,1)S(1)} %get-tuple-element.39), channel_id=1, source_target_pairs={{0,1},{1,2},{2,3},{3,4},{4,5},{5,6},{6,7},{7,8},{8,9},{9,10},{10,1... | collective-permute-start | bytes 122888 | tf_op jit(solution)/shard_map/ppermute | solution.py:211

commit v4 on v3

--- a/solution.py
+++ b/solution.py
@@ -71,7 +71,7 @@
 
 
 def prepare_ahead(
-    rows, taps, lat_count, first, basis, offsets, filters, dec_in, field, ahead, w_fwd, held, near, dec_t, sems
+    rows, taps, lat_count, place, basis, offsets, filters, dec_in, field, ahead, w_fwd, held, near, dec_t, sems
 ):
     moves = ((filters, held), (dec_in, dec_t), (field, near))
     moves = [pltpu.make_async_copy(source, target, sems.at[n]) for n, (source, target) in enumerate(moves)]
@@ -80,7 +80,7 @@
     lag = lags(ahead.shape[1] // REACH)
     for row in range(rows):
         for slot in range(REACH):
-            tap_block(taps, lat_count, lag, first[0], basis, offsets, ahead, row, row, slot, slot, 1)
+            tap_block(taps, lat_count, lag, place[0] * rows, basis, offsets, ahead, row, row, slot, slot, 1)
     kernels, chan = held.shape[:2]
     for move in moves:
         move.wait()
@@ -90,12 +90,12 @@
         w_fwd[:, (k + 1) * chan : (k + 2) * chan] = dot_nt(dec, held[k]).astype(BF)
 
 
-def prepare_back(rows, taps, lat_count, first, basis, offsets, filters, dec_t, back, w_bwd):
+def prepare_back(rows, taps, lat_count, place, basis, offsets, filters, dec_t, back, w_bwd):
     lag = lags(back.shape[1] // REACH)
     for row in range(rows):
         for slot in range(REACH):
             step = REACH - 1 - slot
-            tap_block(taps, lat_count, lag, first[0], basis, offsets, back, row, row + slot - HALO, slot, step, -1)
+            tap_block(taps, lat_count, lag, place[0] * rows, basis, offsets, back, row, row + slot - HALO, slot, step, -1)
     kernels, chan = filters.shape[:2]
     dec = padded_rows(dec_t, w_bwd.shape[2])
     rank = (chan, chan)
@@ -105,10 +105,11 @@
         w_bwd[k + 1] = dot_nt(filters[k], dec).astype(BF)
 
 
-def forward(rows, kernels, field, low, high, ahead, w_fwd, packed, predicted, mixed):
+def forward(rows, kernels, place, field, cross, chip, ahead, w_fwd, packed, predicted, mixed):
     lon = field.shape[2]
     chan = field.shape[1]
-    wide = [low[0], low[1]] + [field[i] for i in range(rows)] + [high[0], high[1]]
+    low, high = sides((place[0] & 1) == 1, cross, chip)
+    wide = low + [field[i] for i in range(rows)] + high
     per = packed.shape[1]
     padded = predicted.shape[1]
     pieces = padded // per
@@ -141,21 +142,27 @@
             sums[m, start : start + 8, :] = totals[m]
 
 
-def gradient(rows, kernels, members, first, area, sums, predicted, target, mixed, pred_grad, partial):
+def gradient(rows, kernels, members, place, area, sums, predicted, target, mixed, pred_grad, cross, chip, partial):
     variables = target.shape[1]
     padded = predicted.shape[1]
     per = sums.shape[1]
     pieces = padded // per
     lon = predicted.shape[2]
     chan = mixed.shape[1] // kernels
-    grads = []
+    grads, edges = [], []
+    odd = (place[0] & 1) == 1
     for i in range(rows):
         pair_sum = jnp.concatenate([sums[i * pieces + q] for q in range(pieces)], axis=0)
         aim = jnp.concatenate([target[i].astype(F32), jnp.zeros((padded - variables, lon), F32)], axis=0)
-        grad = area[first[0] + i] * (smooth_slope(predicted[i] - aim) - pair_sum * (1.0 / (members - 1)))
+        grad = area[place[0] * rows + i] * (smooth_slope(predicted[i] - aim) - pair_sum * (1.0 / (members - 1)))
         grad = grad.astype(BF)
         pred_grad[i] = grad
+        edges.append(grad)
         grads.append(jnp.concatenate([grad, jnp.zeros((lon - padded, lon), BF)], axis=0))
+    for n in range(HALO):
+        top, bottom = edges[rows - HALO + n], edges[n]
+        cross[n] = jnp.where(odd, top, bottom)
+        chip[n] = jnp.where(odd, bottom, top)
     total = dot_nt(
         jnp.concatenate([mixed[i] for i in range(rows)], axis=1), jnp.concatenate(grads, axis=1)
     )
@@ -193,9 +200,10 @@
         owned[k] = turned[k * own : (k + 1) * own, :width]
 
 
-def adjoint(rows, kernels, pred_grad, low, high, back, w_bwd, result):
+def adjoint(rows, kernels, place, pred_grad, cross, chip, back, w_bwd, result):
     lon = pred_grad.shape[2]
-    wide = [low[0], low[1]] + [pred_grad[i] for i in range(rows)] + [high[0], high[1]]
+    low, high = sides((place[0] & 1) == 1, cross, chip)
+    wide = low + [pred_grad[i] for i in range(rows)] + high
     for i in range(rows):
         taps = dot_nn(jnp.concatenate(wide[i : i + REACH], axis=1), back[i]).astype(BF)
         total = dot_nn(w_bwd[0], wide[i + HALO])
@@ -204,11 +212,33 @@
         result[i] = total.astype(BF)
 
 
-def halos(block, axis):
+def cut(place, field, cross, chip, sems):
+    rows = field.shape[0]
+    odd = (place[0] & 1)
+    far = (rows - HALO) * odd
+    moves = [
+        pltpu.make_async_copy(field.at[pl.ds(far, HALO)], cross, sems.at[0]),
+        pltpu.make_async_copy(field.at[pl.ds(rows - HALO - far, HALO)], chip, sems.at[1]),
+    ]
+    for move in moves:
+        move.start()
+    for move in moves:
+        move.wait()
+
+
+def sides(odd, cross, chip):
+    low = [jnp.where(odd, chip[n], cross[n]) for n in range(HALO)]
+    high = [jnp.where(odd, cross[n], chip[n]) for n in range(HALO)]
+    return low, high
+
+
+def exchange(cross, chip, axis):
     count = lax.axis_size(axis)
-    up = [(i, i + 1) for i in range(count - 1)]
-    down = [(target, source) for source, target in up]
-    return lax.ppermute(block[-HALO:], axis, up), lax.ppermute(block[:HALO], axis, down)
+    far = [(i, i + 1) for i in range(1, count - 1, 2)]
+    near = [(i, i + 1) for i in range(0, count - 1, 2)]
+    cross = lax.ppermute(cross, axis, far + [(b, a) for a, b in far])
+    chip = lax.ppermute(chip, axis, near + [(b, a) for a, b in near])
+    return cross, chip
 
 
 def body(latent_fields, target_fields, filters, decoder, cycle_basis, cycle_offsets):
@@ -219,15 +249,19 @@
     members, bands = lax.axis_size("ens"), lax.axis_size("lat")
     per = 16
     padded = -(-variables // per) * per
-    first = (lax.axis_index("lat") * rows).astype(jnp.int32).reshape(1)
+    band = lax.axis_index("lat").astype(jnp.int32)
+    place = band.reshape(1)
     area = jnp.asarray(np.cos(np.pi * (np.arange(lat_count) + 0.5) / lat_count - np.pi / 2), F32)
     dec_t = decoder.T
     basis = cycle_basis.transpose(2, 1, 0)
     offsets = cycle_offsets.T
 
-    low, high = halos(field, "lat")
     stay = functools.partial(pltpu.with_memory_space_constraint, memory_space=pltpu.HBM)
     hbm = pl.BlockSpec(memory_space=pltpu.HBM)
+    edge = jax.ShapeDtypeStruct((HALO, chan, lon), BF)
+    pair = pltpu.SemaphoreType.DMA((2,))
+    cross, chip = call(cut, (edge, edge), [SMEM, hbm], 0, 500_000, [pair])(place, stay(field))
+    cross, chip = exchange(cross, chip, "lat")
     ahead, w_fwd, held, near, dec_near = call(
         functools.partial(prepare_ahead, rows, taps, lat_count),
         (
@@ -241,7 +275,7 @@
         30_000_000,
         2_000_000,
         [pltpu.SemaphoreType.DMA((3,))],
-    )(first, stay(basis), stay(offsets), stay(filters), stay(dec_t), stay(field))
+    )(place, stay(basis), stay(offsets), stay(filters), stay(dec_t), stay(field))
     back, w_bwd = call(
         functools.partial(prepare_back, rows, taps, lat_count),
         (
@@ -251,7 +285,7 @@
         [SMEM, SMEM, SMEM, VMEM, VMEM],
         50_000_000,
         2_000_000,
-    )(first, stay(basis), stay(offsets), held, dec_near)
+    )(place, stay(basis), stay(offsets), held, dec_near)
     packed, predicted, mixed = call(
         functools.partial(forward, rows, kernels),
         (
@@ -259,35 +293,38 @@
             jax.ShapeDtypeStruct((rows, padded, lon), F32),
             jax.ShapeDtypeStruct((rows, kernels * chan, lon), BF),
         ),
-        [VMEM] * 5,
+        [SMEM] + [VMEM] * 5,
         450_000_000,
         3_000_000,
-    )(near, low, high, ahead, w_fwd)
+    )(place, near, cross, chip, ahead, w_fwd)
     visitors = lax.all_to_all(packed, "ens", 0, 0, tiled=True)
     visitors, back, w_bwd = lax.optimization_barrier((visitors, back, w_bwd))
     sums = call(pairs, jax.ShapeDtypeStruct((members, per, lon), F32), [VMEM], 2_000_000, 200_000)(visitors)
     sums = lax.all_to_all(sums, "ens", 0, 0, tiled=True)
     own = chan // bands
-    pred_grad, partial = call(
+    edge = jax.ShapeDtypeStruct((HALO, padded, lon), BF)
+    pred_grad, cross, chip, partial = call(
         functools.partial(gradient, rows, kernels, members),
         (
             jax.ShapeDtypeStruct((rows, padded, lon), BF),
+            edge,
+            edge,
             jax.ShapeDtypeStruct((bands, kernels * own, lon), BF),
         ),
         [SMEM, SMEM] + [VMEM] * 4,
         80_000_000,
         1_200_000,
-    )(first, area, sums, predicted, target_fields, mixed)
+    )(place, area, sums, predicted, target_fields, mixed)
     parts = lax.all_to_all(partial, "lat", 0, 0, tiled=True)
-    grad_low, grad_high = halos(pred_grad, "lat")
+    cross, chip = exchange(cross, chip, "lat")
+    parts, cross, chip = lax.optimization_barrier((parts, cross, chip))
     latent_grad = call(
         functools.partial(adjoint, rows, kernels),
         jax.ShapeDtypeStruct((rows, chan, lon), BF),
-        [VMEM] * 5,
+        [SMEM] + [VMEM] * 5,
         200_000_000,
         2_000_000,
-    )(pred_grad, grad_low, grad_high, back, w_bwd)
-    parts, latent_grad = lax.optimization_barrier((parts, latent_grad))
+    )(place, pred_grad, cross, chip, back, w_bwd)
     factor = 1.0 / math.sqrt(members * lat_count * lon)
     width = chan // members
     spread = call(
@@ -298,6 +335,7 @@
         400_000,
     )(parts, w_bwd)
     spread = lax.all_to_all(spread, "ens", 0, 0, tiled=True)
+    spread, latent_grad = lax.optimization_barrier((spread, latent_grad))
     owned = call(
         member_sum, jax.ShapeDtypeStruct((kernels, own, width), F32), [VMEM], 100_000, 150_000
     )(spread)

time: 83.1 us -> 81.8 us (0.984)
  the two profiles are of different devices: /device:TPU:64 before, /device:TPU:1 now
where the time goes in v4:
time: 81.8 us; the launch traced here: 80.9 us
  starting transfers between devices  41.6 us (51%)
  waiting for transfers between devices  16.2 us (20%)
  Pallas kernels  12.2 us (15%)
  blocking collectives  10.1 us (12%)
    all_to_all x1, starting transfers between devices, body(): parts = lax.all_to_all(partial, 'lat', 0, 0, tiled=True)  16.2 us
    ppermute x2, starting transfers between devices, exchange(): cross = lax.ppermute(cross, axis, far + [(b, a) for a, b in far])  11.1 us
    all_to_all x1, blocking collectives, body(): sums = lax.all_to_all(sums, 'ens', 0, 0, tiled=True)  10.1 us
    all_to_all x1, waiting for transfers between devices, body(): spread = lax.all_to_all(spread, 'ens', 0, 0, tiled=True)  5.81 us
    all_to_all x1, waiting for transfers between devices, body(): visitors = lax.all_to_all(packed, 'ens', 0, 0, tiled=True)  5.53 us
    all_to_all x1, starting transfers between devices, body(): visitors = lax.all_to_all(packed, 'ens', 0, 0, tiled=True)  5.46 us
    ppermute x2, starting transfers between devices, exchange(): chip = lax.ppermute(chip, axis, near + [(b, a) for a, b in near])  5.33 us
    all_to_all x1, waiting for transfers between devices, body(): parts = lax.all_to_all(partial, 'lat', 0, 0, tiled=True)  3.68 us
  transfers between devices with their start and end apart: 7, of which 5 were waited for; matrix products, arithmetic and copies ran while one was open for 0% of the time, Pallas kernels for 7%

profile of v4, /device:TPU:1, one launch (start us, length us, event | category | flops | bytes accessed | tf_op | source)
XLA Modules:
  0.0 80.9 jit_solution(12045521877998711542)
XLA Ops:
  0.6 1.0 %shard_map.87 = (bf16[2,256,128]{2,1,0:T(8,128)(2,1)S(1)}, bf16[2,256,128]{2,1,0:T(8,128)(2,1)S(1)}) custom-call(s32[1]{0:T(128)} %bitcast.place, bf16[3,256,128]{2,1,0:T(8,128)(2,1)} %bitcast.7), custom_call_target="tpu_custom_call" | custom-call | bytes 500000 | tf_op jit(solution)/shard_map/pallas_call | solution.py:263
  1.6 6.0 %collective-permute-start = (bf16[2,256,128]{2,1,0:T(8,128)(2,1)S(1)}, bf16[2,256,128]{2,1,0:T(8,128)(2,1)S(1)}, u32[]{:S(2)}, u32[]{:S(2)}) collective-permute-start(bf16[2,256,128]{2,1,0:T(8,128)(2,1)S(1)} %get-tuple-element.27), channel_id=1, source_target_pairs={{1,2},{3,4},{5,6},{7,8},{9,10},{11,12},{13,14},{15,16},{17,18},{19... | collective-permute-start | bytes 393224 | tf_op jit(solution)/shard_map/ppermute | solution.py:239
  7.7 3.4 %collective-permute-start.1 = (bf16[2,256,128]{2,1,0:T(8,128)(2,1)S(1)}, bf16[2,256,128]{2,1,0:T(8,128)(2,1)S(1)}, u32[]{:S(2)}, u32[]{:S(2)}) collective-permute-start(bf16[2,256,128]{2,1,0:T(8,128)(2,1)S(1)} %get-tuple-element.28), channel_id=1, source_target_pairs={{0,1},{2,3},{4,5},{6,7},{8,9},{10,11},{12,13},{14,15},{16,17},{18,... | collective-permute-start | bytes 393224 | tf_op jit(solution)/shard_map/ppermute | solution.py:240
  11.1 2.5 %shard_map.86 = (bf16[3,640,384]{2,1,0:T(8,128)(2,1)S(1)}, bf16[80,1024]{1,0:T(8,128)(2,1)S(1)}, bf16[3,256,256]{2,1,0:T(8,128)(2,1)S(1)}, bf16[3,256,128]{2,1,0:T(8,128)(2,1)S(1)}, bf16[72,256]{1,0:T(8,128)(2,1)S(1)}) custom-call(s32[1]{0:T(128)} %bitcast.place, f32[10,3,96]{2,1,0:T(4,128)} %bitcast.10, s32[10,96]{1,0:T(8,128)} %bitcast.13, ...), custom_call_target="tpu_custom_call" | custom-call | flops 30000000 | bytes 2000000 | tf_op jit(solution)/shard_map/pallas_call | solution.py:265
  13.6 0.0 collective-permute-done.cross
  13.6 0.0 collective-permute-done.1.chip
  13.6 0.0 copy-start
  13.6 0.0 copy-start.1
  13.7 1.9 %shard_map.88 = (bf16[16,16,128]{2,1,0:T(8,128)(2,1)}, f32[3,80,128]{2,1,0:T(8,128)S(1)}, bf16[3,768,128]{2,1,0:T(8,128)(2,1)S(1)}) custom-call(s32[1]{0:T(128)} %bitcast.place, bf16[3,256,128]{2,1,0:T(8,128)(2,1)S(1)} %get-tuple-element.26.field, bf16[2,256,128]{2,1,0:T(8,128)(2,1)S(1)} %collective-permute-done.cross, ...), custom_call_target="tpu_custom_call" | custom-call | flops 450000000 | bytes 3000000 | tf_op jit(solution)/shard_map/pallas_call | solution.py:289
  15.6 5.5 %all-to-all-start = ((bf16[16,16,128]{2,1,0:T(8,128)(2,1)}), bf16[16,16,128]{2,1,0:T(8,128)(2,1)S(1)}, u32[]{:S(2)}, u32[]{:S(2)}) async-start(bf16[16,16,128]{2,1,0:T(8,128)(2,1)} %get-tuple-element.31), calls=%async_computation | async-start | bytes 131072 | tf_op jit(solution)/shard_map/all_to_all | solution.py:300
  21.0 1.8 %shard_map.89 = (bf16[3,640,384]{2,1,0:T(8,128)(2,1)S(1)}, bf16[4,256,80]{2,1,0:T(8,128)(2,1)S(1)}) custom-call(s32[1]{0:T(128)} %bitcast.place, f32[10,3,96]{2,1,0:T(4,128)} %bitcast.11, s32[10,96]{1,0:T(8,128)} %bitcast.14, bf16[3,256,256]{2,1,0:T(8,128)(2,1)S(1)} %get-tuple-element.32.filters, bf16[72,256]{1,0:T(8,128)(2,1)S(1)} %get-tuple-element.33.dec_t), custom_call_target="tpu_custom_call" | custom-call | flops 50000000 | bytes 2000000 | tf_op jit(solution)/shard_map/pallas_call | solution.py:279
  22.9 5.5 %all-to-all-done.visitors = bf16[16,16,128]{2,1,0:T(8,128)(2,1)S(1)} async-done(((bf16[16,16,128]{2,1,0:T(8,128)(2,1)}), bf16[16,16,128]{2,1,0:T(8,128)(2,1)S(1)}, u32[]{:S(2)}, u32[]{:S(2)}) %all-to-all-start) | async-done | bytes 65568 | tf_op jit(solution)/shard_map/all_to_all | solution.py:300
  28.4 0.2 shard_map.90
  28.6 10.1 %all_to_all.20.sums = f32[16,16,128]{2,1,0:T(8,128)S(1)} all-to-all(f32[16,16,128]{2,1,0:T(8,128)S(1)} %shard_map.90), channel_id=1, replica_groups=mesh['ens'=16,'lat'=32] {'ens'}, dimensions={0} | all-to-all | bytes 262144 | tf_op jit(solution)/shard_map/all_to_all | solution.py:303
  38.7 0.0 copy-done
  38.7 0.0 copy-done.1
  38.7 1.5 %shard_map.91 = (bf16[3,80,128]{2,1,0:T(8,128)(2,1)S(1)}, bf16[2,80,128]{2,1,0:T(8,128)(2,1)S(1)}, bf16[2,80,128]{2,1,0:T(8,128)(2,1)S(1)}, bf16[32,24,128]{2,1,0:T(8,128)(2,1)}) custom-call(s32[1]{0:T(128)} %bitcast.place, f32[96]{0:T(128)S(1)} %copy-done.1, f32[16,16,128]{2,1,0:T(8,128)S(1)} %all_to_all.20.sums, ...), custom_call_target="tpu_custom_call" | custom-call | flops 80000000 | bytes 1200000 | tf_op jit(solution)/shard_map/pallas_call | solution.py:306
  40.3 16.2 %all-to-all-start.2 = ((bf16[32,24,128]{2,1,0:T(8,128)(2,1)}), bf16[32,24,128]{2,1,0:T(8,128)(2,1)S(1)}, u32[]{:S(2)}, u32[]{:S(2)}) async-start(bf16[32,24,128]{2,1,0:T(8,128)(2,1)} %get-tuple-element.39), calls=%async_computation.2 | async-start | bytes 393216 | tf_op jit(solution)/shard_map/all_to_all | solution.py:318
  56.5 5.0 %collective-permute-start.2 = (bf16[2,80,128]{2,1,0:T(8,128)(2,1)S(1)}, bf16[2,80,128]{2,1,0:T(8,128)(2,1)S(1)}, u32[]{:S(2)}, u32[]{:S(2)}) collective-permute-start(bf16[2,80,128]{2,1,0:T(8,128)(2,1)S(1)} %get-tuple-element.40), channel_id=1, source_target_pairs={{1,2},{3,4},{5,6},{7,8},{9,10},{11,12},{13,14},{15,16},{17,18},{19... | collective-permute-start | bytes 122888 | tf_op jit(solution)/shard_map/ppermute | solution.py:239
  61.5 1.9 %collective-permute-start.3 = (bf16[2,80,128]{2,1,0:T(8,128)(2,1)S(1)}, bf16[2,80,128]{2,1,0:T(8,128)(2,1)S(1)}, u32[]{:S(2)}, u32[]{:S(2)}) collective-permute-start(bf16[2,80,128]{2,1,0:T(8,128)(2,1)S(1)} %get-tuple-element.41), channel_id=1, source_target_pairs={{0,1},{2,3},{4,5},{6,7},{8,9},{10,11},{12,13},{14,15},{16,17},{18,... | collective-permute-start | bytes 122888 | tf_op jit(solution)/shard_map/ppermute | solution.py:240
  63.5 0.3 collective-permute-done.2.cross
  63.8 0.9 %collective-permute-done.3.chip = bf16[2,80,128]{2,1,0:T(8,128)(2,1)S(1)} collective-permute-done((bf16[2,80,128]{2,1,0:T(8,128)(2,1)S(1)}, bf16[2,80,128]{2,1,0:T(8,128)(2,1)S(1)}, u32[]{:S(2)}, u32[]{:S(2)}) %collective-permute-start.3) | collective-permute-done | bytes 40992 | tf_op jit(solution)/shard_map/ppermute | solution.py:240
  64.6 3.7 %all-to-all-done.2.parts = bf16[32,24,128]{2,1,0:T(8,128)(2,1)S(1)} async-done(((bf16[32,24,128]{2,1,0:T(8,128)(2,1)}), bf16[32,24,128]{2,1,0:T(8,128)(2,1)S(1)}, u32[]{:S(2)}, u32[]{:S(2)}) %all-to-all-start.2) | async-done | bytes 196640 | tf_op jit(solution)/shard_map/all_to_all | solution.py:318
  68.3 0.9 %shard_map.92 = f32[16,16,128]{2,1,0:T(8,128)} custom-call(bf16[32,24,128]{2,1,0:T(8,128)(2,1)S(1)} %all-to-all-done.2.parts, bf16[4,256,80]{2,1,0:T(8,128)(2,1)S(1)} %get-tuple-element.43.w_bwd), custom_call_target="tpu_custom_call" | custom-call | flops 20000000 | bytes 400000 | tf_op jit(solution)/shard_map/pallas_call | solution.py:330
  69.2 3.5 %all-to-all-start.3 = ((f32[16,16,128]{2,1,0:T(8,128)}), f32[16,16,128]{2,1,0:T(8,128)S(1)}, u32[]{:S(2)}, u32[]{:S(2)}) async-start(f32[16,16,128]{2,1,0:T(8,128)} %shard_map.92), calls=%async_computation.3 | async-start | bytes 262144 | tf_op jit(solution)/shard_map/all_to_all | solution.py:337
  72.7 1.7 %shard_map.93 = bf16[3,256,128]{2,1,0:T(8,128)(2,1)} custom-call(s32[1]{0:T(128)} %bitcast.place, bf16[3,80,128]{2,1,0:T(8,128)(2,1)S(1)} %get-tuple-element.44.pred_grad, bf16[2,80,128]{2,1,0:T(8,128)(2,1)S(1)} %collective-permute-done.2.cross, bf16[2,80,128]{2,1,0:T(8,128)(2,1)S(1)} %collective-permute-done.3.chip, ...), custom_call_target="tpu_custom_call" | custom-call | flops 200000000 | bytes 2000000 | tf_op jit(solution)/shard_map/pallas_call | solution.py:321
  74.4 5.8 %all-to-all-done.3.parts = f32[16,16,128]{2,1,0:T(8,128)S(1)} async-done(((f32[16,16,128]{2,1,0:T(8,128)}), f32[16,16,128]{2,1,0:T(8,128)S(1)}, u32[]{:S(2)}, u32[]{:S(2)}) %all-to-all-start.3) | async-done | bytes 131104 | tf_op jit(solution)/shard_map/all_to_all | solution.py:337
  80.2 0.7 shard_map.94
Async XLA Ops:
  1.6 12.0 %collective-permute-start = (bf16[2,256,128]{2,1,0:T(8,128)(2,1)S(1)}, bf16[2,256,128]{2,1,0:T(8,128)(2,1)S(1)}, u32[]{:S(2)}, u32[]{:S(2)}) collective-permute-start(bf16[2,256,128]{2,1,0:T(8,128)(2,1)S(1)} %get-tuple-element.27), channel_id=1, source_target_pairs={{1,2},{3,4},{5,6},{7,8},{9,10},{11,12},{13,14},{15,16},{17,18},{19... | collective-permute-start | bytes 393224 | tf_op jit(solution)/shard_map/ppermute | solution.py:239
  7.7 5.9 %collective-permute-start.1 = (bf16[2,256,128]{2,1,0:T(8,128)(2,1)S(1)}, bf16[2,256,128]{2,1,0:T(8,128)(2,1)S(1)}, u32[]{:S(2)}, u32[]{:S(2)}) collective-permute-start(bf16[2,256,128]{2,1,0:T(8,128)(2,1)S(1)} %get-tuple-element.28), channel_id=1, source_target_pairs={{0,1},{2,3},{4,5},{6,7},{8,9},{10,11},{12,13},{14,15},{16,17},{18,... | collective-permute-start | bytes 393224 | tf_op jit(solution)/shard_map/ppermute | solution.py:240
  13.6 25.1 %copy-start = (bf16[3,72,128]{2,1,0:T(8,128)(2,1)S(1)}, bf16[3,72,128]{2,1,0:T(8,128)(2,1)}, u32[]{:S(2)}) copy-start(bf16[3,72,128]{2,1,0:T(8,128)(2,1)} %target.1) | copy-start | bytes 165892
  13.6 25.1 %copy-start.1 = (f32[96]{0:T(128)S(1)}, f32[96]{0:T(128)}, u32[]{:S(2)}) copy-start(f32[96]{0:T(128)} %constant.6.clone.area) | copy-start | bytes 1156
  15.6 12.8 %all-to-all-start = ((bf16[16,16,128]{2,1,0:T(8,128)(2,1)}), bf16[16,16,128]{2,1,0:T(8,128)(2,1)S(1)}, u32[]{:S(2)}, u32[]{:S(2)}) async-start(bf16[16,16,128]{2,1,0:T(8,128)(2,1)} %get-tuple-element.31), calls=%async_computation | async-start | bytes 131072 | tf_op jit(solution)/shard_map/all_to_all | solution.py:300
  40.3 28.0 %all-to-all-start.2 = ((bf16[32,24,128]{2,1,0:T(8,128)(2,1)}), bf16[32,24,128]{2,1,0:T(8,128)(2,1)S(1)}, u32[]{:S(2)}, u32[]{:S(2)}) async-start(bf16[32,24,128]{2,1,0:T(8,128)(2,1)} %get-tuple-element.39), calls=%async_computation.2 | async-start | bytes 393216 | tf_op jit(solution)/shard_map/all_to_all | solution.py:318
  56.5 7.3 %collective-permute-start.2 = (bf16[2,80,128]{2,1,0:T(8,128)(2,1)S(1)}, bf16[2,80,128]{2,1,0:T(8,128)(2,1)S(1)}, u32[]{:S(2)}, u32[]{:S(2)}) collective-permute-start(bf16[2,80,128]{2,1,0:T(8,128)(2,1)S(1)} %get-tuple-element.40), channel_id=1, source_target_pairs={{1,2},{3,4},{5,6},{7,8},{9,10},{11,12},{13,14},{15,16},{17,18},{19... | collective-permute-start | bytes 122888 | tf_op jit(solution)/shard_map/ppermute | solution.py:239
  61.5 3.1 %collective-permute-start.3 = (bf16[2,80,128]{2,1,0:T(8,128)(2,1)S(1)}, bf16[2,80,128]{2,1,0:T(8,128)(2,1)S(1)}, u32[]{:S(2)}, u32[]{:S(2)}) collective-permute-start(bf16[2,80,128]{2,1,0:T(8,128)(2,1)S(1)} %get-tuple-element.41), channel_id=1, source_target_pairs={{0,1},{2,3},{4,5},{6,7},{8,9},{10,11},{12,13},{14,15},{16,17},{18,... | collective-permute-start | bytes 122888 | tf_op jit(solution)/shard_map/ppermute | solution.py:240
  69.2 11.0 %all-to-all-start.3 = ((f32[16,16,128]{2,1,0:T(8,128)}), f32[16,16,128]{2,1,0:T(8,128)S(1)}, u32[]{:S(2)}, u32[]{:S(2)}) async-start(f32[16,16,128]{2,1,0:T(8,128)} %shard_map.92), calls=%async_computation.3 | async-start | bytes 262144 | tf_op jit(solution)/shard_map/all_to_all | solution.py:337

commit v5 on v4

--- a/solution.py
+++ b/solution.py
@@ -130,6 +130,7 @@
 
 def pairs(visitors, sums):
     members, height, _ = visitors.shape
+    pieces = []
     for start in range(0, height, 8):
         values = [visitors[m].astype(F32)[start : start + 8] for m in range(members)]
         totals = [None] * members
@@ -138,8 +139,9 @@
                 slope = smooth_slope(values[m] - values[n])
                 totals[m] = slope if totals[m] is None else totals[m] + slope
                 totals[n] = -slope if totals[n] is None else totals[n] - slope
-        for m in range(members):
-            sums[m, start : start + 8, :] = totals[m]
+        pieces.append(totals)
+    for m in range(members):
+        sums[m] = jnp.concatenate([totals[m] for totals in pieces], axis=0).astype(BF)
 
 
 def gradient(rows, kernels, members, place, area, sums, predicted, target, mixed, pred_grad, cross, chip, partial):
@@ -152,7 +154,7 @@
     grads, edges = [], []
     odd = (place[0] & 1) == 1
     for i in range(rows):
-        pair_sum = jnp.concatenate([sums[i * pieces + q] for q in range(pieces)], axis=0)
+        pair_sum = jnp.concatenate([sums[i * pieces + q].astype(F32) for q in range(pieces)], axis=0)
         aim = jnp.concatenate([target[i].astype(F32), jnp.zeros((padded - variables, lon), F32)], axis=0)
         grad = area[place[0] * rows + i] * (smooth_slope(predicted[i] - aim) - pair_sum * (1.0 / (members - 1)))
         grad = grad.astype(BF)
@@ -187,14 +189,14 @@
     result = dot_nt(dec, upper[:, :padded]) + dot_nt(dec, lower[:, :padded])
     per = spread.shape[1]
     for member in range(spread.shape[0]):
-        spread[member] = result[member * per : (member + 1) * per]
+        spread[member] = result[member * per : (member + 1) * per].astype(BF)
 
 
 def member_sum(parts, owned):
     kernels, own, width = owned.shape
-    total = parts[0]
+    total = parts[0].astype(F32)
     for member in range(1, parts.shape[0]):
-        total = total + parts[member]
+        total = total + parts[member].astype(F32)
     turned = total.T
     for k in range(kernels):
         owned[k] = turned[k * own : (k + 1) * own, :width]
@@ -298,8 +300,7 @@
         3_000_000,
     )(place, near, cross, chip, ahead, w_fwd)
     visitors = lax.all_to_all(packed, "ens", 0, 0, tiled=True)
-    visitors, back, w_bwd = lax.optimization_barrier((visitors, back, w_bwd))
-    sums = call(pairs, jax.ShapeDtypeStruct((members, per, lon), F32), [VMEM], 2_000_000, 200_000)(visitors)
+    sums = call(pairs, jax.ShapeDtypeStruct((members, per, lon), BF), [VMEM], 2_000_000, 200_000)(visitors)
     sums = lax.all_to_all(sums, "ens", 0, 0, tiled=True)
     own = chan // bands
     edge = jax.ShapeDtypeStruct((HALO, padded, lon), BF)
@@ -317,7 +318,6 @@
     )(place, area, sums, predicted, target_fields, mixed)
     parts = lax.all_to_all(partial, "lat", 0, 0, tiled=True)
     cross, chip = exchange(cross, chip, "lat")
-    parts, cross, chip = lax.optimization_barrier((parts, cross, chip))
     latent_grad = call(
         functools.partial(adjoint, rows, kernels),
         jax.ShapeDtypeStruct((rows, chan, lon), BF),
@@ -325,17 +325,17 @@
         200_000_000,
         2_000_000,
     )(place, pred_grad, cross, chip, back, w_bwd)
+    parts, latent_grad = lax.optimization_barrier((parts, latent_grad))
     factor = 1.0 / math.sqrt(members * lat_count * lon)
     width = chan // members
     spread = call(
         functools.partial(band_sum, factor),
-        jax.ShapeDtypeStruct((members, width, lon), F32),
+        jax.ShapeDtypeStruct((members, width, lon), BF),
         [VMEM] * 2,
         20_000_000,
         400_000,
     )(parts, w_bwd)
     spread = lax.all_to_all(spread, "ens", 0, 0, tiled=True)
-    spread, latent_grad = lax.optimization_barrier((spread, latent_grad))
     owned = call(
         member_sum, jax.ShapeDtypeStruct((kernels, own, width), F32), [VMEM], 100_000, 150_000
     )(spread)

time: 81.8 us -> 79 us (0.966)
  blocking collectives: 10.1 us -> 32.6 us
  waiting for transfers between devices: 16.2 us -> 1.34 us
  starting transfers between devices: 41.6 us -> 32.6 us
  Pallas kernels: 12.2 us -> 11.1 us
    all_to_all x0 -> x2, blocking collectives: none -> 22.7 us  [the longest x1 12.6 us: body(): visitors = lax.all_to_all(packed, 'ens', 0, 0, tiled=True)]
    all_to_all x2 -> x0, waiting for transfers between devices: 11.3 us -> none  [the longest x1 5.81 us: body(): spread = lax.all_to_all(spread, 'ens', 0, 0, tiled=True)]
    all_to_all x2 -> x0, starting transfers between devices: 8.97 us -> none  [the longest x1 5.46 us: body(): visitors = lax.all_to_all(packed, 'ens', 0, 0, tiled=True)]
    all_to_all x1, waiting for transfers between devices: 3.68 us -> 1.33 us  [body(): parts = lax.all_to_all(partial, 'lat', 0, 0, tiled=True)]
    ppermute x2, waiting for transfers between devices: 0.9 us -> 0.01 us  [exchange(): chip = lax.ppermute(chip, axis, near + [(b, a) for a, b in near])]
  transfers between devices with their start and end apart: 7 -> 5, of which waited for: 5 -> 1; matrix products, arithmetic and copies ran while one was open for 0% -> 0% of each run, Pallas kernels for 7% -> 8%
where the time goes in v5:
time: 79 us; the launch traced here: 78.4 us
  starting transfers between devices  32.6 us (41%)
  blocking collectives  32.6 us (41%)
  Pallas kernels  11.1 us (14%)
  waiting for transfers between devices  1.34 us (2%)
    all_to_all x1, starting transfers between devices, body(): parts = lax.all_to_all(partial, 'lat', 0, 0, tiled=True)  16.2 us
    all_to_all x1, blocking collectives, body(): visitors = lax.all_to_all(packed, 'ens', 0, 0, tiled=True)  12.6 us
    ppermute x2, starting transfers between devices, exchange(): cross = lax.ppermute(cross, axis, far + [(b, a) for a, b in far])  11.1 us
    all_to_all x1, blocking collectives, body(): spread = lax.all_to_all(spread, 'ens', 0, 0, tiled=True)  10.1 us
    all_to_all x1, blocking collectives, body(): sums = lax.all_to_all(sums, 'ens', 0, 0, tiled=True)  9.95 us
    ppermute x2, starting transfers between devices, exchange(): chip = lax.ppermute(chip, axis, near + [(b, a) for a, b in near])  5.33 us
    pallas_call x1, Pallas kernels, body(): call(functools.partial(prepare_ahead, rows, taps, lat_count), (jax.ShapeD...  2.62 us
    pallas_call x1, Pallas kernels, body(): call(functools.partial(prepare_back, rows, taps, lat_count), (jax.ShapeDt...  1.84 us
  transfers between devices with their start and end apart: 5, of which 1 were waited for; matrix products, arithmetic and copies ran while one was open for 0% of the time, Pallas kernels for 8%

profile of v5, /device:TPU:1, one launch (start us, length us, event | category | flops | bytes accessed | tf_op | source)
XLA Modules:
  0.0 78.4 jit_solution(17131767547000083731)
XLA Ops:
  0.6 1.0 %shard_map.87 = (bf16[2,256,128]{2,1,0:T(8,128)(2,1)S(1)}, bf16[2,256,128]{2,1,0:T(8,128)(2,1)S(1)}) custom-call(s32[1]{0:T(128)} %bitcast.place, bf16[3,256,128]{2,1,0:T(8,128)(2,1)} %bitcast.7), custom_call_target="tpu_custom_call" | custom-call | bytes 500000 | tf_op jit(solution)/shard_map/pallas_call | solution.py:265
  1.6 6.0 %collective-permute-start = (bf16[2,256,128]{2,1,0:T(8,128)(2,1)S(1)}, bf16[2,256,128]{2,1,0:T(8,128)(2,1)S(1)}, u32[]{:S(2)}, u32[]{:S(2)}) collective-permute-start(bf16[2,256,128]{2,1,0:T(8,128)(2,1)S(1)} %get-tuple-element.21), channel_id=1, source_target_pairs={{1,2},{3,4},{5,6},{7,8},{9,10},{11,12},{13,14},{15,16},{17,18},{19... | collective-permute-start | bytes 393224 | tf_op jit(solution)/shard_map/ppermute | solution.py:241
  7.7 3.4 %collective-permute-start.1 = (bf16[2,256,128]{2,1,0:T(8,128)(2,1)S(1)}, bf16[2,256,128]{2,1,0:T(8,128)(2,1)S(1)}, u32[]{:S(2)}, u32[]{:S(2)}) collective-permute-start(bf16[2,256,128]{2,1,0:T(8,128)(2,1)S(1)} %get-tuple-element.22), channel_id=1, source_target_pairs={{0,1},{2,3},{4,5},{6,7},{8,9},{10,11},{12,13},{14,15},{16,17},{18,... | collective-permute-start | bytes 393224 | tf_op jit(solution)/shard_map/ppermute | solution.py:242
  11.1 0.0 copy-start
  11.1 0.0 copy-start.1
  11.1 2.6 %shard_map.86 = (bf16[3,640,384]{2,1,0:T(8,128)(2,1)S(1)}, bf16[80,1024]{1,0:T(8,128)(2,1)S(1)}, bf16[3,256,256]{2,1,0:T(8,128)(2,1)S(1)}, bf16[3,256,128]{2,1,0:T(8,128)(2,1)S(1)}, bf16[72,256]{1,0:T(8,128)(2,1)S(1)}) custom-call(s32[1]{0:T(128)} %bitcast.place, f32[10,3,96]{2,1,0:T(4,128)} %bitcast.10, s32[10,96]{1,0:T(8,128)} %bitcast.13, ...), custom_call_target="tpu_custom_call" | custom-call | flops 30000000 | bytes 2000000 | tf_op jit(solution)/shard_map/pallas_call | solution.py:267
  13.8 0.0 collective-permute-done.cross
  13.8 0.0 collective-permute-done.1.chip
  13.8 1.3 %shard_map.88 = (bf16[16,16,128]{2,1,0:T(8,128)(2,1)S(1)}, f32[3,80,128]{2,1,0:T(8,128)S(1)}, bf16[3,768,128]{2,1,0:T(8,128)(2,1)S(1)}) custom-call(s32[1]{0:T(128)} %bitcast.place, bf16[3,256,128]{2,1,0:T(8,128)(2,1)S(1)} %get-tuple-element.20.field, bf16[2,256,128]{2,1,0:T(8,128)(2,1)S(1)} %collective-permute-done.cross, ...), custom_call_target="tpu_custom_call" | custom-call | flops 450000000 | bytes 3000000 | tf_op jit(solution)/shard_map/pallas_call | solution.py:291
  15.1 12.6 %all_to_all.20.visitors = bf16[16,16,128]{2,1,0:T(8,128)(2,1)S(1)} all-to-all(bf16[16,16,128]{2,1,0:T(8,128)(2,1)S(1)} %get-tuple-element.25), channel_id=1, replica_groups=mesh['ens'=16,'lat'=32] {'ens'}, dimensions={0} | all-to-all | bytes 131072 | tf_op jit(solution)/shard_map/all_to_all | solution.py:302
  27.7 0.2 shard_map.89
  27.9 10.0 %all_to_all.21.sums = bf16[16,16,128]{2,1,0:T(8,128)(2,1)S(1)} all-to-all(bf16[16,16,128]{2,1,0:T(8,128)(2,1)S(1)} %shard_map.89), channel_id=1, replica_groups=mesh['ens'=16,'lat'=32] {'ens'}, dimensions={0} | all-to-all | bytes 131072 | tf_op jit(solution)/shard_map/all_to_all | solution.py:304
  37.9 0.0 copy-done
  37.9 0.0 copy-done.1
  37.9 1.5 %shard_map.90 = (bf16[3,80,128]{2,1,0:T(8,128)(2,1)S(1)}, bf16[2,80,128]{2,1,0:T(8,128)(2,1)S(1)}, bf16[2,80,128]{2,1,0:T(8,128)(2,1)S(1)}, bf16[32,24,128]{2,1,0:T(8,128)(2,1)}) custom-call(s32[1]{0:T(128)} %bitcast.place, f32[96]{0:T(128)S(1)} %copy-done.1, bf16[16,16,128]{2,1,0:T(8,128)(2,1)S(1)} %all_to_all.21.sums, ...), custom_call_target="tpu_custom_call" | custom-call | flops 80000000 | bytes 1200000 | tf_op jit(solution)/shard_map/pallas_call | solution.py:307
  39.5 16.2 %all-to-all-start.2 = ((bf16[32,24,128]{2,1,0:T(8,128)(2,1)}), bf16[32,24,128]{2,1,0:T(8,128)(2,1)S(1)}, u32[]{:S(2)}, u32[]{:S(2)}) async-start(bf16[32,24,128]{2,1,0:T(8,128)(2,1)} %get-tuple-element.28), calls=%async_computation.2 | async-start | bytes 393216 | tf_op jit(solution)/shard_map/all_to_all | solution.py:319
  55.6 5.0 %collective-permute-start.2 = (bf16[2,80,128]{2,1,0:T(8,128)(2,1)S(1)}, bf16[2,80,128]{2,1,0:T(8,128)(2,1)S(1)}, u32[]{:S(2)}, u32[]{:S(2)}) collective-permute-start(bf16[2,80,128]{2,1,0:T(8,128)(2,1)S(1)} %get-tuple-element.30), channel_id=1, source_target_pairs={{1,2},{3,4},{5,6},{7,8},{9,10},{11,12},{13,14},{15,16},{17,18},{19... | collective-permute-start | bytes 122888 | tf_op jit(solution)/shard_map/ppermute | solution.py:241
  60.7 1.9 %collective-permute-start.3 = (bf16[2,80,128]{2,1,0:T(8,128)(2,1)S(1)}, bf16[2,80,128]{2,1,0:T(8,128)(2,1)S(1)}, u32[]{:S(2)}, u32[]{:S(2)}) collective-permute-start(bf16[2,80,128]{2,1,0:T(8,128)(2,1)S(1)} %get-tuple-element.31), channel_id=1, source_target_pairs={{0,1},{2,3},{4,5},{6,7},{8,9},{10,11},{12,13},{14,15},{16,17},{18,... | collective-permute-start | bytes 122888 | tf_op jit(solution)/shard_map/ppermute | solution.py:242
  62.6 1.8 %shard_map.91 = (bf16[3,640,384]{2,1,0:T(8,128)(2,1)S(1)}, bf16[4,256,80]{2,1,0:T(8,128)(2,1)S(1)}) custom-call(s32[1]{0:T(128)} %bitcast.place, f32[10,3,96]{2,1,0:T(4,128)} %bitcast.11, s32[10,96]{1,0:T(8,128)} %bitcast.14, bf16[3,256,256]{2,1,0:T(8,128)(2,1)S(1)} %get-tuple-element.32.filters, bf16[72,256]{1,0:T(8,128)(2,1)S(1)} %get-tuple-element.33.dec_t), custom_call_target="tpu_custom_call" | custom-call | flops 50000000 | bytes 2000000 | tf_op jit(solution)/shard_map/pallas_call | solution.py:281
  64.4 0.0 collective-permute-done.2.cross
  64.4 0.0 collective-permute-done.3.chip
  64.4 1.7 %shard_map.92 = bf16[3,256,128]{2,1,0:T(8,128)(2,1)} custom-call(s32[1]{0:T(128)} %bitcast.place, bf16[3,80,128]{2,1,0:T(8,128)(2,1)S(1)} %get-tuple-element.29.pred_grad, bf16[2,80,128]{2,1,0:T(8,128)(2,1)S(1)} %collective-permute-done.2.cross, bf16[2,80,128]{2,1,0:T(8,128)(2,1)S(1)} %collective-permute-done.3.chip, ...), custom_call_target="tpu_custom_call" | custom-call | flops 200000000 | bytes 2000000 | tf_op jit(solution)/shard_map/pallas_call | solution.py:321
  66.1 1.3 %all-to-all-done.2.parts = bf16[32,24,128]{2,1,0:T(8,128)(2,1)S(1)} async-done(((bf16[32,24,128]{2,1,0:T(8,128)(2,1)}), bf16[32,24,128]{2,1,0:T(8,128)(2,1)S(1)}, u32[]{:S(2)}, u32[]{:S(2)}) %all-to-all-start.2) | async-done | bytes 196640 | tf_op jit(solution)/shard_map/all_to_all | solution.py:319
  67.5 0.2 shard_map.93
  67.7 10.1 %all_to_all.22.parts = bf16[16,16,128]{2,1,0:T(8,128)(2,1)S(1)} all-to-all(bf16[16,16,128]{2,1,0:T(8,128)(2,1)S(1)} %shard_map.93), channel_id=1, replica_groups=mesh['ens'=16,'lat'=32] {'ens'}, dimensions={0} | all-to-all | bytes 131072 | tf_op jit(solution)/shard_map/all_to_all | solution.py:338
  77.7 0.7 shard_map.94
Async XLA Ops:
  1.6 12.1 %collective-permute-start = (bf16[2,256,128]{2,1,0:T(8,128)(2,1)S(1)}, bf16[2,256,128]{2,1,0:T(8,128)(2,1)S(1)}, u32[]{:S(2)}, u32[]{:S(2)}) collective-permute-start(bf16[2,256,128]{2,1,0:T(8,128)(2,1)S(1)} %get-tuple-element.21), channel_id=1, source_target_pairs={{1,2},{3,4},{5,6},{7,8},{9,10},{11,12},{13,14},{15,16},{17,18},{19... | collective-permute-start | bytes 393224 | tf_op jit(solution)/shard_map/ppermute | solution.py:241
  7.7 6.1 %collective-permute-start.1 = (bf16[2,256,128]{2,1,0:T(8,128)(2,1)S(1)}, bf16[2,256,128]{2,1,0:T(8,128)(2,1)S(1)}, u32[]{:S(2)}, u32[]{:S(2)}) collective-permute-start(bf16[2,256,128]{2,1,0:T(8,128)(2,1)S(1)} %get-tuple-element.22), channel_id=1, source_target_pairs={{0,1},{2,3},{4,5},{6,7},{8,9},{10,11},{12,13},{14,15},{16,17},{18,... | collective-permute-start | bytes 393224 | tf_op jit(solution)/shard_map/ppermute | solution.py:242
  11.1 26.8 %copy-start = (bf16[3,72,128]{2,1,0:T(8,128)(2,1)S(1)}, bf16[3,72,128]{2,1,0:T(8,128)(2,1)}, u32[]{:S(2)}) copy-start(bf16[3,72,128]{2,1,0:T(8,128)(2,1)} %target.1) | copy-start | bytes 165892
  11.1 26.8 %copy-start.1 = (f32[96]{0:T(128)S(1)}, f32[96]{0:T(128)}, u32[]{:S(2)}) copy-start(f32[96]{0:T(128)} %constant.6.clone.area) | copy-start | bytes 1156
  39.5 28.0 %all-to-all-start.2 = ((bf16[32,24,128]{2,1,0:T(8,128)(2,1)}), bf16[32,24,128]{2,1,0:T(8,128)(2,1)S(1)}, u32[]{:S(2)}, u32[]{:S(2)}) async-start(bf16[32,24,128]{2,1,0:T(8,128)(2,1)} %get-tuple-element.28), calls=%async_computation.2 | async-start | bytes 393216 | tf_op jit(solution)/shard_map/all_to_all | solution.py:319
  55.6 8.8 %collective-permute-start.2 = (bf16[2,80,128]{2,1,0:T(8,128)(2,1)S(1)}, bf16[2,80,128]{2,1,0:T(8,128)(2,1)S(1)}, u32[]{:S(2)}, u32[]{:S(2)}) collective-permute-start(bf16[2,80,128]{2,1,0:T(8,128)(2,1)S(1)} %get-tuple-element.30), channel_id=1, source_target_pairs={{1,2},{3,4},{5,6},{7,8},{9,10},{11,12},{13,14},{15,16},{17,18},{19... | collective-permute-start | bytes 122888 | tf_op jit(solution)/shard_map/ppermute | solution.py:241
  60.7 3.8 %collective-permute-start.3 = (bf16[2,80,128]{2,1,0:T(8,128)(2,1)S(1)}, bf16[2,80,128]{2,1,0:T(8,128)(2,1)S(1)}, u32[]{:S(2)}, u32[]{:S(2)}) collective-permute-start(bf16[2,80,128]{2,1,0:T(8,128)(2,1)S(1)} %get-tuple-element.31), channel_id=1, source_target_pairs={{0,1},{2,3},{4,5},{6,7},{8,9},{10,11},{12,13},{14,15},{16,17},{18,... | collective-permute-start | bytes 122888 | tf_op jit(solution)/shard_map/ppermute | solution.py:242

commit v6 on v5

--- a/solution.py
+++ b/solution.py
@@ -29,6 +29,14 @@
 
 def dot_nt(a, b):
     return lax.dot_general(a, b, (((1,), (1,)), ((), ())), preferred_element_type=F32)
+
+
+def dot_tn(a, b):
+    return lax.dot_general(a, b, (((0,), (0,)), ((), ())), preferred_element_type=F32)
+
+
+def dot_tt(a, b):
+    return lax.dot_general(a, b, (((0,), (1,)), ((), ())), preferred_element_type=F32)
 
 
 def call(kernel, out, specs, flops, moved, scratch=()):
@@ -44,21 +52,26 @@
     )
 
 
-def tap_block(taps, lat_count, lag, base, basis, offsets, out, row, source, slot, step, sign):
+def tap_block(lat_count, lag, place, rows, basis, offsets, source, step, store):
     kernels, lon = basis.shape[1], lag.shape[0]
-    cycle = base + source
+    cycle = place[0] * rows + source
     inside = jnp.logical_and(cycle >= 0, cycle < lat_count)
     cycle = jnp.clip(cycle, 0, lat_count - 1)
     one, two = SIDE * step, SIDE * step + 1
     off_one, off_two = offsets[one, cycle], offsets[two, cycle]
-    mask_one = lag == ((sign * off_one) & (lon - 1))
-    mask_two = lag == ((sign * off_two) & (lon - 1))
+    mask_one = lag == (off_one & (lon - 1))
+    mask_two = lag == (off_two & (lon - 1))
     for k in range(kernels):
         weight_one = jnp.where(inside, basis[one, k, cycle], 0.0)
         weight_two = jnp.where(inside, basis[two, k, cycle], 0.0)
         weight_two = weight_two + jnp.where(off_one == off_two, weight_one, 0.0)
         value = jnp.where(mask_two, weight_two, jnp.where(mask_one, weight_one, 0.0))
-        out[row, slot * lon : (slot + 1) * lon, k * lon : (k + 1) * lon] = value.astype(BF)
+        store[:, k * lon : (k + 1) * lon] = value.astype(BF)
+
+
+def edge_taps(rows):
+    outside = list(range(-HALO, 0)) + list(range(rows, rows + HALO))
+    return [(at, step) for at in outside for step in range(REACH) if 0 <= at + step - HALO < rows]
 
 
 def lags(lon):
@@ -70,17 +83,20 @@
     return jnp.concatenate([dec_t[...].astype(F32), jnp.zeros((padded - rows, chan), F32)], axis=0).astype(BF)
 
 
-def prepare_ahead(
-    rows, taps, lat_count, place, basis, offsets, filters, dec_in, field, ahead, w_fwd, held, near, dec_t, sems
+def prepare(
+    rows, lat_count, place, basis, offsets, filters, dec_in, field, ahead, edge, w_fwd, near, held, dec_t, sems
 ):
     moves = ((filters, held), (dec_in, dec_t), (field, near))
     moves = [pltpu.make_async_copy(source, target, sems.at[n]) for n, (source, target) in enumerate(moves)]
     for move in moves:
         move.start()
-    lag = lags(ahead.shape[1] // REACH)
+    lon = ahead.shape[1] // REACH
+    lag = lags(lon)
     for row in range(rows):
-        for slot in range(REACH):
-            tap_block(taps, lat_count, lag, place[0] * rows, basis, offsets, ahead, row, row, slot, slot, 1)
+        for step in range(REACH):
+            tap_block(lat_count, lag, place, rows, basis, offsets, row, step, ahead.at[row, step * lon : (step + 1) * lon])
+    for n, (at, step) in enumerate(edge_taps(rows)):
+        tap_block(lat_count, lag, place, rows, basis, offsets, at, step, edge.at[n])
     kernels, chan = held.shape[:2]
     for move in moves:
         move.wait()
@@ -88,21 +104,6 @@
     w_fwd[:, :chan] = dec
     for k in range(kernels):
         w_fwd[:, (k + 1) * chan : (k + 2) * chan] = dot_nt(dec, held[k]).astype(BF)
-
-
-def prepare_back(rows, taps, lat_count, place, basis, offsets, filters, dec_t, back, w_bwd):
-    lag = lags(back.shape[1] // REACH)
-    for row in range(rows):
-        for slot in range(REACH):
-            step = REACH - 1 - slot
-            tap_block(taps, lat_count, lag, place[0] * rows, basis, offsets, back, row, row + slot - HALO, slot, step, -1)
-    kernels, chan = filters.shape[:2]
-    dec = padded_rows(dec_t, w_bwd.shape[2])
-    rank = (chan, chan)
-    unit = lax.broadcasted_iota(jnp.int32, rank, 0) == lax.broadcasted_iota(jnp.int32, rank, 1)
-    w_bwd[0] = dot_nt(jnp.where(unit, 1.0, 0.0).astype(BF), dec).astype(BF)
-    for k in range(kernels):
-        w_bwd[k + 1] = dot_nt(filters[k], dec).astype(BF)
 
 
 def forward(rows, kernels, place, field, cross, chip, ahead, w_fwd, packed, predicted, mixed):
@@ -176,7 +177,7 @@
         ).astype(BF)
 
 
-def band_sum(factor, parts, w_bwd, spread):
+def band_sum(factor, parts, w_fwd, spread):
     owners, height, lanes = parts.shape
     total = parts[0].astype(F32)
     for owner in range(1, owners):
@@ -184,10 +185,10 @@
     total = jnp.concatenate([total * factor, jnp.zeros((lanes - height, lanes), F32)], axis=0)
     upper = total.astype(BF)
     lower = (total - upper.astype(F32)).astype(BF)
-    dec = w_bwd[0]
-    padded = dec.shape[1]
-    result = dot_nt(dec, upper[:, :padded]) + dot_nt(dec, lower[:, :padded])
     per = spread.shape[1]
+    padded = w_fwd.shape[0]
+    dec = w_fwd[:, : per * spread.shape[0]]
+    result = dot_tt(dec, upper[:, :padded]) + dot_tt(dec, lower[:, :padded])
     for member in range(spread.shape[0]):
         spread[member] = result[member * per : (member + 1) * per].astype(BF)
 
@@ -202,16 +203,36 @@
         owned[k] = turned[k * own : (k + 1) * own, :width]
 
 
-def adjoint(rows, kernels, place, pred_grad, cross, chip, back, w_bwd, result):
+def adjoint_own(rows, kernels, pred_grad, ahead, turned):
     lon = pred_grad.shape[2]
+    for k in range(kernels):
+        sums = [None] * rows
+        for at in range(rows):
+            least = HALO - at
+            taps = ahead[at, least * lon : (least + rows) * lon, k * lon : (k + 1) * lon]
+            found = dot_nt(pred_grad[at], taps)
+            for row in range(rows):
+                piece = found[:, row * lon : (row + 1) * lon]
+                sums[row] = piece if sums[row] is None else sums[row] + piece
+        for row in range(rows):
+            turned[k, :, row * lon : (row + 1) * lon] = sums[row]
+
+
+def adjoint_rest(rows, kernels, place, pred_grad, cross, chip, turned, edge, w_fwd, result):
+    lon = pred_grad.shape[2]
+    chan = result.shape[1]
     low, high = sides((place[0] & 1) == 1, cross, chip)
-    wide = low + [pred_grad[i] for i in range(rows)] + high
+    outer = dict(enumerate(low, -HALO)) | dict(enumerate(high, rows))
+    total = dot_tn(w_fwd[:, :chan], jnp.concatenate([pred_grad[i] for i in range(rows)], axis=1))
+    for k in range(kernels):
+        sums = [turned[k, :, row * lon : (row + 1) * lon] for row in range(rows)]
+        for n, (at, step) in enumerate(edge_taps(rows)):
+            row = at + step - HALO
+            sums[row] = sums[row] + dot_nt(outer[at], edge[n, :, k * lon : (k + 1) * lon])
+        taps = jnp.concatenate(sums, axis=1).astype(BF)
+        total = total + dot_tn(w_fwd[:, (k + 1) * chan : (k + 2) * chan], taps)
     for i in range(rows):
-        taps = dot_nn(jnp.concatenate(wide[i : i + REACH], axis=1), back[i]).astype(BF)
-        total = dot_nn(w_bwd[0], wide[i + HALO])
-        for k in range(kernels):
-            total = total + dot_nn(w_bwd[k + 1], taps[:, k * lon : (k + 1) * lon])
-        result[i] = total.astype(BF)
+        result[i] = total[:, i * lon : (i + 1) * lon].astype(BF)
 
 
 def cut(place, field, cross, chip, sems):
@@ -264,30 +285,19 @@
     pair = pltpu.SemaphoreType.DMA((2,))
     cross, chip = call(cut, (edge, edge), [SMEM, hbm], 0, 500_000, [pair])(place, stay(field))
     cross, chip = exchange(cross, chip, "lat")
-    ahead, w_fwd, held, near, dec_near = call(
-        functools.partial(prepare_ahead, rows, taps, lat_count),
+    ahead, tap_edge, w_fwd, near = call(
+        functools.partial(prepare, rows, lat_count),
         (
             jax.ShapeDtypeStruct((rows, REACH * lon, kernels * lon), BF),
+            jax.ShapeDtypeStruct((len(edge_taps(rows)), lon, kernels * lon), BF),
             jax.ShapeDtypeStruct((padded, (kernels + 1) * chan), BF),
-            jax.ShapeDtypeStruct(filters.shape, BF),
             jax.ShapeDtypeStruct(field.shape, BF),
-            jax.ShapeDtypeStruct(dec_t.shape, BF),
         ),
         [SMEM, SMEM, SMEM, hbm, hbm, hbm],
         30_000_000,
         2_000_000,
-        [pltpu.SemaphoreType.DMA((3,))],
+        [pltpu.VMEM(filters.shape, BF), pltpu.VMEM(dec_t.shape, BF), pltpu.SemaphoreType.DMA((3,))],
     )(place, stay(basis), stay(offsets), stay(filters), stay(dec_t), stay(field))
-    back, w_bwd = call(
-        functools.partial(prepare_back, rows, taps, lat_count),
-        (
-            jax.ShapeDtypeStruct((rows, REACH * lon, kernels * lon), BF),
-            jax.ShapeDtypeStruct((kernels + 1, chan, padded), BF),
-        ),
-        [SMEM, SMEM, SMEM, VMEM, VMEM],
-        50_000_000,
-        2_000_000,
-    )(place, stay(basis), stay(offsets), held, dec_near)
     packed, predicted, mixed = call(
         functools.partial(forward, rows, kernels),
         (
@@ -318,13 +328,20 @@
     )(place, area, sums, predicted, target_fields, mixed)
     parts = lax.all_to_all(partial, "lat", 0, 0, tiled=True)
     cross, chip = exchange(cross, chip, "lat")
+    turned = call(
+        functools.partial(adjoint_own, rows, kernels),
+        jax.ShapeDtypeStruct((kernels, padded, rows * lon), F32),
+        [VMEM] * 2,
+        80_000_000,
+        1_500_000,
+    )(pred_grad, ahead)
     latent_grad = call(
-        functools.partial(adjoint, rows, kernels),
+        functools.partial(adjoint_rest, rows, kernels),
         jax.ShapeDtypeStruct((rows, chan, lon), BF),
-        [SMEM] + [VMEM] * 5,
-        200_000_000,
-        2_000_000,
-    )(place, pred_grad, cross, chip, back, w_bwd)
+        [SMEM] + [VMEM] * 6,
+        150_000_000,
+        1_500_000,
+    )(place, pred_grad, cross, chip, turned, tap_edge, w_fwd)
     parts, latent_grad = lax.optimization_barrier((parts, latent_grad))
     factor = 1.0 / math.sqrt(members * lat_count * lon)
     width = chan // members
@@ -334,7 +351,7 @@
         [VMEM] * 2,
         20_000_000,
         400_000,
-    )(parts, w_bwd)
+    )(parts, w_fwd)
     spread = lax.all_to_all(spread, "ens", 0, 0, tiled=True)
     owned = call(
         member_sum, jax.ShapeDtypeStruct((kernels, own, width), F32), [VMEM], 100_000, 150_000

time: 79 us -> 78.9 us (level)
  waiting for transfers between devices: 1.34 us -> 2.62 us
  Pallas kernels: 11.1 us -> 9.86 us
    pallas_call x3, Pallas kernels: 6.13 us -> 4.87 us  [the longest x1 2.62 us: body(): call(functools.partial(prepare, rows, lat_count), (jax.ShapeDtypeStruct((...]
  transfers between devices with their start and end apart: 5 -> 5, of which waited for: 1 -> 2; matrix products, arithmetic and copies ran while one was open for 0% -> 0% of each run, Pallas kernels for 8% -> 6%
where the time goes in v6:
time: 78.9 us; the launch traced here: 78.4 us
  starting transfers between devices  32.6 us (41%)
  blocking collectives  32.6 us (41%)
  Pallas kernels  9.86 us (12%)
  waiting for transfers between devices  2.62 us (3%)
    all_to_all x1, starting transfers between devices, body(): parts = lax.all_to_all(partial, 'lat', 0, 0, tiled=True)  16.2 us
    all_to_all x1, blocking collectives, body(): visitors = lax.all_to_all(packed, 'ens', 0, 0, tiled=True)  12.6 us
    ppermute x2, starting transfers between devices, exchange(): cross = lax.ppermute(cross, axis, far + [(b, a) for a, b in far])  11.1 us
    all_to_all x1, blocking collectives, body(): spread = lax.all_to_all(spread, 'ens', 0, 0, tiled=True)  10.1 us
    all_to_all x1, blocking collectives, body(): sums = lax.all_to_all(sums, 'ens', 0, 0, tiled=True)  9.95 us
    ppermute x2, starting transfers between devices, exchange(): chip = lax.ppermute(chip, axis, near + [(b, a) for a, b in near])  5.33 us
    pallas_call x1, Pallas kernels, body(): call(functools.partial(prepare, rows, lat_count), (jax.ShapeDtypeStruct((...  2.62 us
    all_to_all x1, waiting for transfers between devices, body(): parts = lax.all_to_all(partial, 'lat', 0, 0, tiled=True)  1.96 us
  transfers between devices with their start and end apart: 5, of which 2 were waited for; matrix products, arithmetic and copies ran while one was open for 0% of the time, Pallas kernels for 6%

profile of v6, /device:TPU:1, one launch (start us, length us, event | category | flops | bytes accessed | tf_op | source)
XLA Modules:
  0.0 78.4 jit_solution(16240001740106954554)
XLA Ops:
  0.6 1.0 %shard_map.87 = (bf16[2,256,128]{2,1,0:T(8,128)(2,1)S(1)}, bf16[2,256,128]{2,1,0:T(8,128)(2,1)S(1)}) custom-call(s32[1]{0:T(128)} %bitcast.place, bf16[3,256,128]{2,1,0:T(8,128)(2,1)} %bitcast.7), custom_call_target="tpu_custom_call" | custom-call | bytes 500000 | tf_op jit(solution)/shard_map/pallas_call | solution.py:286
  1.6 6.0 %collective-permute-start = (bf16[2,256,128]{2,1,0:T(8,128)(2,1)S(1)}, bf16[2,256,128]{2,1,0:T(8,128)(2,1)S(1)}, u32[]{:S(2)}, u32[]{:S(2)}) collective-permute-start(bf16[2,256,128]{2,1,0:T(8,128)(2,1)S(1)} %get-tuple-element.18), channel_id=1, source_target_pairs={{1,2},{3,4},{5,6},{7,8},{9,10},{11,12},{13,14},{15,16},{17,18},{19... | collective-permute-start | bytes 393224 | tf_op jit(solution)/shard_map/ppermute | solution.py:262
  7.7 3.4 %collective-permute-start.1 = (bf16[2,256,128]{2,1,0:T(8,128)(2,1)S(1)}, bf16[2,256,128]{2,1,0:T(8,128)(2,1)S(1)}, u32[]{:S(2)}, u32[]{:S(2)}) collective-permute-start(bf16[2,256,128]{2,1,0:T(8,128)(2,1)S(1)} %get-tuple-element.19), channel_id=1, source_target_pairs={{0,1},{2,3},{4,5},{6,7},{8,9},{10,11},{12,13},{14,15},{16,17},{18,... | collective-permute-start | bytes 393224 | tf_op jit(solution)/shard_map/ppermute | solution.py:263
  11.1 0.0 copy-start
  11.1 0.0 copy-start.1
  11.1 2.6 %shard_map.86 = (bf16[3,640,384]{2,1,0:T(8,128)(2,1)S(1)}, bf16[6,128,384]{2,1,0:T(8,128)(2,1)S(1)}, bf16[80,1024]{1,0:T(8,128)(2,1)S(1)}, bf16[3,256,128]{2,1,0:T(8,128)(2,1)S(1)}) custom-call(s32[1]{0:T(128)} %bitcast.place, f32[10,3,96]{2,1,0:T(4,128)} %bitcast.11, s32[10,96]{1,0:T(8,128)} %bitcast.13, bf16[3,256,256]{2,1,0:T(8,128)(2,1)} %filters.1, ...), custom_call_target="tpu_custom_call" | custom-call | flops 30000000 | bytes 2000000 | tf_op jit(solution)/shard_map/pallas_call | solution.py:288
  13.8 0.0 collective-permute-done.cross
  13.8 0.0 collective-permute-done.1.chip
  13.8 1.3 %shard_map.88 = (bf16[16,16,128]{2,1,0:T(8,128)(2,1)S(1)}, f32[3,80,128]{2,1,0:T(8,128)S(1)}, bf16[3,768,128]{2,1,0:T(8,128)(2,1)S(1)}) custom-call(s32[1]{0:T(128)} %bitcast.place, bf16[3,256,128]{2,1,0:T(8,128)(2,1)S(1)} %get-tuple-element.17.field, bf16[2,256,128]{2,1,0:T(8,128)(2,1)S(1)} %collective-permute-done.cross, ...), custom_call_target="tpu_custom_call" | custom-call | flops 450000000 | bytes 3000000 | tf_op jit(solution)/shard_map/pallas_call | solution.py:301
  15.1 12.6 %all_to_all.20.visitors = bf16[16,16,128]{2,1,0:T(8,128)(2,1)S(1)} all-to-all(bf16[16,16,128]{2,1,0:T(8,128)(2,1)S(1)} %get-tuple-element.22), channel_id=1, replica_groups=mesh['ens'=16,'lat'=32] {'ens'}, dimensions={0} | all-to-all | bytes 131072 | tf_op jit(solution)/shard_map/all_to_all | solution.py:312
  27.7 0.2 shard_map.89
  28.0 10.0 %all_to_all.21.sums = bf16[16,16,128]{2,1,0:T(8,128)(2,1)S(1)} all-to-all(bf16[16,16,128]{2,1,0:T(8,128)(2,1)S(1)} %shard_map.89), channel_id=1, replica_groups=mesh['ens'=16,'lat'=32] {'ens'}, dimensions={0} | all-to-all | bytes 131072 | tf_op jit(solution)/shard_map/all_to_all | solution.py:314
  37.9 0.0 copy-done
  37.9 0.0 copy-done.1
  37.9 1.5 %shard_map.90 = (bf16[3,80,128]{2,1,0:T(8,128)(2,1)S(1)}, bf16[2,80,128]{2,1,0:T(8,128)(2,1)S(1)}, bf16[2,80,128]{2,1,0:T(8,128)(2,1)S(1)}, bf16[32,24,128]{2,1,0:T(8,128)(2,1)}) custom-call(s32[1]{0:T(128)} %bitcast.place, f32[96]{0:T(128)S(1)} %copy-done.1, bf16[16,16,128]{2,1,0:T(8,128)(2,1)S(1)} %all_to_all.21.sums, ...), custom_call_target="tpu_custom_call" | custom-call | flops 80000000 | bytes 1200000 | tf_op jit(solution)/shard_map/pallas_call | solution.py:317
  39.5 16.2 %all-to-all-start.2 = ((bf16[32,24,128]{2,1,0:T(8,128)(2,1)}), bf16[32,24,128]{2,1,0:T(8,128)(2,1)S(1)}, u32[]{:S(2)}, u32[]{:S(2)}) async-start(bf16[32,24,128]{2,1,0:T(8,128)(2,1)} %get-tuple-element.25), calls=%async_computation.2 | async-start | bytes 393216 | tf_op jit(solution)/shard_map/all_to_all | solution.py:329
  55.6 5.0 %collective-permute-start.2 = (bf16[2,80,128]{2,1,0:T(8,128)(2,1)S(1)}, bf16[2,80,128]{2,1,0:T(8,128)(2,1)S(1)}, u32[]{:S(2)}, u32[]{:S(2)}) collective-permute-start(bf16[2,80,128]{2,1,0:T(8,128)(2,1)S(1)} %get-tuple-element.27), channel_id=1, source_target_pairs={{1,2},{3,4},{5,6},{7,8},{9,10},{11,12},{13,14},{15,16},{17,18},{19... | collective-permute-start | bytes 122888 | tf_op jit(solution)/shard_map/ppermute | solution.py:262
  60.7 1.9 %collective-permute-start.3 = (bf16[2,80,128]{2,1,0:T(8,128)(2,1)S(1)}, bf16[2,80,128]{2,1,0:T(8,128)(2,1)S(1)}, u32[]{:S(2)}, u32[]{:S(2)}) collective-permute-start(bf16[2,80,128]{2,1,0:T(8,128)(2,1)S(1)} %get-tuple-element.28), channel_id=1, source_target_pairs={{0,1},{2,3},{4,5},{6,7},{8,9},{10,11},{12,13},{14,15},{16,17},{18,... | collective-permute-start | bytes 122888 | tf_op jit(solution)/shard_map/ppermute | solution.py:263
  62.6 0.5 shard_map.91.turned
  63.1 0.0 collective-permute-done.2.cross
  63.1 0.7 collective-permute-done.3.chip
  63.8 1.7 %shard_map.92 = bf16[3,256,128]{2,1,0:T(8,128)(2,1)} custom-call(s32[1]{0:T(128)} %bitcast.place, bf16[3,80,128]{2,1,0:T(8,128)(2,1)S(1)} %get-tuple-element.26.pred_grad, bf16[2,80,128]{2,1,0:T(8,128)(2,1)S(1)} %collective-permute-done.2.cross, bf16[2,80,128]{2,1,0:T(8,128)(2,1)S(1)} %collective-permute-done.3.chip, f32[3,80,384]{2,1,0:T(8,128)S(1)} %shard_map.91.turned, ...), custom_call_target="tpu_custom_call" | custom-call | flops 150000000 | bytes 1500000 | tf_op jit(solution)/shard_map/pallas_call | solution.py:338
  65.5 2.0 %all-to-all-done.2.parts = bf16[32,24,128]{2,1,0:T(8,128)(2,1)S(1)} async-done(((bf16[32,24,128]{2,1,0:T(8,128)(2,1)}), bf16[32,24,128]{2,1,0:T(8,128)(2,1)S(1)}, u32[]{:S(2)}, u32[]{:S(2)}) %all-to-all-start.2) | async-done | bytes 196640 | tf_op jit(solution)/shard_map/all_to_all | solution.py:329
  67.5 0.2 shard_map.93
  67.7 10.1 %all_to_all.22.parts = bf16[16,16,128]{2,1,0:T(8,128)(2,1)S(1)} all-to-all(bf16[16,16,128]{2,1,0:T(8,128)(2,1)S(1)} %shard_map.93), channel_id=1, replica_groups=mesh['ens'=16,'lat'=32] {'ens'}, dimensions={0} | all-to-all | bytes 131072 | tf_op jit(solution)/shard_map/all_to_all | solution.py:355
  77.8 0.7 shard_map.94
Async XLA Ops:
  1.6 12.1 %collective-permute-start = (bf16[2,256,128]{2,1,0:T(8,128)(2,1)S(1)}, bf16[2,256,128]{2,1,0:T(8,128)(2,1)S(1)}, u32[]{:S(2)}, u32[]{:S(2)}) collective-permute-start(bf16[2,256,128]{2,1,0:T(8,128)(2,1)S(1)} %get-tuple-element.18), channel_id=1, source_target_pairs={{1,2},{3,4},{5,6},{7,8},{9,10},{11,12},{13,14},{15,16},{17,18},{19... | collective-permute-start | bytes 393224 | tf_op jit(solution)/shard_map/ppermute | solution.py:262
  7.7 6.1 %collective-permute-start.1 = (bf16[2,256,128]{2,1,0:T(8,128)(2,1)S(1)}, bf16[2,256,128]{2,1,0:T(8,128)(2,1)S(1)}, u32[]{:S(2)}, u32[]{:S(2)}) collective-permute-start(bf16[2,256,128]{2,1,0:T(8,128)(2,1)S(1)} %get-tuple-element.19), channel_id=1, source_target_pairs={{0,1},{2,3},{4,5},{6,7},{8,9},{10,11},{12,13},{14,15},{16,17},{18,... | collective-permute-start | bytes 393224 | tf_op jit(solution)/shard_map/ppermute | solution.py:263
  11.1 26.8 %copy-start = (bf16[3,72,128]{2,1,0:T(8,128)(2,1)S(1)}, bf16[3,72,128]{2,1,0:T(8,128)(2,1)}, u32[]{:S(2)}) copy-start(bf16[3,72,128]{2,1,0:T(8,128)(2,1)} %target.1) | copy-start | bytes 165892
  11.1 26.8 %copy-start.1 = (f32[96]{0:T(128)S(1)}, f32[96]{0:T(128)}, u32[]{:S(2)}) copy-start(f32[96]{0:T(128)} %constant.6.clone.area) | copy-start | bytes 1156
  39.5 28.0 %all-to-all-start.2 = ((bf16[32,24,128]{2,1,0:T(8,128)(2,1)}), bf16[32,24,128]{2,1,0:T(8,128)(2,1)S(1)}, u32[]{:S(2)}, u32[]{:S(2)}) async-start(bf16[32,24,128]{2,1,0:T(8,128)(2,1)} %get-tuple-element.25), calls=%async_computation.2 | async-start | bytes 393216 | tf_op jit(solution)/shard_map/all_to_all | solution.py:329
  55.6 7.5 %collective-permute-start.2 = (bf16[2,80,128]{2,1,0:T(8,128)(2,1)S(1)}, bf16[2,80,128]{2,1,0:T(8,128)(2,1)S(1)}, u32[]{:S(2)}, u32[]{:S(2)}) collective-permute-start(bf16[2,80,128]{2,1,0:T(8,128)(2,1)S(1)} %get-tuple-element.27), channel_id=1, source_target_pairs={{1,2},{3,4},{5,6},{7,8},{9,10},{11,12},{13,14},{15,16},{17,18},{19... | collective-permute-start | bytes 122888 | tf_op jit(solution)/shard_map/ppermute | solution.py:262
  60.7 3.1 %collective-permute-start.3 = (bf16[2,80,128]{2,1,0:T(8,128)(2,1)S(1)}, bf16[2,80,128]{2,1,0:T(8,128)(2,1)S(1)}, u32[]{:S(2)}, u32[]{:S(2)}) collective-permute-start(bf16[2,80,128]{2,1,0:T(8,128)(2,1)S(1)} %get-tuple-element.28), channel_id=1, source_target_pairs={{0,1},{2,3},{4,5},{6,7},{8,9},{10,11},{12,13},{14,15},{16,17},{18,... | collective-permute-start | bytes 122888 | tf_op jit(solution)/shard_map/ppermute | solution.py:263

commit v7 on v6

--- a/solution.py
+++ b/solution.py
@@ -29,14 +29,6 @@
 
 def dot_nt(a, b):
     return lax.dot_general(a, b, (((1,), (1,)), ((), ())), preferred_element_type=F32)
-
-
-def dot_tn(a, b):
-    return lax.dot_general(a, b, (((0,), (0,)), ((), ())), preferred_element_type=F32)
-
-
-def dot_tt(a, b):
-    return lax.dot_general(a, b, (((0,), (1,)), ((), ())), preferred_element_type=F32)
 
 
 def call(kernel, out, specs, flops, moved, scratch=()):
@@ -84,7 +76,7 @@
 
 
 def prepare(
-    rows, lat_count, place, basis, offsets, filters, dec_in, field, ahead, edge, w_fwd, near, held, dec_t, sems
+    rows, lat_count, place, basis, offsets, filters, dec_in, field, ahead, edge, w_fwd, w_bwd, near, held, dec_t, sems
 ):
     moves = ((filters, held), (dec_in, dec_t), (field, near))
     moves = [pltpu.make_async_copy(source, target, sems.at[n]) for n, (source, target) in enumerate(moves)]
@@ -104,6 +96,10 @@
     w_fwd[:, :chan] = dec
     for k in range(kernels):
         w_fwd[:, (k + 1) * chan : (k + 2) * chan] = dot_nt(dec, held[k]).astype(BF)
+        w_bwd[k + 1] = dot_nt(held[k], dec).astype(BF)
+    square = (chan, chan)
+    unit = lax.broadcasted_iota(jnp.int32, square, 0) == lax.broadcasted_iota(jnp.int32, square, 1)
+    w_bwd[0] = dot_nt(jnp.where(unit, 1.0, 0.0).astype(BF), dec).astype(BF)
 
 
 def forward(rows, kernels, place, field, cross, chip, ahead, w_fwd, packed, predicted, mixed):
@@ -169,26 +165,40 @@
     total = dot_nt(
         jnp.concatenate([mixed[i] for i in range(rows)], axis=1), jnp.concatenate(grads, axis=1)
     )
+    first, second, third = [total[k * chan : (k + 1) * chan] for k in range(kernels)]
+    lane = lax.broadcasted_iota(jnp.int32, first.shape, 1)
+    spare = lon - variables
+    upper = jnp.where(lane < variables, first, pltpu.roll(third, variables, 1))
+    tail = jnp.where(lane < 2 * variables - spare, pltpu.roll(third, variables - spare, 1), 0.0)
+    lower = jnp.where(lane < variables, second, tail)
     owners = partial.shape[0]
     own = chan // owners
     for owner in range(owners):
-        partial[owner] = jnp.concatenate(
-            [total[k * chan + owner * own : k * chan + (owner + 1) * own] for k in range(kernels)], axis=0
-        ).astype(BF)
-
-
-def band_sum(factor, parts, w_fwd, spread):
-    owners, height, lanes = parts.shape
+        mine = slice(owner * own, (owner + 1) * own)
+        partial[owner] = jnp.concatenate([upper[mine], lower[mine]], axis=0).astype(BF)
+
+
+def band_sum(factor, variables, parts, w_bwd, spread):
+    owners, height, lon = parts.shape
     total = parts[0].astype(F32)
     for owner in range(1, owners):
         total = total + parts[owner].astype(F32)
-    total = jnp.concatenate([total * factor, jnp.zeros((lanes - height, lanes), F32)], axis=0)
+    total = total * factor
+    own = height // 2
+    spare = lon - variables
+    lane = lax.broadcasted_iota(jnp.int32, (own, lon), 1)
+    front = pltpu.roll(total[:own], lon - variables, 1)
+    rest = pltpu.roll(total[own:], lon + spare - variables, 1)
+    third = jnp.where(lane < spare, front, jnp.where(lane < variables, rest, 0.0))
+    wide = lax.broadcasted_iota(jnp.int32, total.shape, 1)
+    total = jnp.where(wide < variables, total, 0.0)
+    total = jnp.concatenate([total, third, jnp.zeros((lon - height - own, lon), F32)], axis=0)
     upper = total.astype(BF)
     lower = (total - upper.astype(F32)).astype(BF)
+    dec = w_bwd[0]
+    padded = dec.shape[1]
+    result = dot_nt(dec, upper[:, :padded]) + dot_nt(dec, lower[:, :padded])
     per = spread.shape[1]
-    padded = w_fwd.shape[0]
-    dec = w_fwd[:, : per * spread.shape[0]]
-    result = dot_tt(dec, upper[:, :padded]) + dot_tt(dec, lower[:, :padded])
     for member in range(spread.shape[0]):
         spread[member] = result[member * per : (member + 1) * per].astype(BF)
 
@@ -218,19 +228,18 @@
             turned[k, :, row * lon : (row + 1) * lon] = sums[row]
 
 
-def adjoint_rest(rows, kernels, place, pred_grad, cross, chip, turned, edge, w_fwd, result):
+def adjoint_rest(rows, kernels, place, pred_grad, cross, chip, turned, edge, w_bwd, result):
     lon = pred_grad.shape[2]
-    chan = result.shape[1]
     low, high = sides((place[0] & 1) == 1, cross, chip)
     outer = dict(enumerate(low, -HALO)) | dict(enumerate(high, rows))
-    total = dot_tn(w_fwd[:, :chan], jnp.concatenate([pred_grad[i] for i in range(rows)], axis=1))
+    total = dot_nn(w_bwd[0], jnp.concatenate([pred_grad[i] for i in range(rows)], axis=1))
     for k in range(kernels):
         sums = [turned[k, :, row * lon : (row + 1) * lon] for row in range(rows)]
         for n, (at, step) in enumerate(edge_taps(rows)):
             row = at + step - HALO
             sums[row] = sums[row] + dot_nt(outer[at], edge[n, :, k * lon : (k + 1) * lon])
         taps = jnp.concatenate(sums, axis=1).astype(BF)
-        total = total + dot_tn(w_fwd[:, (k + 1) * chan : (k + 2) * chan], taps)
+        total = total + dot_nn(w_bwd[k + 1], taps)
     for i in range(rows):
         result[i] = total[:, i * lon : (i + 1) * lon].astype(BF)
 
@@ -285,12 +294,13 @@
     pair = pltpu.SemaphoreType.DMA((2,))
     cross, chip = call(cut, (edge, edge), [SMEM, hbm], 0, 500_000, [pair])(place, stay(field))
     cross, chip = exchange(cross, chip, "lat")
-    ahead, tap_edge, w_fwd, near = call(
+    ahead, tap_edge, w_fwd, w_bwd, near = call(
         functools.partial(prepare, rows, lat_count),
         (
             jax.ShapeDtypeStruct((rows, REACH * lon, kernels * lon), BF),
             jax.ShapeDtypeStruct((len(edge_taps(rows)), lon, kernels * lon), BF),
             jax.ShapeDtypeStruct((padded, (kernels + 1) * chan), BF),
+            jax.ShapeDtypeStruct((kernels + 1, chan, padded), BF),
             jax.ShapeDtypeStruct(field.shape, BF),
         ),
         [SMEM, SMEM, SMEM, hbm, hbm, hbm],
@@ -320,7 +330,7 @@
             jax.ShapeDtypeStruct((rows, padded, lon), BF),
             edge,
             edge,
-            jax.ShapeDtypeStruct((bands, kernels * own, lon), BF),
+            jax.ShapeDtypeStruct((bands, 2 * own, lon), BF),
         ),
         [SMEM, SMEM] + [VMEM] * 4,
         80_000_000,
@@ -341,17 +351,17 @@
         [SMEM] + [VMEM] * 6,
         150_000_000,
         1_500_000,
-    )(place, pred_grad, cross, chip, turned, tap_edge, w_fwd)
+    )(place, pred_grad, cross, chip, turned, tap_edge, w_bwd)
     parts, latent_grad = lax.optimization_barrier((parts, latent_grad))
     factor = 1.0 / math.sqrt(members * lat_count * lon)
     width = chan // members
     spread = call(
-        functools.partial(band_sum, factor),
+        functools.partial(band_sum, factor, variables),
         jax.ShapeDtypeStruct((members, width, lon), BF),
         [VMEM] * 2,
         20_000_000,
         400_000,
-    )(parts, w_fwd)
+    )(parts, w_bwd)
     spread = lax.all_to_all(spread, "ens", 0, 0, tiled=True)
     owned = call(
         member_sum, jax.ShapeDtypeStruct((kernels, own, width), F32), [VMEM], 100_000, 150_000

time: 78.9 us -> 77.9 us (0.987)
  waiting for transfers between devices: 2.62 us -> 1.54 us
    all_to_all x1, waiting for transfers between devices: 1.96 us -> 0.88 us  [body(): parts = lax.all_to_all(partial, 'lat', 0, 0, tiled=True)]
where the time goes in v7:
time: 77.9 us; the launch traced here: 77.4 us
  blocking collectives  32.6 us (42%)
  starting transfers between devices  32.5 us (42%)
  Pallas kernels  10 us (13%)
  waiting for transfers between devices  1.54 us (2%)
    all_to_all x1, starting transfers between devices, body(): parts = lax.all_to_all(partial, 'lat', 0, 0, tiled=True)  16.1 us
    all_to_all x1, blocking collectives, body(): visitors = lax.all_to_all(packed, 'ens', 0, 0, tiled=True)  12.6 us
    ppermute x2, starting transfers between devices, exchange(): cross = lax.ppermute(cross, axis, far + [(b, a) for a, b in far])  11.1 us
    all_to_all x1, blocking collectives, body(): spread = lax.all_to_all(spread, 'ens', 0, 0, tiled=True)  10 us
    all_to_all x1, blocking collectives, body(): sums = lax.all_to_all(sums, 'ens', 0, 0, tiled=True)  9.95 us
    ppermute x2, starting transfers between devices, exchange(): chip = lax.ppermute(chip, axis, near + [(b, a) for a, b in near])  5.33 us
    pallas_call x1, Pallas kernels, body(): call(functools.partial(prepare, rows, lat_count), (jax.ShapeDtypeStruct((...  2.68 us
    pallas_call x1, Pallas kernels, body(): call(functools.partial(adjoint_rest, rows, kernels), jax.ShapeDtypeStruct...  1.72 us
  transfers between devices with their start and end apart: 5, of which 2 were waited for; matrix products, arithmetic and copies ran while one was open for 0% of the time, Pallas kernels for 6%

profile of v7, /device:TPU:1, one launch (start us, length us, event | category | flops | bytes accessed | tf_op | source)
XLA Modules:
  0.0 77.4 jit_solution(14964405360352092611)
XLA Ops:
  0.6 1.0 %shard_map.87 = (bf16[2,256,128]{2,1,0:T(8,128)(2,1)S(1)}, bf16[2,256,128]{2,1,0:T(8,128)(2,1)S(1)}) custom-call(s32[1]{0:T(128)} %bitcast.place, bf16[3,256,128]{2,1,0:T(8,128)(2,1)} %bitcast.7), custom_call_target="tpu_custom_call" | custom-call | bytes 500000 | tf_op jit(solution)/shard_map/pallas_call | solution.py:295
  1.6 6.0 %collective-permute-start = (bf16[2,256,128]{2,1,0:T(8,128)(2,1)S(1)}, bf16[2,256,128]{2,1,0:T(8,128)(2,1)S(1)}, u32[]{:S(2)}, u32[]{:S(2)}) collective-permute-start(bf16[2,256,128]{2,1,0:T(8,128)(2,1)S(1)} %get-tuple-element.19), channel_id=1, source_target_pairs={{1,2},{3,4},{5,6},{7,8},{9,10},{11,12},{13,14},{15,16},{17,18},{19... | collective-permute-start | bytes 393224 | tf_op jit(solution)/shard_map/ppermute | solution.py:271
  7.7 3.4 %collective-permute-start.1 = (bf16[2,256,128]{2,1,0:T(8,128)(2,1)S(1)}, bf16[2,256,128]{2,1,0:T(8,128)(2,1)S(1)}, u32[]{:S(2)}, u32[]{:S(2)}) collective-permute-start(bf16[2,256,128]{2,1,0:T(8,128)(2,1)S(1)} %get-tuple-element.20), channel_id=1, source_target_pairs={{0,1},{2,3},{4,5},{6,7},{8,9},{10,11},{12,13},{14,15},{16,17},{18,... | collective-permute-start | bytes 393224 | tf_op jit(solution)/shard_map/ppermute | solution.py:272
  11.1 0.0 copy-start
  11.1 0.0 copy-start.1
  11.1 2.7 %shard_map.86 = (bf16[3,640,384]{2,1,0:T(8,128)(2,1)S(1)}, bf16[6,128,384]{2,1,0:T(8,128)(2,1)S(1)}, bf16[80,1024]{1,0:T(8,128)(2,1)S(1)}, bf16[4,256,80]{2,1,0:T(8,128)(2,1)S(1)}, bf16[3,256,128]{2,1,0:T(8,128)(2,1)S(1)}) custom-call(s32[1]{0:T(128)} %bitcast.place, f32[10,3,96]{2,1,0:T(4,128)} %bitcast.11, s32[10,96]{1,0:T(8,128)} %bitcast.13, ...), custom_call_target="tpu_custom_call" | custom-call | flops 30000000 | bytes 2000000 | tf_op jit(solution)/shard_map/pallas_call | solution.py:297
  13.8 0.0 collective-permute-done.cross
  13.8 0.0 collective-permute-done.1.chip
  13.8 1.3 %shard_map.88 = (bf16[16,16,128]{2,1,0:T(8,128)(2,1)S(1)}, f32[3,80,128]{2,1,0:T(8,128)S(1)}, bf16[3,768,128]{2,1,0:T(8,128)(2,1)S(1)}) custom-call(s32[1]{0:T(128)} %bitcast.place, bf16[3,256,128]{2,1,0:T(8,128)(2,1)S(1)} %get-tuple-element.18.field, bf16[2,256,128]{2,1,0:T(8,128)(2,1)S(1)} %collective-permute-done.cross, ...), custom_call_target="tpu_custom_call" | custom-call | flops 450000000 | bytes 3000000 | tf_op jit(solution)/shard_map/pallas_call | solution.py:311
  15.1 12.6 %all_to_all.20.visitors = bf16[16,16,128]{2,1,0:T(8,128)(2,1)S(1)} all-to-all(bf16[16,16,128]{2,1,0:T(8,128)(2,1)S(1)} %get-tuple-element.23), channel_id=1, replica_groups=mesh['ens'=16,'lat'=32] {'ens'}, dimensions={0} | all-to-all | bytes 131072 | tf_op jit(solution)/shard_map/all_to_all | solution.py:322
  27.8 0.2 shard_map.89
  28.0 10.0 %all_to_all.21.sums = bf16[16,16,128]{2,1,0:T(8,128)(2,1)S(1)} all-to-all(bf16[16,16,128]{2,1,0:T(8,128)(2,1)S(1)} %shard_map.89), channel_id=1, replica_groups=mesh['ens'=16,'lat'=32] {'ens'}, dimensions={0} | all-to-all | bytes 131072 | tf_op jit(solution)/shard_map/all_to_all | solution.py:324
  38.0 0.0 copy-done
  38.0 0.0 copy-done.1
  38.0 1.6 %shard_map.90 = (bf16[3,80,128]{2,1,0:T(8,128)(2,1)S(1)}, bf16[2,80,128]{2,1,0:T(8,128)(2,1)S(1)}, bf16[2,80,128]{2,1,0:T(8,128)(2,1)S(1)}, bf16[32,16,128]{2,1,0:T(8,128)(2,1)}) custom-call(s32[1]{0:T(128)} %bitcast.place, f32[96]{0:T(128)S(1)} %copy-done.1, bf16[16,16,128]{2,1,0:T(8,128)(2,1)S(1)} %all_to_all.21.sums, ...), custom_call_target="tpu_custom_call" | custom-call | flops 80000000 | bytes 1200000 | tf_op jit(solution)/shard_map/pallas_call | solution.py:327
  39.6 16.1 %all-to-all-start.2 = ((bf16[32,16,128]{2,1,0:T(8,128)(2,1)}), bf16[32,16,128]{2,1,0:T(8,128)(2,1)S(1)}, u32[]{:S(2)}, u32[]{:S(2)}) async-start(bf16[32,16,128]{2,1,0:T(8,128)(2,1)} %get-tuple-element.26), calls=%async_computation.2 | async-start | bytes 262144 | tf_op jit(solution)/shard_map/all_to_all | solution.py:339
  55.7 5.0 %collective-permute-start.2 = (bf16[2,80,128]{2,1,0:T(8,128)(2,1)S(1)}, bf16[2,80,128]{2,1,0:T(8,128)(2,1)S(1)}, u32[]{:S(2)}, u32[]{:S(2)}) collective-permute-start(bf16[2,80,128]{2,1,0:T(8,128)(2,1)S(1)} %get-tuple-element.28), channel_id=1, source_target_pairs={{1,2},{3,4},{5,6},{7,8},{9,10},{11,12},{13,14},{15,16},{17,18},{19... | collective-permute-start | bytes 122888 | tf_op jit(solution)/shard_map/ppermute | solution.py:271
  60.7 1.9 %collective-permute-start.3 = (bf16[2,80,128]{2,1,0:T(8,128)(2,1)S(1)}, bf16[2,80,128]{2,1,0:T(8,128)(2,1)S(1)}, u32[]{:S(2)}, u32[]{:S(2)}) collective-permute-start(bf16[2,80,128]{2,1,0:T(8,128)(2,1)S(1)} %get-tuple-element.29), channel_id=1, source_target_pairs={{0,1},{2,3},{4,5},{6,7},{8,9},{10,11},{12,13},{14,15},{16,17},{18,... | collective-permute-start | bytes 122888 | tf_op jit(solution)/shard_map/ppermute | solution.py:272
  62.6 0.5 shard_map.91.turned
  63.2 0.0 collective-permute-done.2.cross
  63.2 0.7 collective-permute-done.3.chip
  63.8 1.7 %shard_map.92 = bf16[3,256,128]{2,1,0:T(8,128)(2,1)} custom-call(s32[1]{0:T(128)} %bitcast.place, bf16[3,80,128]{2,1,0:T(8,128)(2,1)S(1)} %get-tuple-element.27.pred_grad, bf16[2,80,128]{2,1,0:T(8,128)(2,1)S(1)} %collective-permute-done.2.cross, bf16[2,80,128]{2,1,0:T(8,128)(2,1)S(1)} %collective-permute-done.3.chip, f32[3,80,384]{2,1,0:T(8,128)S(1)} %shard_map.91.turned, ...), custom_call_target="tpu_custom_call" | custom-call | flops 150000000 | bytes 1500000 | tf_op jit(solution)/shard_map/pallas_call | solution.py:348
  65.6 0.9 %all-to-all-done.2.parts = bf16[32,16,128]{2,1,0:T(8,128)(2,1)S(1)} async-done(((bf16[32,16,128]{2,1,0:T(8,128)(2,1)}), bf16[32,16,128]{2,1,0:T(8,128)(2,1)S(1)}, u32[]{:S(2)}, u32[]{:S(2)}) %all-to-all-start.2) | async-done | bytes 131104 | tf_op jit(solution)/shard_map/all_to_all | solution.py:339
  66.4 0.3 shard_map.93
  66.7 10.0 %all_to_all.22.parts = bf16[16,16,128]{2,1,0:T(8,128)(2,1)S(1)} all-to-all(bf16[16,16,128]{2,1,0:T(8,128)(2,1)S(1)} %shard_map.93), channel_id=1, replica_groups=mesh['ens'=16,'lat'=32] {'ens'}, dimensions={0} | all-to-all | bytes 131072 | tf_op jit(solution)/shard_map/all_to_all | solution.py:365
  76.7 0.7 shard_map.94
Async XLA Ops:
  1.6 12.2 %collective-permute-start = (bf16[2,256,128]{2,1,0:T(8,128)(2,1)S(1)}, bf16[2,256,128]{2,1,0:T(8,128)(2,1)S(1)}, u32[]{:S(2)}, u32[]{:S(2)}) collective-permute-start(bf16[2,256,128]{2,1,0:T(8,128)(2,1)S(1)} %get-tuple-element.19), channel_id=1, source_target_pairs={{1,2},{3,4},{5,6},{7,8},{9,10},{11,12},{13,14},{15,16},{17,18},{19... | collective-permute-start | bytes 393224 | tf_op jit(solution)/shard_map/ppermute | solution.py:271
  7.7 6.2 %collective-permute-start.1 = (bf16[2,256,128]{2,1,0:T(8,128)(2,1)S(1)}, bf16[2,256,128]{2,1,0:T(8,128)(2,1)S(1)}, u32[]{:S(2)}, u32[]{:S(2)}) collective-permute-start(bf16[2,256,128]{2,1,0:T(8,128)(2,1)S(1)} %get-tuple-element.20), channel_id=1, source_target_pairs={{0,1},{2,3},{4,5},{6,7},{8,9},{10,11},{12,13},{14,15},{16,17},{18,... | collective-permute-start | bytes 393224 | tf_op jit(solution)/shard_map/ppermute | solution.py:272
  11.1 26.9 %copy-start = (bf16[3,72,128]{2,1,0:T(8,128)(2,1)S(1)}, bf16[3,72,128]{2,1,0:T(8,128)(2,1)}, u32[]{:S(2)}) copy-start(bf16[3,72,128]{2,1,0:T(8,128)(2,1)} %target.1) | copy-start | bytes 165892
  11.1 26.9 %copy-start.1 = (f32[96]{0:T(128)S(1)}, f32[96]{0:T(128)}, u32[]{:S(2)}) copy-start(f32[96]{0:T(128)} %constant.6.clone.area) | copy-start | bytes 1156
  39.6 26.9 %all-to-all-start.2 = ((bf16[32,16,128]{2,1,0:T(8,128)(2,1)}), bf16[32,16,128]{2,1,0:T(8,128)(2,1)S(1)}, u32[]{:S(2)}, u32[]{:S(2)}) async-start(bf16[32,16,128]{2,1,0:T(8,128)(2,1)} %get-tuple-element.26), calls=%async_computation.2 | async-start | bytes 262144 | tf_op jit(solution)/shard_map/all_to_all | solution.py:339
  55.7 7.5 %collective-permute-start.2 = (bf16[2,80,128]{2,1,0:T(8,128)(2,1)S(1)}, bf16[2,80,128]{2,1,0:T(8,128)(2,1)S(1)}, u32[]{:S(2)}, u32[]{:S(2)}) collective-permute-start(bf16[2,80,128]{2,1,0:T(8,128)(2,1)S(1)} %get-tuple-element.28), channel_id=1, source_target_pairs={{1,2},{3,4},{5,6},{7,8},{9,10},{11,12},{13,14},{15,16},{17,18},{19... | collective-permute-start | bytes 122888 | tf_op jit(solution)/shard_map/ppermute | solution.py:271
  60.7 3.1 %collective-permute-start.3 = (bf16[2,80,128]{2,1,0:T(8,128)(2,1)S(1)}, bf16[2,80,128]{2,1,0:T(8,128)(2,1)S(1)}, u32[]{:S(2)}, u32[]{:S(2)}) collective-permute-start(bf16[2,80,128]{2,1,0:T(8,128)(2,1)S(1)} %get-tuple-element.29), channel_id=1, source_target_pairs={{0,1},{2,3},{4,5},{6,7},{8,9},{10,11},{12,13},{14,15},{16,17},{18,... | collective-permute-start | bytes 122888 | tf_op jit(solution)/shard_map/ppermute | solution.py:272

commit v8 on v7

--- a/solution.py
+++ b/solution.py
@@ -7,12 +7,13 @@
 from jax import lax
 from jax.experimental import pallas as pl
 from jax.experimental.pallas import tpu as pltpu
-from jax.sharding import PartitionSpec as P
+from jax.sharding import Mesh, PartitionSpec as P
 
 HALO = 2
 SIDE = 2
 REACH = 2 * HALO + 1
 DELTA = 0.25
+LAT = ("pair", "core")
 BF = jnp.bfloat16
 F32 = jnp.float32
 VMEM = pl.BlockSpec(memory_space=pltpu.VMEM)
@@ -31,22 +32,22 @@
     return lax.dot_general(a, b, (((1,), (1,)), ((), ())), preferred_element_type=F32)
 
 
-def call(kernel, out, specs, flops, moved, scratch=()):
+def call(kernel, out, specs, flops, moved, scratch=(), home=VMEM):
     many = isinstance(out, (tuple, list))
     return pl.pallas_call(
         kernel,
         out_shape=out,
         in_specs=specs,
-        out_specs=tuple([VMEM] * len(out)) if many else VMEM,
+        out_specs=tuple([home] * len(out)) if many else home,
         scratch_shapes=list(scratch),
         compiler_params=pltpu.CompilerParams(vmem_limit_bytes=32 * 2**20),
         cost_estimate=pl.CostEstimate(flops=flops, bytes_accessed=moved, transcendentals=0),
     )
 
 
-def tap_block(lat_count, lag, place, rows, basis, offsets, source, step, store):
+def tap_block(lat_count, lag, band, rows, basis, offsets, source, step, put):
     kernels, lon = basis.shape[1], lag.shape[0]
-    cycle = place[0] * rows + source
+    cycle = band * rows + source
     inside = jnp.logical_and(cycle >= 0, cycle < lat_count)
     cycle = jnp.clip(cycle, 0, lat_count - 1)
     one, two = SIDE * step, SIDE * step + 1
@@ -58,12 +59,12 @@
         weight_two = jnp.where(inside, basis[two, k, cycle], 0.0)
         weight_two = weight_two + jnp.where(off_one == off_two, weight_one, 0.0)
         value = jnp.where(mask_two, weight_two, jnp.where(mask_one, weight_one, 0.0))
-        store[:, k * lon : (k + 1) * lon] = value.astype(BF)
-
-
-def edge_taps(rows):
+        put(k, value.astype(BF))
+
+
+def edge_taps(rows, row):
     outside = list(range(-HALO, 0)) + list(range(rows, rows + HALO))
-    return [(at, step) for at in outside for step in range(REACH) if 0 <= at + step - HALO < rows]
+    return [(at, row - at + HALO) for at in outside if 0 <= row - at + HALO < REACH]
 
 
 def lags(lon):
@@ -84,22 +85,44 @@
         move.start()
     lon = ahead.shape[1] // REACH
     lag = lags(lon)
+    def block(source, step, put):
+        tap_block(lat_count, lag, place[0], rows, basis, offsets, source, step, put)
+
+    def ahead_put(row, step):
+        def put(k, value):
+            ahead[row, step * lon : (step + 1) * lon, k * lon : (k + 1) * lon] = value
+
+        return put
+
+    def edge_put(row, slot):
+        def put(k, value):
+            edge[row, k * lon : (k + 1) * lon, slot * lon : (slot + 1) * lon] = value
+
+        return put
+
     for row in range(rows):
         for step in range(REACH):
-            tap_block(lat_count, lag, place, rows, basis, offsets, row, step, ahead.at[row, step * lon : (step + 1) * lon])
-    for n, (at, step) in enumerate(edge_taps(rows)):
-        tap_block(lat_count, lag, place, rows, basis, offsets, at, step, edge.at[n])
+            block(row, step, ahead_put(row, step))
+        for slot, (at, step) in enumerate(edge_taps(rows, row)):
+            block(at, step, edge_put(row, slot))
     kernels, chan = held.shape[:2]
+    padded = w_fwd.shape[0]
     for move in moves:
         move.wait()
-    dec = padded_rows(dec_t, w_fwd.shape[0])
+    dec = padded_rows(dec_t, padded)
+
+    def placed(k):
+        above, below = jnp.zeros((k * padded, chan), BF), jnp.zeros(((kernels - k) * padded, chan), BF)
+        return jnp.concatenate([part for part in (above, dec, below) if part.shape[0]], axis=0)
+
+    square = (chan, chan)
+    unit = lax.broadcasted_iota(jnp.int32, square, 0) == lax.broadcasted_iota(jnp.int32, square, 1)
+    columns = dot_nt(jnp.where(unit, 1.0, 0.0).astype(BF), placed(0))
     w_fwd[:, :chan] = dec
     for k in range(kernels):
         w_fwd[:, (k + 1) * chan : (k + 2) * chan] = dot_nt(dec, held[k]).astype(BF)
-        w_bwd[k + 1] = dot_nt(held[k], dec).astype(BF)
-    square = (chan, chan)
-    unit = lax.broadcasted_iota(jnp.int32, square, 0) == lax.broadcasted_iota(jnp.int32, square, 1)
-    w_bwd[0] = dot_nt(jnp.where(unit, 1.0, 0.0).astype(BF), dec).astype(BF)
+        columns = columns + dot_nt(held[k], placed(k + 1))
+    w_bwd[...] = columns.astype(BF)
 
 
 def forward(rows, kernels, place, field, cross, chip, ahead, w_fwd, packed, predicted, mixed):
@@ -141,7 +164,7 @@
         sums[m] = jnp.concatenate([totals[m] for totals in pieces], axis=0).astype(BF)
 
 
-def gradient(rows, kernels, members, place, area, sums, predicted, target, mixed, pred_grad, cross, chip, partial):
+def gradient(rows, kernels, members, place, area, sums, predicted, target, mixed, pred_grad, cross, give, keep):
     variables = target.shape[1]
     padded = predicted.shape[1]
     per = sums.shape[1]
@@ -161,7 +184,9 @@
     for n in range(HALO):
         top, bottom = edges[rows - HALO + n], edges[n]
         cross[n] = jnp.where(odd, top, bottom)
-        chip[n] = jnp.where(odd, bottom, top)
+        near = jnp.where(odd, bottom, top)
+        for q in range(pieces):
+            give[n * pieces + q] = near[q * per : (q + 1) * per]
     total = dot_nt(
         jnp.concatenate([mixed[i] for i in range(rows)], axis=1), jnp.concatenate(grads, axis=1)
     )
@@ -171,14 +196,27 @@
     upper = jnp.where(lane < variables, first, pltpu.roll(third, variables, 1))
     tail = jnp.where(lane < 2 * variables - spare, pltpu.roll(third, variables - spare, 1), 0.0)
     lower = jnp.where(lane < variables, second, tail)
-    owners = partial.shape[0]
-    own = chan // owners
+    owners = keep.shape[0]
+    own = chan // (2 * owners)
+
+    def chunk(owner):
+        mine = slice(owner * own, (owner + 1) * own)
+        return jnp.concatenate([upper[mine], lower[mine]], axis=0)
+
     for owner in range(owners):
-        mine = slice(owner * own, (owner + 1) * own)
-        partial[owner] = jnp.concatenate([upper[mine], lower[mine]], axis=0).astype(BF)
-
-
-def band_sum(factor, variables, parts, w_bwd, spread):
+        even, uneven = chunk(2 * owner), chunk(2 * owner + 1)
+        keep[owner] = jnp.where(odd, uneven, even)
+        give[HALO * pieces + owner] = jnp.where(odd, even, uneven).astype(BF)
+
+
+def fold(got, keep, merged):
+    owners = keep.shape[0]
+    skip = got.shape[0] - owners
+    for owner in range(owners):
+        merged[owner] = (keep[owner] + got[skip + owner].astype(F32)).astype(BF)
+
+
+def band_sum(factor, variables, padded, parts, w_bwd, spread):
     owners, height, lon = parts.shape
     total = parts[0].astype(F32)
     for owner in range(1, owners):
@@ -195,8 +233,7 @@
     total = jnp.concatenate([total, third, jnp.zeros((lon - height - own, lon), F32)], axis=0)
     upper = total.astype(BF)
     lower = (total - upper.astype(F32)).astype(BF)
-    dec = w_bwd[0]
-    padded = dec.shape[1]
+    dec = w_bwd[:, :padded]
     result = dot_nt(dec, upper[:, :padded]) + dot_nt(dec, lower[:, :padded])
     per = spread.shape[1]
     for member in range(spread.shape[0]):
@@ -225,23 +262,25 @@
                 piece = found[:, row * lon : (row + 1) * lon]
                 sums[row] = piece if sums[row] is None else sums[row] + piece
         for row in range(rows):
-            turned[k, :, row * lon : (row + 1) * lon] = sums[row]
-
-
-def adjoint_rest(rows, kernels, place, pred_grad, cross, chip, turned, edge, w_bwd, result):
-    lon = pred_grad.shape[2]
+            turned[row, :, k * lon : (k + 1) * lon] = sums[row]
+
+
+def adjoint_rest(rows, kernels, place, pred_grad, cross, got, turned, edge, w_bwd, result, buffer, sems):
+    padded, lon = pred_grad.shape[1:]
+    pieces = padded // got.shape[1]
+    chip = [jnp.concatenate([got[n * pieces + q] for q in range(pieces)], axis=0) for n in range(HALO)]
     low, high = sides((place[0] & 1) == 1, cross, chip)
     outer = dict(enumerate(low, -HALO)) | dict(enumerate(high, rows))
-    total = dot_nn(w_bwd[0], jnp.concatenate([pred_grad[i] for i in range(rows)], axis=1))
-    for k in range(kernels):
-        sums = [turned[k, :, row * lon : (row + 1) * lon] for row in range(rows)]
-        for n, (at, step) in enumerate(edge_taps(rows)):
-            row = at + step - HALO
-            sums[row] = sums[row] + dot_nt(outer[at], edge[n, :, k * lon : (k + 1) * lon])
-        taps = jnp.concatenate(sums, axis=1).astype(BF)
-        total = total + dot_nn(w_bwd[k + 1], taps)
-    for i in range(rows):
-        result[i] = total[:, i * lon : (i + 1) * lon].astype(BF)
+    moves = []
+    for row in range(rows):
+        sources = jnp.concatenate([outer[at] for at, _ in edge_taps(rows, row)], axis=1)
+        taps = (turned[row] + dot_nt(sources, edge[row])).astype(BF)
+        stack = [pred_grad[row]] + [taps[:, k * lon : (k + 1) * lon] for k in range(kernels)]
+        buffer[row] = dot_nn(w_bwd[...], jnp.concatenate(stack, axis=0)).astype(BF)
+        moves.append(pltpu.make_async_copy(buffer.at[row], result.at[row], sems.at[row]))
+        moves[-1].start()
+    for move in moves:
+        move.wait()
 
 
 def cut(place, field, cross, chip, sems):
@@ -264,13 +303,10 @@
     return low, high
 
 
-def exchange(cross, chip, axis):
-    count = lax.axis_size(axis)
-    far = [(i, i + 1) for i in range(1, count - 1, 2)]
-    near = [(i, i + 1) for i in range(0, count - 1, 2)]
-    cross = lax.ppermute(cross, axis, far + [(b, a) for a, b in far])
-    chip = lax.ppermute(chip, axis, near + [(b, a) for a, b in near])
-    return cross, chip
+def across(block, axes, start):
+    count = lax.axis_size(axes)
+    pairs_up = [(i, i + 1) for i in range(start, count - 1, 2)]
+    return lax.ppermute(block, axes, pairs_up + [(b, a) for a, b in pairs_up])
 
 
 def body(latent_fields, target_fields, filters, decoder, cycle_basis, cycle_offsets):
@@ -278,10 +314,10 @@
     rows, chan, lon = field.shape
     lat_count, kernels, taps = cycle_basis.shape
     variables = decoder.shape[1]
-    members, bands = lax.axis_size("ens"), lax.axis_size("lat")
+    members, bands = lax.axis_size("ens"), lax.axis_size(LAT)
     per = 16
     padded = -(-variables // per) * per
-    band = lax.axis_index("lat").astype(jnp.int32)
+    band = lax.axis_index(LAT).astype(jnp.int32)
     place = band.reshape(1)
     area = jnp.asarray(np.cos(np.pi * (np.arange(lat_count) + 0.5) / lat_count - np.pi / 2), F32)
     dec_t = decoder.T
@@ -293,14 +329,14 @@
     edge = jax.ShapeDtypeStruct((HALO, chan, lon), BF)
     pair = pltpu.SemaphoreType.DMA((2,))
     cross, chip = call(cut, (edge, edge), [SMEM, hbm], 0, 500_000, [pair])(place, stay(field))
-    cross, chip = exchange(cross, chip, "lat")
+    cross, chip = across(cross, LAT, 1), across(chip, LAT, 0)
     ahead, tap_edge, w_fwd, w_bwd, near = call(
         functools.partial(prepare, rows, lat_count),
         (
             jax.ShapeDtypeStruct((rows, REACH * lon, kernels * lon), BF),
-            jax.ShapeDtypeStruct((len(edge_taps(rows)), lon, kernels * lon), BF),
+            jax.ShapeDtypeStruct((rows, kernels * lon, (REACH - rows) * lon), BF),
             jax.ShapeDtypeStruct((padded, (kernels + 1) * chan), BF),
-            jax.ShapeDtypeStruct((kernels + 1, chan, padded), BF),
+            jax.ShapeDtypeStruct((chan, (kernels + 1) * padded), BF),
             jax.ShapeDtypeStruct(field.shape, BF),
         ),
         [SMEM, SMEM, SMEM, hbm, hbm, hbm],
@@ -323,40 +359,47 @@
     sums = call(pairs, jax.ShapeDtypeStruct((members, per, lon), BF), [VMEM], 2_000_000, 200_000)(visitors)
     sums = lax.all_to_all(sums, "ens", 0, 0, tiled=True)
     own = chan // bands
-    edge = jax.ShapeDtypeStruct((HALO, padded, lon), BF)
-    pred_grad, cross, chip, partial = call(
+    pieces = padded // per
+    owners = bands // 2
+    pred_grad, cross, give, keep = call(
         functools.partial(gradient, rows, kernels, members),
         (
             jax.ShapeDtypeStruct((rows, padded, lon), BF),
-            edge,
-            edge,
-            jax.ShapeDtypeStruct((bands, 2 * own, lon), BF),
+            jax.ShapeDtypeStruct((HALO, padded, lon), BF),
+            jax.ShapeDtypeStruct((HALO * pieces + owners, per, lon), BF),
+            jax.ShapeDtypeStruct((owners, 2 * own, lon), F32),
         ),
         [SMEM, SMEM] + [VMEM] * 4,
         80_000_000,
         1_200_000,
     )(place, area, sums, predicted, target_fields, mixed)
-    parts = lax.all_to_all(partial, "lat", 0, 0, tiled=True)
-    cross, chip = exchange(cross, chip, "lat")
+    got = across(give, LAT, 0)
     turned = call(
         functools.partial(adjoint_own, rows, kernels),
-        jax.ShapeDtypeStruct((kernels, padded, rows * lon), F32),
+        jax.ShapeDtypeStruct((rows, padded, kernels * lon), F32),
         [VMEM] * 2,
         80_000_000,
         1_500_000,
     )(pred_grad, ahead)
+    got, turned = lax.optimization_barrier((got, turned))
+    merged = call(fold, jax.ShapeDtypeStruct((owners, 2 * own, lon), BF), [VMEM] * 2, 100_000, 300_000)(got, keep)
+    cross, merged = lax.optimization_barrier((cross, merged))
+    parts = lax.all_to_all(merged, "pair", 0, 0, tiled=True)
+    cross = across(cross, LAT, 1)
     latent_grad = call(
         functools.partial(adjoint_rest, rows, kernels),
         jax.ShapeDtypeStruct((rows, chan, lon), BF),
         [SMEM] + [VMEM] * 6,
         150_000_000,
         1_500_000,
-    )(place, pred_grad, cross, chip, turned, tap_edge, w_bwd)
+        [pltpu.VMEM((rows, chan, lon), BF), pltpu.SemaphoreType.DMA((rows,))],
+        hbm,
+    )(place, pred_grad, cross, got, turned, tap_edge, w_bwd)
     parts, latent_grad = lax.optimization_barrier((parts, latent_grad))
     factor = 1.0 / math.sqrt(members * lat_count * lon)
     width = chan // members
     spread = call(
-        functools.partial(band_sum, factor, variables),
+        functools.partial(band_sum, factor, variables, padded),
         jax.ShapeDtypeStruct((members, width, lon), BF),
         [VMEM] * 2,
         20_000_000,
@@ -370,11 +413,13 @@
 
 
 def solution(mesh):
-    placed = (P("ens", "lat", None, None), P("lat", None, None), P(), P(), P(), P())
+    members, bands = mesh.devices.shape
+    split = Mesh(mesh.devices.reshape(members, bands // 2, 2), ("ens", "pair", "core"))
+    placed = (P("ens", LAT, None, None), P(LAT, None, None), P(), P(), P(), P())
     return jax.shard_map(
         body,
-        mesh=mesh,
+        mesh=split,
         in_specs=placed,
-        out_specs=(P("ens", "lat", None, None), P("lat", None, "ens")),
+        out_specs=(P("ens", LAT, None, None), P(LAT, None, "ens")),
         check_vma=False,
     )

time: 77.9 us -> 79.9 us (1.026); the launches traced: 77.4 us -> 78.6 us
  waiting for transfers between devices: 1.54 us -> 2.7 us
    ppermute x4, starting transfers between devices: 16.4 us -> 20 us  [across(): return lax.ppermute(block, axes, pairs_up + [(b, a) for a, b in pairs_up])]
    all_to_all x1, starting transfers between devices: 16.1 us -> 12.5 us  [body(): parts = lax.all_to_all(merged, 'pair', 0, 0, tiled=True)]
    ppermute x4, waiting for transfers between devices: 0.67 us -> 2.5 us  [across(): return lax.ppermute(block, axes, pairs_up + [(b, a) for a, b in pairs_up])]
  transfers between devices with their start and end apart: 5 -> 5, of which waited for: 2 -> 3; matrix products, arithmetic and copies ran while one was open for 0% -> 0% of each run, Pallas kernels for 6% -> 6%
where the time goes in v8:
time: 79.9 us; the launch traced here: 78.6 us
  starting transfers between devices  32.6 us (41%)
  blocking collectives  32.6 us (41%)
  Pallas kernels  10 us (13%)
  waiting for transfers between devices  2.7 us (3%)
    ppermute x4, starting transfers between devices, across(): return lax.ppermute(block, axes, pairs_up + [(b, a) for a, b in pairs_up])  20 us
    all_to_all x1, blocking collectives, body(): visitors = lax.all_to_all(packed, 'ens', 0, 0, tiled=True)  12.7 us
    all_to_all x1, starting transfers between devices, body(): parts = lax.all_to_all(merged, 'pair', 0, 0, tiled=True)  12.5 us
    all_to_all x1, blocking collectives, body(): sums = lax.all_to_all(sums, 'ens', 0, 0, tiled=True)  9.95 us
    all_to_all x1, blocking collectives, body(): spread = lax.all_to_all(spread, 'ens', 0, 0, tiled=True)  9.95 us
    pallas_call x1, Pallas kernels, body(): call(functools.partial(prepare, rows, lat_count), (jax.ShapeDtypeStruct((...  2.86 us
    ppermute x4, waiting for transfers between devices, across(): return lax.ppermute(block, axes, pairs_up + [(b, a) for a, b in pairs_up])  2.5 us
  transfers between devices with their start and end apart: 5, of which 3 were waited for; matrix products, arithmetic and copies ran while one was open for 0% of the time, Pallas kernels for 6%

profile of v8, /device:TPU:1, one launch (start us, length us, event | category | flops | bytes accessed | tf_op | source)
XLA Modules:
  0.0 78.6 jit_solution(4749750598372526317)
XLA Ops:
  0.6 1.0 %shard_map.87 = (bf16[2,256,128]{2,1,0:T(8,128)(2,1)S(1)}, bf16[2,256,128]{2,1,0:T(8,128)(2,1)S(1)}) custom-call(s32[1]{0:T(128)} %bitcast.place, bf16[3,256,128]{2,1,0:T(8,128)(2,1)} %bitcast.7), custom_call_target="tpu_custom_call" | custom-call | bytes 500000 | tf_op jit(solution)/shard_map/pallas_call | solution.py:331
  1.6 6.0 %collective-permute-start = (bf16[2,256,128]{2,1,0:T(8,128)(2,1)S(1)}, bf16[2,256,128]{2,1,0:T(8,128)(2,1)S(1)}, u32[]{:S(2)}, u32[]{:S(2)}) collective-permute-start(bf16[2,256,128]{2,1,0:T(8,128)(2,1)S(1)} %get-tuple-element.23), channel_id=1, source_target_pairs={{1,2},{3,4},{5,6},{7,8},{9,10},{11,12},{13,14},{15,16},{17,18},{19... | collective-permute-start | bytes 393224 | tf_op jit(solution)/shard_map/ppermute | solution.py:309
  7.7 3.4 %collective-permute-start.1 = (bf16[2,256,128]{2,1,0:T(8,128)(2,1)S(1)}, bf16[2,256,128]{2,1,0:T(8,128)(2,1)S(1)}, u32[]{:S(2)}, u32[]{:S(2)}) collective-permute-start(bf16[2,256,128]{2,1,0:T(8,128)(2,1)S(1)} %get-tuple-element.24), channel_id=1, source_target_pairs={{0,1},{2,3},{4,5},{6,7},{8,9},{10,11},{12,13},{14,15},{16,17},{18,... | collective-permute-start | bytes 393224 | tf_op jit(solution)/shard_map/ppermute | solution.py:309
  11.1 0.0 copy-start
  11.1 0.0 copy-start.1
  11.1 2.9 %shard_map.86 = (bf16[3,640,384]{2,1,0:T(8,128)(2,1)S(1)}, bf16[3,384,256]{2,1,0:T(8,128)(2,1)S(1)}, bf16[80,1024]{1,0:T(8,128)(2,1)S(1)}, bf16[256,320]{1,0:T(8,128)(2,1)S(1)}, bf16[3,256,128]{2,1,0:T(8,128)(2,1)S(1)}) custom-call(s32[1]{0:T(128)} %bitcast.place, f32[10,3,96]{2,1,0:T(4,128)} %bitcast.11, s32[10,96]{1,0:T(8,128)} %bitcast.13, ...), custom_call_target="tpu_custom_call" | custom-call | flops 30000000 | bytes 2000000 | tf_op jit(solution)/shard_map/pallas_call | solution.py:333
  14.0 0.0 collective-permute-done.cross
  14.0 0.0 collective-permute-done.1.chip
  14.0 1.3 %shard_map.88 = (bf16[16,16,128]{2,1,0:T(8,128)(2,1)S(1)}, f32[3,80,128]{2,1,0:T(8,128)S(1)}, bf16[3,768,128]{2,1,0:T(8,128)(2,1)S(1)}) custom-call(s32[1]{0:T(128)} %bitcast.place, bf16[3,256,128]{2,1,0:T(8,128)(2,1)S(1)} %get-tuple-element.22.field, bf16[2,256,128]{2,1,0:T(8,128)(2,1)S(1)} %collective-permute-done.cross, ...), custom_call_target="tpu_custom_call" | custom-call | flops 450000000 | bytes 3000000 | tf_op jit(solution)/shard_map/pallas_call | solution.py:347
  15.3 12.7 %all_to_all.20.visitors = bf16[16,16,128]{2,1,0:T(8,128)(2,1)S(1)} all-to-all(bf16[16,16,128]{2,1,0:T(8,128)(2,1)S(1)} %get-tuple-element.27), channel_id=1, replica_groups=mesh['ens'=16,'pair'=16,'core'=2] {'ens'}, dimensions={0} | all-to-all | bytes 131072 | tf_op jit(solution)/shard_map/all_to_all | solution.py:358
  28.0 0.2 shard_map.89
  28.2 10.0 %all_to_all.21.sums = bf16[16,16,128]{2,1,0:T(8,128)(2,1)S(1)} all-to-all(bf16[16,16,128]{2,1,0:T(8,128)(2,1)S(1)} %shard_map.89), channel_id=1, replica_groups=mesh['ens'=16,'pair'=16,'core'=2] {'ens'}, dimensions={0} | all-to-all | bytes 131072 | tf_op jit(solution)/shard_map/all_to_all | solution.py:360
  38.2 0.0 copy-done
  38.2 0.0 copy-done.1
  38.2 1.0 %shard_map.90 = (bf16[3,80,128]{2,1,0:T(8,128)(2,1)S(1)}, bf16[2,80,128]{2,1,0:T(8,128)(2,1)S(1)}, bf16[26,16,128]{2,1,0:T(8,128)(2,1)S(1)}, f32[16,16,128]{2,1,0:T(8,128)S(1)}) custom-call(s32[1]{0:T(128)} %bitcast.place, f32[96]{0:T(128)S(1)} %copy-done.1, bf16[16,16,128]{2,1,0:T(8,128)(2,1)S(1)} %all_to_all.21.sums, ...), custom_call_target="tpu_custom_call" | custom-call | flops 80000000 | bytes 1200000 | tf_op jit(solution)/shard_map/pallas_call | solution.py:364
  39.2 5.0 %collective-permute-start.2 = (bf16[26,16,128]{2,1,0:T(8,128)(2,1)S(1)}, bf16[26,16,128]{2,1,0:T(8,128)(2,1)S(1)}, u32[]{:S(2)}, u32[]{:S(2)}) collective-permute-start(bf16[26,16,128]{2,1,0:T(8,128)(2,1)S(1)} %get-tuple-element.31), channel_id=1, source_target_pairs={{0,1},{2,3},{4,5},{6,7},{8,9},{10,11},{12,13},{14,15},{16,17},{18,... | collective-permute-start | bytes 319496 | tf_op jit(solution)/shard_map/ppermute | solution.py:309
  44.2 0.5 shard_map.91.turned
  44.7 0.4 collective-permute-done.2.got
  45.1 0.6 shard_map.92
  45.7 12.5 %all-to-all-start.2 = ((bf16[16,16,128]{2,1,0:T(8,128)(2,1)}), bf16[16,16,128]{2,1,0:T(8,128)(2,1)S(1)}, u32[]{:S(2)}, u32[]{:S(2)}) async-start(bf16[16,16,128]{2,1,0:T(8,128)(2,1)} %shard_map.92), calls=%async_computation.2 | async-start | bytes 131072 | tf_op jit(solution)/shard_map/all_to_all | solution.py:387
  58.3 5.6 %collective-permute-start.3 = (bf16[2,80,128]{2,1,0:T(8,128)(2,1)S(1)}, bf16[2,80,128]{2,1,0:T(8,128)(2,1)S(1)}, u32[]{:S(2)}, u32[]{:S(2)}) collective-permute-start(bf16[2,80,128]{2,1,0:T(8,128)(2,1)S(1)} %get-tuple-element.36), channel_id=1, source_target_pairs={{1,2},{3,4},{5,6},{7,8},{9,10},{11,12},{13,14},{15,16},{17,18},{19... | collective-permute-start | bytes 122888 | tf_op jit(solution)/shard_map/ppermute | solution.py:309
  63.8 2.1 %collective-permute-done.3.cross = bf16[2,80,128]{2,1,0:T(8,128)(2,1)S(1)} collective-permute-done((bf16[2,80,128]{2,1,0:T(8,128)(2,1)S(1)}, bf16[2,80,128]{2,1,0:T(8,128)(2,1)S(1)}, u32[]{:S(2)}, u32[]{:S(2)}) %collective-permute-start.3) | collective-permute-done | bytes 40992 | tf_op jit(solution)/shard_map/ppermute | solution.py:309
  65.9 1.5 %shard_map.93 = bf16[3,256,128]{2,1,0:T(8,128)(2,1)} custom-call(s32[1]{0:T(128)} %bitcast.place, bf16[3,80,128]{2,1,0:T(8,128)(2,1)S(1)} %get-tuple-element.32.pred_grad, bf16[2,80,128]{2,1,0:T(8,128)(2,1)S(1)} %collective-permute-done.3.cross, bf16[26,16,128]{2,1,0:T(8,128)(2,1)S(1)} %collective-permute-done.2.got, f32[3,80,384]{2,1,0:T(8,128)S(1)} %shard_map.91.turned, ...), custom_call_target="tpu_custom_call" | custom-call | flops 150000000 | bytes 1500000 | tf_op jit(solution)/shard_map/pallas_call | solution.py:389
  67.5 0.2 all-to-all-done.2.parts
  67.7 0.3 shard_map.94
  67.9 10.0 %all_to_all.22.parts = bf16[16,16,128]{2,1,0:T(8,128)(2,1)S(1)} all-to-all(bf16[16,16,128]{2,1,0:T(8,128)(2,1)S(1)} %shard_map.94), channel_id=1, replica_groups=mesh['ens'=16,'pair'=16,'core'=2] {'ens'}, dimensions={0} | all-to-all | bytes 131072 | tf_op jit(solution)/shard_map/all_to_all | solution.py:408
  77.9 0.7 shard_map.95
Async XLA Ops:
  1.6 12.4 %collective-permute-start = (bf16[2,256,128]{2,1,0:T(8,128)(2,1)S(1)}, bf16[2,256,128]{2,1,0:T(8,128)(2,1)S(1)}, u32[]{:S(2)}, u32[]{:S(2)}) collective-permute-start(bf16[2,256,128]{2,1,0:T(8,128)(2,1)S(1)} %get-tuple-element.23), channel_id=1, source_target_pairs={{1,2},{3,4},{5,6},{7,8},{9,10},{11,12},{13,14},{15,16},{17,18},{19... | collective-permute-start | bytes 393224 | tf_op jit(solution)/shard_map/ppermute | solution.py:309
  7.7 6.3 %collective-permute-start.1 = (bf16[2,256,128]{2,1,0:T(8,128)(2,1)S(1)}, bf16[2,256,128]{2,1,0:T(8,128)(2,1)S(1)}, u32[]{:S(2)}, u32[]{:S(2)}) collective-permute-start(bf16[2,256,128]{2,1,0:T(8,128)(2,1)S(1)} %get-tuple-element.24), channel_id=1, source_target_pairs={{0,1},{2,3},{4,5},{6,7},{8,9},{10,11},{12,13},{14,15},{16,17},{18,... | collective-permute-start | bytes 393224 | tf_op jit(solution)/shard_map/ppermute | solution.py:309
  11.1 27.1 %copy-start = (bf16[3,72,128]{2,1,0:T(8,128)(2,1)S(1)}, bf16[3,72,128]{2,1,0:T(8,128)(2,1)}, u32[]{:S(2)}) copy-start(bf16[3,72,128]{2,1,0:T(8,128)(2,1)} %target.1) | copy-start | bytes 165892
  11.1 27.0 %copy-start.1 = (f32[96]{0:T(128)S(1)}, f32[96]{0:T(128)}, u32[]{:S(2)}) copy-start(f32[96]{0:T(128)} %constant.12.clone.area) | copy-start | bytes 1156
  39.2 5.9 %collective-permute-start.2 = (bf16[26,16,128]{2,1,0:T(8,128)(2,1)S(1)}, bf16[26,16,128]{2,1,0:T(8,128)(2,1)S(1)}, u32[]{:S(2)}, u32[]{:S(2)}) collective-permute-start(bf16[26,16,128]{2,1,0:T(8,128)(2,1)S(1)} %get-tuple-element.31), channel_id=1, source_target_pairs={{0,1},{2,3},{4,5},{6,7},{8,9},{10,11},{12,13},{14,15},{16,17},{18,... | collective-permute-start | bytes 319496 | tf_op jit(solution)/shard_map/ppermute | solution.py:309
  45.7 21.9 %all-to-all-start.2 = ((bf16[16,16,128]{2,1,0:T(8,128)(2,1)}), bf16[16,16,128]{2,1,0:T(8,128)(2,1)S(1)}, u32[]{:S(2)}, u32[]{:S(2)}) async-start(bf16[16,16,128]{2,1,0:T(8,128)(2,1)} %shard_map.92), calls=%async_computation.2 | async-start | bytes 131072 | tf_op jit(solution)/shard_map/all_to_all | solution.py:387
  58.3 7.7 %collective-permute-start.3 = (bf16[2,80,128]{2,1,0:T(8,128)(2,1)S(1)}, bf16[2,80,128]{2,1,0:T(8,128)(2,1)S(1)}, u32[]{:S(2)}, u32[]{:S(2)}) collective-permute-start(bf16[2,80,128]{2,1,0:T(8,128)(2,1)S(1)} %get-tuple-element.36), channel_id=1, source_target_pairs={{1,2},{3,4},{5,6},{7,8},{9,10},{11,12},{13,14},{15,16},{17,18},{19... | collective-permute-start | bytes 122888 | tf_op jit(solution)/shard_map/ppermute | solution.py:309

commit v9 on v8

--- a/solution.py
+++ b/solution.py
@@ -383,8 +383,18 @@
     )(pred_grad, ahead)
     got, turned = lax.optimization_barrier((got, turned))
     merged = call(fold, jax.ShapeDtypeStruct((owners, 2 * own, lon), BF), [VMEM] * 2, 100_000, 300_000)(got, keep)
-    cross, merged = lax.optimization_barrier((cross, merged))
     parts = lax.all_to_all(merged, "pair", 0, 0, tiled=True)
+    factor = 1.0 / math.sqrt(members * lat_count * lon)
+    width = chan // members
+    spread = call(
+        functools.partial(band_sum, factor, variables, padded),
+        jax.ShapeDtypeStruct((members, width, lon), BF),
+        [VMEM] * 2,
+        20_000_000,
+        400_000,
+    )(parts, w_bwd)
+    cross, spread = lax.optimization_barrier((cross, spread))
+    spread = lax.all_to_all(spread, "ens", 0, 0, tiled=True)
     cross = across(cross, LAT, 1)
     latent_grad = call(
         functools.partial(adjoint_rest, rows, kernels),
@@ -395,17 +405,7 @@
         [pltpu.VMEM((rows, chan, lon), BF), pltpu.SemaphoreType.DMA((rows,))],
         hbm,
     )(place, pred_grad, cross, got, turned, tap_edge, w_bwd)
-    parts, latent_grad = lax.optimization_barrier((parts, latent_grad))
-    factor = 1.0 / math.sqrt(members * lat_count * lon)
-    width = chan // members
-    spread = call(
-        functools.partial(band_sum, factor, variables, padded),
-        jax.ShapeDtypeStruct((members, width, lon), BF),
-        [VMEM] * 2,
-        20_000_000,
-        400_000,
-    )(parts, w_bwd)
-    spread = lax.all_to_all(spread, "ens", 0, 0, tiled=True)
+    spread, latent_grad = lax.optimization_barrier((spread, latent_grad))
     owned = call(
         member_sum, jax.ShapeDtypeStruct((kernels, own, width), F32), [VMEM], 100_000, 150_000
     )(spread)

time: 79.9 us -> 81.2 us (1.016)
  blocking collectives: 32.6 us -> 44.3 us
  starting transfers between devices: 32.6 us -> 21.9 us
  waiting for transfers between devices: 2.7 us -> 3.65 us
    all_to_all x1, blocking collectives: 9.95 us -> 21.7 us  [body(): parts = lax.all_to_all(merged, 'pair', 0, 0, tiled=True)]
    all_to_all x1, starting transfers between devices: 12.5 us -> 3.49 us  [body(): spread = lax.all_to_all(spread, 'ens', 0, 0, tiled=True)]
    ppermute x4, starting transfers between devices: 20 us -> 18.4 us  [across(): return lax.ppermute(block, axes, pairs_up + [(b, a) for a, b in pairs_up])]
    ppermute x4, waiting for transfers between devices: 2.5 us -> 3.65 us  [across(): return lax.ppermute(block, axes, pairs_up + [(b, a) for a, b in pairs_up])]
  transfers between devices with their start and end apart: 5 -> 5, of which waited for: 3 -> 2; matrix products, arithmetic and copies ran while one was open for 0% -> 0% of each run, Pallas kernels for 6% -> 6%
where the time goes in v9:
time: 81.2 us; the launch traced here: 80.7 us
  blocking collectives  44.3 us (55%)
  starting transfers between devices  21.9 us (27%)
  Pallas kernels  10 us (12%)
  waiting for transfers between devices  3.65 us (4%)
    all_to_all x1, blocking collectives, body(): parts = lax.all_to_all(merged, 'pair', 0, 0, tiled=True)  21.7 us
    ppermute x4, starting transfers between devices, across(): return lax.ppermute(block, axes, pairs_up + [(b, a) for a, b in pairs_up])  18.4 us
    all_to_all x1, blocking collectives, body(): visitors = lax.all_to_all(packed, 'ens', 0, 0, tiled=True)  12.7 us
    all_to_all x1, blocking collectives, body(): sums = lax.all_to_all(sums, 'ens', 0, 0, tiled=True)  9.95 us
    ppermute x4, waiting for transfers between devices, across(): return lax.ppermute(block, axes, pairs_up + [(b, a) for a, b in pairs_up])  3.65 us
    all_to_all x1, starting transfers between devices, body(): spread = lax.all_to_all(spread, 'ens', 0, 0, tiled=True)  3.49 us
    pallas_call x1, Pallas kernels, body(): call(functools.partial(prepare, rows, lat_count), (jax.ShapeDtypeStruct((...  2.86 us
  transfers between devices with their start and end apart: 5, of which 2 were waited for; matrix products, arithmetic and copies ran while one was open for 0% of the time, Pallas kernels for 6%

profile of v9, /device:TPU:1, one launch (start us, length us, event | category | flops | bytes accessed | tf_op | source)
XLA Modules:
  0.0 80.7 jit_solution(14705666474428793194)
XLA Ops:
  0.6 1.0 %shard_map.87 = (bf16[2,256,128]{2,1,0:T(8,128)(2,1)S(1)}, bf16[2,256,128]{2,1,0:T(8,128)(2,1)S(1)}) custom-call(s32[1]{0:T(128)} %bitcast.place, bf16[3,256,128]{2,1,0:T(8,128)(2,1)} %bitcast.7), custom_call_target="tpu_custom_call" | custom-call | bytes 500000 | tf_op jit(solution)/shard_map/pallas_call | solution.py:331
  1.6 6.0 %collective-permute-start = (bf16[2,256,128]{2,1,0:T(8,128)(2,1)S(1)}, bf16[2,256,128]{2,1,0:T(8,128)(2,1)S(1)}, u32[]{:S(2)}, u32[]{:S(2)}) collective-permute-start(bf16[2,256,128]{2,1,0:T(8,128)(2,1)S(1)} %get-tuple-element.23), channel_id=1, source_target_pairs={{1,2},{3,4},{5,6},{7,8},{9,10},{11,12},{13,14},{15,16},{17,18},{19... | collective-permute-start | bytes 393224 | tf_op jit(solution)/shard_map/ppermute | solution.py:309
  7.7 3.4 %collective-permute-start.1 = (bf16[2,256,128]{2,1,0:T(8,128)(2,1)S(1)}, bf16[2,256,128]{2,1,0:T(8,128)(2,1)S(1)}, u32[]{:S(2)}, u32[]{:S(2)}) collective-permute-start(bf16[2,256,128]{2,1,0:T(8,128)(2,1)S(1)} %get-tuple-element.24), channel_id=1, source_target_pairs={{0,1},{2,3},{4,5},{6,7},{8,9},{10,11},{12,13},{14,15},{16,17},{18,... | collective-permute-start | bytes 393224 | tf_op jit(solution)/shard_map/ppermute | solution.py:309
  11.1 0.0 copy-start
  11.1 0.0 copy-start.1
  11.1 2.9 %shard_map.86 = (bf16[3,640,384]{2,1,0:T(8,128)(2,1)S(1)}, bf16[3,384,256]{2,1,0:T(8,128)(2,1)S(1)}, bf16[80,1024]{1,0:T(8,128)(2,1)S(1)}, bf16[256,320]{1,0:T(8,128)(2,1)S(1)}, bf16[3,256,128]{2,1,0:T(8,128)(2,1)S(1)}) custom-call(s32[1]{0:T(128)} %bitcast.place, f32[10,3,96]{2,1,0:T(4,128)} %bitcast.11, s32[10,96]{1,0:T(8,128)} %bitcast.13, ...), custom_call_target="tpu_custom_call" | custom-call | flops 30000000 | bytes 2000000 | tf_op jit(solution)/shard_map/pallas_call | solution.py:333
  14.0 0.0 collective-permute-done.cross
  14.0 0.0 collective-permute-done.1.chip
  14.0 1.3 %shard_map.88 = (bf16[16,16,128]{2,1,0:T(8,128)(2,1)S(1)}, f32[3,80,128]{2,1,0:T(8,128)S(1)}, bf16[3,768,128]{2,1,0:T(8,128)(2,1)S(1)}) custom-call(s32[1]{0:T(128)} %bitcast.place, bf16[3,256,128]{2,1,0:T(8,128)(2,1)S(1)} %get-tuple-element.22.field, bf16[2,256,128]{2,1,0:T(8,128)(2,1)S(1)} %collective-permute-done.cross, ...), custom_call_target="tpu_custom_call" | custom-call | flops 450000000 | bytes 3000000 | tf_op jit(solution)/shard_map/pallas_call | solution.py:347
  15.3 12.7 %all_to_all.20.visitors = bf16[16,16,128]{2,1,0:T(8,128)(2,1)S(1)} all-to-all(bf16[16,16,128]{2,1,0:T(8,128)(2,1)S(1)} %get-tuple-element.27), channel_id=1, replica_groups=mesh['ens'=16,'pair'=16,'core'=2] {'ens'}, dimensions={0} | all-to-all | bytes 131072 | tf_op jit(solution)/shard_map/all_to_all | solution.py:358
  28.0 0.2 shard_map.89
  28.2 10.0 %all_to_all.21.sums = bf16[16,16,128]{2,1,0:T(8,128)(2,1)S(1)} all-to-all(bf16[16,16,128]{2,1,0:T(8,128)(2,1)S(1)} %shard_map.89), channel_id=1, replica_groups=mesh['ens'=16,'pair'=16,'core'=2] {'ens'}, dimensions={0} | all-to-all | bytes 131072 | tf_op jit(solution)/shard_map/all_to_all | solution.py:360
  38.2 0.0 copy-done
  38.2 0.0 copy-done.1
  38.2 1.0 %shard_map.90 = (bf16[3,80,128]{2,1,0:T(8,128)(2,1)S(1)}, bf16[2,80,128]{2,1,0:T(8,128)(2,1)S(1)}, bf16[26,16,128]{2,1,0:T(8,128)(2,1)S(1)}, f32[16,16,128]{2,1,0:T(8,128)S(1)}) custom-call(s32[1]{0:T(128)} %bitcast.place, f32[96]{0:T(128)S(1)} %copy-done.1, bf16[16,16,128]{2,1,0:T(8,128)(2,1)S(1)} %all_to_all.21.sums, ...), custom_call_target="tpu_custom_call" | custom-call | flops 80000000 | bytes 1200000 | tf_op jit(solution)/shard_map/pallas_call | solution.py:364
  39.2 5.0 %collective-permute-start.2 = (bf16[26,16,128]{2,1,0:T(8,128)(2,1)S(1)}, bf16[26,16,128]{2,1,0:T(8,128)(2,1)S(1)}, u32[]{:S(2)}, u32[]{:S(2)}) collective-permute-start(bf16[26,16,128]{2,1,0:T(8,128)(2,1)S(1)} %get-tuple-element.31), channel_id=1, source_target_pairs={{0,1},{2,3},{4,5},{6,7},{8,9},{10,11},{12,13},{14,15},{16,17},{18,... | collective-permute-start | bytes 319496 | tf_op jit(solution)/shard_map/ppermute | solution.py:309
  44.2 0.5 shard_map.91.turned
  44.7 0.4 collective-permute-done.2.got
  45.1 21.7 %all_to_all.22.parts = bf16[16,16,128]{2,1,0:T(8,128)(2,1)S(1)} all-to-all(bf16[16,16,128]{2,1,0:T(8,128)(2,1)S(1)} %shard_map.92), channel_id=1, replica_groups=mesh['ens'=16,'pair'=16,'core'=2] {'pair'}, dimensions={0} | all-to-all | bytes 131072 | tf_op jit(solution)/shard_map/all_to_all | solution.py:386
  66.9 0.9 %shard_map.93 = bf16[16,16,128]{2,1,0:T(8,128)(2,1)} custom-call(bf16[16,16,128]{2,1,0:T(8,128)(2,1)S(1)} %all_to_all.22.parts, bf16[256,320]{1,0:T(8,128)(2,1)S(1)} %get-tuple-element.35.w_bwd), custom_call_target="tpu_custom_call" | custom-call | flops 20000000 | bytes 400000 | tf_op jit(solution)/shard_map/pallas_call | solution.py:389
  67.7 3.5 %all-to-all-start.3 = ((bf16[16,16,128]{2,1,0:T(8,128)(2,1)}), bf16[16,16,128]{2,1,0:T(8,128)(2,1)S(1)}, u32[]{:S(2)}, u32[]{:S(2)}) async-start(bf16[16,16,128]{2,1,0:T(8,128)(2,1)} %shard_map.93), calls=%async_computation.3 | async-start | bytes 131072 | tf_op jit(solution)/shard_map/all_to_all | solution.py:397
  71.2 4.0 %collective-permute-start.3 = (bf16[2,80,128]{2,1,0:T(8,128)(2,1)S(1)}, bf16[2,80,128]{2,1,0:T(8,128)(2,1)S(1)}, u32[]{:S(2)}, u32[]{:S(2)}) collective-permute-start(bf16[2,80,128]{2,1,0:T(8,128)(2,1)S(1)} %get-tuple-element.37), channel_id=1, source_target_pairs={{1,2},{3,4},{5,6},{7,8},{9,10},{11,12},{13,14},{15,16},{17,18},{19... | collective-permute-start | bytes 122888 | tf_op jit(solution)/shard_map/ppermute | solution.py:309
  75.2 3.2 %collective-permute-done.3.cross = bf16[2,80,128]{2,1,0:T(8,128)(2,1)S(1)} collective-permute-done((bf16[2,80,128]{2,1,0:T(8,128)(2,1)S(1)}, bf16[2,80,128]{2,1,0:T(8,128)(2,1)S(1)}, u32[]{:S(2)}, u32[]{:S(2)}) %collective-permute-start.3) | collective-permute-done | bytes 40992 | tf_op jit(solution)/shard_map/ppermute | solution.py:309
  78.4 1.5 %shard_map.94 = bf16[3,256,128]{2,1,0:T(8,128)(2,1)} custom-call(s32[1]{0:T(128)} %bitcast.place, bf16[3,80,128]{2,1,0:T(8,128)(2,1)S(1)} %get-tuple-element.32.pred_grad, bf16[2,80,128]{2,1,0:T(8,128)(2,1)S(1)} %collective-permute-done.3.cross, bf16[26,16,128]{2,1,0:T(8,128)(2,1)S(1)} %collective-permute-done.2.got, f32[3,80,384]{2,1,0:T(8,128)S(1)} %shard_map.91.turned, ...), custom_call_target="tpu_custom_call" | custom-call | flops 150000000 | bytes 1500000 | tf_op jit(solution)/shard_map/pallas_call | solution.py:399
  80.0 0.0 all-to-all-done.3.parts
  80.0 0.7 shard_map.95
  (1 shorter events, 0.0 us)
Async XLA Ops:
  1.6 12.4 %collective-permute-start = (bf16[2,256,128]{2,1,0:T(8,128)(2,1)S(1)}, bf16[2,256,128]{2,1,0:T(8,128)(2,1)S(1)}, u32[]{:S(2)}, u32[]{:S(2)}) collective-permute-start(bf16[2,256,128]{2,1,0:T(8,128)(2,1)S(1)} %get-tuple-element.23), channel_id=1, source_target_pairs={{1,2},{3,4},{5,6},{7,8},{9,10},{11,12},{13,14},{15,16},{17,18},{19... | collective-permute-start | bytes 393224 | tf_op jit(solution)/shard_map/ppermute | solution.py:309
  7.7 6.3 %collective-permute-start.1 = (bf16[2,256,128]{2,1,0:T(8,128)(2,1)S(1)}, bf16[2,256,128]{2,1,0:T(8,128)(2,1)S(1)}, u32[]{:S(2)}, u32[]{:S(2)}) collective-permute-start(bf16[2,256,128]{2,1,0:T(8,128)(2,1)S(1)} %get-tuple-element.24), channel_id=1, source_target_pairs={{0,1},{2,3},{4,5},{6,7},{8,9},{10,11},{12,13},{14,15},{16,17},{18,... | collective-permute-start | bytes 393224 | tf_op jit(solution)/shard_map/ppermute | solution.py:309
  11.1 27.1 %copy-start = (bf16[3,72,128]{2,1,0:T(8,128)(2,1)S(1)}, bf16[3,72,128]{2,1,0:T(8,128)(2,1)}, u32[]{:S(2)}) copy-start(bf16[3,72,128]{2,1,0:T(8,128)(2,1)} %target.1) | copy-start | bytes 165892
  11.1 27.0 %copy-start.1 = (f32[96]{0:T(128)S(1)}, f32[96]{0:T(128)}, u32[]{:S(2)}) copy-start(f32[96]{0:T(128)} %constant.12.clone.area) | copy-start | bytes 1156
  39.2 5.9 %collective-permute-start.2 = (bf16[26,16,128]{2,1,0:T(8,128)(2,1)S(1)}, bf16[26,16,128]{2,1,0:T(8,128)(2,1)S(1)}, u32[]{:S(2)}, u32[]{:S(2)}) collective-permute-start(bf16[26,16,128]{2,1,0:T(8,128)(2,1)S(1)} %get-tuple-element.31), channel_id=1, source_target_pairs={{0,1},{2,3},{4,5},{6,7},{8,9},{10,11},{12,13},{14,15},{16,17},{18,... | collective-permute-start | bytes 319496 | tf_op jit(solution)/shard_map/ppermute | solution.py:309
  67.7 12.2 %all-to-all-start.3 = ((bf16[16,16,128]{2,1,0:T(8,128)(2,1)}), bf16[16,16,128]{2,1,0:T(8,128)(2,1)S(1)}, u32[]{:S(2)}, u32[]{:S(2)}) async-start(bf16[16,16,128]{2,1,0:T(8,128)(2,1)} %shard_map.93), calls=%async_computation.3 | async-start | bytes 131072 | tf_op jit(solution)/shard_map/all_to_all | solution.py:397
  71.2 7.2 %collective-permute-start.3 = (bf16[2,80,128]{2,1,0:T(8,128)(2,1)S(1)}, bf16[2,80,128]{2,1,0:T(8,128)(2,1)S(1)}, u32[]{:S(2)}, u32[]{:S(2)}) collective-permute-start(bf16[2,80,128]{2,1,0:T(8,128)(2,1)S(1)} %get-tuple-element.37), channel_id=1, source_target_pairs={{1,2},{3,4},{5,6},{7,8},{9,10},{11,12},{13,14},{15,16},{17,18},{19... | collective-permute-start | bytes 122888 | tf_op jit(solution)/shard_map/ppermute | solution.py:309

commit v10 on v7

--- a/solution.py
+++ b/solution.py
@@ -16,7 +16,6 @@
 BF = jnp.bfloat16
 F32 = jnp.float32
 VMEM = pl.BlockSpec(memory_space=pltpu.VMEM)
-SMEM = pl.BlockSpec(memory_space=pltpu.SMEM)
 
 
 def smooth_slope(differ):
@@ -31,22 +30,26 @@
     return lax.dot_general(a, b, (((1,), (1,)), ((), ())), preferred_element_type=F32)
 
 
-def call(kernel, out, specs, flops, moved, scratch=()):
+def call(kernel, out, specs, flops, moved, scratch=(), home=VMEM):
     many = isinstance(out, (tuple, list))
     return pl.pallas_call(
         kernel,
         out_shape=out,
         in_specs=specs,
-        out_specs=tuple([VMEM] * len(out)) if many else VMEM,
+        out_specs=tuple([home] * len(out)) if many else home,
         scratch_shapes=list(scratch),
         compiler_params=pltpu.CompilerParams(vmem_limit_bytes=32 * 2**20),
         cost_estimate=pl.CostEstimate(flops=flops, bytes_accessed=moved, transcendentals=0),
     )
 
 
-def tap_block(lat_count, lag, place, rows, basis, offsets, source, step, store):
+def odd_band():
+    return (lax.axis_index("lat") & 1) == 1
+
+
+def tap_block(lat_count, lag, band, rows, basis, offsets, source, step, put):
     kernels, lon = basis.shape[1], lag.shape[0]
-    cycle = place[0] * rows + source
+    cycle = band * rows + source
     inside = jnp.logical_and(cycle >= 0, cycle < lat_count)
     cycle = jnp.clip(cycle, 0, lat_count - 1)
     one, two = SIDE * step, SIDE * step + 1
@@ -58,12 +61,12 @@
         weight_two = jnp.where(inside, basis[two, k, cycle], 0.0)
         weight_two = weight_two + jnp.where(off_one == off_two, weight_one, 0.0)
         value = jnp.where(mask_two, weight_two, jnp.where(mask_one, weight_one, 0.0))
-        store[:, k * lon : (k + 1) * lon] = value.astype(BF)
-
-
-def edge_taps(rows):
+        put(k, value.astype(BF))
+
+
+def edge_taps(rows, row):
     outside = list(range(-HALO, 0)) + list(range(rows, rows + HALO))
-    return [(at, step) for at in outside for step in range(REACH) if 0 <= at + step - HALO < rows]
+    return [(at, row - at + HALO) for at in outside if 0 <= row - at + HALO < REACH]
 
 
 def lags(lon):
@@ -76,36 +79,59 @@
 
 
 def prepare(
-    rows, lat_count, place, basis, offsets, filters, dec_in, field, ahead, edge, w_fwd, w_bwd, near, held, dec_t, sems
+    rows, lat_count, basis_in, offsets_in, filters, dec_in, field,
+    ahead, edge, w_fwd, w_bwd, near, held, dec_t, basis, offsets, sems,
 ):
-    moves = ((filters, held), (dec_in, dec_t), (field, near))
+    moves = ((offsets_in, offsets), (basis_in, basis), (dec_in, dec_t), (filters, held), (field, near))
     moves = [pltpu.make_async_copy(source, target, sems.at[n]) for n, (source, target) in enumerate(moves)]
     for move in moves:
         move.start()
     lon = ahead.shape[1] // REACH
     lag = lags(lon)
+    band = lax.axis_index("lat")
+
+    def block(source, step, put):
+        tap_block(lat_count, lag, band, rows, basis, offsets, source, step, put)
+
+    def ahead_put(row, step):
+        def put(k, value):
+            ahead[row, step * lon : (step + 1) * lon, k * lon : (k + 1) * lon] = value
+
+        return put
+
+    def edge_put(row, slot):
+        def put(k, value):
+            edge[row, k * lon : (k + 1) * lon, slot * lon : (slot + 1) * lon] = value
+
+        return put
+
+    for move in moves[:2]:
+        move.wait()
     for row in range(rows):
         for step in range(REACH):
-            tap_block(lat_count, lag, place, rows, basis, offsets, row, step, ahead.at[row, step * lon : (step + 1) * lon])
-    for n, (at, step) in enumerate(edge_taps(rows)):
-        tap_block(lat_count, lag, place, rows, basis, offsets, at, step, edge.at[n])
+            block(row, step, ahead_put(row, step))
+        for slot, (at, step) in enumerate(edge_taps(rows, row)):
+            block(at, step, edge_put(row, slot))
     kernels, chan = held.shape[:2]
-    for move in moves:
+    padded = w_fwd.shape[0]
+    for move in moves[2:]:
         move.wait()
-    dec = padded_rows(dec_t, w_fwd.shape[0])
+    dec = padded_rows(dec_t, padded)
+
+    square = (chan, chan)
+    unit = lax.broadcasted_iota(jnp.int32, square, 0) == lax.broadcasted_iota(jnp.int32, square, 1)
+    columns = [dot_nt(jnp.where(unit, 1.0, 0.0).astype(BF), dec)]
     w_fwd[:, :chan] = dec
     for k in range(kernels):
         w_fwd[:, (k + 1) * chan : (k + 2) * chan] = dot_nt(dec, held[k]).astype(BF)
-        w_bwd[k + 1] = dot_nt(held[k], dec).astype(BF)
-    square = (chan, chan)
-    unit = lax.broadcasted_iota(jnp.int32, square, 0) == lax.broadcasted_iota(jnp.int32, square, 1)
-    w_bwd[0] = dot_nt(jnp.where(unit, 1.0, 0.0).astype(BF), dec).astype(BF)
-
-
-def forward(rows, kernels, place, field, cross, chip, ahead, w_fwd, packed, predicted, mixed):
+        columns.append(dot_nt(held[k], dec))
+    w_bwd[...] = jnp.concatenate(columns, axis=1).astype(BF)
+
+
+def forward(rows, kernels, field, cross, chip, ahead, w_fwd, packed, predicted, mixed):
     lon = field.shape[2]
     chan = field.shape[1]
-    low, high = sides((place[0] & 1) == 1, cross, chip)
+    low, high = sides(odd_band(), cross, chip)
     wide = low + [field[i] for i in range(rows)] + high
     per = packed.shape[1]
     padded = predicted.shape[1]
@@ -141,7 +167,7 @@
         sums[m] = jnp.concatenate([totals[m] for totals in pieces], axis=0).astype(BF)
 
 
-def gradient(rows, kernels, members, place, area, sums, predicted, target, mixed, pred_grad, cross, chip, partial):
+def gradient(rows, kernels, members, area, sums, predicted, target, mixed, pred_grad, cross, chip, partial):
     variables = target.shape[1]
     padded = predicted.shape[1]
     per = sums.shape[1]
@@ -149,11 +175,12 @@
     lon = predicted.shape[2]
     chan = mixed.shape[1] // kernels
     grads, edges = [], []
-    odd = (place[0] & 1) == 1
+    odd = odd_band()
+    band = lax.axis_index("lat")
     for i in range(rows):
         pair_sum = jnp.concatenate([sums[i * pieces + q].astype(F32) for q in range(pieces)], axis=0)
         aim = jnp.concatenate([target[i].astype(F32), jnp.zeros((padded - variables, lon), F32)], axis=0)
-        grad = area[place[0] * rows + i] * (smooth_slope(predicted[i] - aim) - pair_sum * (1.0 / (members - 1)))
+        grad = area[pl.ds(band * rows + i, 1), :] * (smooth_slope(predicted[i] - aim) - pair_sum * (1.0 / (members - 1)))
         grad = grad.astype(BF)
         pred_grad[i] = grad
         edges.append(grad)
@@ -178,7 +205,7 @@
         partial[owner] = jnp.concatenate([upper[mine], lower[mine]], axis=0).astype(BF)
 
 
-def band_sum(factor, variables, parts, w_bwd, spread):
+def band_sum(factor, variables, padded, parts, w_bwd, spread):
     owners, height, lon = parts.shape
     total = parts[0].astype(F32)
     for owner in range(1, owners):
@@ -195,8 +222,7 @@
     total = jnp.concatenate([total, third, jnp.zeros((lon - height - own, lon), F32)], axis=0)
     upper = total.astype(BF)
     lower = (total - upper.astype(F32)).astype(BF)
-    dec = w_bwd[0]
-    padded = dec.shape[1]
+    dec = w_bwd[:, :padded]
     result = dot_nt(dec, upper[:, :padded]) + dot_nt(dec, lower[:, :padded])
     per = spread.shape[1]
     for member in range(spread.shape[0]):
@@ -225,28 +251,28 @@
                 piece = found[:, row * lon : (row + 1) * lon]
                 sums[row] = piece if sums[row] is None else sums[row] + piece
         for row in range(rows):
-            turned[k, :, row * lon : (row + 1) * lon] = sums[row]
-
-
-def adjoint_rest(rows, kernels, place, pred_grad, cross, chip, turned, edge, w_bwd, result):
+            turned[row, :, k * lon : (k + 1) * lon] = sums[row]
+
+
+def adjoint_rest(rows, kernels, pred_grad, cross, chip, turned, edge, w_bwd, result, buffer, sems):
     lon = pred_grad.shape[2]
-    low, high = sides((place[0] & 1) == 1, cross, chip)
+    low, high = sides(odd_band(), cross, chip)
     outer = dict(enumerate(low, -HALO)) | dict(enumerate(high, rows))
-    total = dot_nn(w_bwd[0], jnp.concatenate([pred_grad[i] for i in range(rows)], axis=1))
-    for k in range(kernels):
-        sums = [turned[k, :, row * lon : (row + 1) * lon] for row in range(rows)]
-        for n, (at, step) in enumerate(edge_taps(rows)):
-            row = at + step - HALO
-            sums[row] = sums[row] + dot_nt(outer[at], edge[n, :, k * lon : (k + 1) * lon])
-        taps = jnp.concatenate(sums, axis=1).astype(BF)
-        total = total + dot_nn(w_bwd[k + 1], taps)
-    for i in range(rows):
-        result[i] = total[:, i * lon : (i + 1) * lon].astype(BF)
-
-
-def cut(place, field, cross, chip, sems):
+    moves = []
+    for row in range(rows):
+        sources = jnp.concatenate([outer[at] for at, _ in edge_taps(rows, row)], axis=1)
+        taps = (turned[row] + dot_nt(sources, edge[row])).astype(BF)
+        stack = [pred_grad[row]] + [taps[:, k * lon : (k + 1) * lon] for k in range(kernels)]
+        buffer[row] = dot_nn(w_bwd[...], jnp.concatenate(stack, axis=0)).astype(BF)
+        moves.append(pltpu.make_async_copy(buffer.at[row], result.at[row], sems.at[row]))
+        moves[-1].start()
+    for move in moves:
+        move.wait()
+
+
+def cut(field, cross, chip, sems):
     rows = field.shape[0]
-    odd = (place[0] & 1)
+    odd = lax.axis_index("lat") & 1
     far = (rows - HALO) * odd
     moves = [
         pltpu.make_async_copy(field.at[pl.ds(far, HALO)], cross, sems.at[0]),
@@ -281,9 +307,8 @@
     members, bands = lax.axis_size("ens"), lax.axis_size("lat")
     per = 16
     padded = -(-variables // per) * per
-    band = lax.axis_index("lat").astype(jnp.int32)
-    place = band.reshape(1)
-    area = jnp.asarray(np.cos(np.pi * (np.arange(lat_count) + 0.5) / lat_count - np.pi / 2), F32)
+    area = np.cos(np.pi * (np.arange(lat_count) + 0.5) / lat_count - np.pi / 2)
+    area = jnp.asarray(np.broadcast_to(area[:, None], (lat_count, lon)), F32)
     dec_t = decoder.T
     basis = cycle_basis.transpose(2, 1, 0)
     offsets = cycle_offsets.T
@@ -292,22 +317,28 @@
     hbm = pl.BlockSpec(memory_space=pltpu.HBM)
     edge = jax.ShapeDtypeStruct((HALO, chan, lon), BF)
     pair = pltpu.SemaphoreType.DMA((2,))
-    cross, chip = call(cut, (edge, edge), [SMEM, hbm], 0, 500_000, [pair])(place, stay(field))
+    cross, chip = call(cut, (edge, edge), [hbm], 0, 500_000, [pair])(stay(field))
     cross, chip = exchange(cross, chip, "lat")
     ahead, tap_edge, w_fwd, w_bwd, near = call(
         functools.partial(prepare, rows, lat_count),
         (
             jax.ShapeDtypeStruct((rows, REACH * lon, kernels * lon), BF),
-            jax.ShapeDtypeStruct((len(edge_taps(rows)), lon, kernels * lon), BF),
+            jax.ShapeDtypeStruct((rows, kernels * lon, (REACH - rows) * lon), BF),
             jax.ShapeDtypeStruct((padded, (kernels + 1) * chan), BF),
-            jax.ShapeDtypeStruct((kernels + 1, chan, padded), BF),
+            jax.ShapeDtypeStruct((chan, (kernels + 1) * padded), BF),
             jax.ShapeDtypeStruct(field.shape, BF),
         ),
-        [SMEM, SMEM, SMEM, hbm, hbm, hbm],
+        [hbm] * 5,
         30_000_000,
         2_000_000,
-        [pltpu.VMEM(filters.shape, BF), pltpu.VMEM(dec_t.shape, BF), pltpu.SemaphoreType.DMA((3,))],
-    )(place, stay(basis), stay(offsets), stay(filters), stay(dec_t), stay(field))
+        [
+            pltpu.VMEM(filters.shape, BF),
+            pltpu.VMEM(dec_t.shape, BF),
+            pltpu.SMEM(basis.shape, F32),
+            pltpu.SMEM(offsets.shape, jnp.int32),
+            pltpu.SemaphoreType.DMA((5,)),
+        ],
+    )(stay(basis), stay(offsets), stay(filters), stay(dec_t), stay(field))
     packed, predicted, mixed = call(
         functools.partial(forward, rows, kernels),
         (
@@ -315,10 +346,10 @@
             jax.ShapeDtypeStruct((rows, padded, lon), F32),
             jax.ShapeDtypeStruct((rows, kernels * chan, lon), BF),
         ),
-        [SMEM] + [VMEM] * 5,
+        [VMEM] * 5,
         450_000_000,
         3_000_000,
-    )(place, near, cross, chip, ahead, w_fwd)
+    )(near, cross, chip, ahead, w_fwd)
     visitors = lax.all_to_all(packed, "ens", 0, 0, tiled=True)
     sums = call(pairs, jax.ShapeDtypeStruct((members, per, lon), BF), [VMEM], 2_000_000, 200_000)(visitors)
     sums = lax.all_to_all(sums, "ens", 0, 0, tiled=True)
@@ -332,15 +363,15 @@
             edge,
             jax.ShapeDtypeStruct((bands, 2 * own, lon), BF),
         ),
-        [SMEM, SMEM] + [VMEM] * 4,
+        [VMEM] * 5,
         80_000_000,
         1_200_000,
-    )(place, area, sums, predicted, target_fields, mixed)
+    )(area, sums, predicted, target_fields, mixed)
     parts = lax.all_to_all(partial, "lat", 0, 0, tiled=True)
     cross, chip = exchange(cross, chip, "lat")
     turned = call(
         functools.partial(adjoint_own, rows, kernels),
-        jax.ShapeDtypeStruct((kernels, padded, rows * lon), F32),
+        jax.ShapeDtypeStruct((rows, padded, kernels * lon), F32),
         [VMEM] * 2,
         80_000_000,
         1_500_000,
@@ -348,15 +379,17 @@
     latent_grad = call(
         functools.partial(adjoint_rest, rows, kernels),
         jax.ShapeDtypeStruct((rows, chan, lon), BF),
-        [SMEM] + [VMEM] * 6,
+        [VMEM] * 6,
         150_000_000,
         1_500_000,
-    )(place, pred_grad, cross, chip, turned, tap_edge, w_bwd)
+        [pltpu.VMEM((rows, chan, lon), BF), pltpu.SemaphoreType.DMA((rows,))],
+        hbm,
+    )(pred_grad, cross, chip, turned, tap_edge, w_bwd)
     parts, latent_grad = lax.optimization_barrier((parts, latent_grad))
     factor = 1.0 / math.sqrt(members * lat_count * lon)
     width = chan // members
     spread = call(
-        functools.partial(band_sum, factor, variables),
+        functools.partial(band_sum, factor, variables, padded),
         jax.ShapeDtypeStruct((members, width, lon), BF),
         [VMEM] * 2,
         20_000_000,

time: 77.9 us -> 77.3 us (level)
  Pallas kernels: 10 us -> 8.8 us
where the time goes in v10:
time: 77.3 us; the launch traced here: 76.9 us
  starting transfers between devices  33 us (43%)
  blocking collectives  32.6 us (42%)
  Pallas kernels  8.8 us (11%)
  waiting for transfers between devices  1.74 us (2%)
    all_to_all x1, starting transfers between devices, body(): parts = lax.all_to_all(partial, 'lat', 0, 0, tiled=True)  16.6 us
    all_to_all x1, blocking collectives, body(): visitors = lax.all_to_all(packed, 'ens', 0, 0, tiled=True)  12.6 us
    ppermute x2, starting transfers between devices, exchange(): cross = lax.ppermute(cross, axis, far + [(b, a) for a, b in far])  11.1 us
    all_to_all x1, blocking collectives, body(): spread = lax.all_to_all(spread, 'ens', 0, 0, tiled=True)  10 us
    all_to_all x1, blocking collectives, body(): sums = lax.all_to_all(sums, 'ens', 0, 0, tiled=True)  9.95 us
    ppermute x2, starting transfers between devices, exchange(): chip = lax.ppermute(chip, axis, near + [(b, a) for a, b in near])  5.33 us
    pallas_call x1, Pallas kernels, body(): call(functools.partial(prepare, rows, lat_count), (jax.ShapeDtypeStruct((...  2.23 us
  transfers between devices with their start and end apart: 5, of which 2 were waited for; matrix products, arithmetic and copies ran while one was open for 0% of the time, Pallas kernels for 6%

profile of v10, /device:TPU:1, one launch (start us, length us, event | category | flops | bytes accessed | tf_op | source)
XLA Modules:
  0.0 76.9 jit_solution(5735381250719899932)
XLA Ops:
  0.6 1.0 %shard_map.87 = (bf16[2,256,128]{2,1,0:T(8,128)(2,1)S(1)}, bf16[2,256,128]{2,1,0:T(8,128)(2,1)S(1)}) custom-call(bf16[3,256,128]{2,1,0:T(8,128)(2,1)} %bitcast.6), custom_call_target="tpu_custom_call" | custom-call | bytes 500000 | tf_op jit(solution)/shard_map/pallas_call | solution.py:320
  1.6 6.0 %collective-permute-start = (bf16[2,256,128]{2,1,0:T(8,128)(2,1)S(1)}, bf16[2,256,128]{2,1,0:T(8,128)(2,1)S(1)}, u32[]{:S(2)}, u32[]{:S(2)}) collective-permute-start(bf16[2,256,128]{2,1,0:T(8,128)(2,1)S(1)} %get-tuple-element.19), channel_id=1, source_target_pairs={{1,2},{3,4},{5,6},{7,8},{9,10},{11,12},{13,14},{15,16},{17,18},{19... | collective-permute-start | bytes 393224 | tf_op jit(solution)/shard_map/ppermute | solution.py:297
  7.7 3.4 %collective-permute-start.1 = (bf16[2,256,128]{2,1,0:T(8,128)(2,1)S(1)}, bf16[2,256,128]{2,1,0:T(8,128)(2,1)S(1)}, u32[]{:S(2)}, u32[]{:S(2)}) collective-permute-start(bf16[2,256,128]{2,1,0:T(8,128)(2,1)S(1)} %get-tuple-element.20), channel_id=1, source_target_pairs={{0,1},{2,3},{4,5},{6,7},{8,9},{10,11},{12,13},{14,15},{16,17},{18,... | collective-permute-start | bytes 393224 | tf_op jit(solution)/shard_map/ppermute | solution.py:298
  11.1 0.0 copy-start
  11.1 0.0 copy-start.1
  11.1 2.2 %shard_map.86 = (bf16[3,640,384]{2,1,0:T(8,128)(2,1)S(1)}, bf16[3,384,256]{2,1,0:T(8,128)(2,1)S(1)}, bf16[80,1024]{1,0:T(8,128)(2,1)S(1)}, bf16[256,320]{1,0:T(8,128)(2,1)S(1)}, bf16[3,256,128]{2,1,0:T(8,128)(2,1)S(1)}) custom-call(f32[10,3,96]{2,1,0:T(4,128)} %bitcast.10, s32[10,96]{1,0:T(8,128)} %bitcast.12, bf16[3,256,256]{2,1,0:T(8,128)(2,1)} %filters.1, ...), custom_call_target="tpu_custom_call" | custom-call | flops 30000000 | bytes 2000000 | tf_op jit(solution)/shard_map/pallas_call | solution.py:322
  13.4 0.0 collective-permute-done.cross
  13.4 0.0 collective-permute-done.1.chip
  13.4 1.3 %shard_map.88 = (bf16[16,16,128]{2,1,0:T(8,128)(2,1)S(1)}, f32[3,80,128]{2,1,0:T(8,128)S(1)}, bf16[3,768,128]{2,1,0:T(8,128)(2,1)S(1)}) custom-call(bf16[3,256,128]{2,1,0:T(8,128)(2,1)S(1)} %get-tuple-element.18.field, bf16[2,256,128]{2,1,0:T(8,128)(2,1)S(1)} %collective-permute-done.cross, bf16[2,256,128]{2,1,0:T(8,128)(2,1)S(1)} %collective-permute-done.1.chip, ...), custom_call_target="tpu_custom_call" | custom-call | flops 450000000 | bytes 3000000 | tf_op jit(solution)/shard_map/pallas_call | solution.py:342
  14.7 12.6 %all_to_all.20.visitors = bf16[16,16,128]{2,1,0:T(8,128)(2,1)S(1)} all-to-all(bf16[16,16,128]{2,1,0:T(8,128)(2,1)S(1)} %get-tuple-element.23), channel_id=1, replica_groups=mesh['ens'=16,'lat'=32] {'ens'}, dimensions={0} | all-to-all | bytes 131072 | tf_op jit(solution)/shard_map/all_to_all | solution.py:353
  27.3 0.2 shard_map.89
  27.5 10.0 %all_to_all.21.sums = bf16[16,16,128]{2,1,0:T(8,128)(2,1)S(1)} all-to-all(bf16[16,16,128]{2,1,0:T(8,128)(2,1)S(1)} %shard_map.89), channel_id=1, replica_groups=mesh['ens'=16,'lat'=32] {'ens'}, dimensions={0} | all-to-all | bytes 131072 | tf_op jit(solution)/shard_map/all_to_all | solution.py:355
  37.5 0.0 copy-done
  37.5 0.0 copy-done.1
  37.5 1.0 %shard_map.90 = (bf16[3,80,128]{2,1,0:T(8,128)(2,1)S(1)}, bf16[2,80,128]{2,1,0:T(8,128)(2,1)S(1)}, bf16[2,80,128]{2,1,0:T(8,128)(2,1)S(1)}, bf16[32,16,128]{2,1,0:T(8,128)(2,1)}) custom-call(f32[96,128]{1,0:T(8,128)S(1)} %copy-done.1, bf16[16,16,128]{2,1,0:T(8,128)(2,1)S(1)} %all_to_all.21.sums, f32[3,80,128]{2,1,0:T(8,128)S(1)} %get-tuple-element.24.predicted, ...), custom_call_target="tpu_custom_call" | custom-call | flops 80000000 | bytes 1200000 | tf_op jit(solution)/shard_map/pallas_call | solution.py:358
  38.5 16.6 %all-to-all-start.2 = ((bf16[32,16,128]{2,1,0:T(8,128)(2,1)}), bf16[32,16,128]{2,1,0:T(8,128)(2,1)S(1)}, u32[]{:S(2)}, u32[]{:S(2)}) async-start(bf16[32,16,128]{2,1,0:T(8,128)(2,1)} %get-tuple-element.26), calls=%async_computation.2 | async-start | bytes 262144 | tf_op jit(solution)/shard_map/all_to_all | solution.py:370
  55.1 5.0 %collective-permute-start.2 = (bf16[2,80,128]{2,1,0:T(8,128)(2,1)S(1)}, bf16[2,80,128]{2,1,0:T(8,128)(2,1)S(1)}, u32[]{:S(2)}, u32[]{:S(2)}) collective-permute-start(bf16[2,80,128]{2,1,0:T(8,128)(2,1)S(1)} %get-tuple-element.28), channel_id=1, source_target_pairs={{1,2},{3,4},{5,6},{7,8},{9,10},{11,12},{13,14},{15,16},{17,18},{19... | collective-permute-start | bytes 122888 | tf_op jit(solution)/shard_map/ppermute | solution.py:297
  60.2 1.9 %collective-permute-start.3 = (bf16[2,80,128]{2,1,0:T(8,128)(2,1)S(1)}, bf16[2,80,128]{2,1,0:T(8,128)(2,1)S(1)}, u32[]{:S(2)}, u32[]{:S(2)}) collective-permute-start(bf16[2,80,128]{2,1,0:T(8,128)(2,1)S(1)} %get-tuple-element.29), channel_id=1, source_target_pairs={{0,1},{2,3},{4,5},{6,7},{8,9},{10,11},{12,13},{14,15},{16,17},{18,... | collective-permute-start | bytes 122888 | tf_op jit(solution)/shard_map/ppermute | solution.py:298
  62.1 0.5 shard_map.91.turned
  62.6 0.0 collective-permute-done.2.cross
  62.6 0.7 collective-permute-done.3.chip
  63.3 1.5 %shard_map.92 = bf16[3,256,128]{2,1,0:T(8,128)(2,1)} custom-call(bf16[3,80,128]{2,1,0:T(8,128)(2,1)S(1)} %get-tuple-element.27.pred_grad, bf16[2,80,128]{2,1,0:T(8,128)(2,1)S(1)} %collective-permute-done.2.cross, bf16[2,80,128]{2,1,0:T(8,128)(2,1)S(1)} %collective-permute-done.3.chip, f32[3,80,384]{2,1,0:T(8,128)S(1)} %shard_map.91.turned, ...), custom_call_target="tpu_custom_call" | custom-call | flops 150000000 | bytes 1500000 | tf_op jit(solution)/shard_map/pallas_call | solution.py:379
  64.8 1.1 %all-to-all-done.2.parts = bf16[32,16,128]{2,1,0:T(8,128)(2,1)S(1)} async-done(((bf16[32,16,128]{2,1,0:T(8,128)(2,1)}), bf16[32,16,128]{2,1,0:T(8,128)(2,1)S(1)}, u32[]{:S(2)}, u32[]{:S(2)}) %all-to-all-start.2) | async-done | bytes 131104 | tf_op jit(solution)/shard_map/all_to_all | solution.py:370
  65.9 0.3 shard_map.93
  66.2 10.0 %all_to_all.22.parts = bf16[16,16,128]{2,1,0:T(8,128)(2,1)S(1)} all-to-all(bf16[16,16,128]{2,1,0:T(8,128)(2,1)S(1)} %shard_map.93), channel_id=1, replica_groups=mesh['ens'=16,'lat'=32] {'ens'}, dimensions={0} | all-to-all | bytes 131072 | tf_op jit(solution)/shard_map/all_to_all | solution.py:398
  76.2 0.7 shard_map.94
Async XLA Ops:
  1.6 11.7 %collective-permute-start = (bf16[2,256,128]{2,1,0:T(8,128)(2,1)S(1)}, bf16[2,256,128]{2,1,0:T(8,128)(2,1)S(1)}, u32[]{:S(2)}, u32[]{:S(2)}) collective-permute-start(bf16[2,256,128]{2,1,0:T(8,128)(2,1)S(1)} %get-tuple-element.19), channel_id=1, source_target_pairs={{1,2},{3,4},{5,6},{7,8},{9,10},{11,12},{13,14},{15,16},{17,18},{19... | collective-permute-start | bytes 393224 | tf_op jit(solution)/shard_map/ppermute | solution.py:297
  7.7 5.7 %collective-permute-start.1 = (bf16[2,256,128]{2,1,0:T(8,128)(2,1)S(1)}, bf16[2,256,128]{2,1,0:T(8,128)(2,1)S(1)}, u32[]{:S(2)}, u32[]{:S(2)}) collective-permute-start(bf16[2,256,128]{2,1,0:T(8,128)(2,1)S(1)} %get-tuple-element.20), channel_id=1, source_target_pairs={{0,1},{2,3},{4,5},{6,7},{8,9},{10,11},{12,13},{14,15},{16,17},{18,... | collective-permute-start | bytes 393224 | tf_op jit(solution)/shard_map/ppermute | solution.py:298
  11.1 26.4 %copy-start = (bf16[3,72,128]{2,1,0:T(8,128)(2,1)S(1)}, bf16[3,72,128]{2,1,0:T(8,128)(2,1)}, u32[]{:S(2)}) copy-start(bf16[3,72,128]{2,1,0:T(8,128)(2,1)} %target.1) | copy-start | bytes 165892
  11.1 26.4 %copy-start.1 = (f32[96,128]{1,0:T(8,128)S(1)}, f32[96,128]{1,0:T(8,128)}, u32[]{:S(2)}) copy-start(f32[96,128]{1,0:T(8,128)} %constant.2.clone.area) | copy-start | bytes 147460
  38.5 27.3 %all-to-all-start.2 = ((bf16[32,16,128]{2,1,0:T(8,128)(2,1)}), bf16[32,16,128]{2,1,0:T(8,128)(2,1)S(1)}, u32[]{:S(2)}, u32[]{:S(2)}) async-start(bf16[32,16,128]{2,1,0:T(8,128)(2,1)} %get-tuple-element.26), calls=%async_computation.2 | async-start | bytes 262144 | tf_op jit(solution)/shard_map/all_to_all | solution.py:370
  55.1 7.5 %collective-permute-start.2 = (bf16[2,80,128]{2,1,0:T(8,128)(2,1)S(1)}, bf16[2,80,128]{2,1,0:T(8,128)(2,1)S(1)}, u32[]{:S(2)}, u32[]{:S(2)}) collective-permute-start(bf16[2,80,128]{2,1,0:T(8,128)(2,1)S(1)} %get-tuple-element.28), channel_id=1, source_target_pairs={{1,2},{3,4},{5,6},{7,8},{9,10},{11,12},{13,14},{15,16},{17,18},{19... | collective-permute-start | bytes 122888 | tf_op jit(solution)/shard_map/ppermute | solution.py:297
  60.2 3.1 %collective-permute-start.3 = (bf16[2,80,128]{2,1,0:T(8,128)(2,1)S(1)}, bf16[2,80,128]{2,1,0:T(8,128)(2,1)S(1)}, u32[]{:S(2)}, u32[]{:S(2)}) collective-permute-start(bf16[2,80,128]{2,1,0:T(8,128)(2,1)S(1)} %get-tuple-element.29), channel_id=1, source_target_pairs={{0,1},{2,3},{4,5},{6,7},{8,9},{10,11},{12,13},{14,15},{16,17},{18,... | collective-permute-start | bytes 122888 | tf_op jit(solution)/shard_map/ppermute | solution.py:298

commit v11 on v10

--- a/solution.py
+++ b/solution.py
@@ -229,16 +229,6 @@
         spread[member] = result[member * per : (member + 1) * per].astype(BF)
 
 
-def member_sum(parts, owned):
-    kernels, own, width = owned.shape
-    total = parts[0].astype(F32)
-    for member in range(1, parts.shape[0]):
-        total = total + parts[member].astype(F32)
-    turned = total.T
-    for k in range(kernels):
-        owned[k] = turned[k * own : (k + 1) * own, :width]
-
-
 def adjoint_own(rows, kernels, pred_grad, ahead, turned):
     lon = pred_grad.shape[2]
     for k in range(kernels):
@@ -254,11 +244,19 @@
             turned[row, :, k * lon : (k + 1) * lon] = sums[row]
 
 
-def adjoint_rest(rows, kernels, pred_grad, cross, chip, turned, edge, w_bwd, result, buffer, sems):
+def finish(rows, kernels, pred_grad, cross, chip, turned, edge, w_bwd, parts, result, owned, buffer, small, sems):
+    own, width = owned.shape[1:]
+    total = parts[0].astype(F32)
+    for member in range(1, parts.shape[0]):
+        total = total + parts[member].astype(F32)
+    turned_sum = total.T
+    for k in range(kernels):
+        small[k] = turned_sum[k * own : (k + 1) * own, :width]
+    moves = [pltpu.make_async_copy(small, owned, sems.at[rows])]
+    moves[0].start()
     lon = pred_grad.shape[2]
     low, high = sides(odd_band(), cross, chip)
     outer = dict(enumerate(low, -HALO)) | dict(enumerate(high, rows))
-    moves = []
     for row in range(rows):
         sources = jnp.concatenate([outer[at] for at, _ in edge_taps(rows, row)], axis=1)
         taps = (turned[row] + dot_nt(sources, edge[row])).astype(BF)
@@ -376,16 +374,7 @@
         80_000_000,
         1_500_000,
     )(pred_grad, ahead)
-    latent_grad = call(
-        functools.partial(adjoint_rest, rows, kernels),
-        jax.ShapeDtypeStruct((rows, chan, lon), BF),
-        [VMEM] * 6,
-        150_000_000,
-        1_500_000,
-        [pltpu.VMEM((rows, chan, lon), BF), pltpu.SemaphoreType.DMA((rows,))],
-        hbm,
-    )(pred_grad, cross, chip, turned, tap_edge, w_bwd)
-    parts, latent_grad = lax.optimization_barrier((parts, latent_grad))
+    parts, turned, cross, chip = lax.optimization_barrier((parts, turned, cross, chip))
     factor = 1.0 / math.sqrt(members * lat_count * lon)
     width = chan // members
     spread = call(
@@ -396,9 +385,19 @@
         400_000,
     )(parts, w_bwd)
     spread = lax.all_to_all(spread, "ens", 0, 0, tiled=True)
-    owned = call(
-        member_sum, jax.ShapeDtypeStruct((kernels, own, width), F32), [VMEM], 100_000, 150_000
-    )(spread)
+    latent_grad, owned = call(
+        functools.partial(finish, rows, kernels),
+        (jax.ShapeDtypeStruct((rows, chan, lon), BF), jax.ShapeDtypeStruct((kernels, own, width), F32)),
+        [VMEM] * 7,
+        150_000_000,
+        1_500_000,
+        [
+            pltpu.VMEM((rows, chan, lon), BF),
+            pltpu.VMEM((kernels, own, width), F32),
+            pltpu.SemaphoreType.DMA((rows + 1,)),
+        ],
+        hbm,
+    )(pred_grad, cross, chip, turned, tap_edge, w_bwd, spread)
     return latent_grad[None], owned.transpose(1, 0, 2)
 
 

time: 77.3 us -> 78.1 us (1.010)
  waiting for transfers between devices: 1.74 us -> 3.26 us
    all_to_all x1, waiting for transfers between devices: 1.08 us -> 2.6 us  [body(): parts = lax.all_to_all(partial, 'lat', 0, 0, tiled=True)]
    pallas_call x2 -> x1, Pallas kernels: 2.2 us -> 1.53 us  [body(): call(functools.partial(finish, rows, kernels), (jax.ShapeDtypeStruct((row...]
  transfers between devices with their start and end apart: 5 -> 5, of which waited for: 2 -> 2; matrix products, arithmetic and copies ran while one was open for 0% -> 0% of each run, Pallas kernels for 6% -> 4%
where the time goes in v11:
time: 78.1 us; the launch traced here: 77.7 us
  starting transfers between devices  33 us (42%)
  blocking collectives  32.6 us (42%)
  Pallas kernels  8.15 us (10%)
  waiting for transfers between devices  3.26 us (4%)
    all_to_all x1, starting transfers between devices, body(): parts = lax.all_to_all(partial, 'lat', 0, 0, tiled=True)  16.6 us
    all_to_all x1, blocking collectives, body(): visitors = lax.all_to_all(packed, 'ens', 0, 0, tiled=True)  12.6 us
    ppermute x2, starting transfers between devices, exchange(): cross = lax.ppermute(cross, axis, far + [(b, a) for a, b in far])  11.1 us
    all_to_all x1, blocking collectives, body(): spread = lax.all_to_all(spread, 'ens', 0, 0, tiled=True)  10 us
    all_to_all x1, blocking collectives, body(): sums = lax.all_to_all(sums, 'ens', 0, 0, tiled=True)  9.95 us
    ppermute x2, starting transfers between devices, exchange(): chip = lax.ppermute(chip, axis, near + [(b, a) for a, b in near])  5.33 us
    all_to_all x1, waiting for transfers between devices, body(): parts = lax.all_to_all(partial, 'lat', 0, 0, tiled=True)  2.6 us
    pallas_call x1, Pallas kernels, body(): call(functools.partial(prepare, rows, lat_count), (jax.ShapeDtypeStruct((...  2.23 us
  transfers between devices with their start and end apart: 5, of which 2 were waited for; matrix products, arithmetic and copies ran while one was open for 0% of the time, Pallas kernels for 4%

profile of v11, /device:TPU:1, one launch (start us, length us, event | category | flops | bytes accessed | tf_op | source)
XLA Modules:
  0.0 77.7 jit_solution(707694088211517443)
XLA Ops:
  0.6 1.0 %shard_map.87 = (bf16[2,256,128]{2,1,0:T(8,128)(2,1)S(1)}, bf16[2,256,128]{2,1,0:T(8,128)(2,1)S(1)}) custom-call(bf16[3,256,128]{2,1,0:T(8,128)(2,1)} %bitcast.6), custom_call_target="tpu_custom_call" | custom-call | bytes 500000 | tf_op jit(solution)/shard_map/pallas_call | solution.py:318
  1.6 6.0 %collective-permute-start = (bf16[2,256,128]{2,1,0:T(8,128)(2,1)S(1)}, bf16[2,256,128]{2,1,0:T(8,128)(2,1)S(1)}, u32[]{:S(2)}, u32[]{:S(2)}) collective-permute-start(bf16[2,256,128]{2,1,0:T(8,128)(2,1)S(1)} %get-tuple-element.23), channel_id=1, source_target_pairs={{1,2},{3,4},{5,6},{7,8},{9,10},{11,12},{13,14},{15,16},{17,18},{19... | collective-permute-start | bytes 393224 | tf_op jit(solution)/shard_map/ppermute | solution.py:295
  7.7 3.4 %collective-permute-start.1 = (bf16[2,256,128]{2,1,0:T(8,128)(2,1)S(1)}, bf16[2,256,128]{2,1,0:T(8,128)(2,1)S(1)}, u32[]{:S(2)}, u32[]{:S(2)}) collective-permute-start(bf16[2,256,128]{2,1,0:T(8,128)(2,1)S(1)} %get-tuple-element.24), channel_id=1, source_target_pairs={{0,1},{2,3},{4,5},{6,7},{8,9},{10,11},{12,13},{14,15},{16,17},{18,... | collective-permute-start | bytes 393224 | tf_op jit(solution)/shard_map/ppermute | solution.py:296
  11.1 0.0 copy-start
  11.1 0.0 copy-start.1
  11.1 2.2 %shard_map.86 = (bf16[3,640,384]{2,1,0:T(8,128)(2,1)S(1)}, bf16[3,384,256]{2,1,0:T(8,128)(2,1)S(1)}, bf16[80,1024]{1,0:T(8,128)(2,1)S(1)}, bf16[256,320]{1,0:T(8,128)(2,1)S(1)}, bf16[3,256,128]{2,1,0:T(8,128)(2,1)S(1)}) custom-call(f32[10,3,96]{2,1,0:T(4,128)} %bitcast.9, s32[10,96]{1,0:T(8,128)} %bitcast.10, bf16[3,256,256]{2,1,0:T(8,128)(2,1)} %filters.1, ...), custom_call_target="tpu_custom_call" | custom-call | flops 30000000 | bytes 2000000 | tf_op jit(solution)/shard_map/pallas_call | solution.py:320
  13.4 0.0 collective-permute-done.cross
  13.4 0.0 collective-permute-done.1.chip
  13.4 1.3 %shard_map.88 = (bf16[16,16,128]{2,1,0:T(8,128)(2,1)S(1)}, f32[3,80,128]{2,1,0:T(8,128)S(1)}, bf16[3,768,128]{2,1,0:T(8,128)(2,1)S(1)}) custom-call(bf16[3,256,128]{2,1,0:T(8,128)(2,1)S(1)} %get-tuple-element.22.field, bf16[2,256,128]{2,1,0:T(8,128)(2,1)S(1)} %collective-permute-done.cross, bf16[2,256,128]{2,1,0:T(8,128)(2,1)S(1)} %collective-permute-done.1.chip, ...), custom_call_target="tpu_custom_call" | custom-call | flops 450000000 | bytes 3000000 | tf_op jit(solution)/shard_map/pallas_call | solution.py:340
  14.7 12.6 %all_to_all.20.visitors = bf16[16,16,128]{2,1,0:T(8,128)(2,1)S(1)} all-to-all(bf16[16,16,128]{2,1,0:T(8,128)(2,1)S(1)} %get-tuple-element.27), channel_id=1, replica_groups=mesh['ens'=16,'lat'=32] {'ens'}, dimensions={0} | all-to-all | bytes 131072 | tf_op jit(solution)/shard_map/all_to_all | solution.py:351
  27.3 0.2 shard_map.89
  27.5 10.0 %all_to_all.21.sums = bf16[16,16,128]{2,1,0:T(8,128)(2,1)S(1)} all-to-all(bf16[16,16,128]{2,1,0:T(8,128)(2,1)S(1)} %shard_map.89), channel_id=1, replica_groups=mesh['ens'=16,'lat'=32] {'ens'}, dimensions={0} | all-to-all | bytes 131072 | tf_op jit(solution)/shard_map/all_to_all | solution.py:353
  37.5 0.0 copy-done
  37.5 0.0 copy-done.1
  37.5 1.1 %shard_map.90 = (bf16[3,80,128]{2,1,0:T(8,128)(2,1)S(1)}, bf16[2,80,128]{2,1,0:T(8,128)(2,1)S(1)}, bf16[2,80,128]{2,1,0:T(8,128)(2,1)S(1)}, bf16[32,16,128]{2,1,0:T(8,128)(2,1)}) custom-call(f32[96,128]{1,0:T(8,128)S(1)} %copy-done.1, bf16[16,16,128]{2,1,0:T(8,128)(2,1)S(1)} %all_to_all.21.sums, f32[3,80,128]{2,1,0:T(8,128)S(1)} %get-tuple-element.28.predicted, ...), custom_call_target="tpu_custom_call" | custom-call | flops 80000000 | bytes 1200000 | tf_op jit(solution)/shard_map/pallas_call | solution.py:356
  38.6 16.6 %all-to-all-start.2 = ((bf16[32,16,128]{2,1,0:T(8,128)(2,1)}), bf16[32,16,128]{2,1,0:T(8,128)(2,1)S(1)}, u32[]{:S(2)}, u32[]{:S(2)}) async-start(bf16[32,16,128]{2,1,0:T(8,128)(2,1)} %get-tuple-element.31), calls=%async_computation.2 | async-start | bytes 262144 | tf_op jit(solution)/shard_map/all_to_all | solution.py:368
  55.1 5.0 %collective-permute-start.2 = (bf16[2,80,128]{2,1,0:T(8,128)(2,1)S(1)}, bf16[2,80,128]{2,1,0:T(8,128)(2,1)S(1)}, u32[]{:S(2)}, u32[]{:S(2)}) collective-permute-start(bf16[2,80,128]{2,1,0:T(8,128)(2,1)S(1)} %get-tuple-element.32), channel_id=1, source_target_pairs={{1,2},{3,4},{5,6},{7,8},{9,10},{11,12},{13,14},{15,16},{17,18},{19... | collective-permute-start | bytes 122888 | tf_op jit(solution)/shard_map/ppermute | solution.py:295
  60.2 1.9 %collective-permute-start.3 = (bf16[2,80,128]{2,1,0:T(8,128)(2,1)S(1)}, bf16[2,80,128]{2,1,0:T(8,128)(2,1)S(1)}, u32[]{:S(2)}, u32[]{:S(2)}) collective-permute-start(bf16[2,80,128]{2,1,0:T(8,128)(2,1)S(1)} %get-tuple-element.33), channel_id=1, source_target_pairs={{0,1},{2,3},{4,5},{6,7},{8,9},{10,11},{12,13},{14,15},{16,17},{18,... | collective-permute-start | bytes 122888 | tf_op jit(solution)/shard_map/ppermute | solution.py:296
  62.1 0.5 shard_map.91.turned
  62.6 0.0 collective-permute-done.2.cross
  62.6 0.7 collective-permute-done.3.chip
  63.3 2.6 %all-to-all-done.2.parts = bf16[32,16,128]{2,1,0:T(8,128)(2,1)S(1)} async-done(((bf16[32,16,128]{2,1,0:T(8,128)(2,1)}), bf16[32,16,128]{2,1,0:T(8,128)(2,1)S(1)}, u32[]{:S(2)}, u32[]{:S(2)}) %all-to-all-start.2) | async-done | bytes 131104 | tf_op jit(solution)/shard_map/all_to_all | solution.py:368
  65.9 0.3 shard_map.92
  66.2 10.0 %all_to_all.22.parts = bf16[16,16,128]{2,1,0:T(8,128)(2,1)S(1)} all-to-all(bf16[16,16,128]{2,1,0:T(8,128)(2,1)S(1)} %shard_map.92), channel_id=1, replica_groups=mesh['ens'=16,'lat'=32] {'ens'}, dimensions={0} | all-to-all | bytes 131072 | tf_op jit(solution)/shard_map/all_to_all | solution.py:387
  76.2 1.5 %shard_map.93 = (bf16[3,256,128]{2,1,0:T(8,128)(2,1)}, f32[3,8,16]{2,1,0:T(8,128)}) custom-call(bf16[3,80,128]{2,1,0:T(8,128)(2,1)S(1)} %get-tuple-element.30.pred_grad, bf16[2,80,128]{2,1,0:T(8,128)(2,1)S(1)} %collective-permute-done.2.cross, bf16[2,80,128]{2,1,0:T(8,128)(2,1)S(1)} %collective-permute-done.3.chip, f32[3,80,384]{2,1,0:T(8,128)S(1)} %shard_map.91.turned, ...), custom_call_target="tpu_custom_call" | custom-call | flops 150000000 | bytes 1500000 | tf_op jit(solution)/shard_map/pallas_call | solution.py:388
Async XLA Ops:
  1.6 11.7 %collective-permute-start = (bf16[2,256,128]{2,1,0:T(8,128)(2,1)S(1)}, bf16[2,256,128]{2,1,0:T(8,128)(2,1)S(1)}, u32[]{:S(2)}, u32[]{:S(2)}) collective-permute-start(bf16[2,256,128]{2,1,0:T(8,128)(2,1)S(1)} %get-tuple-element.23), channel_id=1, source_target_pairs={{1,2},{3,4},{5,6},{7,8},{9,10},{11,12},{13,14},{15,16},{17,18},{19... | collective-permute-start | bytes 393224 | tf_op jit(solution)/shard_map/ppermute | solution.py:295
  7.7 5.7 %collective-permute-start.1 = (bf16[2,256,128]{2,1,0:T(8,128)(2,1)S(1)}, bf16[2,256,128]{2,1,0:T(8,128)(2,1)S(1)}, u32[]{:S(2)}, u32[]{:S(2)}) collective-permute-start(bf16[2,256,128]{2,1,0:T(8,128)(2,1)S(1)} %get-tuple-element.24), channel_id=1, source_target_pairs={{0,1},{2,3},{4,5},{6,7},{8,9},{10,11},{12,13},{14,15},{16,17},{18,... | collective-permute-start | bytes 393224 | tf_op jit(solution)/shard_map/ppermute | solution.py:296
  11.1 26.4 %copy-start = (bf16[3,72,128]{2,1,0:T(8,128)(2,1)S(1)}, bf16[3,72,128]{2,1,0:T(8,128)(2,1)}, u32[]{:S(2)}) copy-start(bf16[3,72,128]{2,1,0:T(8,128)(2,1)} %target.1) | copy-start | bytes 165892
  11.1 26.4 %copy-start.1 = (f32[96,128]{1,0:T(8,128)S(1)}, f32[96,128]{1,0:T(8,128)}, u32[]{:S(2)}) copy-start(f32[96,128]{1,0:T(8,128)} %constant.2.clone.area) | copy-start | bytes 147460
  38.6 27.3 %all-to-all-start.2 = ((bf16[32,16,128]{2,1,0:T(8,128)(2,1)}), bf16[32,16,128]{2,1,0:T(8,128)(2,1)S(1)}, u32[]{:S(2)}, u32[]{:S(2)}) async-start(bf16[32,16,128]{2,1,0:T(8,128)(2,1)} %get-tuple-element.31), calls=%async_computation.2 | async-start | bytes 262144 | tf_op jit(solution)/shard_map/all_to_all | solution.py:368
  55.1 7.5 %collective-permute-start.2 = (bf16[2,80,128]{2,1,0:T(8,128)(2,1)S(1)}, bf16[2,80,128]{2,1,0:T(8,128)(2,1)S(1)}, u32[]{:S(2)}, u32[]{:S(2)}) collective-permute-start(bf16[2,80,128]{2,1,0:T(8,128)(2,1)S(1)} %get-tuple-element.32), channel_id=1, source_target_pairs={{1,2},{3,4},{5,6},{7,8},{9,10},{11,12},{13,14},{15,16},{17,18},{19... | collective-permute-start | bytes 122888 | tf_op jit(solution)/shard_map/ppermute | solution.py:295
  60.2 3.1 %collective-permute-start.3 = (bf16[2,80,128]{2,1,0:T(8,128)(2,1)S(1)}, bf16[2,80,128]{2,1,0:T(8,128)(2,1)S(1)}, u32[]{:S(2)}, u32[]{:S(2)}) collective-permute-start(bf16[2,80,128]{2,1,0:T(8,128)(2,1)S(1)} %get-tuple-element.33), channel_id=1, source_target_pairs={{0,1},{2,3},{4,5},{6,7},{8,9},{10,11},{12,13},{14,15},{16,17},{18,... | collective-permute-start | bytes 122888 | tf_op jit(solution)/shard_map/ppermute | solution.py:296

commit v12 on v10

--- a/solution.py
+++ b/solution.py
@@ -128,21 +128,31 @@
     w_bwd[...] = jnp.concatenate(columns, axis=1).astype(BF)
 
 
-def forward(rows, kernels, field, cross, chip, ahead, w_fwd, packed, predicted, mixed):
-    lon = field.shape[2]
-    chan = field.shape[1]
+def forward_own(rows, kernels, field, ahead, w_fwd, mixed, predicted):
+    chan, lon = field.shape[1:]
+    source = jnp.concatenate([field[i] for i in range(rows)], axis=1)
+    for i in range(rows):
+        mixed[i] = dot_nn(source, ahead[i, (HALO - i) * lon : (HALO - i + rows) * lon, :])
+        predicted[i] = dot_nn(w_fwd[:, :chan], field[i])
+
+
+def forward_rest(rows, kernels, cross, chip, begun, based, ahead, w_fwd, packed, predicted, mixed):
+    chan, lon = cross.shape[1:]
     low, high = sides(odd_band(), cross, chip)
-    wide = low + [field[i] for i in range(rows)] + high
+    outer = dict(enumerate(low, -HALO)) | dict(enumerate(high, rows))
     per = packed.shape[1]
     padded = predicted.shape[1]
     pieces = padded // per
     for i in range(rows):
-        source = jnp.concatenate(wide[i : i + REACH], axis=1)
-        taps = dot_nn(source, ahead[i]).astype(BF)
+        reach = [at for at in outer if 0 <= at - i + HALO < REACH]
+        source = jnp.concatenate([outer[at] for at in reach], axis=1)
+        steps = [at - i + HALO for at in reach]
+        table = jnp.concatenate([ahead[i, step * lon : (step + 1) * lon, :] for step in steps], axis=0)
+        taps = (begun[i] + dot_nn(source, table)).astype(BF)
+        stack = [taps[:, k * lon : (k + 1) * lon] for k in range(kernels)]
         for k in range(kernels):
-            mixed[i, k * chan : (k + 1) * chan, :] = taps[:, k * lon : (k + 1) * lon]
-        stack = jnp.concatenate([wide[i + HALO]] + [taps[:, k * lon : (k + 1) * lon] for k in range(kernels)], axis=0)
-        pred = dot_nn(w_fwd[...], stack)
+            mixed[i, k * chan : (k + 1) * chan, :] = stack[k]
+        pred = based[i] + dot_nn(w_fwd[:, chan:], jnp.concatenate(stack, axis=0))
         predicted[i] = pred
         rounded = pred.astype(BF)
         for q in range(pieces):
@@ -290,13 +300,10 @@
     return low, high
 
 
-def exchange(cross, chip, axis):
+def across(block, axis, start):
     count = lax.axis_size(axis)
-    far = [(i, i + 1) for i in range(1, count - 1, 2)]
-    near = [(i, i + 1) for i in range(0, count - 1, 2)]
-    cross = lax.ppermute(cross, axis, far + [(b, a) for a, b in far])
-    chip = lax.ppermute(chip, axis, near + [(b, a) for a, b in near])
-    return cross, chip
+    up = [(i, i + 1) for i in range(start, count - 1, 2)]
+    return lax.ppermute(block, axis, up + [(b, a) for a, b in up])
 
 
 def body(latent_fields, target_fields, filters, decoder, cycle_basis, cycle_offsets):
@@ -318,7 +325,7 @@
     edge = jax.ShapeDtypeStruct((HALO, chan, lon), BF)
     pair = pltpu.SemaphoreType.DMA((2,))
     cross, chip = call(cut, (edge, edge), [hbm], 0, 500_000, [pair])(stay(field))
-    cross, chip = exchange(cross, chip, "lat")
+    cross = across(cross, "lat", 1)
     ahead, tap_edge, w_fwd, w_bwd, near = call(
         functools.partial(prepare, rows, lat_count),
         (
@@ -339,17 +346,26 @@
             pltpu.SemaphoreType.DMA((5,)),
         ],
     )(stay(basis), stay(offsets), stay(filters), stay(dec_t), stay(field))
+    chip, ahead = lax.optimization_barrier((chip, ahead))
+    chip = across(chip, "lat", 0)
+    begun, based = call(
+        functools.partial(forward_own, rows, kernels),
+        (jax.ShapeDtypeStruct((rows, chan, kernels * lon), F32), jax.ShapeDtypeStruct((rows, padded, lon), F32)),
+        [VMEM] * 3,
+        250_000_000,
+        3_000_000,
+    )(near, ahead, w_fwd)
     packed, predicted, mixed = call(
-        functools.partial(forward, rows, kernels),
+        functools.partial(forward_rest, rows, kernels),
         (
             jax.ShapeDtypeStruct((members, per, lon), BF),
             jax.ShapeDtypeStruct((rows, padded, lon), F32),
             jax.ShapeDtypeStruct((rows, kernels * chan, lon), BF),
         ),
-        [VMEM] * 5,
-        450_000_000,
+        [VMEM] * 6,
+        200_000_000,
         3_000_000,
-    )(near, cross, chip, ahead, w_fwd)
+    )(cross, chip, begun, based, ahead, w_fwd)
     visitors = lax.all_to_all(packed, "ens", 0, 0, tiled=True)
     sums = call(pairs, jax.ShapeDtypeStruct((members, per, lon), BF), [VMEM], 2_000_000, 200_000)(visitors)
     sums = lax.all_to_all(sums, "ens", 0, 0, tiled=True)
@@ -368,7 +384,7 @@
         1_200_000,
     )(area, sums, predicted, target_fields, mixed)
     parts = lax.all_to_all(partial, "lat", 0, 0, tiled=True)
-    cross, chip = exchange(cross, chip, "lat")
+    cross, chip = across(cross, "lat", 1), across(chip, "lat", 0)
     turned = call(
         functools.partial(adjoint_own, rows, kernels),
         jax.ShapeDtypeStruct((rows, padded, kernels * lon), F32),

time: 77.3 us -> 77 us (level)
  starting transfers between devices: 33 us -> 32 us
    all_to_all x1, starting transfers between devices: 16.6 us -> 15.6 us  [body(): parts = lax.all_to_all(partial, 'lat', 0, 0, tiled=True)]
  transfers between devices with their start and end apart: 5 -> 5, of which waited for: 2 -> 3; matrix products, arithmetic and copies ran while one was open for 0% -> 0% of each run, Pallas kernels for 6% -> 6%
where the time goes in v12:
time: 77 us; the launch traced here: 76.6 us
  blocking collectives  32.9 us (43%)
  starting transfers between devices  32 us (42%)
  Pallas kernels  8.8 us (11%)
  waiting for transfers between devices  2.15 us (3%)
    ppermute x4, starting transfers between devices, across(): return lax.ppermute(block, axis, up + [(b, a) for a, b in up])  16.4 us
    all_to_all x1, starting transfers between devices, body(): parts = lax.all_to_all(partial, 'lat', 0, 0, tiled=True)  15.6 us
    all_to_all x1, blocking collectives, body(): visitors = lax.all_to_all(packed, 'ens', 0, 0, tiled=True)  13 us
    all_to_all x1, blocking collectives, body(): spread = lax.all_to_all(spread, 'ens', 0, 0, tiled=True)  10 us
    all_to_all x1, blocking collectives, body(): sums = lax.all_to_all(sums, 'ens', 0, 0, tiled=True)  9.95 us
    pallas_call x1, Pallas kernels, body(): call(functools.partial(prepare, rows, lat_count), (jax.ShapeDtypeStruct((...  2.1 us
  transfers between devices with their start and end apart: 5, of which 3 were waited for; matrix products, arithmetic and copies ran while one was open for 0% of the time, Pallas kernels for 6%

profile of v12, /device:TPU:1, one launch (start us, length us, event | category | flops | bytes accessed | tf_op | source)
XLA Modules:
  0.0 76.6 jit_solution(798060939863083310)
XLA Ops:
  0.6 1.0 %shard_map.86 = (bf16[2,256,128]{2,1,0:T(8,128)(2,1)S(1)}, bf16[2,256,128]{2,1,0:T(8,128)(2,1)S(1)}) custom-call(bf16[3,256,128]{2,1,0:T(8,128)(2,1)} %bitcast.6), custom_call_target="tpu_custom_call" | custom-call | bytes 500000 | tf_op jit(solution)/shard_map/pallas_call | solution.py:327
  1.6 6.0 %collective-permute-start = (bf16[2,256,128]{2,1,0:T(8,128)(2,1)S(1)}, bf16[2,256,128]{2,1,0:T(8,128)(2,1)S(1)}, u32[]{:S(2)}, u32[]{:S(2)}) collective-permute-start(bf16[2,256,128]{2,1,0:T(8,128)(2,1)S(1)} %get-tuple-element.22), channel_id=1, source_target_pairs={{1,2},{3,4},{5,6},{7,8},{9,10},{11,12},{13,14},{15,16},{17,18},{19... | collective-permute-start | bytes 393224 | tf_op jit(solution)/shard_map/ppermute | solution.py:306
  7.7 2.1 %shard_map.87 = (bf16[3,640,384]{2,1,0:T(8,128)(2,1)S(1)}, bf16[3,384,256]{2,1,0:T(8,128)(2,1)S(1)}, bf16[80,1024]{1,0:T(8,128)(2,1)S(1)}, bf16[256,320]{1,0:T(8,128)(2,1)S(1)}, bf16[3,256,128]{2,1,0:T(8,128)(2,1)S(1)}) custom-call(f32[10,3,96]{2,1,0:T(4,128)} %bitcast.10, s32[10,96]{1,0:T(8,128)} %bitcast.12, bf16[3,256,256]{2,1,0:T(8,128)(2,1)} %filters.1, ...), custom_call_target="tpu_custom_call" | custom-call | flops 30000000 | bytes 2000000 | tf_op jit(solution)/shard_map/pallas_call | solution.py:329
  9.8 3.4 %collective-permute-start.1 = (bf16[2,256,128]{2,1,0:T(8,128)(2,1)S(1)}, bf16[2,256,128]{2,1,0:T(8,128)(2,1)S(1)}, u32[]{:S(2)}, u32[]{:S(2)}) collective-permute-start(bf16[2,256,128]{2,1,0:T(8,128)(2,1)S(1)} %get-tuple-element.25), channel_id=1, source_target_pairs={{0,1},{2,3},{4,5},{6,7},{8,9},{10,11},{12,13},{14,15},{16,17},{18,... | collective-permute-start | bytes 393224 | tf_op jit(solution)/shard_map/ppermute | solution.py:306
  13.2 0.5 shard_map.88
  13.8 0.0 collective-permute-done.cross
  13.8 0.4 collective-permute-done.1.chip
  14.2 0.0 copy-start
  14.2 0.0 copy-start.1
  14.2 0.8 %shard_map.89 = (bf16[16,16,128]{2,1,0:T(8,128)(2,1)S(1)}, f32[3,80,128]{2,1,0:T(8,128)S(1)}, bf16[3,768,128]{2,1,0:T(8,128)(2,1)S(1)}) custom-call(bf16[2,256,128]{2,1,0:T(8,128)(2,1)S(1)} %collective-permute-done.cross, bf16[2,256,128]{2,1,0:T(8,128)(2,1)S(1)} %collective-permute-done.1.chip, f32[3,256,384]{2,1,0:T(8,128)S(1)} %get-tuple-element.29.begun, ...), custom_call_target="tpu_custom_call" | custom-call | flops 200000000 | bytes 3000000 | tf_op jit(solution)/shard_map/pallas_call | solution.py:358
  15.0 13.0 %all_to_all.20.visitors = bf16[16,16,128]{2,1,0:T(8,128)(2,1)S(1)} all-to-all(bf16[16,16,128]{2,1,0:T(8,128)(2,1)S(1)} %get-tuple-element.31), channel_id=1, replica_groups=mesh['ens'=16,'lat'=32] {'ens'}, dimensions={0} | all-to-all | bytes 131072 | tf_op jit(solution)/shard_map/all_to_all | solution.py:369
  28.0 0.2 shard_map.90
  28.3 10.0 %all_to_all.21.sums = bf16[16,16,128]{2,1,0:T(8,128)(2,1)S(1)} all-to-all(bf16[16,16,128]{2,1,0:T(8,128)(2,1)S(1)} %shard_map.90), channel_id=1, replica_groups=mesh['ens'=16,'lat'=32] {'ens'}, dimensions={0} | all-to-all | bytes 131072 | tf_op jit(solution)/shard_map/all_to_all | solution.py:371
  38.2 0.0 copy-done
  38.2 0.0 copy-done.1
  38.2 1.1 %shard_map.91 = (bf16[3,80,128]{2,1,0:T(8,128)(2,1)S(1)}, bf16[2,80,128]{2,1,0:T(8,128)(2,1)S(1)}, bf16[2,80,128]{2,1,0:T(8,128)(2,1)S(1)}, bf16[32,16,128]{2,1,0:T(8,128)(2,1)}) custom-call(f32[96,128]{1,0:T(8,128)S(1)} %copy-done.1, bf16[16,16,128]{2,1,0:T(8,128)(2,1)S(1)} %all_to_all.21.sums, f32[3,80,128]{2,1,0:T(8,128)S(1)} %get-tuple-element.32.predicted, ...), custom_call_target="tpu_custom_call" | custom-call | flops 80000000 | bytes 1200000 | tf_op jit(solution)/shard_map/pallas_call | solution.py:374
  39.3 15.6 %all-to-all-start.2 = ((bf16[32,16,128]{2,1,0:T(8,128)(2,1)}), bf16[32,16,128]{2,1,0:T(8,128)(2,1)S(1)}, u32[]{:S(2)}, u32[]{:S(2)}) async-start(bf16[32,16,128]{2,1,0:T(8,128)(2,1)} %get-tuple-element.34), calls=%async_computation.2 | async-start | bytes 262144 | tf_op jit(solution)/shard_map/all_to_all | solution.py:386
  54.8 5.0 %collective-permute-start.2 = (bf16[2,80,128]{2,1,0:T(8,128)(2,1)S(1)}, bf16[2,80,128]{2,1,0:T(8,128)(2,1)S(1)}, u32[]{:S(2)}, u32[]{:S(2)}) collective-permute-start(bf16[2,80,128]{2,1,0:T(8,128)(2,1)S(1)} %get-tuple-element.36), channel_id=1, source_target_pairs={{1,2},{3,4},{5,6},{7,8},{9,10},{11,12},{13,14},{15,16},{17,18},{19... | collective-permute-start | bytes 122888 | tf_op jit(solution)/shard_map/ppermute | solution.py:306
  59.9 1.9 %collective-permute-start.3 = (bf16[2,80,128]{2,1,0:T(8,128)(2,1)S(1)}, bf16[2,80,128]{2,1,0:T(8,128)(2,1)S(1)}, u32[]{:S(2)}, u32[]{:S(2)}) collective-permute-start(bf16[2,80,128]{2,1,0:T(8,128)(2,1)S(1)} %get-tuple-element.37), channel_id=1, source_target_pairs={{0,1},{2,3},{4,5},{6,7},{8,9},{10,11},{12,13},{14,15},{16,17},{18,... | collective-permute-start | bytes 122888 | tf_op jit(solution)/shard_map/ppermute | solution.py:306
  61.8 0.5 shard_map.92.turned
  62.4 0.0 collective-permute-done.2.cross
  62.4 0.7 collective-permute-done.3.chip
  63.0 1.5 %shard_map.93 = bf16[3,256,128]{2,1,0:T(8,128)(2,1)} custom-call(bf16[3,80,128]{2,1,0:T(8,128)(2,1)S(1)} %get-tuple-element.35.pred_grad, bf16[2,80,128]{2,1,0:T(8,128)(2,1)S(1)} %collective-permute-done.2.cross, bf16[2,80,128]{2,1,0:T(8,128)(2,1)S(1)} %collective-permute-done.3.chip, f32[3,80,384]{2,1,0:T(8,128)S(1)} %shard_map.92.turned, ...), custom_call_target="tpu_custom_call" | custom-call | flops 150000000 | bytes 1500000 | tf_op jit(solution)/shard_map/pallas_call | solution.py:395
  64.5 1.1 %all-to-all-done.2.parts = bf16[32,16,128]{2,1,0:T(8,128)(2,1)S(1)} async-done(((bf16[32,16,128]{2,1,0:T(8,128)(2,1)}), bf16[32,16,128]{2,1,0:T(8,128)(2,1)S(1)}, u32[]{:S(2)}, u32[]{:S(2)}) %all-to-all-start.2) | async-done | bytes 131104 | tf_op jit(solution)/shard_map/all_to_all | solution.py:386
  65.6 0.3 shard_map.94
  65.9 10.0 %all_to_all.22.parts = bf16[16,16,128]{2,1,0:T(8,128)(2,1)S(1)} all-to-all(bf16[16,16,128]{2,1,0:T(8,128)(2,1)S(1)} %shard_map.94), channel_id=1, replica_groups=mesh['ens'=16,'lat'=32] {'ens'}, dimensions={0} | all-to-all | bytes 131072 | tf_op jit(solution)/shard_map/all_to_all | solution.py:414
  75.9 0.7 shard_map.95
Async XLA Ops:
  1.6 12.1 %collective-permute-start = (bf16[2,256,128]{2,1,0:T(8,128)(2,1)S(1)}, bf16[2,256,128]{2,1,0:T(8,128)(2,1)S(1)}, u32[]{:S(2)}, u32[]{:S(2)}) collective-permute-start(bf16[2,256,128]{2,1,0:T(8,128)(2,1)S(1)} %get-tuple-element.22), channel_id=1, source_target_pairs={{1,2},{3,4},{5,6},{7,8},{9,10},{11,12},{13,14},{15,16},{17,18},{19... | collective-permute-start | bytes 393224 | tf_op jit(solution)/shard_map/ppermute | solution.py:306
  9.8 4.4 %collective-permute-start.1 = (bf16[2,256,128]{2,1,0:T(8,128)(2,1)S(1)}, bf16[2,256,128]{2,1,0:T(8,128)(2,1)S(1)}, u32[]{:S(2)}, u32[]{:S(2)}) collective-permute-start(bf16[2,256,128]{2,1,0:T(8,128)(2,1)S(1)} %get-tuple-element.25), channel_id=1, source_target_pairs={{0,1},{2,3},{4,5},{6,7},{8,9},{10,11},{12,13},{14,15},{16,17},{18,... | collective-permute-start | bytes 393224 | tf_op jit(solution)/shard_map/ppermute | solution.py:306
  14.2 24.0 %copy-start = (bf16[3,72,128]{2,1,0:T(8,128)(2,1)S(1)}, bf16[3,72,128]{2,1,0:T(8,128)(2,1)}, u32[]{:S(2)}) copy-start(bf16[3,72,128]{2,1,0:T(8,128)(2,1)} %target.1) | copy-start | bytes 165892
  14.2 24.0 %copy-start.1 = (f32[96,128]{1,0:T(8,128)S(1)}, f32[96,128]{1,0:T(8,128)}, u32[]{:S(2)}) copy-start(f32[96,128]{1,0:T(8,128)} %constant.2.clone.area) | copy-start | bytes 147460
  39.3 26.3 %all-to-all-start.2 = ((bf16[32,16,128]{2,1,0:T(8,128)(2,1)}), bf16[32,16,128]{2,1,0:T(8,128)(2,1)S(1)}, u32[]{:S(2)}, u32[]{:S(2)}) async-start(bf16[32,16,128]{2,1,0:T(8,128)(2,1)} %get-tuple-element.34), calls=%async_computation.2 | async-start | bytes 262144 | tf_op jit(solution)/shard_map/all_to_all | solution.py:386
  54.8 7.5 %collective-permute-start.2 = (bf16[2,80,128]{2,1,0:T(8,128)(2,1)S(1)}, bf16[2,80,128]{2,1,0:T(8,128)(2,1)S(1)}, u32[]{:S(2)}, u32[]{:S(2)}) collective-permute-start(bf16[2,80,128]{2,1,0:T(8,128)(2,1)S(1)} %get-tuple-element.36), channel_id=1, source_target_pairs={{1,2},{3,4},{5,6},{7,8},{9,10},{11,12},{13,14},{15,16},{17,18},{19... | collective-permute-start | bytes 122888 | tf_op jit(solution)/shard_map/ppermute | solution.py:306
  59.9 3.1 %collective-permute-start.3 = (bf16[2,80,128]{2,1,0:T(8,128)(2,1)S(1)}, bf16[2,80,128]{2,1,0:T(8,128)(2,1)S(1)}, u32[]{:S(2)}, u32[]{:S(2)}) collective-permute-start(bf16[2,80,128]{2,1,0:T(8,128)(2,1)S(1)} %get-tuple-element.37), channel_id=1, source_target_pairs={{0,1},{2,3},{4,5},{6,7},{8,9},{10,11},{12,13},{14,15},{16,17},{18,... | collective-permute-start | bytes 122888 | tf_op jit(solution)/shard_map/ppermute | solution.py:306

commit v13 on v12

--- a/solution.py
+++ b/solution.py
@@ -325,7 +325,7 @@
     edge = jax.ShapeDtypeStruct((HALO, chan, lon), BF)
     pair = pltpu.SemaphoreType.DMA((2,))
     cross, chip = call(cut, (edge, edge), [hbm], 0, 500_000, [pair])(stay(field))
-    cross = across(cross, "lat", 1)
+    cross, chip = across(cross, "lat", 1), across(chip, "lat", 0)
     ahead, tap_edge, w_fwd, w_bwd, near = call(
         functools.partial(prepare, rows, lat_count),
         (
@@ -346,8 +346,6 @@
             pltpu.SemaphoreType.DMA((5,)),
         ],
     )(stay(basis), stay(offsets), stay(filters), stay(dec_t), stay(field))
-    chip, ahead = lax.optimization_barrier((chip, ahead))
-    chip = across(chip, "lat", 0)
     begun, based = call(
         functools.partial(forward_own, rows, kernels),
         (jax.ShapeDtypeStruct((rows, chan, kernels * lon), F32), jax.ShapeDtypeStruct((rows, padded, lon), F32)),

time: 77 us -> 76.9 us (level)
  transfers between devices with their start and end apart: 5 -> 5, of which waited for: 3 -> 2; matrix products, arithmetic and copies ran while one was open for 0% -> 0% of each run, Pallas kernels for 6% -> 6%
where the time goes in v13:
time: 76.9 us; the launch traced here: 76.5 us
  blocking collectives  32.6 us (42%)
  starting transfers between devices  32.5 us (42%)
  Pallas kernels  8.8 us (11%)
  waiting for transfers between devices  1.74 us (2%)
    ppermute x4, starting transfers between devices, across(): return lax.ppermute(block, axis, up + [(b, a) for a, b in up])  16.4 us
    all_to_all x1, starting transfers between devices, body(): parts = lax.all_to_all(partial, 'lat', 0, 0, tiled=True)  16.1 us
    all_to_all x1, blocking collectives, body(): visitors = lax.all_to_all(packed, 'ens', 0, 0, tiled=True)  12.6 us
    all_to_all x1, blocking collectives, body(): spread = lax.all_to_all(spread, 'ens', 0, 0, tiled=True)  10 us
    all_to_all x1, blocking collectives, body(): sums = lax.all_to_all(sums, 'ens', 0, 0, tiled=True)  9.95 us
    pallas_call x1, Pallas kernels, body(): call(functools.partial(prepare, rows, lat_count), (jax.ShapeDtypeStruct((...  2.09 us
  transfers between devices with their start and end apart: 5, of which 2 were waited for; matrix products, arithmetic and copies ran while one was open for 0% of the time, Pallas kernels for 6%

profile of v13, /device:TPU:1, one launch (start us, length us, event | category | flops | bytes accessed | tf_op | source)
XLA Modules:
  0.0 76.5 jit_solution(6304453774860028546)
XLA Ops:
  0.6 1.0 %shard_map.86 = (bf16[2,256,128]{2,1,0:T(8,128)(2,1)S(1)}, bf16[2,256,128]{2,1,0:T(8,128)(2,1)S(1)}) custom-call(bf16[3,256,128]{2,1,0:T(8,128)(2,1)} %bitcast.6), custom_call_target="tpu_custom_call" | custom-call | bytes 500000 | tf_op jit(solution)/shard_map/pallas_call | solution.py:327
  1.6 6.0 %collective-permute-start = (bf16[2,256,128]{2,1,0:T(8,128)(2,1)S(1)}, bf16[2,256,128]{2,1,0:T(8,128)(2,1)S(1)}, u32[]{:S(2)}, u32[]{:S(2)}) collective-permute-start(bf16[2,256,128]{2,1,0:T(8,128)(2,1)S(1)} %get-tuple-element.20), channel_id=1, source_target_pairs={{1,2},{3,4},{5,6},{7,8},{9,10},{11,12},{13,14},{15,16},{17,18},{19... | collective-permute-start | bytes 393224 | tf_op jit(solution)/shard_map/ppermute | solution.py:306
  7.7 3.4 %collective-permute-start.1 = (bf16[2,256,128]{2,1,0:T(8,128)(2,1)S(1)}, bf16[2,256,128]{2,1,0:T(8,128)(2,1)S(1)}, u32[]{:S(2)}, u32[]{:S(2)}) collective-permute-start(bf16[2,256,128]{2,1,0:T(8,128)(2,1)S(1)} %get-tuple-element.21), channel_id=1, source_target_pairs={{0,1},{2,3},{4,5},{6,7},{8,9},{10,11},{12,13},{14,15},{16,17},{18,... | collective-permute-start | bytes 393224 | tf_op jit(solution)/shard_map/ppermute | solution.py:306
  11.1 2.1 %shard_map.87 = (bf16[3,640,384]{2,1,0:T(8,128)(2,1)S(1)}, bf16[3,384,256]{2,1,0:T(8,128)(2,1)S(1)}, bf16[80,1024]{1,0:T(8,128)(2,1)S(1)}, bf16[256,320]{1,0:T(8,128)(2,1)S(1)}, bf16[3,256,128]{2,1,0:T(8,128)(2,1)S(1)}) custom-call(f32[10,3,96]{2,1,0:T(4,128)} %bitcast.10, s32[10,96]{1,0:T(8,128)} %bitcast.12, bf16[3,256,256]{2,1,0:T(8,128)(2,1)} %filters.1, ...), custom_call_target="tpu_custom_call" | custom-call | flops 30000000 | bytes 2000000 | tf_op jit(solution)/shard_map/pallas_call | solution.py:329
  13.2 0.5 shard_map.88
  13.8 0.0 collective-permute-done.cross
  13.8 0.0 collective-permute-done.1.chip
  13.8 0.0 copy-start
  13.8 0.0 copy-start.1
  13.8 0.8 %shard_map.89 = (bf16[16,16,128]{2,1,0:T(8,128)(2,1)S(1)}, f32[3,80,128]{2,1,0:T(8,128)S(1)}, bf16[3,768,128]{2,1,0:T(8,128)(2,1)S(1)}) custom-call(bf16[2,256,128]{2,1,0:T(8,128)(2,1)S(1)} %collective-permute-done.cross, bf16[2,256,128]{2,1,0:T(8,128)(2,1)S(1)} %collective-permute-done.1.chip, f32[3,256,384]{2,1,0:T(8,128)S(1)} %get-tuple-element.25.begun, ...), custom_call_target="tpu_custom_call" | custom-call | flops 200000000 | bytes 3000000 | tf_op jit(solution)/shard_map/pallas_call | solution.py:356
  14.7 12.6 %all_to_all.20.visitors = bf16[16,16,128]{2,1,0:T(8,128)(2,1)S(1)} all-to-all(bf16[16,16,128]{2,1,0:T(8,128)(2,1)S(1)} %get-tuple-element.27), channel_id=1, replica_groups=mesh['ens'=16,'lat'=32] {'ens'}, dimensions={0} | all-to-all | bytes 131072 | tf_op jit(solution)/shard_map/all_to_all | solution.py:367
  27.3 0.2 shard_map.90
  27.5 10.0 %all_to_all.21.sums = bf16[16,16,128]{2,1,0:T(8,128)(2,1)S(1)} all-to-all(bf16[16,16,128]{2,1,0:T(8,128)(2,1)S(1)} %shard_map.90), channel_id=1, replica_groups=mesh['ens'=16,'lat'=32] {'ens'}, dimensions={0} | all-to-all | bytes 131072 | tf_op jit(solution)/shard_map/all_to_all | solution.py:369
  37.5 0.0 copy-done
  37.5 0.0 copy-done.1
  37.5 1.1 %shard_map.91 = (bf16[3,80,128]{2,1,0:T(8,128)(2,1)S(1)}, bf16[2,80,128]{2,1,0:T(8,128)(2,1)S(1)}, bf16[2,80,128]{2,1,0:T(8,128)(2,1)S(1)}, bf16[32,16,128]{2,1,0:T(8,128)(2,1)}) custom-call(f32[96,128]{1,0:T(8,128)S(1)} %copy-done.1, bf16[16,16,128]{2,1,0:T(8,128)(2,1)S(1)} %all_to_all.21.sums, f32[3,80,128]{2,1,0:T(8,128)S(1)} %get-tuple-element.28.predicted, ...), custom_call_target="tpu_custom_call" | custom-call | flops 80000000 | bytes 1200000 | tf_op jit(solution)/shard_map/pallas_call | solution.py:372
  38.6 16.1 %all-to-all-start.2 = ((bf16[32,16,128]{2,1,0:T(8,128)(2,1)}), bf16[32,16,128]{2,1,0:T(8,128)(2,1)S(1)}, u32[]{:S(2)}, u32[]{:S(2)}) async-start(bf16[32,16,128]{2,1,0:T(8,128)(2,1)} %get-tuple-element.30), calls=%async_computation.2 | async-start | bytes 262144 | tf_op jit(solution)/shard_map/all_to_all | solution.py:384
  54.7 5.0 %collective-permute-start.2 = (bf16[2,80,128]{2,1,0:T(8,128)(2,1)S(1)}, bf16[2,80,128]{2,1,0:T(8,128)(2,1)S(1)}, u32[]{:S(2)}, u32[]{:S(2)}) collective-permute-start(bf16[2,80,128]{2,1,0:T(8,128)(2,1)S(1)} %get-tuple-element.32), channel_id=1, source_target_pairs={{1,2},{3,4},{5,6},{7,8},{9,10},{11,12},{13,14},{15,16},{17,18},{19... | collective-permute-start | bytes 122888 | tf_op jit(solution)/shard_map/ppermute | solution.py:306
  59.8 1.9 %collective-permute-start.3 = (bf16[2,80,128]{2,1,0:T(8,128)(2,1)S(1)}, bf16[2,80,128]{2,1,0:T(8,128)(2,1)S(1)}, u32[]{:S(2)}, u32[]{:S(2)}) collective-permute-start(bf16[2,80,128]{2,1,0:T(8,128)(2,1)S(1)} %get-tuple-element.33), channel_id=1, source_target_pairs={{0,1},{2,3},{4,5},{6,7},{8,9},{10,11},{12,13},{14,15},{16,17},{18,... | collective-permute-start | bytes 122888 | tf_op jit(solution)/shard_map/ppermute | solution.py:306
  61.7 0.5 shard_map.92.turned
  62.2 0.0 collective-permute-done.2.cross
  62.2 0.7 collective-permute-done.3.chip
  62.9 1.5 %shard_map.93 = bf16[3,256,128]{2,1,0:T(8,128)(2,1)} custom-call(bf16[3,80,128]{2,1,0:T(8,128)(2,1)S(1)} %get-tuple-element.31.pred_grad, bf16[2,80,128]{2,1,0:T(8,128)(2,1)S(1)} %collective-permute-done.2.cross, bf16[2,80,128]{2,1,0:T(8,128)(2,1)S(1)} %collective-permute-done.3.chip, f32[3,80,384]{2,1,0:T(8,128)S(1)} %shard_map.92.turned, ...), custom_call_target="tpu_custom_call" | custom-call | flops 150000000 | bytes 1500000 | tf_op jit(solution)/shard_map/pallas_call | solution.py:393
  64.4 1.1 %all-to-all-done.2.parts = bf16[32,16,128]{2,1,0:T(8,128)(2,1)S(1)} async-done(((bf16[32,16,128]{2,1,0:T(8,128)(2,1)}), bf16[32,16,128]{2,1,0:T(8,128)(2,1)S(1)}, u32[]{:S(2)}, u32[]{:S(2)}) %all-to-all-start.2) | async-done | bytes 131104 | tf_op jit(solution)/shard_map/all_to_all | solution.py:384
  65.5 0.3 shard_map.94
  65.8 10.0 %all_to_all.22.parts = bf16[16,16,128]{2,1,0:T(8,128)(2,1)S(1)} all-to-all(bf16[16,16,128]{2,1,0:T(8,128)(2,1)S(1)} %shard_map.94), channel_id=1, replica_groups=mesh['ens'=16,'lat'=32] {'ens'}, dimensions={0} | all-to-all | bytes 131072 | tf_op jit(solution)/shard_map/all_to_all | solution.py:412
  75.8 0.7 shard_map.95
Async XLA Ops:
  1.6 12.1 %collective-permute-start = (bf16[2,256,128]{2,1,0:T(8,128)(2,1)S(1)}, bf16[2,256,128]{2,1,0:T(8,128)(2,1)S(1)}, u32[]{:S(2)}, u32[]{:S(2)}) collective-permute-start(bf16[2,256,128]{2,1,0:T(8,128)(2,1)S(1)} %get-tuple-element.20), channel_id=1, source_target_pairs={{1,2},{3,4},{5,6},{7,8},{9,10},{11,12},{13,14},{15,16},{17,18},{19... | collective-permute-start | bytes 393224 | tf_op jit(solution)/shard_map/ppermute | solution.py:306
  7.7 6.1 %collective-permute-start.1 = (bf16[2,256,128]{2,1,0:T(8,128)(2,1)S(1)}, bf16[2,256,128]{2,1,0:T(8,128)(2,1)S(1)}, u32[]{:S(2)}, u32[]{:S(2)}) collective-permute-start(bf16[2,256,128]{2,1,0:T(8,128)(2,1)S(1)} %get-tuple-element.21), channel_id=1, source_target_pairs={{0,1},{2,3},{4,5},{6,7},{8,9},{10,11},{12,13},{14,15},{16,17},{18,... | collective-permute-start | bytes 393224 | tf_op jit(solution)/shard_map/ppermute | solution.py:306
  13.8 23.7 %copy-start = (bf16[3,72,128]{2,1,0:T(8,128)(2,1)S(1)}, bf16[3,72,128]{2,1,0:T(8,128)(2,1)}, u32[]{:S(2)}) copy-start(bf16[3,72,128]{2,1,0:T(8,128)(2,1)} %target.1) | copy-start | bytes 165892
  13.8 23.7 %copy-start.1 = (f32[96,128]{1,0:T(8,128)S(1)}, f32[96,128]{1,0:T(8,128)}, u32[]{:S(2)}) copy-start(f32[96,128]{1,0:T(8,128)} %constant.2.clone.area) | copy-start | bytes 147460
  38.6 26.9 %all-to-all-start.2 = ((bf16[32,16,128]{2,1,0:T(8,128)(2,1)}), bf16[32,16,128]{2,1,0:T(8,128)(2,1)S(1)}, u32[]{:S(2)}, u32[]{:S(2)}) async-start(bf16[32,16,128]{2,1,0:T(8,128)(2,1)} %get-tuple-element.30), calls=%async_computation.2 | async-start | bytes 262144 | tf_op jit(solution)/shard_map/all_to_all | solution.py:384
  54.7 7.5 %collective-permute-start.2 = (bf16[2,80,128]{2,1,0:T(8,128)(2,1)S(1)}, bf16[2,80,128]{2,1,0:T(8,128)(2,1)S(1)}, u32[]{:S(2)}, u32[]{:S(2)}) collective-permute-start(bf16[2,80,128]{2,1,0:T(8,128)(2,1)S(1)} %get-tuple-element.32), channel_id=1, source_target_pairs={{1,2},{3,4},{5,6},{7,8},{9,10},{11,12},{13,14},{15,16},{17,18},{19... | collective-permute-start | bytes 122888 | tf_op jit(solution)/shard_map/ppermute | solution.py:306
  59.8 3.1 %collective-permute-start.3 = (bf16[2,80,128]{2,1,0:T(8,128)(2,1)S(1)}, bf16[2,80,128]{2,1,0:T(8,128)(2,1)S(1)}, u32[]{:S(2)}, u32[]{:S(2)}) collective-permute-start(bf16[2,80,128]{2,1,0:T(8,128)(2,1)S(1)} %get-tuple-element.33), channel_id=1, source_target_pairs={{0,1},{2,3},{4,5},{6,7},{8,9},{10,11},{12,13},{14,15},{16,17},{18,... | collective-permute-start | bytes 122888 | tf_op jit(solution)/shard_map/ppermute | solution.py:306

commit v14 on v13

--- a/solution.py
+++ b/solution.py
@@ -80,7 +80,7 @@
 
 def prepare(
     rows, lat_count, basis_in, offsets_in, filters, dec_in, field,
-    ahead, edge, w_fwd, w_bwd, near, held, dec_t, basis, offsets, sems,
+    ahead, edge, w_fwd, near, held, dec_t, basis, offsets, sems,
 ):
     moves = ((offsets_in, offsets), (basis_in, basis), (dec_in, dec_t), (filters, held), (field, near))
     moves = [pltpu.make_async_copy(source, target, sems.at[n]) for n, (source, target) in enumerate(moves)]
@@ -118,14 +118,9 @@
         move.wait()
     dec = padded_rows(dec_t, padded)
 
-    square = (chan, chan)
-    unit = lax.broadcasted_iota(jnp.int32, square, 0) == lax.broadcasted_iota(jnp.int32, square, 1)
-    columns = [dot_nt(jnp.where(unit, 1.0, 0.0).astype(BF), dec)]
     w_fwd[:, :chan] = dec
     for k in range(kernels):
         w_fwd[:, (k + 1) * chan : (k + 2) * chan] = dot_nt(dec, held[k]).astype(BF)
-        columns.append(dot_nt(held[k], dec))
-    w_bwd[...] = jnp.concatenate(columns, axis=1).astype(BF)
 
 
 def forward_own(rows, kernels, field, ahead, w_fwd, mixed, predicted):
@@ -249,7 +244,14 @@
         owned[k] = turned[k * own : (k + 1) * own, :width]
 
 
-def adjoint_own(rows, kernels, pred_grad, ahead, turned):
+def adjoint_own(rows, kernels, pred_grad, ahead, held, w_fwd, turned, w_bwd):
+    chan = held.shape[1]
+    dec = w_fwd[:, :chan]
+    square = (chan, chan)
+    unit = lax.broadcasted_iota(jnp.int32, square, 0) == lax.broadcasted_iota(jnp.int32, square, 1)
+    columns = [dot_nt(jnp.where(unit, 1.0, 0.0).astype(BF), dec)]
+    columns = columns + [dot_nt(held[k], dec) for k in range(kernels)]
+    w_bwd[...] = jnp.concatenate(columns, axis=1).astype(BF)
     lon = pred_grad.shape[2]
     for k in range(kernels):
         sums = [None] * rows
@@ -326,20 +328,19 @@
     pair = pltpu.SemaphoreType.DMA((2,))
     cross, chip = call(cut, (edge, edge), [hbm], 0, 500_000, [pair])(stay(field))
     cross, chip = across(cross, "lat", 1), across(chip, "lat", 0)
-    ahead, tap_edge, w_fwd, w_bwd, near = call(
+    ahead, tap_edge, w_fwd, near, held = call(
         functools.partial(prepare, rows, lat_count),
         (
             jax.ShapeDtypeStruct((rows, REACH * lon, kernels * lon), BF),
             jax.ShapeDtypeStruct((rows, kernels * lon, (REACH - rows) * lon), BF),
             jax.ShapeDtypeStruct((padded, (kernels + 1) * chan), BF),
-            jax.ShapeDtypeStruct((chan, (kernels + 1) * padded), BF),
             jax.ShapeDtypeStruct(field.shape, BF),
+            jax.ShapeDtypeStruct(filters.shape, BF),
         ),
         [hbm] * 5,
         30_000_000,
         2_000_000,
         [
-            pltpu.VMEM(filters.shape, BF),
             pltpu.VMEM(dec_t.shape, BF),
             pltpu.SMEM(basis.shape, F32),
             pltpu.SMEM(offsets.shape, jnp.int32),
@@ -383,13 +384,16 @@
     )(area, sums, predicted, target_fields, mixed)
     parts = lax.all_to_all(partial, "lat", 0, 0, tiled=True)
     cross, chip = across(cross, "lat", 1), across(chip, "lat", 0)
-    turned = call(
+    turned, w_bwd = call(
         functools.partial(adjoint_own, rows, kernels),
-        jax.ShapeDtypeStruct((rows, padded, kernels * lon), F32),
-        [VMEM] * 2,
-        80_000_000,
-        1_500_000,
-    )(pred_grad, ahead)
+        (
+            jax.ShapeDtypeStruct((rows, padded, kernels * lon), F32),
+            jax.ShapeDtypeStruct((chan, (kernels + 1) * padded), BF),
+        ),
+        [VMEM] * 4,
+        120_000_000,
+        2_000_000,
+    )(pred_grad, ahead, held, w_fwd)
     latent_grad = call(
         functools.partial(adjoint_rest, rows, kernels),
         jax.ShapeDtypeStruct((rows, chan, lon), BF),

time: 76.9 us -> 76.9 us (level)
  no operation moved by 1% of the time
where the time goes in v14:
time: 76.9 us; the launch traced here: 76.5 us
  starting transfers between devices  32.7 us (43%)
  blocking collectives  32.6 us (42%)
  Pallas kernels  8.79 us (11%)
  waiting for transfers between devices  1.6 us (2%)
    ppermute x4, starting transfers between devices, across(): return lax.ppermute(block, axis, up + [(b, a) for a, b in up])  16.4 us
    all_to_all x1, starting transfers between devices, body(): parts = lax.all_to_all(partial, 'lat', 0, 0, tiled=True)  16.3 us
    all_to_all x1, blocking collectives, body(): visitors = lax.all_to_all(packed, 'ens', 0, 0, tiled=True)  12.6 us
    all_to_all x1, blocking collectives, body(): spread = lax.all_to_all(spread, 'ens', 0, 0, tiled=True)  10 us
    all_to_all x1, blocking collectives, body(): sums = lax.all_to_all(sums, 'ens', 0, 0, tiled=True)  9.95 us
    pallas_call x1, Pallas kernels, body(): call(functools.partial(prepare, rows, lat_count), (jax.ShapeDtypeStruct((...  1.93 us
  transfers between devices with their start and end apart: 5, of which 2 were waited for; matrix products, arithmetic and copies ran while one was open for 0% of the time, Pallas kernels for 6%

profile of v14, /device:TPU:1, one launch (start us, length us, event | category | flops | bytes accessed | tf_op | source)
XLA Modules:
  0.0 76.5 jit_solution(12284590938550959778)
XLA Ops:
  0.6 1.0 %shard_map.86 = (bf16[2,256,128]{2,1,0:T(8,128)(2,1)S(1)}, bf16[2,256,128]{2,1,0:T(8,128)(2,1)S(1)}) custom-call(bf16[3,256,128]{2,1,0:T(8,128)(2,1)} %bitcast.6), custom_call_target="tpu_custom_call" | custom-call | bytes 500000 | tf_op jit(solution)/shard_map/pallas_call | solution.py:329
  1.6 6.0 %collective-permute-start = (bf16[2,256,128]{2,1,0:T(8,128)(2,1)S(1)}, bf16[2,256,128]{2,1,0:T(8,128)(2,1)S(1)}, u32[]{:S(2)}, u32[]{:S(2)}) collective-permute-start(bf16[2,256,128]{2,1,0:T(8,128)(2,1)S(1)} %get-tuple-element.22), channel_id=1, source_target_pairs={{1,2},{3,4},{5,6},{7,8},{9,10},{11,12},{13,14},{15,16},{17,18},{19... | collective-permute-start | bytes 393224 | tf_op jit(solution)/shard_map/ppermute | solution.py:308
  7.7 3.4 %collective-permute-start.1 = (bf16[2,256,128]{2,1,0:T(8,128)(2,1)S(1)}, bf16[2,256,128]{2,1,0:T(8,128)(2,1)S(1)}, u32[]{:S(2)}, u32[]{:S(2)}) collective-permute-start(bf16[2,256,128]{2,1,0:T(8,128)(2,1)S(1)} %get-tuple-element.23), channel_id=1, source_target_pairs={{0,1},{2,3},{4,5},{6,7},{8,9},{10,11},{12,13},{14,15},{16,17},{18,... | collective-permute-start | bytes 393224 | tf_op jit(solution)/shard_map/ppermute | solution.py:308
  11.1 1.9 %shard_map.87 = (bf16[3,640,384]{2,1,0:T(8,128)(2,1)S(1)}, bf16[3,384,256]{2,1,0:T(8,128)(2,1)S(1)}, bf16[80,1024]{1,0:T(8,128)(2,1)S(1)}, bf16[3,256,128]{2,1,0:T(8,128)(2,1)S(1)}, bf16[3,256,256]{2,1,0:T(8,128)(2,1)S(1)}) custom-call(f32[10,3,96]{2,1,0:T(4,128)} %bitcast.10, s32[10,96]{1,0:T(8,128)} %bitcast.12, bf16[3,256,256]{2,1,0:T(8,128)(2,1)} %filters.1, ...), custom_call_target="tpu_custom_call" | custom-call | flops 30000000 | bytes 2000000 | tf_op jit(solution)/shard_map/pallas_call | solution.py:331
  13.1 0.5 shard_map.88
  13.6 0.0 collective-permute-done.cross
  13.6 0.0 collective-permute-done.1.chip
  13.6 0.0 copy-start
  13.6 0.0 copy-start.1
  13.7 0.8 %shard_map.89 = (bf16[16,16,128]{2,1,0:T(8,128)(2,1)S(1)}, f32[3,80,128]{2,1,0:T(8,128)S(1)}, bf16[3,768,128]{2,1,0:T(8,128)(2,1)S(1)}) custom-call(bf16[2,256,128]{2,1,0:T(8,128)(2,1)S(1)} %collective-permute-done.cross, bf16[2,256,128]{2,1,0:T(8,128)(2,1)S(1)} %collective-permute-done.1.chip, f32[3,256,384]{2,1,0:T(8,128)S(1)} %get-tuple-element.27.begun, ...), custom_call_target="tpu_custom_call" | custom-call | flops 200000000 | bytes 3000000 | tf_op jit(solution)/shard_map/pallas_call | solution.py:357
  14.5 12.6 %all_to_all.20.visitors = bf16[16,16,128]{2,1,0:T(8,128)(2,1)S(1)} all-to-all(bf16[16,16,128]{2,1,0:T(8,128)(2,1)S(1)} %get-tuple-element.29), channel_id=1, replica_groups=mesh['ens'=16,'lat'=32] {'ens'}, dimensions={0} | all-to-all | bytes 131072 | tf_op jit(solution)/shard_map/all_to_all | solution.py:368
  27.1 0.2 shard_map.90
  27.4 10.0 %all_to_all.21.sums = bf16[16,16,128]{2,1,0:T(8,128)(2,1)S(1)} all-to-all(bf16[16,16,128]{2,1,0:T(8,128)(2,1)S(1)} %shard_map.90), channel_id=1, replica_groups=mesh['ens'=16,'lat'=32] {'ens'}, dimensions={0} | all-to-all | bytes 131072 | tf_op jit(solution)/shard_map/all_to_all | solution.py:370
  37.3 0.0 copy-done
  37.3 0.0 copy-done.1
  37.3 1.1 %shard_map.91 = (bf16[3,80,128]{2,1,0:T(8,128)(2,1)S(1)}, bf16[2,80,128]{2,1,0:T(8,128)(2,1)S(1)}, bf16[2,80,128]{2,1,0:T(8,128)(2,1)S(1)}, bf16[32,16,128]{2,1,0:T(8,128)(2,1)}) custom-call(f32[96,128]{1,0:T(8,128)S(1)} %copy-done.1, bf16[16,16,128]{2,1,0:T(8,128)(2,1)S(1)} %all_to_all.21.sums, f32[3,80,128]{2,1,0:T(8,128)S(1)} %get-tuple-element.30.predicted, ...), custom_call_target="tpu_custom_call" | custom-call | flops 80000000 | bytes 1200000 | tf_op jit(solution)/shard_map/pallas_call | solution.py:373
  38.4 16.3 %all-to-all-start.2 = ((bf16[32,16,128]{2,1,0:T(8,128)(2,1)}), bf16[32,16,128]{2,1,0:T(8,128)(2,1)S(1)}, u32[]{:S(2)}, u32[]{:S(2)}) async-start(bf16[32,16,128]{2,1,0:T(8,128)(2,1)} %get-tuple-element.32), calls=%async_computation.2 | async-start | bytes 262144 | tf_op jit(solution)/shard_map/all_to_all | solution.py:385
  54.7 5.0 %collective-permute-start.2 = (bf16[2,80,128]{2,1,0:T(8,128)(2,1)S(1)}, bf16[2,80,128]{2,1,0:T(8,128)(2,1)S(1)}, u32[]{:S(2)}, u32[]{:S(2)}) collective-permute-start(bf16[2,80,128]{2,1,0:T(8,128)(2,1)S(1)} %get-tuple-element.34), channel_id=1, source_target_pairs={{1,2},{3,4},{5,6},{7,8},{9,10},{11,12},{13,14},{15,16},{17,18},{19... | collective-permute-start | bytes 122888 | tf_op jit(solution)/shard_map/ppermute | solution.py:308
  59.8 1.9 %collective-permute-start.3 = (bf16[2,80,128]{2,1,0:T(8,128)(2,1)S(1)}, bf16[2,80,128]{2,1,0:T(8,128)(2,1)S(1)}, u32[]{:S(2)}, u32[]{:S(2)}) collective-permute-start(bf16[2,80,128]{2,1,0:T(8,128)(2,1)S(1)} %get-tuple-element.35), channel_id=1, source_target_pairs={{0,1},{2,3},{4,5},{6,7},{8,9},{10,11},{12,13},{14,15},{16,17},{18,... | collective-permute-start | bytes 122888 | tf_op jit(solution)/shard_map/ppermute | solution.py:308
  61.7 0.7 shard_map.92
  62.4 0.0 collective-permute-done.2.cross
  62.4 0.5 collective-permute-done.3.chip
  62.9 1.5 %shard_map.93 = bf16[3,256,128]{2,1,0:T(8,128)(2,1)} custom-call(bf16[3,80,128]{2,1,0:T(8,128)(2,1)S(1)} %get-tuple-element.33.pred_grad, bf16[2,80,128]{2,1,0:T(8,128)(2,1)S(1)} %collective-permute-done.2.cross, bf16[2,80,128]{2,1,0:T(8,128)(2,1)S(1)} %collective-permute-done.3.chip, f32[3,80,384]{2,1,0:T(8,128)S(1)} %get-tuple-element.37.turned, ...), custom_call_target="tpu_custom_call" | custom-call | flops 150000000 | bytes 1500000 | tf_op jit(solution)/shard_map/pallas_call | solution.py:397
  64.4 1.1 %all-to-all-done.2.parts = bf16[32,16,128]{2,1,0:T(8,128)(2,1)S(1)} async-done(((bf16[32,16,128]{2,1,0:T(8,128)(2,1)}), bf16[32,16,128]{2,1,0:T(8,128)(2,1)S(1)}, u32[]{:S(2)}, u32[]{:S(2)}) %all-to-all-start.2) | async-done | bytes 131104 | tf_op jit(solution)/shard_map/all_to_all | solution.py:385
  65.5 0.3 shard_map.94
  65.8 10.0 %all_to_all.22.parts = bf16[16,16,128]{2,1,0:T(8,128)(2,1)S(1)} all-to-all(bf16[16,16,128]{2,1,0:T(8,128)(2,1)S(1)} %shard_map.94), channel_id=1, replica_groups=mesh['ens'=16,'lat'=32] {'ens'}, dimensions={0} | all-to-all | bytes 131072 | tf_op jit(solution)/shard_map/all_to_all | solution.py:416
  75.8 0.7 shard_map.95
Async XLA Ops:
  1.6 12.0 %collective-permute-start = (bf16[2,256,128]{2,1,0:T(8,128)(2,1)S(1)}, bf16[2,256,128]{2,1,0:T(8,128)(2,1)S(1)}, u32[]{:S(2)}, u32[]{:S(2)}) collective-permute-start(bf16[2,256,128]{2,1,0:T(8,128)(2,1)S(1)} %get-tuple-element.22), channel_id=1, source_target_pairs={{1,2},{3,4},{5,6},{7,8},{9,10},{11,12},{13,14},{15,16},{17,18},{19... | collective-permute-start | bytes 393224 | tf_op jit(solution)/shard_map/ppermute | solution.py:308
  7.7 5.9 %collective-permute-start.1 = (bf16[2,256,128]{2,1,0:T(8,128)(2,1)S(1)}, bf16[2,256,128]{2,1,0:T(8,128)(2,1)S(1)}, u32[]{:S(2)}, u32[]{:S(2)}) collective-permute-start(bf16[2,256,128]{2,1,0:T(8,128)(2,1)S(1)} %get-tuple-element.23), channel_id=1, source_target_pairs={{0,1},{2,3},{4,5},{6,7},{8,9},{10,11},{12,13},{14,15},{16,17},{18,... | collective-permute-start | bytes 393224 | tf_op jit(solution)/shard_map/ppermute | solution.py:308
  13.6 23.7 %copy-start = (bf16[3,72,128]{2,1,0:T(8,128)(2,1)S(1)}, bf16[3,72,128]{2,1,0:T(8,128)(2,1)}, u32[]{:S(2)}) copy-start(bf16[3,72,128]{2,1,0:T(8,128)(2,1)} %target.1) | copy-start | bytes 165892
  13.6 23.7 %copy-start.1 = (f32[96,128]{1,0:T(8,128)S(1)}, f32[96,128]{1,0:T(8,128)}, u32[]{:S(2)}) copy-start(f32[96,128]{1,0:T(8,128)} %constant.2.clone.area) | copy-start | bytes 147460
  38.4 27.1 %all-to-all-start.2 = ((bf16[32,16,128]{2,1,0:T(8,128)(2,1)}), bf16[32,16,128]{2,1,0:T(8,128)(2,1)S(1)}, u32[]{:S(2)}, u32[]{:S(2)}) async-start(bf16[32,16,128]{2,1,0:T(8,128)(2,1)} %get-tuple-element.32), calls=%async_computation.2 | async-start | bytes 262144 | tf_op jit(solution)/shard_map/all_to_all | solution.py:385
  54.7 7.7 %collective-permute-start.2 = (bf16[2,80,128]{2,1,0:T(8,128)(2,1)S(1)}, bf16[2,80,128]{2,1,0:T(8,128)(2,1)S(1)}, u32[]{:S(2)}, u32[]{:S(2)}) collective-permute-start(bf16[2,80,128]{2,1,0:T(8,128)(2,1)S(1)} %get-tuple-element.34), channel_id=1, source_target_pairs={{1,2},{3,4},{5,6},{7,8},{9,10},{11,12},{13,14},{15,16},{17,18},{19... | collective-permute-start | bytes 122888 | tf_op jit(solution)/shard_map/ppermute | solution.py:308
  59.8 3.1 %collective-permute-start.3 = (bf16[2,80,128]{2,1,0:T(8,128)(2,1)S(1)}, bf16[2,80,128]{2,1,0:T(8,128)(2,1)S(1)}, u32[]{:S(2)}, u32[]{:S(2)}) collective-permute-start(bf16[2,80,128]{2,1,0:T(8,128)(2,1)S(1)} %get-tuple-element.35), channel_id=1, source_target_pairs={{0,1},{2,3},{4,5},{6,7},{8,9},{10,11},{12,13},{14,15},{16,17},{18,... | collective-permute-start | bytes 122888 | tf_op jit(solution)/shard_map/ppermute | solution.py:308

commit v15 on v13

--- a/solution.py
+++ b/solution.py
@@ -36,7 +36,7 @@
         kernel,
         out_shape=out,
         in_specs=specs,
-        out_specs=tuple([home] * len(out)) if many else home,
+        out_specs=tuple(home if isinstance(home, list) else [home] * len(out)) if many else home,
         scratch_shapes=list(scratch),
         compiler_params=pltpu.CompilerParams(vmem_limit_bytes=32 * 2**20),
         cost_estimate=pl.CostEstimate(flops=flops, bytes_accessed=moved, transcendentals=0),
@@ -177,7 +177,7 @@
         sums[m] = jnp.concatenate([totals[m] for totals in pieces], axis=0).astype(BF)
 
 
-def gradient(rows, kernels, members, area, sums, predicted, target, mixed, pred_grad, cross, chip, partial):
+def gradient(rows, kernels, members, area, sums, predicted, target, mixed, pred_grad, cross, chip, partial, buffer, sems):
     variables = target.shape[1]
     padded = predicted.shape[1]
     per = sums.shape[1]
@@ -210,9 +210,18 @@
     lower = jnp.where(lane < variables, second, tail)
     owners = partial.shape[0]
     own = chan // owners
-    for owner in range(owners):
-        mine = slice(owner * own, (owner + 1) * own)
-        partial[owner] = jnp.concatenate([upper[mine], lower[mine]], axis=0).astype(BF)
+    groups = sems.shape[0]
+    size = owners // groups
+    moves = []
+    for group in range(groups):
+        for owner in range(group * size, (group + 1) * size):
+            mine = slice(owner * own, (owner + 1) * own)
+            buffer[owner] = jnp.concatenate([upper[mine], lower[mine]], axis=0).astype(BF)
+        part = pl.ds(group * size, size)
+        moves.append(pltpu.make_async_copy(buffer.at[part], partial.at[part], sems.at[group]))
+        moves[-1].start()
+    for move in moves:
+        move.wait()
 
 
 def band_sum(factor, variables, padded, parts, w_bwd, spread):
@@ -380,6 +389,8 @@
         [VMEM] * 5,
         80_000_000,
         1_200_000,
+        [pltpu.VMEM((bands, 2 * own, lon), BF), pltpu.SemaphoreType.DMA((4,))],
+        [VMEM, VMEM, VMEM, hbm],
     )(area, sums, predicted, target_fields, mixed)
     parts = lax.all_to_all(partial, "lat", 0, 0, tiled=True)
     cross, chip = across(cross, "lat", 1), across(chip, "lat", 0)

time: 76.9 us -> 76.9 us (level)
  no operation moved by 1% of the time
where the time goes in v15:
time: 76.9 us; the launch traced here: 76.5 us
  starting transfers between devices  32.6 us (42%)
  blocking collectives  32.6 us (42%)
  Pallas kernels  8.83 us (11%)
  waiting for transfers between devices  1.74 us (2%)
    ppermute x4, starting transfers between devices, across(): return lax.ppermute(block, axis, up + [(b, a) for a, b in up])  16.4 us
    all_to_all x1, starting transfers between devices, body(): parts = lax.all_to_all(partial, 'lat', 0, 0, tiled=True)  16.1 us
    all_to_all x1, blocking collectives, body(): visitors = lax.all_to_all(packed, 'ens', 0, 0, tiled=True)  12.6 us
    all_to_all x1, blocking collectives, body(): spread = lax.all_to_all(spread, 'ens', 0, 0, tiled=True)  10 us
    all_to_all x1, blocking collectives, body(): sums = lax.all_to_all(sums, 'ens', 0, 0, tiled=True)  9.95 us
    pallas_call x1, Pallas kernels, body(): call(functools.partial(prepare, rows, lat_count), (jax.ShapeDtypeStruct((...  2.09 us
  transfers between devices with their start and end apart: 5, of which 2 were waited for; matrix products, arithmetic and copies ran while one was open for 0% of the time, Pallas kernels for 6%

profile of v15, /device:TPU:1, one launch (start us, length us, event | category | flops | bytes accessed | tf_op | source)
XLA Modules:
  0.0 76.5 jit_solution(11937358183521954740)
XLA Ops:
  0.6 1.0 %shard_map.86 = (bf16[2,256,128]{2,1,0:T(8,128)(2,1)S(1)}, bf16[2,256,128]{2,1,0:T(8,128)(2,1)S(1)}) custom-call(bf16[3,256,128]{2,1,0:T(8,128)(2,1)} %bitcast.6), custom_call_target="tpu_custom_call" | custom-call | bytes 500000 | tf_op jit(solution)/shard_map/pallas_call | solution.py:336
  1.6 6.0 %collective-permute-start = (bf16[2,256,128]{2,1,0:T(8,128)(2,1)S(1)}, bf16[2,256,128]{2,1,0:T(8,128)(2,1)S(1)}, u32[]{:S(2)}, u32[]{:S(2)}) collective-permute-start(bf16[2,256,128]{2,1,0:T(8,128)(2,1)S(1)} %get-tuple-element.20), channel_id=1, source_target_pairs={{1,2},{3,4},{5,6},{7,8},{9,10},{11,12},{13,14},{15,16},{17,18},{19... | collective-permute-start | bytes 393224 | tf_op jit(solution)/shard_map/ppermute | solution.py:315
  7.7 3.4 %collective-permute-start.1 = (bf16[2,256,128]{2,1,0:T(8,128)(2,1)S(1)}, bf16[2,256,128]{2,1,0:T(8,128)(2,1)S(1)}, u32[]{:S(2)}, u32[]{:S(2)}) collective-permute-start(bf16[2,256,128]{2,1,0:T(8,128)(2,1)S(1)} %get-tuple-element.21), channel_id=1, source_target_pairs={{0,1},{2,3},{4,5},{6,7},{8,9},{10,11},{12,13},{14,15},{16,17},{18,... | collective-permute-start | bytes 393224 | tf_op jit(solution)/shard_map/ppermute | solution.py:315
  11.1 2.1 %shard_map.87 = (bf16[3,640,384]{2,1,0:T(8,128)(2,1)S(1)}, bf16[3,384,256]{2,1,0:T(8,128)(2,1)S(1)}, bf16[80,1024]{1,0:T(8,128)(2,1)S(1)}, bf16[256,320]{1,0:T(8,128)(2,1)S(1)}, bf16[3,256,128]{2,1,0:T(8,128)(2,1)S(1)}) custom-call(f32[10,3,96]{2,1,0:T(4,128)} %bitcast.10, s32[10,96]{1,0:T(8,128)} %bitcast.12, bf16[3,256,256]{2,1,0:T(8,128)(2,1)} %filters.1, ...), custom_call_target="tpu_custom_call" | custom-call | flops 30000000 | bytes 2000000 | tf_op jit(solution)/shard_map/pallas_call | solution.py:338
  13.2 0.5 shard_map.88
  13.8 0.0 collective-permute-done.cross
  13.8 0.0 collective-permute-done.1.chip
  13.8 0.0 copy-start
  13.8 0.0 copy-start.1
  13.8 0.8 %shard_map.89 = (bf16[16,16,128]{2,1,0:T(8,128)(2,1)S(1)}, f32[3,80,128]{2,1,0:T(8,128)S(1)}, bf16[3,768,128]{2,1,0:T(8,128)(2,1)S(1)}) custom-call(bf16[2,256,128]{2,1,0:T(8,128)(2,1)S(1)} %collective-permute-done.cross, bf16[2,256,128]{2,1,0:T(8,128)(2,1)S(1)} %collective-permute-done.1.chip, f32[3,256,384]{2,1,0:T(8,128)S(1)} %get-tuple-element.25.begun, ...), custom_call_target="tpu_custom_call" | custom-call | flops 200000000 | bytes 3000000 | tf_op jit(solution)/shard_map/pallas_call | solution.py:365
  14.7 12.6 %all_to_all.20.visitors = bf16[16,16,128]{2,1,0:T(8,128)(2,1)S(1)} all-to-all(bf16[16,16,128]{2,1,0:T(8,128)(2,1)S(1)} %get-tuple-element.27), channel_id=1, replica_groups=mesh['ens'=16,'lat'=32] {'ens'}, dimensions={0} | all-to-all | bytes 131072 | tf_op jit(solution)/shard_map/all_to_all | solution.py:376
  27.3 0.2 shard_map.90
  27.5 10.0 %all_to_all.21.sums = bf16[16,16,128]{2,1,0:T(8,128)(2,1)S(1)} all-to-all(bf16[16,16,128]{2,1,0:T(8,128)(2,1)S(1)} %shard_map.90), channel_id=1, replica_groups=mesh['ens'=16,'lat'=32] {'ens'}, dimensions={0} | all-to-all | bytes 131072 | tf_op jit(solution)/shard_map/all_to_all | solution.py:378
  37.5 0.0 copy-done
  37.5 0.0 copy-done.1
  37.5 1.1 %shard_map.91 = (bf16[3,80,128]{2,1,0:T(8,128)(2,1)S(1)}, bf16[2,80,128]{2,1,0:T(8,128)(2,1)S(1)}, bf16[2,80,128]{2,1,0:T(8,128)(2,1)S(1)}, bf16[32,16,128]{2,1,0:T(8,128)(2,1)}) custom-call(f32[96,128]{1,0:T(8,128)S(1)} %copy-done.1, bf16[16,16,128]{2,1,0:T(8,128)(2,1)S(1)} %all_to_all.21.sums, f32[3,80,128]{2,1,0:T(8,128)S(1)} %get-tuple-element.28.predicted, ...), custom_call_target="tpu_custom_call" | custom-call | flops 80000000 | bytes 1200000 | tf_op jit(solution)/shard_map/pallas_call | solution.py:381
  38.6 16.1 %all-to-all-start.2 = ((bf16[32,16,128]{2,1,0:T(8,128)(2,1)}), bf16[32,16,128]{2,1,0:T(8,128)(2,1)S(1)}, u32[]{:S(2)}, u32[]{:S(2)}) async-start(bf16[32,16,128]{2,1,0:T(8,128)(2,1)} %get-tuple-element.30), calls=%async_computation.2 | async-start | bytes 262144 | tf_op jit(solution)/shard_map/all_to_all | solution.py:395
  54.7 5.0 %collective-permute-start.2 = (bf16[2,80,128]{2,1,0:T(8,128)(2,1)S(1)}, bf16[2,80,128]{2,1,0:T(8,128)(2,1)S(1)}, u32[]{:S(2)}, u32[]{:S(2)}) collective-permute-start(bf16[2,80,128]{2,1,0:T(8,128)(2,1)S(1)} %get-tuple-element.32), channel_id=1, source_target_pairs={{1,2},{3,4},{5,6},{7,8},{9,10},{11,12},{13,14},{15,16},{17,18},{19... | collective-permute-start | bytes 122888 | tf_op jit(solution)/shard_map/ppermute | solution.py:315
  59.8 1.9 %collective-permute-start.3 = (bf16[2,80,128]{2,1,0:T(8,128)(2,1)S(1)}, bf16[2,80,128]{2,1,0:T(8,128)(2,1)S(1)}, u32[]{:S(2)}, u32[]{:S(2)}) collective-permute-start(bf16[2,80,128]{2,1,0:T(8,128)(2,1)S(1)} %get-tuple-element.33), channel_id=1, source_target_pairs={{0,1},{2,3},{4,5},{6,7},{8,9},{10,11},{12,13},{14,15},{16,17},{18,... | collective-permute-start | bytes 122888 | tf_op jit(solution)/shard_map/ppermute | solution.py:315
  61.7 0.5 shard_map.92.turned
  62.3 0.0 collective-permute-done.2.cross
  62.3 0.7 collective-permute-done.3.chip
  62.9 1.5 %shard_map.93 = bf16[3,256,128]{2,1,0:T(8,128)(2,1)} custom-call(bf16[3,80,128]{2,1,0:T(8,128)(2,1)S(1)} %get-tuple-element.31.pred_grad, bf16[2,80,128]{2,1,0:T(8,128)(2,1)S(1)} %collective-permute-done.2.cross, bf16[2,80,128]{2,1,0:T(8,128)(2,1)S(1)} %collective-permute-done.3.chip, f32[3,80,384]{2,1,0:T(8,128)S(1)} %shard_map.92.turned, ...), custom_call_target="tpu_custom_call" | custom-call | flops 150000000 | bytes 1500000 | tf_op jit(solution)/shard_map/pallas_call | solution.py:404
  64.4 1.1 %all-to-all-done.2.parts = bf16[32,16,128]{2,1,0:T(8,128)(2,1)S(1)} async-done(((bf16[32,16,128]{2,1,0:T(8,128)(2,1)}), bf16[32,16,128]{2,1,0:T(8,128)(2,1)S(1)}, u32[]{:S(2)}, u32[]{:S(2)}) %all-to-all-start.2) | async-done | bytes 131104 | tf_op jit(solution)/shard_map/all_to_all | solution.py:395
  65.5 0.3 shard_map.94
  65.8 10.0 %all_to_all.22.parts = bf16[16,16,128]{2,1,0:T(8,128)(2,1)S(1)} all-to-all(bf16[16,16,128]{2,1,0:T(8,128)(2,1)S(1)} %shard_map.94), channel_id=1, replica_groups=mesh['ens'=16,'lat'=32] {'ens'}, dimensions={0} | all-to-all | bytes 131072 | tf_op jit(solution)/shard_map/all_to_all | solution.py:423
  75.8 0.7 shard_map.95
Async XLA Ops:
  1.6 12.1 %collective-permute-start = (bf16[2,256,128]{2,1,0:T(8,128)(2,1)S(1)}, bf16[2,256,128]{2,1,0:T(8,128)(2,1)S(1)}, u32[]{:S(2)}, u32[]{:S(2)}) collective-permute-start(bf16[2,256,128]{2,1,0:T(8,128)(2,1)S(1)} %get-tuple-element.20), channel_id=1, source_target_pairs={{1,2},{3,4},{5,6},{7,8},{9,10},{11,12},{13,14},{15,16},{17,18},{19... | collective-permute-start | bytes 393224 | tf_op jit(solution)/shard_map/ppermute | solution.py:315
  7.7 6.1 %collective-permute-start.1 = (bf16[2,256,128]{2,1,0:T(8,128)(2,1)S(1)}, bf16[2,256,128]{2,1,0:T(8,128)(2,1)S(1)}, u32[]{:S(2)}, u32[]{:S(2)}) collective-permute-start(bf16[2,256,128]{2,1,0:T(8,128)(2,1)S(1)} %get-tuple-element.21), channel_id=1, source_target_pairs={{0,1},{2,3},{4,5},{6,7},{8,9},{10,11},{12,13},{14,15},{16,17},{18,... | collective-permute-start | bytes 393224 | tf_op jit(solution)/shard_map/ppermute | solution.py:315
  13.8 23.7 %copy-start = (bf16[3,72,128]{2,1,0:T(8,128)(2,1)S(1)}, bf16[3,72,128]{2,1,0:T(8,128)(2,1)}, u32[]{:S(2)}) copy-start(bf16[3,72,128]{2,1,0:T(8,128)(2,1)} %target.1) | copy-start | bytes 165892
  13.8 23.7 %copy-start.1 = (f32[96,128]{1,0:T(8,128)S(1)}, f32[96,128]{1,0:T(8,128)}, u32[]{:S(2)}) copy-start(f32[96,128]{1,0:T(8,128)} %constant.2.clone.area) | copy-start | bytes 147460
  38.6 26.9 %all-to-all-start.2 = ((bf16[32,16,128]{2,1,0:T(8,128)(2,1)}), bf16[32,16,128]{2,1,0:T(8,128)(2,1)S(1)}, u32[]{:S(2)}, u32[]{:S(2)}) async-start(bf16[32,16,128]{2,1,0:T(8,128)(2,1)} %get-tuple-element.30), calls=%async_computation.2 | async-start | bytes 262144 | tf_op jit(solution)/shard_map/all_to_all | solution.py:395
  54.7 7.5 %collective-permute-start.2 = (bf16[2,80,128]{2,1,0:T(8,128)(2,1)S(1)}, bf16[2,80,128]{2,1,0:T(8,128)(2,1)S(1)}, u32[]{:S(2)}, u32[]{:S(2)}) collective-permute-start(bf16[2,80,128]{2,1,0:T(8,128)(2,1)S(1)} %get-tuple-element.32), channel_id=1, source_target_pairs={{1,2},{3,4},{5,6},{7,8},{9,10},{11,12},{13,14},{15,16},{17,18},{19... | collective-permute-start | bytes 122888 | tf_op jit(solution)/shard_map/ppermute | solution.py:315
  59.8 3.1 %collective-permute-start.3 = (bf16[2,80,128]{2,1,0:T(8,128)(2,1)S(1)}, bf16[2,80,128]{2,1,0:T(8,128)(2,1)S(1)}, u32[]{:S(2)}, u32[]{:S(2)}) collective-permute-start(bf16[2,80,128]{2,1,0:T(8,128)(2,1)S(1)} %get-tuple-element.33), channel_id=1, source_target_pairs={{0,1},{2,3},{4,5},{6,7},{8,9},{10,11},{12,13},{14,15},{16,17},{18,... | collective-permute-start | bytes 122888 | tf_op jit(solution)/shard_map/ppermute | solution.py:315

commit v16 on v14

--- a/solution.py
+++ b/solution.py
@@ -36,7 +36,7 @@
         kernel,
         out_shape=out,
         in_specs=specs,
-        out_specs=tuple([home] * len(out)) if many else home,
+        out_specs=tuple(home if isinstance(home, list) else [home] * len(out)) if many else home,
         scratch_shapes=list(scratch),
         compiler_params=pltpu.CompilerParams(vmem_limit_bytes=32 * 2**20),
         cost_estimate=pl.CostEstimate(flops=flops, bytes_accessed=moved, transcendentals=0),
@@ -172,7 +172,7 @@
         sums[m] = jnp.concatenate([totals[m] for totals in pieces], axis=0).astype(BF)
 
 
-def gradient(rows, kernels, members, area, sums, predicted, target, mixed, pred_grad, cross, chip, partial):
+def gradient(rows, kernels, members, area, sums, predicted, target, mixed, pred_grad, cross, chip, partial, buffer, sems):
     variables = target.shape[1]
     padded = predicted.shape[1]
     per = sums.shape[1]
@@ -205,9 +205,18 @@
     lower = jnp.where(lane < variables, second, tail)
     owners = partial.shape[0]
     own = chan // owners
-    for owner in range(owners):
-        mine = slice(owner * own, (owner + 1) * own)
-        partial[owner] = jnp.concatenate([upper[mine], lower[mine]], axis=0).astype(BF)
+    groups = sems.shape[0]
+    size = owners // groups
+    moves = []
+    for group in range(groups):
+        for owner in range(group * size, (group + 1) * size):
+            mine = slice(owner * own, (owner + 1) * own)
+            buffer[owner] = jnp.concatenate([upper[mine], lower[mine]], axis=0).astype(BF)
+        part = pl.ds(group * size, size)
+        moves.append(pltpu.make_async_copy(buffer.at[part], partial.at[part], sems.at[group]))
+        moves[-1].start()
+    for move in moves:
+        move.wait()
 
 
 def band_sum(factor, variables, padded, parts, w_bwd, spread):
@@ -381,6 +390,8 @@
         [VMEM] * 5,
         80_000_000,
         1_200_000,
+        [pltpu.VMEM((bands, 2 * own, lon), BF), pltpu.SemaphoreType.DMA((4,))],
+        [VMEM, VMEM, VMEM, hbm],
     )(area, sums, predicted, target_fields, mixed)
     parts = lax.all_to_all(partial, "lat", 0, 0, tiled=True)
     cross, chip = across(cross, "lat", 1), across(chip, "lat", 0)

time: 76.9 us -> 76.9 us (level)
  no operation moved by 1% of the time
where the time goes in v16:
time: 76.9 us; the launch traced here: 76.5 us
  starting transfers between devices  32.7 us (43%)
  blocking collectives  32.6 us (42%)
  Pallas kernels  8.81 us (11%)
  waiting for transfers between devices  1.6 us (2%)
    ppermute x4, starting transfers between devices, across(): return lax.ppermute(block, axis, up + [(b, a) for a, b in up])  16.4 us
    all_to_all x1, starting transfers between devices, body(): parts = lax.all_to_all(partial, 'lat', 0, 0, tiled=True)  16.3 us
    all_to_all x1, blocking collectives, body(): visitors = lax.all_to_all(packed, 'ens', 0, 0, tiled=True)  12.6 us
    all_to_all x1, blocking collectives, body(): spread = lax.all_to_all(spread, 'ens', 0, 0, tiled=True)  10 us
    all_to_all x1, blocking collectives, body(): sums = lax.all_to_all(sums, 'ens', 0, 0, tiled=True)  9.95 us
    pallas_call x1, Pallas kernels, body(): call(functools.partial(prepare, rows, lat_count), (jax.ShapeDtypeStruct((...  1.93 us
  transfers between devices with their start and end apart: 5, of which 2 were waited for; matrix products, arithmetic and copies ran while one was open for 0% of the time, Pallas kernels for 6%

profile of v16, /device:TPU:1, one launch (start us, length us, event | category | flops | bytes accessed | tf_op | source)
XLA Modules:
  0.0 76.5 jit_solution(6751093026148149048)
XLA Ops:
  0.6 1.0 %shard_map.86 = (bf16[2,256,128]{2,1,0:T(8,128)(2,1)S(1)}, bf16[2,256,128]{2,1,0:T(8,128)(2,1)S(1)}) custom-call(bf16[3,256,128]{2,1,0:T(8,128)(2,1)} %bitcast.6), custom_call_target="tpu_custom_call" | custom-call | bytes 500000 | tf_op jit(solution)/shard_map/pallas_call | solution.py:338
  1.6 6.0 %collective-permute-start = (bf16[2,256,128]{2,1,0:T(8,128)(2,1)S(1)}, bf16[2,256,128]{2,1,0:T(8,128)(2,1)S(1)}, u32[]{:S(2)}, u32[]{:S(2)}) collective-permute-start(bf16[2,256,128]{2,1,0:T(8,128)(2,1)S(1)} %get-tuple-element.22), channel_id=1, source_target_pairs={{1,2},{3,4},{5,6},{7,8},{9,10},{11,12},{13,14},{15,16},{17,18},{19... | collective-permute-start | bytes 393224 | tf_op jit(solution)/shard_map/ppermute | solution.py:317
  7.7 3.4 %collective-permute-start.1 = (bf16[2,256,128]{2,1,0:T(8,128)(2,1)S(1)}, bf16[2,256,128]{2,1,0:T(8,128)(2,1)S(1)}, u32[]{:S(2)}, u32[]{:S(2)}) collective-permute-start(bf16[2,256,128]{2,1,0:T(8,128)(2,1)S(1)} %get-tuple-element.23), channel_id=1, source_target_pairs={{0,1},{2,3},{4,5},{6,7},{8,9},{10,11},{12,13},{14,15},{16,17},{18,... | collective-permute-start | bytes 393224 | tf_op jit(solution)/shard_map/ppermute | solution.py:317
  11.1 1.9 %shard_map.87 = (bf16[3,640,384]{2,1,0:T(8,128)(2,1)S(1)}, bf16[3,384,256]{2,1,0:T(8,128)(2,1)S(1)}, bf16[80,1024]{1,0:T(8,128)(2,1)S(1)}, bf16[3,256,128]{2,1,0:T(8,128)(2,1)S(1)}, bf16[3,256,256]{2,1,0:T(8,128)(2,1)S(1)}) custom-call(f32[10,3,96]{2,1,0:T(4,128)} %bitcast.10, s32[10,96]{1,0:T(8,128)} %bitcast.12, bf16[3,256,256]{2,1,0:T(8,128)(2,1)} %filters.1, ...), custom_call_target="tpu_custom_call" | custom-call | flops 30000000 | bytes 2000000 | tf_op jit(solution)/shard_map/pallas_call | solution.py:340
  13.1 0.5 shard_map.88
  13.6 0.0 collective-permute-done.cross
  13.6 0.0 collective-permute-done.1.chip
  13.6 0.0 copy-start
  13.6 0.0 copy-start.1
  13.7 0.8 %shard_map.89 = (bf16[16,16,128]{2,1,0:T(8,128)(2,1)S(1)}, f32[3,80,128]{2,1,0:T(8,128)S(1)}, bf16[3,768,128]{2,1,0:T(8,128)(2,1)S(1)}) custom-call(bf16[2,256,128]{2,1,0:T(8,128)(2,1)S(1)} %collective-permute-done.cross, bf16[2,256,128]{2,1,0:T(8,128)(2,1)S(1)} %collective-permute-done.1.chip, f32[3,256,384]{2,1,0:T(8,128)S(1)} %get-tuple-element.27.begun, ...), custom_call_target="tpu_custom_call" | custom-call | flops 200000000 | bytes 3000000 | tf_op jit(solution)/shard_map/pallas_call | solution.py:366
  14.5 12.6 %all_to_all.20.visitors = bf16[16,16,128]{2,1,0:T(8,128)(2,1)S(1)} all-to-all(bf16[16,16,128]{2,1,0:T(8,128)(2,1)S(1)} %get-tuple-element.29), channel_id=1, replica_groups=mesh['ens'=16,'lat'=32] {'ens'}, dimensions={0} | all-to-all | bytes 131072 | tf_op jit(solution)/shard_map/all_to_all | solution.py:377
  27.1 0.2 shard_map.90
  27.4 10.0 %all_to_all.21.sums = bf16[16,16,128]{2,1,0:T(8,128)(2,1)S(1)} all-to-all(bf16[16,16,128]{2,1,0:T(8,128)(2,1)S(1)} %shard_map.90), channel_id=1, replica_groups=mesh['ens'=16,'lat'=32] {'ens'}, dimensions={0} | all-to-all | bytes 131072 | tf_op jit(solution)/shard_map/all_to_all | solution.py:379
  37.3 0.0 copy-done
  37.3 0.0 copy-done.1
  37.3 1.1 %shard_map.91 = (bf16[3,80,128]{2,1,0:T(8,128)(2,1)S(1)}, bf16[2,80,128]{2,1,0:T(8,128)(2,1)S(1)}, bf16[2,80,128]{2,1,0:T(8,128)(2,1)S(1)}, bf16[32,16,128]{2,1,0:T(8,128)(2,1)}) custom-call(f32[96,128]{1,0:T(8,128)S(1)} %copy-done.1, bf16[16,16,128]{2,1,0:T(8,128)(2,1)S(1)} %all_to_all.21.sums, f32[3,80,128]{2,1,0:T(8,128)S(1)} %get-tuple-element.30.predicted, ...), custom_call_target="tpu_custom_call" | custom-call | flops 80000000 | bytes 1200000 | tf_op jit(solution)/shard_map/pallas_call | solution.py:382
  38.4 16.3 %all-to-all-start.2 = ((bf16[32,16,128]{2,1,0:T(8,128)(2,1)}), bf16[32,16,128]{2,1,0:T(8,128)(2,1)S(1)}, u32[]{:S(2)}, u32[]{:S(2)}) async-start(bf16[32,16,128]{2,1,0:T(8,128)(2,1)} %get-tuple-element.32), calls=%async_computation.2 | async-start | bytes 262144 | tf_op jit(solution)/shard_map/all_to_all | solution.py:396
  54.7 5.0 %collective-permute-start.2 = (bf16[2,80,128]{2,1,0:T(8,128)(2,1)S(1)}, bf16[2,80,128]{2,1,0:T(8,128)(2,1)S(1)}, u32[]{:S(2)}, u32[]{:S(2)}) collective-permute-start(bf16[2,80,128]{2,1,0:T(8,128)(2,1)S(1)} %get-tuple-element.34), channel_id=1, source_target_pairs={{1,2},{3,4},{5,6},{7,8},{9,10},{11,12},{13,14},{15,16},{17,18},{19... | collective-permute-start | bytes 122888 | tf_op jit(solution)/shard_map/ppermute | solution.py:317
  59.8 1.9 %collective-permute-start.3 = (bf16[2,80,128]{2,1,0:T(8,128)(2,1)S(1)}, bf16[2,80,128]{2,1,0:T(8,128)(2,1)S(1)}, u32[]{:S(2)}, u32[]{:S(2)}) collective-permute-start(bf16[2,80,128]{2,1,0:T(8,128)(2,1)S(1)} %get-tuple-element.35), channel_id=1, source_target_pairs={{0,1},{2,3},{4,5},{6,7},{8,9},{10,11},{12,13},{14,15},{16,17},{18,... | collective-permute-start | bytes 122888 | tf_op jit(solution)/shard_map/ppermute | solution.py:317
  61.7 0.7 shard_map.92
  62.4 0.0 collective-permute-done.2.cross
  62.4 0.5 collective-permute-done.3.chip
  62.9 1.5 %shard_map.93 = bf16[3,256,128]{2,1,0:T(8,128)(2,1)} custom-call(bf16[3,80,128]{2,1,0:T(8,128)(2,1)S(1)} %get-tuple-element.33.pred_grad, bf16[2,80,128]{2,1,0:T(8,128)(2,1)S(1)} %collective-permute-done.2.cross, bf16[2,80,128]{2,1,0:T(8,128)(2,1)S(1)} %collective-permute-done.3.chip, f32[3,80,384]{2,1,0:T(8,128)S(1)} %get-tuple-element.37.turned, ...), custom_call_target="tpu_custom_call" | custom-call | flops 150000000 | bytes 1500000 | tf_op jit(solution)/shard_map/pallas_call | solution.py:408
  64.4 1.1 %all-to-all-done.2.parts = bf16[32,16,128]{2,1,0:T(8,128)(2,1)S(1)} async-done(((bf16[32,16,128]{2,1,0:T(8,128)(2,1)}), bf16[32,16,128]{2,1,0:T(8,128)(2,1)S(1)}, u32[]{:S(2)}, u32[]{:S(2)}) %all-to-all-start.2) | async-done | bytes 131104 | tf_op jit(solution)/shard_map/all_to_all | solution.py:396
  65.5 0.3 shard_map.94
  65.8 10.0 %all_to_all.22.parts = bf16[16,16,128]{2,1,0:T(8,128)(2,1)S(1)} all-to-all(bf16[16,16,128]{2,1,0:T(8,128)(2,1)S(1)} %shard_map.94), channel_id=1, replica_groups=mesh['ens'=16,'lat'=32] {'ens'}, dimensions={0} | all-to-all | bytes 131072 | tf_op jit(solution)/shard_map/all_to_all | solution.py:427
  75.8 0.7 shard_map.95
Async XLA Ops:
  1.6 12.0 %collective-permute-start = (bf16[2,256,128]{2,1,0:T(8,128)(2,1)S(1)}, bf16[2,256,128]{2,1,0:T(8,128)(2,1)S(1)}, u32[]{:S(2)}, u32[]{:S(2)}) collective-permute-start(bf16[2,256,128]{2,1,0:T(8,128)(2,1)S(1)} %get-tuple-element.22), channel_id=1, source_target_pairs={{1,2},{3,4},{5,6},{7,8},{9,10},{11,12},{13,14},{15,16},{17,18},{19... | collective-permute-start | bytes 393224 | tf_op jit(solution)/shard_map/ppermute | solution.py:317
  7.7 5.9 %collective-permute-start.1 = (bf16[2,256,128]{2,1,0:T(8,128)(2,1)S(1)}, bf16[2,256,128]{2,1,0:T(8,128)(2,1)S(1)}, u32[]{:S(2)}, u32[]{:S(2)}) collective-permute-start(bf16[2,256,128]{2,1,0:T(8,128)(2,1)S(1)} %get-tuple-element.23), channel_id=1, source_target_pairs={{0,1},{2,3},{4,5},{6,7},{8,9},{10,11},{12,13},{14,15},{16,17},{18,... | collective-permute-start | bytes 393224 | tf_op jit(solution)/shard_map/ppermute | solution.py:317
  13.6 23.7 %copy-start = (bf16[3,72,128]{2,1,0:T(8,128)(2,1)S(1)}, bf16[3,72,128]{2,1,0:T(8,128)(2,1)}, u32[]{:S(2)}) copy-start(bf16[3,72,128]{2,1,0:T(8,128)(2,1)} %target.1) | copy-start | bytes 165892
  13.6 23.7 %copy-start.1 = (f32[96,128]{1,0:T(8,128)S(1)}, f32[96,128]{1,0:T(8,128)}, u32[]{:S(2)}) copy-start(f32[96,128]{1,0:T(8,128)} %constant.2.clone.area) | copy-start | bytes 147460
  38.4 27.1 %all-to-all-start.2 = ((bf16[32,16,128]{2,1,0:T(8,128)(2,1)}), bf16[32,16,128]{2,1,0:T(8,128)(2,1)S(1)}, u32[]{:S(2)}, u32[]{:S(2)}) async-start(bf16[32,16,128]{2,1,0:T(8,128)(2,1)} %get-tuple-element.32), calls=%async_computation.2 | async-start | bytes 262144 | tf_op jit(solution)/shard_map/all_to_all | solution.py:396
  54.7 7.7 %collective-permute-start.2 = (bf16[2,80,128]{2,1,0:T(8,128)(2,1)S(1)}, bf16[2,80,128]{2,1,0:T(8,128)(2,1)S(1)}, u32[]{:S(2)}, u32[]{:S(2)}) collective-permute-start(bf16[2,80,128]{2,1,0:T(8,128)(2,1)S(1)} %get-tuple-element.34), channel_id=1, source_target_pairs={{1,2},{3,4},{5,6},{7,8},{9,10},{11,12},{13,14},{15,16},{17,18},{19... | collective-permute-start | bytes 122888 | tf_op jit(solution)/shard_map/ppermute | solution.py:317
  59.8 3.1 %collective-permute-start.3 = (bf16[2,80,128]{2,1,0:T(8,128)(2,1)S(1)}, bf16[2,80,128]{2,1,0:T(8,128)(2,1)S(1)}, u32[]{:S(2)}, u32[]{:S(2)}) collective-permute-start(bf16[2,80,128]{2,1,0:T(8,128)(2,1)S(1)} %get-tuple-element.35), channel_id=1, source_target_pairs={{0,1},{2,3},{4,5},{6,7},{8,9},{10,11},{12,13},{14,15},{16,17},{18,... | collective-permute-start | bytes 122888 | tf_op jit(solution)/shard_map/ppermute | solution.py:317
